TPU v7x, 32 devices: a whole 2x2x4 slice. The times are simulated.
32 devices in a mesh: slides: 2 (over x), cols: 8 (over z, y), rows: 2 (over core).
Axes of the slice: x: 2, y: 2, z: 4, core: 2. Of those that a mesh axis runs over, the one named last changes fastest.
Arguments:
- pixels: bfloat16 [3, 256, 8192], P(None, 'rows', ('slides', 'cols')), parts along dimension 2, may hold values from -6 to 6
- patch_weight: bfloat16 [24, 24, 3, 768], replicated, may hold values from -0.15625 to 0.15625
- patch_bias: float32 [768], replicated, may hold values from -3 to 3
- norm_gain: float32 [768], replicated, may hold values from 0.1 to 1.9
- gate_weight: bfloat16 [768, 1536], replicated, may hold values from -0.21875 to 0.21875
- mix_weight: bfloat16 [768, 1664], replicated, may hold values from -0.21875 to 0.21875
- step_weight: bfloat16 [768, 24], replicated, may hold values from -0.21875 to 0.21875
- step_bias: float32 [24], replicated, may hold values from -5 to -2
- log_rate: float32 [24], replicated, may hold values from -11 to 2
- conv_weight: float32 [4, 1664], replicated, may hold values from -3 to 3
- conv_bias: float32 [1664], replicated, may hold values from -3 to 3
- skip_gain: float32 [24], replicated, may hold values from 0.25 to 2
- out_gain: float32 [1536], replicated, may hold values from 0.1 to 1.9
- out_weight: bfloat16 [1536, 768], replicated, may hold values from -0.15625 to 0.15625
Outputs:
- layer_out: bfloat16 [8192, 768], P(('slides', 'cols', 'rows')), parts along dimension 0
There are 2 independent parts, one for each index of `slides`. A program takes and returns all parts, laid end to end along the dimension named above; an argument that names none is the same for every part. Nothing has to cross between parts.
All inputs are finite; a program needn't handle non-finite values.
Results may differ from a plain program's by a relative error of at most 0.011.
Values may be sent and summed in bfloat16 or wider, within the bound.
No kernel may reach another device: no remote copies, remote signals or barrier semaphores. Data moves between devices by JAX's collectives and lax.ppermute only.
A program may use at most 192 MiB of HBM per device.

v0:
```python
from functools import partial

import jax
import jax.numpy as jnp
from jax import lax
from jax.experimental import pallas as pl
from jax.experimental.pallas import tpu as pltpu
from jax.sharding import PartitionSpec as P


E = 1536
D = 768
HDIM = 64
NSTATE = 64
PATCH = 16
KERNEL = 24
HEADS = 24
CHAN = 3
MARGIN = (KERNEL - PATCH) // 2
WIN = CHAN * KERNEL
LEAD = 8
F32 = jnp.float32
BF16 = jnp.bfloat16


def vmem():
    return pl.BlockSpec(memory_space=pltpu.VMEM)


def call(kernel, inputs, outs, scratch=(), limit=4, flops=0, moved=0, scalars=0):
    return pl.pallas_call(
        kernel,
        out_shape=outs,
        in_specs=[pl.BlockSpec(memory_space=pltpu.SMEM)] * scalars + [vmem()] * (len(inputs) - scalars),
        out_specs=jax.tree.map(lambda _: vmem(), outs),
        scratch_shapes=scratch,
        compiler_params=pltpu.CompilerParams(vmem_limit_bytes=limit << 20),
        cost_estimate=pl.CostEstimate(flops=flops, bytes_accessed=moved, transcendentals=0),
    )(*inputs)


def shape(dims, kind=BF16):
    return jax.ShapeDtypeStruct(dims, kind)


def pack_kernel(own, partner, *refs):
    outs, rows = refs[:-1], refs[-1]
    col, row = lax.axis_index("cols"), lax.axis_index("rows")
    local = own.shape[1]
    width = own.shape[2]
    edge = jnp.zeros((CHAN, 32, width), BF16)
    rows[:, 0:32, :] = edge
    rows[:, 32 + 2 * local : 64 + 2 * local, :] = edge
    rows[:, pl.ds(pl.multiple_of(32 + local * row, 32), local), :] = own[...]
    rows[:, pl.ds(pl.multiple_of(32 + local * (1 - row), 32), local), :] = partner[...]
    for step, out in enumerate(outs):
        token_row = 2 * (col ^ step) + row
        first = pl.multiple_of(PATCH * token_row, PATCH)
        pieces, tails = [], []
        for channel in range(CHAN):
            block = rows[channel, pl.ds(first, 64), :].astype(F32)
            pieces.append(block[28:52])
            before = block[12:28, width - 64 :]
            tails += [before[:8], before[8:]]
        tails.append(jnp.zeros((8, width - 64 * len(tails)), F32))
        pieces.append(jnp.concatenate(tails, axis=1))
        out[...] = jnp.concatenate(pieces, axis=0).astype(BF16)


def stage_kernel(pixels, out):
    out[...] = pixels[...]


def embed_kernel(*refs):
    blocks, (weight, bias, out, strip, tail, wide) = refs[:-6], refs[-6:]
    col = lax.axis_index("cols")
    width = blocks[0].shape[1]
    count = len(blocks)
    strip[0:LEAD, :] = jnp.zeros((LEAD, 128), F32)
    strip[LEAD + count * width :, :] = jnp.zeros((LEAD, 128), F32)
    blank = jnp.zeros((128 - WIN, width), F32)
    for step, block in enumerate(blocks):
        source = col ^ step
        values = block[0:WIN, :].astype(F32)
        flipped = jnp.concatenate([values, blank], axis=0).T
        strip[pl.ds(pl.multiple_of(LEAD + source * width, 8), width), :] = flipped

        @pl.when(source == count - 1)
        def _():
            whole = block[...].astype(F32)
            extra = whole[WIN : WIN + 8]
            pieces = []
            for channel in range(CHAN):
                pieces += [extra[:, 128 * channel : 128 * channel + 64]]
                pieces += [extra[:, 128 * channel + 64 : 128 * channel + 128]]
                pieces += [whole[KERNEL * channel : KERNEL * channel + 8, width - 64 :]]
            pieces.append(jnp.zeros((128 - WIN, 64), F32))
            last = jnp.concatenate(pieces, axis=0)
            last = jnp.concatenate([last, jnp.zeros((128, 64), F32)], axis=1).T
            tail[0:72, :] = jnp.zeros((72, 128), F32)
            tail[72:136, :] = last[:64]
            tail[136:144, :] = jnp.zeros((8, 128), F32)

    tokens = count * width // PATCH
    for offset in range(KERNEL):
        start = LEAD - MARGIN + offset
        lanes = pl.ds(offset * 128, 128)
        part = jnp.concatenate(
            [tail[pl.ds(start, LEAD, stride=PATCH), :], strip[pl.ds(start, tokens, stride=PATCH), :]], axis=0
        )
        wide[:, lanes] = part.astype(BF16)
    grid = jnp.dot(wide[...], weight[...], preferred_element_type=F32)
    out[...] = (grid + bias[...]).astype(BF16)


def spread_matrix():
    head = lax.broadcasted_iota(jnp.int32, (HEADS, E), 0)
    lane = lax.broadcasted_iota(jnp.int32, (HEADS, E), 1)
    return ((lane >= head * HDIM) & (lane < (head + 1) * HDIM)).astype(BF16)


def halves(values):
    high = values.astype(BF16)
    return high, (values - high.astype(F32)).astype(BF16)


def spread(values, matrix):
    high, low = halves(values)
    return jnp.dot(high, matrix, preferred_element_type=F32) + jnp.dot(low, matrix, preferred_element_type=F32)


def softplus(values):
    small = jnp.exp(-jnp.abs(values))
    return jnp.maximum(values, 0.0) + jnp.log1p(small)


def mix_kernel(
    embedded, norm_gain, mix_weight, step_weight, step_bias, log_rate, conv_weight, conv_bias,
    normed_out, x_out, b_out, c_out, step_out, cum_out, keep_out, send_out, raw, state,
):
    col, row = lax.axis_index("cols"), lax.axis_index("rows")
    resid = embedded[...].astype(F32)
    mean_sq = jnp.mean(resid * resid, axis=-1, keepdims=True)
    normed_f = resid * lax.rsqrt(mean_sq + 1e-05) * norm_gain[...]
    normed = normed_f.astype(BF16)
    normed_out[...] = normed_f[LEAD:].astype(BF16)
    length = embedded.shape[0] - LEAD
    raw[...] = jnp.dot(normed, mix_weight[...], preferred_element_type=F32).astype(BF16).astype(F32)

    @pl.when((col == 0) & (row == 0))
    def _():
        raw[0:LEAD, :] = jnp.zeros((LEAD, raw.shape[1]), F32)

    step_raw = lax.dot_general(
        normed, step_weight[...], (((1,), (1,)), ((), ())), preferred_element_type=F32
    )[LEAD:]
    step = softplus(step_raw + step_bias[...])
    log_decay = -step * jnp.exp(log_rate[...])
    lower = (
        lax.broadcasted_iota(jnp.int32, (length, length), 0) >= lax.broadcasted_iota(jnp.int32, (length, length), 1)
    ).astype(BF16)
    high = log_decay.astype(BF16)
    middle = (log_decay - high.astype(F32)).astype(BF16)
    cum = jnp.dot(lower, high, preferred_element_type=F32)
    cum = cum + jnp.dot(lower, middle, preferred_element_type=F32)
    low = (log_decay - high.astype(F32) - middle.astype(F32)).astype(BF16)
    cum = cum + jnp.dot(lower, low, preferred_element_type=F32)
    step_out[...] = step
    cum_out[...] = cum
    matrix = spread_matrix()
    last = cum[length - 1 :]
    to_end = spread(jnp.exp(last - cum) * step, matrix)
    decay = spread(jnp.broadcast_to(jnp.exp(last), (8, HEADS)), matrix)
    taps = conv_weight.shape[0]
    chunk = 64
    scaled = []
    maps = []
    for first in range(0, length, chunk):
        total = jnp.broadcast_to(conv_bias[...], (chunk, raw.shape[1]))
        for tap in range(taps):
            total = total + conv_weight[tap : tap + 1, :] * raw[pl.ds(LEAD - taps + 1 + tap + first, chunk), :]
        mixed = (total * jax.nn.sigmoid(total)).astype(BF16)
        x_out[pl.ds(first, chunk), :] = mixed[:, :E]
        mixed_f = mixed[:, E:].astype(F32)
        b_out[pl.ds(first, chunk), :] = mixed_f[:, :NSTATE].astype(BF16)
        c_out[pl.ds(first, chunk), :] = mixed_f[:, NSTATE:].astype(BF16)
        maps.append(mixed_f[:, :NSTATE])
        scaled.append((mixed[:, :E].astype(F32) * to_end[first : first + chunk]).astype(BF16))
    b_t = jnp.concatenate(maps, axis=0).T.astype(BF16)
    state[0:NSTATE, :] = jnp.dot(b_t, jnp.concatenate(scaled, axis=0), preferred_element_type=F32)
    state[NSTATE : NSTATE + 8, :] = decay
    half = E // 2
    mine = pl.ds(pl.multiple_of(row * half, 128), half)
    theirs = pl.ds(pl.multiple_of((1 - row) * half, 128), half)
    keep_out[...] = state[:, mine]
    send_out[...] = wire(state[0:NSTATE, theirs], state[NSTATE : NSTATE + 8, theirs])


def wire(values, decay):
    high = decay.astype(BF16).astype(F32)
    rest = decay - high
    place = lax.broadcasted_iota(jnp.int32, decay.shape, 0)
    return jnp.concatenate([values, jnp.where(place == 0, high, rest)], axis=0).astype(BF16)


def unwire(message):
    values = message[0:NSTATE, :].astype(F32)
    rows = message[NSTATE : NSTATE + 8, :].astype(F32)
    return values, jnp.broadcast_to(rows[0:1] + rows[1:2], rows.shape)


def scale(decay, values):
    return decay[0:1] * values


def pair_kernel(keep, received, total_out, message_out):
    row = lax.axis_index("rows")
    own, own_decay = keep[0:NSTATE, :], keep[NSTATE : NSTATE + 8, :]
    other, other_decay = unwire(received)
    upper = row == 1
    last_decay = jnp.where(upper, own_decay, other_decay)
    values = scale(last_decay, jnp.where(upper, other, own)) + jnp.where(upper, own, other)
    decay = own_decay * other_decay
    total_out[0:NSTATE, :] = values
    total_out[NSTATE : NSTATE + 8, :] = decay
    message_out[...] = wire(values, decay)


def join_kernel(bit, total, before, received, total_out, before_out, message_out):
    col = lax.axis_index("cols")
    later = (col & bit) != 0
    values, decay = total[0:NSTATE, :], total[NSTATE : NSTATE + 8, :]
    came, came_decay = unwire(received)
    last_decay = jnp.where(later, decay, came_decay)
    joined = scale(last_decay, jnp.where(later, came, values)) + jnp.where(later, values, came)
    total_out[0:NSTATE, :] = joined
    total_out[NSTATE : NSTATE + 8, :] = decay * came_decay
    message_out[...] = wire(joined, decay * came_decay)
    if before is None:
        before_out[0:NSTATE, :] = jnp.where(later, came, 0.0)
        before_out[NSTATE : NSTATE + 8, :] = jnp.where(later, came_decay, 1.0)
    else:
        ahead, ahead_decay = before[0:NSTATE, :], before[NSTATE : NSTATE + 8, :]
        before_out[0:NSTATE, :] = jnp.where(later, scale(ahead_decay, came) + ahead, ahead)
        before_out[NSTATE : NSTATE + 8, :] = jnp.where(later, ahead_decay * came_decay, ahead_decay)


def enter_kernel(bit, before, last, keep, received, mine_out, theirs_out):
    col, row = lax.axis_index("cols"), lax.axis_index("rows")
    later = (col & bit) != 0
    ahead, ahead_decay = before[0:NSTATE, :], before[NSTATE : NSTATE + 8, :]
    came, _ = unwire(last)
    ahead = jnp.where(later, scale(ahead_decay, came) + ahead, ahead)
    other, other_decay = unwire(received)
    upper = row == 1
    low = jnp.where(upper, other, keep[0:NSTATE, :])
    low_decay = jnp.where(upper, other_decay, keep[NSTATE : NSTATE + 8, :])
    second = scale(low_decay, ahead) + low
    mine_out[...] = jnp.where(upper, second, ahead).astype(BF16)
    theirs_out[...] = jnp.where(upper, ahead, second).astype(BF16)


def gate_kernel(normed, gate_weight, out):
    gate = jnp.dot(normed[...], gate_weight[...], preferred_element_type=F32).astype(BF16).astype(F32)
    out[...] = gate * jax.nn.sigmoid(gate)


def intra_kernel(first, skip, x, b_mat, c_mat, step, cum, out):
    length = x.shape[0]
    half = length // 2
    scores = lax.dot_general(c_mat[...], b_mat[...], (((1,), (1,)), ((), ())), preferred_element_type=F32)
    causal = lax.broadcasted_iota(jnp.int32, (length, length), 0) >= lax.broadcasted_iota(
        jnp.int32, (length, length), 1
    )
    scores = jnp.where(causal, scores, 0.0)
    wide = jnp.zeros((length, 128 - HEADS), F32)
    cum_v = cum[...]
    cum_t = jnp.concatenate([cum_v, wide], axis=1).T
    step_t = jnp.concatenate([step[...], wide], axis=1).T
    for place in range(out.shape[1] // 128):
        pair = first + place
        x_pair = x[:, pair * 128 : (pair + 1) * 128]
        tops, bottoms = [], []
        for member in range(2):
            head = 2 * pair + member
            column = cum_v[:, head : head + 1]
            cum_row = cum_t[head : head + 1, :]
            step_row = step_t[head : head + 1, :]

            def weights(rows, span):
                gap = jnp.minimum(column[rows] - cum_row[:, span], 0.0)
                return (scores[rows, span] * jnp.exp(gap) * step_row[:, span]).astype(BF16)

            inputs = x_pair[:, member * HDIM : (member + 1) * HDIM]
            top = jnp.dot(weights(slice(0, half), slice(0, half)), inputs[:half], preferred_element_type=F32)
            bottom = jnp.dot(weights(slice(half, length), slice(0, length)), inputs, preferred_element_type=F32)
            tops.append(top)
            bottoms.append(bottom)
        lane = lax.broadcasted_iota(jnp.int32, x_pair.shape, 1)
        direct = jnp.where(lane < HDIM, skip[2 * pair], skip[2 * pair + 1]) * x_pair.astype(F32)
        lanes = slice(place * 128, (place + 1) * 128)
        out[0:half, lanes] = jnp.concatenate(tops, axis=1) + direct[:half]
        out[half:length, lanes] = jnp.concatenate(bottoms, axis=1) + direct[half:]


def finish_kernel(local_a, local_b, gate, c_mat, cum, mine, theirs, embedded, out_gain, out_weight, out, state):
    row = lax.axis_index("rows")
    half = E // 2
    state[:, pl.ds(pl.multiple_of(row * half, 128), half)] = mine[...]
    state[:, pl.ds(pl.multiple_of((1 - row) * half, 128), half)] = theirs[...]
    carried = jnp.dot(c_mat[...], state[...], preferred_element_type=F32)
    carried = carried * spread(jnp.exp(cum[...]), spread_matrix())
    local = jnp.concatenate([local_a[...], local_b[...]], axis=1)
    gated = (local + carried) * gate[...]
    mean_sq = jnp.mean(gated * gated, axis=-1, keepdims=True)
    hidden = (gated * lax.rsqrt(mean_sq + 1e-05) * out_gain[...]).astype(BF16)
    result = jnp.dot(hidden, out_weight[...], preferred_element_type=F32)
    out[...] = (result + embedded[...].astype(F32)[LEAD:]).astype(BF16)


def swap(block, axis, bit):
    return lax.ppermute(block, axis, [(i, i ^ bit) for i in range(lax.axis_size(axis))])


def sending_order(count):
    return (1, *range(count // 2, count), *range(2, count // 2))


def embed_by_rows(pixels, patch_weight, patch_bias):
    col_count = lax.axis_size("cols")
    width = pixels.shape[2]
    partner = swap(pixels, "rows", 1)
    pixels = call(stage_kernel, (pixels,), shape(pixels.shape))
    block = shape((WIN + 8, width))
    scratch = [pltpu.VMEM((CHAN, 2 * pixels.shape[1] + 64, width), BF16)]
    blocks = call(pack_kernel, (pixels, partner), [block] * col_count, scratch, limit=8)
    came = [blocks[0]] + [None] * (col_count - 1)
    for step in sending_order(col_count):
        came[step] = swap(blocks[step], "cols", step)
    weight = patch_weight.transpose(1, 2, 0, 3).reshape(KERNEL, WIN, D)
    weight = jnp.pad(weight, ((0, 0), (0, 128 - WIN), (0, 0))).reshape(KERNEL * 128, D)
    tokens = col_count * width // PATCH
    scratch = [
        pltpu.VMEM((2 * LEAD + col_count * width, 128), F32),
        pltpu.VMEM((144, 128), F32),
        pltpu.VMEM((LEAD + tokens, KERNEL * 128), BF16),
    ]
    flops = 2 * tokens * KERNEL * 128 * D
    return call(
        embed_kernel, (*came, weight, patch_bias.reshape(1, -1)), shape((LEAD + tokens, D)), scratch,
        flops=flops, moved=6 << 20, limit=16,
    )


def extended(block, sides, width):
    for axis, dim in sides:
        count = lax.axis_size(axis)
        forward = [(i, i + 1) for i in range(count - 1)]
        backward = [(target, source) for source, target in forward]
        low = lax.ppermute(
            lax.slice_in_dim(block, block.shape[dim] - width, None, axis=dim), axis, forward
        )
        high = lax.ppermute(lax.slice_in_dim(block, 0, width, axis=dim), axis, backward)
        block = jnp.concatenate([low, block, high], axis=dim)
    return block


def shifted(block, axis, distance):
    devices = range(lax.axis_size(axis))
    route = [(i - distance, i) for i in devices if i - distance in devices]
    return lax.ppermute(block, axis, route)


def embed_by_blocks(pixels, patch_weight, patch_bias):
    padded = extended(pixels, (("cols", 2), ("rows", 1)), MARGIN)
    embed_grid = lax.conv_general_dilated(
        padded[None],
        patch_weight,
        (PATCH, PATCH),
        "VALID",
        dimension_numbers=("NCHW", "HWIO", "NHWC"),
        preferred_element_type=jnp.float32,
    )[0]
    embed_grid = (embed_grid + patch_bias).astype(jnp.bfloat16)
    row_local, col_local, feature_width = embed_grid.shape
    devices = lax.axis_size(("cols", "rows"))
    row_count = lax.axis_size("rows")
    col_count = lax.axis_size("cols")
    groups = col_count // row_local
    piece_len = col_local * feature_width // devices
    outgoing = embed_grid.reshape(row_local, devices, piece_len)
    spread = lax.all_to_all(outgoing, ("cols", "rows"), split_axis=1, concat_axis=1, tiled=True)
    spread = spread.reshape(row_local, groups, row_local, row_count, piece_len).transpose(
        3, 0, 1, 2, 4
    )
    landed = lax.all_to_all(
        spread.reshape(devices, row_local, piece_len),
        ("cols", "rows"),
        split_axis=0,
        concat_axis=0,
        tiled=True,
    )
    tokens = landed.transpose(1, 0, 2).reshape(row_local * col_local, feature_width)
    tail = shifted(tokens[tokens.shape[0] - LEAD :], ("cols", "rows"), 1)
    return jnp.concatenate([tail, tokens], axis=0)


def body(
    pixels,
    patch_weight,
    patch_bias,
    norm_gain,
    gate_weight,
    mix_weight,
    step_weight,
    step_bias,
    log_rate,
    conv_weight,
    conv_bias,
    skip_gain,
    out_gain,
    out_weight,
):
    col_count = lax.axis_size("cols")
    row_local = pixels.shape[1] // PATCH
    if col_count == row_local:
        embedded = embed_by_rows(pixels, patch_weight, patch_bias)
    else:
        embedded = embed_by_blocks(pixels, patch_weight, patch_bias)
    length = embedded.shape[0] - LEAD
    line = lambda a: a.reshape(1, -1)
    mixed_width = mix_weight.shape[1]
    half = E // 2
    packed = NSTATE + 8
    normed, x, b_mat, c_mat, step, cum, keep, send = call(
        mix_kernel,
        (
            embedded, line(norm_gain), mix_weight, step_weight.T, line(step_bias), line(log_rate),
            conv_weight, line(conv_bias),
        ),
        [
            shape((length, D)), shape((length, E)), shape((length, NSTATE)), shape((length, NSTATE)),
            shape((length, HEADS), F32), shape((length, HEADS), F32), shape((packed, half), F32),
            shape((packed, half)),
        ],
        [pltpu.VMEM((LEAD + length, mixed_width), F32), pltpu.VMEM((packed, E), F32)],
        flops=2 * length * D * mixed_width, moved=4 << 20, limit=16,
    )
    came = swap(send, "rows", 1)
    summary, message = shape((packed, half), F32), shape((packed, half))
    total, out = call(pair_kernel, (keep, came), [summary, message])
    gate = call(
        gate_kernel, (normed, gate_weight), shape((length, E), F32),
        flops=2 * length * D * E, moved=4 << 20, limit=8,
    )
    locals_ = []
    for part in range(2):
        locals_.append(
            call(
                partial(intra_kernel, part * HEADS // 4), (skip_gain, x, b_mat, c_mat, step, cum),
                shape((length, half), F32), scalars=1,
                flops=HEADS * length * length * 128, moved=2 << 20, limit=8,
            )
        )
    before, bit = None, 1
    while 2 * bit < col_count:
        arrived = swap(out, "cols", bit)
        if before is None:
            kernel = lambda t, r, *outs, bit=bit: join_kernel(bit, t, None, r, *outs)
            total, before, out = call(kernel, (total, arrived), [summary, summary, message])
        else:
            total, before, out = call(partial(join_kernel, bit), (total, before, arrived), [summary, summary, message])
        bit *= 2
    arrived = swap(out, "cols", bit)
    entering = shape((NSTATE, half))
    mine, theirs = call(partial(enter_kernel, bit), (before, arrived, keep, came), [entering, entering])
    theirs = swap(theirs, "rows", 1)
    return call(
        finish_kernel,
        (*locals_, gate, c_mat, cum, mine, theirs, embedded, line(out_gain), out_weight),
        shape((length, D)),
        [pltpu.VMEM((NSTATE, E), BF16)],
        flops=2 * length * D * E, moved=4 << 20, limit=16,
    )


def solution(mesh):
    placed = (
        P(None, "rows", ("slides", "cols")),
        P(),
        P(),
        P(),
        P(),
        P(),
        P(),
        P(),
        P(),
        P(),
        P(),
        P(),
        P(),
        P(),
    )
    return jax.shard_map(
        body,
        mesh=mesh,
        in_specs=placed,
        out_specs=P(("slides", "cols", "rows"), None),
        check_vma=False,
    )
```

profile of v0, /device:TPU:0, one launch (start us, length us, event | category | flops | bytes accessed | tf_op | source)
XLA Modules:
  0.0 60.4 jit_solution(11806607492201606041)
XLA Ops:
  0.0 0.5 collective-permute-start
  0.5 1.0 %copy-done.3 = bf16[3,128,512]{2,1,0:T(8,128)(2,1)S(1)} copy-done((bf16[3,128,512]{2,1,0:T(8,128)(2,1)S(1)}, bf16[3,128,512]{2,1,0:T(8,128)(2,1)}, u32[]{:S(2)}) %copy-start.3) | copy-done | bytes 393240
  1.5 0.5 collective-permute-done.partner
  2.1 0.3 shard_map.137
  2.3 2.9 %collective-permute-start.1 = (bf16[80,512]{1,0:T(8,128)(2,1)S(1)}, bf16[80,512]{1,0:T(8,128)(2,1)S(1)}, u32[]{:S(2)}, u32[]{:S(2)}) collective-permute-start(bf16[80,512]{1,0:T(8,128)(2,1)S(1)} %get-tuple-element.31), channel_id=1, source_target_pairs={{0,2},{2,0},{4,6},{6,4},{8,10},{10,8},{12,14},{14,12},{1,3},{3,1},... | collective-permute-start | bytes 245768 | tf_op jit(solution)/shard_map/ppermute | solution.py:322
  5.3 1.6 %collective-permute-start.2 = (bf16[80,512]{1,0:T(8,128)(2,1)S(1)}, bf16[80,512]{1,0:T(8,128)(2,1)S(1)}, u32[]{:S(2)}, u32[]{:S(2)}) collective-permute-start(bf16[80,512]{1,0:T(8,128)(2,1)S(1)} %get-tuple-element.32), channel_id=1, source_target_pairs={{0,4},{2,6},{4,0},{6,2},{8,12},{10,14},{12,8},{14,10},{1,5},{3,7},... | collective-permute-start | bytes 245768 | tf_op jit(solution)/shard_map/ppermute | solution.py:322
  6.8 3.0 %collective-permute-start.4 = (bf16[80,512]{1,0:T(8,128)(2,1)S(1)}, bf16[80,512]{1,0:T(8,128)(2,1)S(1)}, u32[]{:S(2)}, u32[]{:S(2)}) collective-permute-start(bf16[80,512]{1,0:T(8,128)(2,1)S(1)} %get-tuple-element.34), channel_id=1, source_target_pairs={{0,8},{2,10},{4,12},{6,14},{8,0},{10,2},{12,4},{14,6},{1,9},{3,11}... | collective-permute-start | bytes 245768 | tf_op jit(solution)/shard_map/ppermute | solution.py:322
  9.8 1.3 %collective-permute-start.5 = (bf16[80,512]{1,0:T(8,128)(2,1)S(1)}, bf16[80,512]{1,0:T(8,128)(2,1)S(1)}, u32[]{:S(2)}, u32[]{:S(2)}) collective-permute-start(bf16[80,512]{1,0:T(8,128)(2,1)S(1)} %get-tuple-element.35), channel_id=1, source_target_pairs={{0,10},{2,8},{4,14},{6,12},{8,2},{10,0},{12,6},{14,4},{1,11},{3,9}... | collective-permute-start | bytes 245768 | tf_op jit(solution)/shard_map/ppermute | solution.py:322
  11.1 3.6 %collective-permute-start.6 = (bf16[80,512]{1,0:T(8,128)(2,1)S(1)}, bf16[80,512]{1,0:T(8,128)(2,1)S(1)}, u32[]{:S(2)}, u32[]{:S(2)}) collective-permute-start(bf16[80,512]{1,0:T(8,128)(2,1)S(1)} %get-tuple-element.36), channel_id=1, source_target_pairs={{0,12},{2,14},{4,8},{6,10},{8,4},{10,6},{12,0},{14,2},{1,13},{3,15... | collective-permute-start | bytes 245768 | tf_op jit(solution)/shard_map/ppermute | solution.py:322
  14.7 0.1 collective-permute-start.7
  14.8 2.3 %copy.15 = bf16[24,24,3,768]{3,0,2,1:T(8,128)(2,1)S(1)} copy(bf16[24,24,3,768]{3,1,2,0:T(8,128)(2,1)} %param.15) | data formatting | bytes 5308416 | tf_op args[1]
  17.1 0.5 pad.4
  17.7 5.2 %collective-permute-done.5.refs_5_ = bf16[80,512]{1,0:T(8,128)(2,1)S(1)} collective-permute-done((bf16[80,512]{1,0:T(8,128)(2,1)S(1)}, bf16[80,512]{1,0:T(8,128)(2,1)S(1)}, u32[]{:S(2)}, u32[]{:S(2)}) %collective-permute-start.5) | collective-permute-done | bytes 81952 | tf_op jit(solution)/shard_map/ppermute | solution.py:322
  23.0 3.5 %shard_map.138.embedded = bf16[264,768]{1,0:T(8,128)(2,1)S(1)} custom-call(bf16[80,512]{1,0:T(8,128)(2,1)S(1)} %get-tuple-element.30.refs_0_, bf16[80,512]{1,0:T(8,128)(2,1)S(1)} %collective-permute-done.1.refs_1_, bf16[80,512]{1,0:T(8,128)(2,1)S(1)} %collective-permute-done.2.refs_2_, bf16[80,512]{1,0:T(8,128)(2,1)S(1)} %collective-permute-done.3.refs_3_, ...), custom_call_target="tpu_custom_call" | custom-call | flops 1207959552 | bytes 6291456 | tf_op jit(solution)/shard_map/pallas_call | solution.py:31
  26.5 4.3 %shard_map.139 = (bf16[256,768]{1,0:T(8,128)(2,1)S(1)}, bf16[256,1536]{1,0:T(8,128)(2,1)S(1)}, bf16[256,64]{1,0:T(8,128)(2,1)S(1)}, bf16[256,64]{1,0:T(8,128)(2,...) custom-call(bf16[264,768]{1,0:T(8,128)(2,1)S(1)} %shard_map.138.embe, ...), custom_call_target="tpu_custom_call" | custom-call | flops 654311424 | bytes 4194304 | tf_op jit(solution)/shard_map/pallas_call | solution.py:31
  30.9 0.1 collective-permute-start.8
  30.9 1.3 %collective-permute-done.8.received = bf16[72,768]{1,0:T(8,128)(2,1)S(1)} collective-permute-done((bf16[72,768]{1,0:T(8,128)(2,1)S(1)}, bf16[72,768]{1,0:T(8,128)(2,1)S(1)}, u32[]{:S(2)}, u32[]{:S(2)}) %collective-permute-start.8) | collective-permute-done | bytes 110624 | tf_op jit(solution)/shard_map/ppermute | solution.py:322
  32.3 1.0 %collective-permute-start.9 = (bf16[72,768]{1,0:T(8,128)(2,1)S(1)}, bf16[72,768]{1,0:T(8,128)(2,1)S(1)}, u32[]{:S(2)}, u32[]{:S(2)}) collective-permute-start(bf16[72,768]{1,0:T(8,128)(2,1)S(1)} %get-tuple-element.47), channel_id=1, source_target_pairs={{0,2},{2,0},{4,6},{6,4},{8,10},{10,8},{12,14},{14,12},{1,3},{3,1},... | collective-permute-start | bytes 331784 | tf_op jit(solution)/shard_map/ppermute | solution.py:322
  33.3 4.2 %collective-permute-done.9.r = bf16[72,768]{1,0:T(8,128)(2,1)S(1)} collective-permute-done((bf16[72,768]{1,0:T(8,128)(2,1)S(1)}, bf16[72,768]{1,0:T(8,128)(2,1)S(1)}, u32[]{:S(2)}, u32[]{:S(2)}) %collective-permute-start.9) | collective-permute-done | bytes 110624 | tf_op jit(solution)/shard_map/ppermute | solution.py:322
  37.5 0.1 shard_map.144
  37.6 3.5 %collective-permute-start.10 = (bf16[72,768]{1,0:T(8,128)(2,1)S(1)}, bf16[72,768]{1,0:T(8,128)(2,1)S(1)}, u32[]{:S(2)}, u32[]{:S(2)}) collective-permute-start(bf16[72,768]{1,0:T(8,128)(2,1)S(1)} %get-tuple-element.50), channel_id=1, source_target_pairs={{0,4},{2,6},{4,0},{6,2},{8,12},{10,14},{12,8},{14,10},{1,5},{3,7},... | collective-permute-start | bytes 331784 | tf_op jit(solution)/shard_map/ppermute | solution.py:322
  41.1 2.7 %collective-permute-done.10.received = bf16[72,768]{1,0:T(8,128)(2,1)S(1)} collective-permute-done((bf16[72,768]{1,0:T(8,128)(2,1)S(1)}, bf16[72,768]{1,0:T(8,128)(2,1)S(1)}, u32[]{:S(2)}, u32[]{:S(2)}) %collective-permute-start.10) | collective-permute-done | bytes 110624 | tf_op jit(solution)/shard_map/ppermute | solution.py:322
  43.8 0.7 %shard_map.145 = (f32[72,768]{1,0:T(8,128)}, f32[72,768]{1,0:T(8,128)S(1)}, bf16[72,768]{1,0:T(8,128)(2,1)S(1)}) custom-call(f32[72,768]{1,0:T(8,128)S(1)} %get-tuple-element.48.total, f32[72,768]{1,0:T(8,128)S(1)} %get-tuple-element.49.before, bf16[72,768]{1,0:T(8,128)(2,1)S(1)} %collective-permute-done.10.received), custom_call_target="tpu_custom_call" | custom-call | tf_op jit(solution)/shard_map/pallas_call | solution.py:31
  44.5 3.3 %collective-permute-start.11 = (bf16[72,768]{1,0:T(8,128)(2,1)S(1)}, bf16[72,768]{1,0:T(8,128)(2,1)S(1)}, u32[]{:S(2)}, u32[]{:S(2)}) collective-permute-start(bf16[72,768]{1,0:T(8,128)(2,1)S(1)} %get-tuple-element.52), channel_id=1, source_target_pairs={{0,8},{2,10},{4,12},{6,14},{8,0},{10,2},{12,4},{14,6},{1,9},{3,11}... | collective-permute-start | bytes 331784 | tf_op jit(solution)/shard_map/ppermute | solution.py:322
  47.8 3.9 %collective-permute-done.11.last = bf16[72,768]{1,0:T(8,128)(2,1)S(1)} collective-permute-done((bf16[72,768]{1,0:T(8,128)(2,1)S(1)}, bf16[72,768]{1,0:T(8,128)(2,1)S(1)}, u32[]{:S(2)}, u32[]{:S(2)}) %collective-permute-start.11) | collective-permute-done | bytes 110624 | tf_op jit(solution)/shard_map/ppermute | solution.py:322
  51.7 0.1 shard_map.146
  51.8 0.1 collective-permute-start.12
  51.9 2.0 %shard_map.141.local_b = f32[256,768]{1,0:T(8,128)S(1)} custom-call(f32[24]{0:T(128)S(1)} %copy-done.6, bf16[256,1536]{1,0:T(8,128)(2,1)S(1)} %get-tuple-element.38.x, bf16[256,64]{1,0:T(8,128)(2,1)S(1)} %get-tuple-element.39.b_mat, bf16[256,64]{1,0:T(8,128)(2,1)S(1)} %get-tuple-element.40.c_mat, f32[256,24]{1,0:T(8,128)S(1)} %get-tuple-element.41.step, ...), custom_call_target="tpu_custom_call" | custom-call | flops 201326592 | bytes 2097152 | tf_op jit(solution)/shard_map/pallas_call | solution.py:31
  53.9 2.0 %shard_map.140.local_a = f32[256,768]{1,0:T(8,128)S(1)} custom-call(f32[24]{0:T(128)S(1)} %copy-done.6, bf16[256,1536]{1,0:T(8,128)(2,1)S(1)} %get-tuple-element.38.x, bf16[256,64]{1,0:T(8,128)(2,1)S(1)} %get-tuple-element.39.b_mat, bf16[256,64]{1,0:T(8,128)(2,1)S(1)} %get-tuple-element.40.c_mat, f32[256,24]{1,0:T(8,128)S(1)} %get-tuple-element.41.step, ...), custom_call_target="tpu_custom_call" | custom-call | flops 201326592 | bytes 2097152 | tf_op jit(solution)/shard_map/pallas_call | solution.py:31
  55.9 0.8 %shard_map.142.gate = f32[256,1536]{1,0:T(8,128)S(1)} custom-call(bf16[256,768]{1,0:T(8,128)(2,1)S(1)} %get-tuple-element.43.normed, bf16[768,1536]{1,0:T(8,128)(2,1)S(1)} %copy-done.1), custom_call_target="tpu_custom_call" | custom-call | flops 603979776 | bytes 4194304 | tf_op jit(solution)/shard_map/pallas_call | solution.py:31
  56.7 0.8 %copy-done.2 = bf16[1536,768]{1,0:T(8,128)(2,1)S(1)} copy-done((bf16[1536,768]{1,0:T(8,128)(2,1)S(1)}, bf16[1536,768]{1,0:T(8,128)(2,1)}, u32[]{:S(2)}) %copy-start.2) | copy-done | bytes 2359320
  57.5 2.9 %shard_map.147 = bf16[256,768]{1,0:T(8,128)(2,1)} custom-call(f32[256,768]{1,0:T(8,128)S(1)} %shard_map.140.local_a, f32[256,768]{1,0:T(8,128)S(1)} %shard_map.141.local_b, f32[256,1536]{1,0:T(8,128)S(1)} %shard_map.142.gate, bf16[256,64]{1,0:T(8,128)(2,1)S(1)} %get-tuple-element.40.c_mat, f32[256,24]{1,0:T(8,128)S(1)} %get-tuple-element.42.cum, ...), custom_call_target="tpu_custom_call" | custom-call | flops 603979776 | bytes 4194304 | tf_op jit(solution)/shard_map/pallas_call | solution.py:31
  (38 shorter events, 0.2 us)
Async XLA Ops:
  0.0 2.1 %collective-permute-start = (bf16[3,128,512]{2,1,0:T(8,128)(2,1)}, bf16[3,128,512]{2,1,0:T(8,128)(2,1)S(1)}, u32[]{:S(2)}, u32[]{:S(2)}) collective-permute-start(bf16[3,128,512]{2,1,0:T(8,128)(2,1)} %pixels.1), channel_id=1, source_target_pairs={{0,1},{1,0},{2,3},{3,2},{4,5},{5,4},{6,7},{7,6},{8,9},{9,8},{10,11... | collective-permute-start | bytes 1179656 | tf_op jit(solution)/shard_map/ppermute | solution.py:322
  0.5 1.0 %copy-start.3 = (bf16[3,128,512]{2,1,0:T(8,128)(2,1)S(1)}, bf16[3,128,512]{2,1,0:T(8,128)(2,1)}, u32[]{:S(2)}) copy-start(bf16[3,128,512]{2,1,0:T(8,128)(2,1)} %pixels.1) | copy-start | bytes 1179652
  2.3 8.8 %collective-permute-start.1 = (bf16[80,512]{1,0:T(8,128)(2,1)S(1)}, bf16[80,512]{1,0:T(8,128)(2,1)S(1)}, u32[]{:S(2)}, u32[]{:S(2)}) collective-permute-start(bf16[80,512]{1,0:T(8,128)(2,1)S(1)} %get-tuple-element.31), channel_id=1, source_target_pairs={{0,2},{2,0},{4,6},{6,4},{8,10},{10,8},{12,14},{14,12},{1,3},{3,1},... | collective-permute-start | bytes 245768 | tf_op jit(solution)/shard_map/ppermute | solution.py:322
  5.3 9.5 %collective-permute-start.2 = (bf16[80,512]{1,0:T(8,128)(2,1)S(1)}, bf16[80,512]{1,0:T(8,128)(2,1)S(1)}, u32[]{:S(2)}, u32[]{:S(2)}) collective-permute-start(bf16[80,512]{1,0:T(8,128)(2,1)S(1)} %get-tuple-element.32), channel_id=1, source_target_pairs={{0,4},{2,6},{4,0},{6,2},{8,12},{10,14},{12,8},{14,10},{1,5},{3,7},... | collective-permute-start | bytes 245768 | tf_op jit(solution)/shard_map/ppermute | solution.py:322
  6.8 10.8 %collective-permute-start.3 = (bf16[80,512]{1,0:T(8,128)(2,1)S(1)}, bf16[80,512]{1,0:T(8,128)(2,1)S(1)}, u32[]{:S(2)}, u32[]{:S(2)}) collective-permute-start(bf16[80,512]{1,0:T(8,128)(2,1)S(1)} %get-tuple-element.33), channel_id=1, source_target_pairs={{0,6},{2,4},{4,2},{6,0},{8,14},{10,12},{12,10},{14,8},{1,7},{3,5},... | collective-permute-start | bytes 245768 | tf_op jit(solution)/shard_map/ppermute | solution.py:322
  6.8 10.8 %collective-permute-start.4 = (bf16[80,512]{1,0:T(8,128)(2,1)S(1)}, bf16[80,512]{1,0:T(8,128)(2,1)S(1)}, u32[]{:S(2)}, u32[]{:S(2)}) collective-permute-start(bf16[80,512]{1,0:T(8,128)(2,1)S(1)} %get-tuple-element.34), channel_id=1, source_target_pairs={{0,8},{2,10},{4,12},{6,14},{8,0},{10,2},{12,4},{14,6},{1,9},{3,11}... | collective-permute-start | bytes 245768 | tf_op jit(solution)/shard_map/ppermute | solution.py:322
  9.8 13.1 %collective-permute-start.5 = (bf16[80,512]{1,0:T(8,128)(2,1)S(1)}, bf16[80,512]{1,0:T(8,128)(2,1)S(1)}, u32[]{:S(2)}, u32[]{:S(2)}) collective-permute-start(bf16[80,512]{1,0:T(8,128)(2,1)S(1)} %get-tuple-element.35), channel_id=1, source_target_pairs={{0,10},{2,8},{4,14},{6,12},{8,2},{10,0},{12,6},{14,4},{1,11},{3,9}... | collective-permute-start | bytes 245768 | tf_op jit(solution)/shard_map/ppermute | solution.py:322
  11.1 11.8 %collective-permute-start.6 = (bf16[80,512]{1,0:T(8,128)(2,1)S(1)}, bf16[80,512]{1,0:T(8,128)(2,1)S(1)}, u32[]{:S(2)}, u32[]{:S(2)}) collective-permute-start(bf16[80,512]{1,0:T(8,128)(2,1)S(1)} %get-tuple-element.36), channel_id=1, source_target_pairs={{0,12},{2,14},{4,8},{6,10},{8,4},{10,6},{12,0},{14,2},{1,13},{3,15... | collective-permute-start | bytes 245768 | tf_op jit(solution)/shard_map/ppermute | solution.py:322
  14.7 2.4 %copy-start.11 = (f32[768]{0:T(1024)S(1)}, f32[768]{0:T(1024)}, u32[]{:S(2)}) copy-start(f32[768]{0:T(1024)} %param.16) | copy-start | bytes 9220
  14.7 2.4 %copy-start.10 = (f32[1664]{0:T(1024)S(1)}, f32[1664]{0:T(1024)}, u32[]{:S(2)}) copy-start(f32[1664]{0:T(1024)} %param.24) | copy-start | bytes 19972
  14.7 2.4 %copy-start.12 = (f32[768]{0:T(1024)S(1)}, f32[768]{0:T(1024)}, u32[]{:S(2)}) copy-start(f32[768]{0:T(1024)} %param.17) | copy-start | bytes 9220
  14.7 8.2 %collective-permute-start.7 = (bf16[80,512]{1,0:T(8,128)(2,1)S(1)}, bf16[80,512]{1,0:T(8,128)(2,1)S(1)}, u32[]{:S(2)}, u32[]{:S(2)}) collective-permute-start(bf16[80,512]{1,0:T(8,128)(2,1)S(1)} %get-tuple-element.37), channel_id=1, source_target_pairs={{0,14},{2,12},{4,10},{6,8},{8,6},{10,4},{12,2},{14,0},{1,15},{3,13... | collective-permute-start | bytes 245768 | tf_op jit(solution)/shard_map/ppermute | solution.py:322
  22.9 3.5 %copy-start = (bf16[768,1664]{1,0:T(8,128)(2,1)S(1)}, bf16[768,1664]{1,0:T(8,128)(2,1)}, u32[]{:S(2)}) copy-start(bf16[768,1664]{1,0:T(8,128)(2,1)} %mix_weight.1) | copy-start | bytes 7667716
  22.9 3.6 %copy-start.4 = (bf16[768,24]{0,1:T(8,128)(2,1)S(1)}, bf16[768,24]{0,1:T(8,128)(2,1)}, u32[]{:S(2)}) copy-start(bf16[768,24]{0,1:T(8,128)(2,1)} %param.20) | copy-start | bytes 110596
  22.9 3.6 %copy-start.5 = (f32[4,1664]{1,0:T(4,128)S(1)}, f32[4,1664]{1,0:T(4,128)}, u32[]{:S(2)}) copy-start(f32[4,1664]{1,0:T(4,128)} %conv_weight.1) | copy-start | bytes 79876
  23.0 3.5 %copy-start.7 = (f32[24]{0:T(128)S(1)}, f32[24]{0:T(128)}, u32[]{:S(2)}) copy-start(f32[24]{0:T(128)} %param.21) | copy-start | bytes 292
  23.0 3.5 %copy-start.8 = (f32[24]{0:T(128)S(1)}, f32[24]{0:T(128)}, u32[]{:S(2)}) copy-start(f32[24]{0:T(128)} %param.22) | copy-start | bytes 292
  26.5 25.5 %copy-start.9 = (f32[1536]{0:T(1024)S(1)}, f32[1536]{0:T(1024)}, u32[]{:S(2)}) copy-start(f32[1536]{0:T(1024)} %param.26) | copy-start | bytes 18436
  26.5 25.5 %copy-start.6 = (f32[24]{0:T(128)S(1)}, f32[24]{0:T(128)}, u32[]{:S(2)}) copy-start(f32[24]{0:T(128)} %skip.3) | copy-start | bytes 292
  30.9 1.4 %collective-permute-start.8 = (bf16[72,768]{1,0:T(8,128)(2,1)S(1)}, bf16[72,768]{1,0:T(8,128)(2,1)S(1)}, u32[]{:S(2)}, u32[]{:S(2)}) collective-permute-start(bf16[72,768]{1,0:T(8,128)(2,1)S(1)} %get-tuple-element.45), channel_id=1, source_target_pairs={{0,1},{1,0},{2,3},{3,2},{4,5},{5,4},{6,7},{7,6},{8,9},{9,8},{10,11... | collective-permute-start | bytes 331784 | tf_op jit(solution)/shard_map/ppermute | solution.py:322
  32.3 5.2 %collective-permute-start.9 = (bf16[72,768]{1,0:T(8,128)(2,1)S(1)}, bf16[72,768]{1,0:T(8,128)(2,1)S(1)}, u32[]{:S(2)}, u32[]{:S(2)}) collective-permute-start(bf16[72,768]{1,0:T(8,128)(2,1)S(1)} %get-tuple-element.47), channel_id=1, source_target_pairs={{0,2},{2,0},{4,6},{6,4},{8,10},{10,8},{12,14},{14,12},{1,3},{3,1},... | collective-permute-start | bytes 331784 | tf_op jit(solution)/shard_map/ppermute | solution.py:322
  37.6 6.2 %collective-permute-start.10 = (bf16[72,768]{1,0:T(8,128)(2,1)S(1)}, bf16[72,768]{1,0:T(8,128)(2,1)S(1)}, u32[]{:S(2)}, u32[]{:S(2)}) collective-permute-start(bf16[72,768]{1,0:T(8,128)(2,1)S(1)} %get-tuple-element.50), channel_id=1, source_target_pairs={{0,4},{2,6},{4,0},{6,2},{8,12},{10,14},{12,8},{14,10},{1,5},{3,7},... | collective-permute-start | bytes 331784 | tf_op jit(solution)/shard_map/ppermute | solution.py:322
  43.8 12.1 %copy-start.1 = (bf16[768,1536]{1,0:T(8,128)(2,1)S(1)}, bf16[768,1536]{1,0:T(8,128)(2,1)}, u32[]{:S(2)}) copy-start(bf16[768,1536]{1,0:T(8,128)(2,1)} %gate_weight.1) | copy-start | bytes 7077892
  44.5 7.2 %collective-permute-start.11 = (bf16[72,768]{1,0:T(8,128)(2,1)S(1)}, bf16[72,768]{1,0:T(8,128)(2,1)S(1)}, u32[]{:S(2)}, u32[]{:S(2)}) collective-permute-start(bf16[72,768]{1,0:T(8,128)(2,1)S(1)} %get-tuple-element.52), channel_id=1, source_target_pairs={{0,8},{2,10},{4,12},{6,14},{8,0},{10,2},{12,4},{14,6},{1,9},{3,11}... | collective-permute-start | bytes 331784 | tf_op jit(solution)/shard_map/ppermute | solution.py:322
  51.8 4.9 %collective-permute-start.12 = (bf16[64,768]{1,0:T(8,128)(2,1)S(1)}, bf16[64,768]{1,0:T(8,128)(2,1)S(1)}, u32[]{:S(2)}, u32[]{:S(2)}) collective-permute-start(bf16[64,768]{1,0:T(8,128)(2,1)S(1)} %get-tuple-element.54), channel_id=1, source_target_pairs={{0,1},{1,0},{2,3},{3,2},{4,5},{5,4},{6,7},{7,6},{8,9},{9,8},{10,11... | collective-permute-start | bytes 294920 | tf_op jit(solution)/shard_map/ppermute | solution.py:322
  55.9 1.7 %copy-start.2 = (bf16[1536,768]{1,0:T(8,128)(2,1)S(1)}, bf16[1536,768]{1,0:T(8,128)(2,1)}, u32[]{:S(2)}) copy-start(bf16[1536,768]{1,0:T(8,128)(2,1)} %out_weight.1) | copy-start | bytes 7077892
where the time goes:
time: 60.7 us; the launch traced here: 60.4 us
  starting transfers between devices  20.9 us (34%)
  waiting for transfers between devices  17.9 us (29%)
  Pallas kernels  16.6 us (27%)
  local copies, waits for them, and re-layouts  4.69 us (8%)
    ppermute x13, starting transfers between devices, swap(): lax.ppermute(block, axis, [(i, i ^ bit) for i in range(lax.axis_size(axis...  20.9 us
    ppermute x13, waiting for transfers between devices, swap(): lax.ppermute(block, axis, [(i, i ^ bit) for i in range(lax.axis_size(axis...  17.9 us
    pallas_call x12, Pallas kernels, call(): pl.pallas_call(kernel, out_shape=outs, in_specs=[pl.BlockSpec(memory_spac...  16.6 us
    unnamed x27, local copies, waits for them, and re-layouts  4.14 us
  transfers between devices with their start and end apart: 13, of which 6 were waited for; matrix products, arithmetic and copies ran while one was open for 5% of the time, Pallas kernels for 8%

commit v1 on v0

--- a/solution.py
+++ b/solution.py
@@ -71,19 +71,35 @@
     out[...] = pixels[...]
 
 
+def pick_matrix():
+    row = lax.broadcasted_iota(jnp.int32, (256, 256), 0)
+    pixel = lax.broadcasted_iota(jnp.int32, (256, 256), 1)
+    return (pixel == (row & 15) * PATCH + (row >> 4)).astype(BF16)
+
+
+def turned(pick, values):
+    return lax.dot_general(pick, values, (((1,), (1,)), ((), ())), preferred_element_type=F32)
+
+
 def embed_kernel(*refs):
-    blocks, (weight, bias, out, strip, tail, wide) = refs[:-6], refs[-6:]
+    blocks, (weight, bias, out, picked, tail, wide) = refs[:-6], refs[-6:]
     col = lax.axis_index("cols")
     width = blocks[0].shape[1]
     count = len(blocks)
-    strip[0:LEAD, :] = jnp.zeros((LEAD, 128), F32)
-    strip[LEAD + count * width :, :] = jnp.zeros((LEAD, 128), F32)
-    blank = jnp.zeros((128 - WIN, width), F32)
+    tokens = count * width // PATCH
+    local = width // PATCH
+    zeros = jnp.zeros((PATCH, LEAD, 128), F32)
+    picked[:, 0:LEAD, :] = zeros
+    picked[:, LEAD + tokens :, :] = zeros
+    blank = jnp.zeros((128 - WIN, width), BF16)
+    pick = pick_matrix()
     for step, block in enumerate(blocks):
         source = col ^ step
-        values = block[0:WIN, :].astype(F32)
-        flipped = jnp.concatenate([values, blank], axis=0).T
-        strip[pl.ds(pl.multiple_of(LEAD + source * width, 8), width), :] = flipped
+        values = jnp.concatenate([block[0:WIN, :], blank], axis=0)
+        for group in range(width // 256):
+            found = turned(pick, values[:, 256 * group : 256 * (group + 1)])
+            first = pl.multiple_of(LEAD + source * local + 16 * group, 8)
+            picked[:, pl.ds(first, 16), :] = found.reshape(PATCH, 16, 128)
 
         @pl.when(source == count - 1)
         def _():
@@ -96,19 +112,17 @@
                 pieces += [whole[KERNEL * channel : KERNEL * channel + 8, width - 64 :]]
             pieces.append(jnp.zeros((128 - WIN, 64), F32))
             last = jnp.concatenate(pieces, axis=0)
-            last = jnp.concatenate([last, jnp.zeros((128, 64), F32)], axis=1).T
-            tail[0:72, :] = jnp.zeros((72, 128), F32)
-            tail[72:136, :] = last[:64]
-            tail[136:144, :] = jnp.zeros((8, 128), F32)
-
-    tokens = count * width // PATCH
+            last = jnp.concatenate([jnp.zeros((128, 64), F32), last, jnp.zeros((128, 128), F32)], axis=1)
+            found = turned(pick, last.astype(BF16)).reshape(PATCH, 16, 128)
+            tail[:, 0:8, :] = zeros
+            tail[:, 8:24, :] = found
+
     for offset in range(KERNEL):
-        start = LEAD - MARGIN + offset
-        lanes = pl.ds(offset * 128, 128)
-        part = jnp.concatenate(
-            [tail[pl.ds(start, LEAD, stride=PATCH), :], strip[pl.ds(start, tokens, stride=PATCH), :]], axis=0
-        )
-        wide[:, lanes] = part.astype(BF16)
+        place = offset - MARGIN + PATCH
+        shift, pixel = place // PATCH - 1, place % PATCH
+        ahead = tail[pixel, 8 + shift : 16 + shift, :]
+        part = jnp.concatenate([ahead, picked[pixel, LEAD + shift : LEAD + shift + tokens, :]], axis=0)
+        wide[:, offset * 128 : (offset + 1) * 128] = part.astype(BF16)
     grid = jnp.dot(wide[...], weight[...], preferred_element_type=F32)
     out[...] = (grid + bias[...]).astype(BF16)
 
@@ -127,6 +141,11 @@
 def spread(values, matrix):
     high, low = halves(values)
     return jnp.dot(high, matrix, preferred_element_type=F32) + jnp.dot(low, matrix, preferred_element_type=F32)
+
+
+def silu(values):
+    half = 0.5 * values
+    return half + half * jnp.tanh(half)
 
 
 def softplus(values):
@@ -179,7 +198,7 @@
         total = jnp.broadcast_to(conv_bias[...], (chunk, raw.shape[1]))
         for tap in range(taps):
             total = total + conv_weight[tap : tap + 1, :] * raw[pl.ds(LEAD - taps + 1 + tap + first, chunk), :]
-        mixed = (total * jax.nn.sigmoid(total)).astype(BF16)
+        mixed = silu(total).astype(BF16)
         x_out[pl.ds(first, chunk), :] = mixed[:, :E]
         mixed_f = mixed[:, E:].astype(F32)
         b_out[pl.ds(first, chunk), :] = mixed_f[:, :NSTATE].astype(BF16)
@@ -226,17 +245,23 @@
     message_out[...] = wire(values, decay)
 
 
-def join_kernel(bit, total, before, received, total_out, before_out, message_out):
+def join_kernel(bit, first, final, *refs):
+    refs = list(refs)
+    total = refs.pop(0)
+    before = None if first else refs.pop(0)
+    received = refs.pop(0)
     col = lax.axis_index("cols")
     later = (col & bit) != 0
     values, decay = total[0:NSTATE, :], total[NSTATE : NSTATE + 8, :]
     came, came_decay = unwire(received)
     last_decay = jnp.where(later, decay, came_decay)
     joined = scale(last_decay, jnp.where(later, came, values)) + jnp.where(later, values, came)
-    total_out[0:NSTATE, :] = joined
-    total_out[NSTATE : NSTATE + 8, :] = decay * came_decay
+    before_out, message_out = refs[:2]
+    if not final:
+        refs[2][0:NSTATE, :] = joined
+        refs[2][NSTATE : NSTATE + 8, :] = decay * came_decay
     message_out[...] = wire(joined, decay * came_decay)
-    if before is None:
+    if first:
         before_out[0:NSTATE, :] = jnp.where(later, came, 0.0)
         before_out[NSTATE : NSTATE + 8, :] = jnp.where(later, came_decay, 1.0)
     else:
@@ -260,9 +285,13 @@
     theirs_out[...] = jnp.where(upper, ahead, second).astype(BF16)
 
 
-def gate_kernel(normed, gate_weight, out):
+def gate_kernel(normed, gate_weight, local_a, local_b, cum, own_out, factor_out):
     gate = jnp.dot(normed[...], gate_weight[...], preferred_element_type=F32).astype(BF16).astype(F32)
-    out[...] = gate * jax.nn.sigmoid(gate)
+    gate = silu(gate)
+    half = local_a.shape[1]
+    own_out[:, :half] = local_a[...] * gate[:, :half]
+    own_out[:, half:] = local_b[...] * gate[:, half:]
+    factor_out[...] = spread(jnp.exp(cum[...]), spread_matrix()) * gate
 
 
 def intra_kernel(first, skip, x, b_mat, c_mat, step, cum, out):
@@ -303,18 +332,30 @@
         out[half:length, lanes] = jnp.concatenate(bottoms, axis=1) + direct[half:]
 
 
-def finish_kernel(local_a, local_b, gate, c_mat, cum, mine, theirs, embedded, out_gain, out_weight, out, state):
-    row = lax.axis_index("rows")
-    half = E // 2
-    state[:, pl.ds(pl.multiple_of(row * half, 128), half)] = mine[...]
-    state[:, pl.ds(pl.multiple_of((1 - row) * half, 128), half)] = theirs[...]
+def half_product(which, state, own, factor, c_mat, out_gain, out_weight):
+    half = own.shape[1] // 2
+    lanes = pl.ds(pl.multiple_of(which * half, 128), half)
     carried = jnp.dot(c_mat[...], state[...], preferred_element_type=F32)
-    carried = carried * spread(jnp.exp(cum[...]), spread_matrix())
-    local = jnp.concatenate([local_a[...], local_b[...]], axis=1)
-    gated = (local + carried) * gate[...]
-    mean_sq = jnp.mean(gated * gated, axis=-1, keepdims=True)
-    hidden = (gated * lax.rsqrt(mean_sq + 1e-05) * out_gain[...]).astype(BF16)
-    result = jnp.dot(hidden, out_weight[...], preferred_element_type=F32)
+    gated = own[:, lanes] + carried * factor[:, lanes]
+    squares = jnp.sum(gated * gated, axis=-1, keepdims=True)
+    hidden = (gated * out_gain[:, lanes]).astype(BF16)
+    return jnp.dot(hidden, out_weight[lanes, :], preferred_element_type=F32), squares
+
+
+def first_kernel(mine, own, factor, c_mat, out_gain, out_weight, product_out, squares_out):
+    product, squares = half_product(
+        lax.axis_index("rows"), mine, own, factor, c_mat, out_gain, out_weight
+    )
+    product_out[...] = product
+    squares_out[...] = jnp.broadcast_to(squares, squares_out.shape)
+
+
+def finish_kernel(theirs, own, factor, c_mat, out_gain, out_weight, product, squares, embedded, out):
+    rest, more = half_product(
+        1 - lax.axis_index("rows"), theirs, own, factor, c_mat, out_gain, out_weight
+    )
+    mean_sq = (squares[:, 0:1] + more) / own.shape[1]
+    result = (product[...] + rest) * lax.rsqrt(mean_sq + 1e-05)
     out[...] = (result + embedded[...].astype(F32)[LEAD:]).astype(BF16)
 
 
@@ -341,8 +382,8 @@
     weight = jnp.pad(weight, ((0, 0), (0, 128 - WIN), (0, 0))).reshape(KERNEL * 128, D)
     tokens = col_count * width // PATCH
     scratch = [
-        pltpu.VMEM((2 * LEAD + col_count * width, 128), F32),
-        pltpu.VMEM((144, 128), F32),
+        pltpu.VMEM((PATCH, 2 * LEAD + tokens, 128), F32),
+        pltpu.VMEM((PATCH, 24, 128), F32),
         pltpu.VMEM((LEAD + tokens, KERNEL * 128), BF16),
     ]
     flops = 2 * tokens * KERNEL * 128 * D
@@ -449,10 +490,6 @@
     came = swap(send, "rows", 1)
     summary, message = shape((packed, half), F32), shape((packed, half))
     total, out = call(pair_kernel, (keep, came), [summary, message])
-    gate = call(
-        gate_kernel, (normed, gate_weight), shape((length, E), F32),
-        flops=2 * length * D * E, moved=4 << 20, limit=8,
-    )
     locals_ = []
     for part in range(2):
         locals_.append(
@@ -462,25 +499,32 @@
                 flops=HEADS * length * length * 128, moved=2 << 20, limit=8,
             )
         )
+    own, factor = call(
+        gate_kernel, (normed, gate_weight, *locals_, cum), [shape((length, E), F32)] * 2,
+        flops=2 * length * D * E, moved=4 << 20, limit=8,
+    )
     before, bit = None, 1
     while 2 * bit < col_count:
         arrived = swap(out, "cols", bit)
-        if before is None:
-            kernel = lambda t, r, *outs, bit=bit: join_kernel(bit, t, None, r, *outs)
-            total, before, out = call(kernel, (total, arrived), [summary, summary, message])
-        else:
-            total, before, out = call(partial(join_kernel, bit), (total, before, arrived), [summary, summary, message])
+        first, final = before is None, 4 * bit >= col_count
+        inputs = (total, arrived) if first else (total, before, arrived)
+        before, out, *total = call(
+            partial(join_kernel, bit, first, final), inputs, [summary, message] + [summary] * (not final)
+        )
+        total = total[0] if total else None
         bit *= 2
     arrived = swap(out, "cols", bit)
     entering = shape((NSTATE, half))
     mine, theirs = call(partial(enter_kernel, bit), (before, arrived, keep, came), [entering, entering])
     theirs = swap(theirs, "rows", 1)
+    common = (own, factor, c_mat, line(out_gain), out_weight)
+    product, squares = call(
+        first_kernel, (mine, *common), [shape((length, D), F32), shape((length, 128), F32)],
+        flops=length * D * E, moved=4 << 20, limit=8,
+    )
     return call(
-        finish_kernel,
-        (*locals_, gate, c_mat, cum, mine, theirs, embedded, line(out_gain), out_weight),
-        shape((length, D)),
-        [pltpu.VMEM((NSTATE, E), BF16)],
-        flops=2 * length * D * E, moved=4 << 20, limit=16,
+        finish_kernel, (theirs, *common, product, squares, embedded), shape((length, D)),
+        flops=length * D * E, moved=4 << 20, limit=8,
     )
 
 

time: 60.7 us -> 57.6 us (0.949)
  waiting for transfers between devices: 17.9 us -> 15.9 us
  Pallas kernels: 16.6 us -> 15.9 us
    ppermute x13, waiting for transfers between devices: 17.9 us -> 15.9 us  [swap(): lax.ppermute(block, axis, [(i, i ^ bit) for i in range(lax.axis_size(axis...]
    pallas_call x12 -> x13, Pallas kernels: 16.6 us -> 15.9 us  [call(): pl.pallas_call(kernel, out_shape=outs, in_specs=[pl.BlockSpec(memory_spac...]
  transfers between devices with their start and end apart: 13 -> 13, of which waited for: 6 -> 6; matrix products, arithmetic and copies ran while one was open for 5% -> 5% of each run, Pallas kernels for 8% -> 10%
where the time goes in v1:
time: 57.6 us; the launch traced here: 57.4 us
  starting transfers between devices  21 us (36%)
  Pallas kernels  15.9 us (28%)
  waiting for transfers between devices  15.9 us (28%)
  local copies, waits for them, and re-layouts  4.25 us (7%)
    ppermute x13, starting transfers between devices, swap(): lax.ppermute(block, axis, [(i, i ^ bit) for i in range(lax.axis_size(axis...  21 us
    ppermute x13, waiting for transfers between devices, swap(): lax.ppermute(block, axis, [(i, i ^ bit) for i in range(lax.axis_size(axis...  15.9 us
    pallas_call x13, Pallas kernels, call(): pl.pallas_call(kernel, out_shape=outs, in_specs=[pl.BlockSpec(memory_spac...  15.9 us
    unnamed x27, local copies, waits for them, and re-layouts  3.71 us
  transfers between devices with their start and end apart: 13, of which 6 were waited for; matrix products, arithmetic and copies ran while one was open for 5% of the time, Pallas kernels for 10%

profile of v1, /device:TPU:0, one launch (start us, length us, event | category | flops | bytes accessed | tf_op | source)
XLA Modules:
  0.0 57.4 jit_solution(15533709395248727585)
XLA Ops:
  0.0 0.5 collective-permute-start
  0.5 1.0 %copy-done.3 = bf16[3,128,512]{2,1,0:T(8,128)(2,1)S(1)} copy-done((bf16[3,128,512]{2,1,0:T(8,128)(2,1)S(1)}, bf16[3,128,512]{2,1,0:T(8,128)(2,1)}, u32[]{:S(2)}) %copy-start.3) | copy-done | bytes 393240
  1.5 0.5 collective-permute-done.partner
  2.1 0.3 shard_map.137
  2.3 2.9 %collective-permute-start.1 = (bf16[80,512]{1,0:T(8,128)(2,1)S(1)}, bf16[80,512]{1,0:T(8,128)(2,1)S(1)}, u32[]{:S(2)}, u32[]{:S(2)}) collective-permute-start(bf16[80,512]{1,0:T(8,128)(2,1)S(1)} %get-tuple-element.35), channel_id=1, source_target_pairs={{0,2},{2,0},{4,6},{6,4},{8,10},{10,8},{12,14},{14,12},{1,3},{3,1},... | collective-permute-start | bytes 245768 | tf_op jit(solution)/shard_map/ppermute | solution.py:363
  5.3 1.6 %collective-permute-start.2 = (bf16[80,512]{1,0:T(8,128)(2,1)S(1)}, bf16[80,512]{1,0:T(8,128)(2,1)S(1)}, u32[]{:S(2)}, u32[]{:S(2)}) collective-permute-start(bf16[80,512]{1,0:T(8,128)(2,1)S(1)} %get-tuple-element.36), channel_id=1, source_target_pairs={{0,4},{2,6},{4,0},{6,2},{8,12},{10,14},{12,8},{14,10},{1,5},{3,7},... | collective-permute-start | bytes 245768 | tf_op jit(solution)/shard_map/ppermute | solution.py:363
  6.8 3.0 %collective-permute-start.4 = (bf16[80,512]{1,0:T(8,128)(2,1)S(1)}, bf16[80,512]{1,0:T(8,128)(2,1)S(1)}, u32[]{:S(2)}, u32[]{:S(2)}) collective-permute-start(bf16[80,512]{1,0:T(8,128)(2,1)S(1)} %get-tuple-element.38), channel_id=1, source_target_pairs={{0,8},{2,10},{4,12},{6,14},{8,0},{10,2},{12,4},{14,6},{1,9},{3,11}... | collective-permute-start | bytes 245768 | tf_op jit(solution)/shard_map/ppermute | solution.py:363
  9.8 1.3 %collective-permute-start.5 = (bf16[80,512]{1,0:T(8,128)(2,1)S(1)}, bf16[80,512]{1,0:T(8,128)(2,1)S(1)}, u32[]{:S(2)}, u32[]{:S(2)}) collective-permute-start(bf16[80,512]{1,0:T(8,128)(2,1)S(1)} %get-tuple-element.39), channel_id=1, source_target_pairs={{0,10},{2,8},{4,14},{6,12},{8,2},{10,0},{12,6},{14,4},{1,11},{3,9}... | collective-permute-start | bytes 245768 | tf_op jit(solution)/shard_map/ppermute | solution.py:363
  11.1 3.6 %collective-permute-start.6 = (bf16[80,512]{1,0:T(8,128)(2,1)S(1)}, bf16[80,512]{1,0:T(8,128)(2,1)S(1)}, u32[]{:S(2)}, u32[]{:S(2)}) collective-permute-start(bf16[80,512]{1,0:T(8,128)(2,1)S(1)} %get-tuple-element.40), channel_id=1, source_target_pairs={{0,12},{2,14},{4,8},{6,10},{8,4},{10,6},{12,0},{14,2},{1,13},{3,15... | collective-permute-start | bytes 245768 | tf_op jit(solution)/shard_map/ppermute | solution.py:363
  14.7 0.1 collective-permute-start.7
  14.8 2.3 %copy.15 = bf16[24,24,3,768]{3,0,2,1:T(8,128)(2,1)S(1)} copy(bf16[24,24,3,768]{3,1,2,0:T(8,128)(2,1)} %param.15) | data formatting | bytes 5308416 | tf_op args[1]
  17.1 0.5 pad.4
  17.7 5.2 %collective-permute-done.5.refs_5_ = bf16[80,512]{1,0:T(8,128)(2,1)S(1)} collective-permute-done((bf16[80,512]{1,0:T(8,128)(2,1)S(1)}, bf16[80,512]{1,0:T(8,128)(2,1)S(1)}, u32[]{:S(2)}, u32[]{:S(2)}) %collective-permute-start.5) | collective-permute-done | bytes 81952 | tf_op jit(solution)/shard_map/ppermute | solution.py:363
  23.0 3.6 %shard_map.138.embedded = bf16[264,768]{1,0:T(8,128)(2,1)S(1)} custom-call(bf16[80,512]{1,0:T(8,128)(2,1)S(1)} %get-tuple-element.34.refs_0_, bf16[80,512]{1,0:T(8,128)(2,1)S(1)} %collective-permute-done.1.refs_1_, bf16[80,512]{1,0:T(8,128)(2,1)S(1)} %collective-permute-done.2.refs_2_, bf16[80,512]{1,0:T(8,128)(2,1)S(1)} %collective-permute-done.3.refs_3_, ...), custom_call_target="tpu_custom_call" | custom-call | flops 1207959552 | bytes 6291456 | tf_op jit(solution)/shard_map/pallas_call | solution.py:31
  26.7 4.5 %shard_map.139 = (bf16[256,768]{1,0:T(8,128)(2,1)S(1)}, bf16[256,1536]{1,0:T(8,128)(2,1)S(1)}, bf16[256,64]{1,0:T(8,128)(2,1)S(1)}, bf16[256,64]{1,0:T(8,128)(2,...) custom-call(bf16[264,768]{1,0:T(8,128)(2,1)S(1)} %shard_map.138.embe, ...), custom_call_target="tpu_custom_call" | custom-call | flops 654311424 | bytes 4194304 | tf_op jit(solution)/shard_map/pallas_call | solution.py:31
  31.2 0.1 collective-permute-start.8
  31.3 1.3 %collective-permute-done.8.received = bf16[72,768]{1,0:T(8,128)(2,1)S(1)} collective-permute-done((bf16[72,768]{1,0:T(8,128)(2,1)S(1)}, bf16[72,768]{1,0:T(8,128)(2,1)S(1)}, u32[]{:S(2)}, u32[]{:S(2)}) %collective-permute-start.8) | collective-permute-done | bytes 110624 | tf_op jit(solution)/shard_map/ppermute | solution.py:363
  32.6 1.0 %collective-permute-start.9 = (bf16[72,768]{1,0:T(8,128)(2,1)S(1)}, bf16[72,768]{1,0:T(8,128)(2,1)S(1)}, u32[]{:S(2)}, u32[]{:S(2)}) collective-permute-start(bf16[72,768]{1,0:T(8,128)(2,1)S(1)} %get-tuple-element.45), channel_id=1, source_target_pairs={{0,2},{2,0},{4,6},{6,4},{8,10},{10,8},{12,14},{14,12},{1,3},{3,1},... | collective-permute-start | bytes 331784 | tf_op jit(solution)/shard_map/ppermute | solution.py:363
  33.6 4.2 %collective-permute-done.9.refs_1_ = bf16[72,768]{1,0:T(8,128)(2,1)S(1)} collective-permute-done((bf16[72,768]{1,0:T(8,128)(2,1)S(1)}, bf16[72,768]{1,0:T(8,128)(2,1)S(1)}, u32[]{:S(2)}, u32[]{:S(2)}) %collective-permute-start.9) | collective-permute-done | bytes 110624 | tf_op jit(solution)/shard_map/ppermute | solution.py:363
  37.9 3.5 %collective-permute-start.10 = (bf16[72,768]{1,0:T(8,128)(2,1)S(1)}, bf16[72,768]{1,0:T(8,128)(2,1)S(1)}, u32[]{:S(2)}, u32[]{:S(2)}) collective-permute-start(bf16[72,768]{1,0:T(8,128)(2,1)S(1)} %get-tuple-element.48), channel_id=1, source_target_pairs={{0,4},{2,6},{4,0},{6,2},{8,12},{10,14},{12,8},{14,10},{1,5},{3,7},... | collective-permute-start | bytes 331784 | tf_op jit(solution)/shard_map/ppermute | solution.py:363
  41.4 2.7 %collective-permute-done.10.refs_2_ = bf16[72,768]{1,0:T(8,128)(2,1)S(1)} collective-permute-done((bf16[72,768]{1,0:T(8,128)(2,1)S(1)}, bf16[72,768]{1,0:T(8,128)(2,1)S(1)}, u32[]{:S(2)}, u32[]{:S(2)}) %collective-permute-start.10) | collective-permute-done | bytes 110624 | tf_op jit(solution)/shard_map/ppermute | solution.py:363
  44.1 0.1 shard_map.142
  44.2 3.4 %collective-permute-start.11 = (bf16[72,768]{1,0:T(8,128)(2,1)S(1)}, bf16[72,768]{1,0:T(8,128)(2,1)S(1)}, u32[]{:S(2)}, u32[]{:S(2)}) collective-permute-start(bf16[72,768]{1,0:T(8,128)(2,1)S(1)} %get-tuple-element.50), channel_id=1, source_target_pairs={{0,8},{2,10},{4,12},{6,14},{8,0},{10,2},{12,4},{14,6},{1,9},{3,11}... | collective-permute-start | bytes 331784 | tf_op jit(solution)/shard_map/ppermute | solution.py:363
  47.6 2.0 %shard_map.145.local_b = f32[256,768]{1,0:T(8,128)S(1)} custom-call(f32[24]{0:T(128)S(1)} %copy-done.6, bf16[256,1536]{1,0:T(8,128)(2,1)S(1)} %get-tuple-element.53.x, bf16[256,64]{1,0:T(8,128)(2,1)S(1)} %get-tuple-element.54.b_mat, bf16[256,64]{1,0:T(8,128)(2,1)S(1)} %get-tuple-element.55.c_mat, f32[256,24]{1,0:T(8,128)S(1)} %get-tuple-element.56.step, ...), custom_call_target="tpu_custom_call" | custom-call | flops 201326592 | bytes 2097152 | tf_op jit(solution)/shard_map/pallas_call | solution.py:31
  49.6 1.9 %collective-permute-done.11.last = bf16[72,768]{1,0:T(8,128)(2,1)S(1)} collective-permute-done((bf16[72,768]{1,0:T(8,128)(2,1)S(1)}, bf16[72,768]{1,0:T(8,128)(2,1)S(1)}, u32[]{:S(2)}, u32[]{:S(2)}) %collective-permute-start.11) | collective-permute-done | bytes 110624 | tf_op jit(solution)/shard_map/ppermute | solution.py:363
  51.5 0.1 shard_map.143
  51.6 0.1 collective-permute-start.12
  51.7 2.0 %shard_map.144.local_a = f32[256,768]{1,0:T(8,128)S(1)} custom-call(f32[24]{0:T(128)S(1)} %copy-done.6, bf16[256,1536]{1,0:T(8,128)(2,1)S(1)} %get-tuple-element.53.x, bf16[256,64]{1,0:T(8,128)(2,1)S(1)} %get-tuple-element.54.b_mat, bf16[256,64]{1,0:T(8,128)(2,1)S(1)} %get-tuple-element.55.c_mat, f32[256,24]{1,0:T(8,128)S(1)} %get-tuple-element.56.step, ...), custom_call_target="tpu_custom_call" | custom-call | flops 201326592 | bytes 2097152 | tf_op jit(solution)/shard_map/pallas_call | solution.py:31
  53.7 1.2 %shard_map.146 = (f32[256,1536]{1,0:T(8,128)S(1)}, f32[256,1536]{1,0:T(8,128)S(1)}) custom-call(bf16[256,768]{1,0:T(8,128)(2,1)S(1)} %get-tuple-element.52.normed, bf16[768,1536]{1,0:T(8,128)(2,1)S(1)} %copy-done.2, f32[256,768]{1,0:T(8,128)S(1)} %shard_map.144.local_a, f32[256,768]{1,0:T(8,128)S(1)} %shard_map.145.local_b, f32[256,24]{1,0:T(8,128)S(1)} %get-tuple-element.57.cum), custom_call_target="tpu_custom_call" | custom-call | flops 603979776 | bytes 4194304 | tf_op jit(solution)/shard_map/pallas_call | solution.py:31
  54.9 0.4 copy-done
  55.3 0.6 %shard_map.147 = (f32[256,768]{1,0:T(8,128)S(1)}, f32[256,128]{1,0:T(8,128)S(1)}) custom-call(bf16[64,768]{1,0:T(8,128)(2,1)S(1)} %get-tuple-element.60.mine, f32[256,1536]{1,0:T(8,128)S(1)} %get-tuple-element.58.own, f32[256,1536]{1,0:T(8,128)S(1)} %get-tuple-element.59.factor, bf16[256,64]{1,0:T(8,128)(2,1)S(1)} %get-tuple-element.55.c_mat, ...), custom_call_target="tpu_custom_call" | custom-call | flops 301989888 | bytes 4194304 | tf_op jit(solution)/shard_map/pallas_call | solution.py:31
  56.0 1.4 %shard_map.148 = bf16[256,768]{1,0:T(8,128)(2,1)} custom-call(bf16[64,768]{1,0:T(8,128)(2,1)S(1)} %collective-permute-done.12.theirs, f32[256,1536]{1,0:T(8,128)S(1)} %get-tuple-element.58.own, f32[256,1536]{1,0:T(8,128)S(1)} %get-tuple-element.59.factor, bf16[256,64]{1,0:T(8,128)(2,1)S(1)} %get-tuple-element.55.c_mat, f32[1,1536]{1,0:T(1,128)S(1)} %reshape.31.out_gain, ...), custom_call_target="tpu_custom_call" | custom-call | flops 301989888 | bytes 4194304 | tf_op jit(solution)/shard_map/pallas_call | solution.py:31
  (39 shorter events, 0.3 us)
Async XLA Ops:
  0.0 2.1 %collective-permute-start = (bf16[3,128,512]{2,1,0:T(8,128)(2,1)}, bf16[3,128,512]{2,1,0:T(8,128)(2,1)S(1)}, u32[]{:S(2)}, u32[]{:S(2)}) collective-permute-start(bf16[3,128,512]{2,1,0:T(8,128)(2,1)} %pixels.1), channel_id=1, source_target_pairs={{0,1},{1,0},{2,3},{3,2},{4,5},{5,4},{6,7},{7,6},{8,9},{9,8},{10,11... | collective-permute-start | bytes 1179656 | tf_op jit(solution)/shard_map/ppermute | solution.py:363
  0.5 1.0 %copy-start.3 = (bf16[3,128,512]{2,1,0:T(8,128)(2,1)S(1)}, bf16[3,128,512]{2,1,0:T(8,128)(2,1)}, u32[]{:S(2)}) copy-start(bf16[3,128,512]{2,1,0:T(8,128)(2,1)} %pixels.1) | copy-start | bytes 1179652
  2.3 8.8 %collective-permute-start.1 = (bf16[80,512]{1,0:T(8,128)(2,1)S(1)}, bf16[80,512]{1,0:T(8,128)(2,1)S(1)}, u32[]{:S(2)}, u32[]{:S(2)}) collective-permute-start(bf16[80,512]{1,0:T(8,128)(2,1)S(1)} %get-tuple-element.35), channel_id=1, source_target_pairs={{0,2},{2,0},{4,6},{6,4},{8,10},{10,8},{12,14},{14,12},{1,3},{3,1},... | collective-permute-start | bytes 245768 | tf_op jit(solution)/shard_map/ppermute | solution.py:363
  5.3 9.5 %collective-permute-start.2 = (bf16[80,512]{1,0:T(8,128)(2,1)S(1)}, bf16[80,512]{1,0:T(8,128)(2,1)S(1)}, u32[]{:S(2)}, u32[]{:S(2)}) collective-permute-start(bf16[80,512]{1,0:T(8,128)(2,1)S(1)} %get-tuple-element.36), channel_id=1, source_target_pairs={{0,4},{2,6},{4,0},{6,2},{8,12},{10,14},{12,8},{14,10},{1,5},{3,7},... | collective-permute-start | bytes 245768 | tf_op jit(solution)/shard_map/ppermute | solution.py:363
  6.8 10.8 %collective-permute-start.3 = (bf16[80,512]{1,0:T(8,128)(2,1)S(1)}, bf16[80,512]{1,0:T(8,128)(2,1)S(1)}, u32[]{:S(2)}, u32[]{:S(2)}) collective-permute-start(bf16[80,512]{1,0:T(8,128)(2,1)S(1)} %get-tuple-element.37), channel_id=1, source_target_pairs={{0,6},{2,4},{4,2},{6,0},{8,14},{10,12},{12,10},{14,8},{1,7},{3,5},... | collective-permute-start | bytes 245768 | tf_op jit(solution)/shard_map/ppermute | solution.py:363
  6.8 10.8 %collective-permute-start.4 = (bf16[80,512]{1,0:T(8,128)(2,1)S(1)}, bf16[80,512]{1,0:T(8,128)(2,1)S(1)}, u32[]{:S(2)}, u32[]{:S(2)}) collective-permute-start(bf16[80,512]{1,0:T(8,128)(2,1)S(1)} %get-tuple-element.38), channel_id=1, source_target_pairs={{0,8},{2,10},{4,12},{6,14},{8,0},{10,2},{12,4},{14,6},{1,9},{3,11}... | collective-permute-start | bytes 245768 | tf_op jit(solution)/shard_map/ppermute | solution.py:363
  9.8 13.1 %collective-permute-start.5 = (bf16[80,512]{1,0:T(8,128)(2,1)S(1)}, bf16[80,512]{1,0:T(8,128)(2,1)S(1)}, u32[]{:S(2)}, u32[]{:S(2)}) collective-permute-start(bf16[80,512]{1,0:T(8,128)(2,1)S(1)} %get-tuple-element.39), channel_id=1, source_target_pairs={{0,10},{2,8},{4,14},{6,12},{8,2},{10,0},{12,6},{14,4},{1,11},{3,9}... | collective-permute-start | bytes 245768 | tf_op jit(solution)/shard_map/ppermute | solution.py:363
  11.1 11.8 %collective-permute-start.6 = (bf16[80,512]{1,0:T(8,128)(2,1)S(1)}, bf16[80,512]{1,0:T(8,128)(2,1)S(1)}, u32[]{:S(2)}, u32[]{:S(2)}) collective-permute-start(bf16[80,512]{1,0:T(8,128)(2,1)S(1)} %get-tuple-element.40), channel_id=1, source_target_pairs={{0,12},{2,14},{4,8},{6,10},{8,4},{10,6},{12,0},{14,2},{1,13},{3,15... | collective-permute-start | bytes 245768 | tf_op jit(solution)/shard_map/ppermute | solution.py:363
  14.7 2.4 %copy-start.11 = (f32[768]{0:T(1024)S(1)}, f32[768]{0:T(1024)}, u32[]{:S(2)}) copy-start(f32[768]{0:T(1024)} %param.16) | copy-start | bytes 9220
  14.7 2.4 %copy-start.10 = (f32[1664]{0:T(1024)S(1)}, f32[1664]{0:T(1024)}, u32[]{:S(2)}) copy-start(f32[1664]{0:T(1024)} %param.24) | copy-start | bytes 19972
  14.7 2.4 %copy-start.12 = (f32[768]{0:T(1024)S(1)}, f32[768]{0:T(1024)}, u32[]{:S(2)}) copy-start(f32[768]{0:T(1024)} %param.17) | copy-start | bytes 9220
  14.7 8.2 %collective-permute-start.7 = (bf16[80,512]{1,0:T(8,128)(2,1)S(1)}, bf16[80,512]{1,0:T(8,128)(2,1)S(1)}, u32[]{:S(2)}, u32[]{:S(2)}) collective-permute-start(bf16[80,512]{1,0:T(8,128)(2,1)S(1)} %get-tuple-element.41), channel_id=1, source_target_pairs={{0,14},{2,12},{4,10},{6,8},{8,6},{10,4},{12,2},{14,0},{1,15},{3,13... | collective-permute-start | bytes 245768 | tf_op jit(solution)/shard_map/ppermute | solution.py:363
  22.9 3.7 %copy-start.1 = (bf16[768,1664]{1,0:T(8,128)(2,1)S(1)}, bf16[768,1664]{1,0:T(8,128)(2,1)}, u32[]{:S(2)}) copy-start(bf16[768,1664]{1,0:T(8,128)(2,1)} %mix_weight.1) | copy-start | bytes 7667716
  22.9 3.7 %copy-start.4 = (bf16[768,24]{0,1:T(8,128)(2,1)S(1)}, bf16[768,24]{0,1:T(8,128)(2,1)}, u32[]{:S(2)}) copy-start(bf16[768,24]{0,1:T(8,128)(2,1)} %param.20) | copy-start | bytes 110596
  22.9 3.7 %copy-start.5 = (f32[4,1664]{1,0:T(4,128)S(1)}, f32[4,1664]{1,0:T(4,128)}, u32[]{:S(2)}) copy-start(f32[4,1664]{1,0:T(4,128)} %conv_weight.1) | copy-start | bytes 79876
  23.0 3.7 %copy-start.7 = (f32[24]{0:T(128)S(1)}, f32[24]{0:T(128)}, u32[]{:S(2)}) copy-start(f32[24]{0:T(128)} %param.21) | copy-start | bytes 292
  23.0 3.7 %copy-start.8 = (f32[24]{0:T(128)S(1)}, f32[24]{0:T(128)}, u32[]{:S(2)}) copy-start(f32[24]{0:T(128)} %param.22) | copy-start | bytes 292
  26.6 21.0 %copy-start.9 = (f32[1536]{0:T(1024)S(1)}, f32[1536]{0:T(1024)}, u32[]{:S(2)}) copy-start(f32[1536]{0:T(1024)} %param.26) | copy-start | bytes 18436
  26.6 21.0 %copy-start.6 = (f32[24]{0:T(128)S(1)}, f32[24]{0:T(128)}, u32[]{:S(2)}) copy-start(f32[24]{0:T(128)} %skip.3) | copy-start | bytes 292
  31.2 1.4 %collective-permute-start.8 = (bf16[72,768]{1,0:T(8,128)(2,1)S(1)}, bf16[72,768]{1,0:T(8,128)(2,1)S(1)}, u32[]{:S(2)}, u32[]{:S(2)}) collective-permute-start(bf16[72,768]{1,0:T(8,128)(2,1)S(1)} %get-tuple-element.43), channel_id=1, source_target_pairs={{0,1},{1,0},{2,3},{3,2},{4,5},{5,4},{6,7},{7,6},{8,9},{9,8},{10,11... | collective-permute-start | bytes 331784 | tf_op jit(solution)/shard_map/ppermute | solution.py:363
  32.6 5.2 %collective-permute-start.9 = (bf16[72,768]{1,0:T(8,128)(2,1)S(1)}, bf16[72,768]{1,0:T(8,128)(2,1)S(1)}, u32[]{:S(2)}, u32[]{:S(2)}) collective-permute-start(bf16[72,768]{1,0:T(8,128)(2,1)S(1)} %get-tuple-element.45), channel_id=1, source_target_pairs={{0,2},{2,0},{4,6},{6,4},{8,10},{10,8},{12,14},{14,12},{1,3},{3,1},... | collective-permute-start | bytes 331784 | tf_op jit(solution)/shard_map/ppermute | solution.py:363
  37.9 6.2 %collective-permute-start.10 = (bf16[72,768]{1,0:T(8,128)(2,1)S(1)}, bf16[72,768]{1,0:T(8,128)(2,1)S(1)}, u32[]{:S(2)}, u32[]{:S(2)}) collective-permute-start(bf16[72,768]{1,0:T(8,128)(2,1)S(1)} %get-tuple-element.48), channel_id=1, source_target_pairs={{0,4},{2,6},{4,0},{6,2},{8,12},{10,14},{12,8},{14,10},{1,5},{3,7},... | collective-permute-start | bytes 331784 | tf_op jit(solution)/shard_map/ppermute | solution.py:363
  44.1 9.6 %copy-start.2 = (bf16[768,1536]{1,0:T(8,128)(2,1)S(1)}, bf16[768,1536]{1,0:T(8,128)(2,1)}, u32[]{:S(2)}) copy-start(bf16[768,1536]{1,0:T(8,128)(2,1)} %gate_weight.1) | copy-start | bytes 7077892
  44.2 7.3 %collective-permute-start.11 = (bf16[72,768]{1,0:T(8,128)(2,1)S(1)}, bf16[72,768]{1,0:T(8,128)(2,1)S(1)}, u32[]{:S(2)}, u32[]{:S(2)}) collective-permute-start(bf16[72,768]{1,0:T(8,128)(2,1)S(1)} %get-tuple-element.50), channel_id=1, source_target_pairs={{0,8},{2,10},{4,12},{6,14},{8,0},{10,2},{12,4},{14,6},{1,9},{3,11}... | collective-permute-start | bytes 331784 | tf_op jit(solution)/shard_map/ppermute | solution.py:363
  51.6 4.3 %collective-permute-start.12 = (bf16[64,768]{1,0:T(8,128)(2,1)S(1)}, bf16[64,768]{1,0:T(8,128)(2,1)S(1)}, u32[]{:S(2)}, u32[]{:S(2)}) collective-permute-start(bf16[64,768]{1,0:T(8,128)(2,1)S(1)} %get-tuple-element.51), channel_id=1, source_target_pairs={{0,1},{1,0},{2,3},{3,2},{4,5},{5,4},{6,7},{7,6},{8,9},{9,8},{10,11... | collective-permute-start | bytes 294920 | tf_op jit(solution)/shard_map/ppermute | solution.py:363
  53.7 1.7 %copy-start = (bf16[1536,768]{1,0:T(8,128)(2,1)S(1)}, bf16[1536,768]{1,0:T(8,128)(2,1)}, u32[]{:S(2)}) copy-start(bf16[1536,768]{1,0:T(8,128)(2,1)} %out_weight.3) | copy-start | bytes 7077892

commit v2 on v1

--- a/solution.py
+++ b/solution.py
@@ -93,6 +93,8 @@
     picked[:, LEAD + tokens :, :] = zeros
     blank = jnp.zeros((128 - WIN, width), BF16)
     pick = pick_matrix()
+    edge = jnp.zeros((WIN + 8, 128), F32)
+    extra = jnp.zeros((8, 128 * CHAN), F32)
     for step, block in enumerate(blocks):
         source = col ^ step
         values = jnp.concatenate([block[0:WIN, :], blank], axis=0)
@@ -100,22 +102,19 @@
             found = turned(pick, values[:, 256 * group : 256 * (group + 1)])
             first = pl.multiple_of(LEAD + source * local + 16 * group, 8)
             picked[:, pl.ds(first, 16), :] = found.reshape(PATCH, 16, 128)
-
-        @pl.when(source == count - 1)
-        def _():
-            whole = block[...].astype(F32)
-            extra = whole[WIN : WIN + 8]
-            pieces = []
-            for channel in range(CHAN):
-                pieces += [extra[:, 128 * channel : 128 * channel + 64]]
-                pieces += [extra[:, 128 * channel + 64 : 128 * channel + 128]]
-                pieces += [whole[KERNEL * channel : KERNEL * channel + 8, width - 64 :]]
-            pieces.append(jnp.zeros((128 - WIN, 64), F32))
-            last = jnp.concatenate(pieces, axis=0)
-            last = jnp.concatenate([jnp.zeros((128, 64), F32), last, jnp.zeros((128, 128), F32)], axis=1)
-            found = turned(pick, last.astype(BF16)).reshape(PATCH, 16, 128)
-            tail[:, 0:8, :] = zeros
-            tail[:, 8:24, :] = found
+        last = source == count - 1
+        edge = jnp.where(last, block[:, width - 128 :].astype(F32), edge)
+        extra = jnp.where(last, block[WIN - 8 : WIN + 8, : 128 * CHAN].astype(F32)[8:], extra)
+    pieces = []
+    for channel in range(CHAN):
+        pieces += [extra[:, 128 * channel : 128 * channel + 64]]
+        pieces += [extra[:, 128 * channel + 64 : 128 * channel + 128]]
+        pieces += [edge[KERNEL * channel : KERNEL * channel + 8, 64:]]
+    pieces.append(jnp.zeros((128 - WIN, 64), F32))
+    last = jnp.concatenate(pieces, axis=0)
+    last = jnp.concatenate([jnp.zeros((128, 64), F32), last, jnp.zeros((128, 128), F32)], axis=1)
+    tail[:, 0:8, :] = zeros
+    tail[:, 8:24, :] = turned(pick, last.astype(BF16)).reshape(PATCH, 16, 128)
 
     for offset in range(KERNEL):
         place = offset - MARGIN + PATCH
@@ -155,21 +154,17 @@
 
 def mix_kernel(
     embedded, norm_gain, mix_weight, step_weight, step_bias, log_rate, conv_weight, conv_bias,
-    normed_out, x_out, b_out, c_out, step_out, cum_out, keep_out, send_out, raw, state,
+    normed_out, x_out, b_out, c_out, step_out, cum_out, keep_out, send_out, state,
 ):
     col, row = lax.axis_index("cols"), lax.axis_index("rows")
     resid = embedded[...].astype(F32)
     mean_sq = jnp.mean(resid * resid, axis=-1, keepdims=True)
     normed_f = resid * lax.rsqrt(mean_sq + 1e-05) * norm_gain[...]
-    normed = normed_f.astype(BF16)
+    rows = lax.broadcasted_iota(jnp.int32, normed_f.shape, 0)
+    blank = (rows < LEAD) & (col == 0) & (row == 0)
+    normed = jnp.where(blank, 0.0, normed_f).astype(BF16)
     normed_out[...] = normed_f[LEAD:].astype(BF16)
     length = embedded.shape[0] - LEAD
-    raw[...] = jnp.dot(normed, mix_weight[...], preferred_element_type=F32).astype(BF16).astype(F32)
-
-    @pl.when((col == 0) & (row == 0))
-    def _():
-        raw[0:LEAD, :] = jnp.zeros((LEAD, raw.shape[1]), F32)
-
     step_raw = lax.dot_general(
         normed, step_weight[...], (((1,), (1,)), ((), ())), preferred_element_type=F32
     )[LEAD:]
@@ -180,34 +175,46 @@
     ).astype(BF16)
     high = log_decay.astype(BF16)
     middle = (log_decay - high.astype(F32)).astype(BF16)
+    low = (log_decay - high.astype(F32) - middle.astype(F32)).astype(BF16)
     cum = jnp.dot(lower, high, preferred_element_type=F32)
     cum = cum + jnp.dot(lower, middle, preferred_element_type=F32)
-    low = (log_decay - high.astype(F32) - middle.astype(F32)).astype(BF16)
     cum = cum + jnp.dot(lower, low, preferred_element_type=F32)
     step_out[...] = step
     cum_out[...] = cum
     matrix = spread_matrix()
     last = cum[length - 1 :]
-    to_end = spread(jnp.exp(last - cum) * step, matrix)
-    decay = spread(jnp.broadcast_to(jnp.exp(last), (8, HEADS)), matrix)
+    scales = (jnp.exp(last - cum) * step).astype(BF16)
+    state[NSTATE : NSTATE + 8, :] = spread(jnp.broadcast_to(jnp.exp(last), (8, HEADS)), matrix)
     taps = conv_weight.shape[0]
-    chunk = 64
-    scaled = []
-    maps = []
-    for first in range(0, length, chunk):
-        total = jnp.broadcast_to(conv_bias[...], (chunk, raw.shape[1]))
-        for tap in range(taps):
-            total = total + conv_weight[tap : tap + 1, :] * raw[pl.ds(LEAD - taps + 1 + tap + first, chunk), :]
-        mixed = silu(total).astype(BF16)
-        x_out[pl.ds(first, chunk), :] = mixed[:, :E]
-        mixed_f = mixed[:, E:].astype(F32)
-        b_out[pl.ds(first, chunk), :] = mixed_f[:, :NSTATE].astype(BF16)
-        c_out[pl.ds(first, chunk), :] = mixed_f[:, NSTATE:].astype(BF16)
-        maps.append(mixed_f[:, :NSTATE])
-        scaled.append((mixed[:, :E].astype(F32) * to_end[first : first + chunk]).astype(BF16))
-    b_t = jnp.concatenate(maps, axis=0).T.astype(BF16)
-    state[0:NSTATE, :] = jnp.dot(b_t, jnp.concatenate(scaled, axis=0), preferred_element_type=F32)
-    state[NSTATE : NSTATE + 8, :] = decay
+
+    def project(lanes):
+        return jnp.dot(normed, mix_weight[:, lanes], preferred_element_type=F32).astype(BF16)
+
+    def mixed(raw, lanes):
+        raw = raw.astype(F32)
+        total = conv_weight[0:1, lanes] * raw
+        for tap in range(1, taps):
+            total = pltpu.roll(total, 1, 0) + conv_weight[tap : tap + 1, lanes] * raw
+        return silu(total[LEAD:] + conv_bias[:, lanes]).astype(BF16)
+
+    chunk = 512
+    spans = [slice(E, E + 2 * NSTATE)] + [slice(first, first + chunk) for first in range(0, E, chunk)]
+    ahead = project(spans[0])
+    for place, lanes in enumerate(spans):
+        raw = ahead
+        if place + 1 < len(spans):
+            ahead = project(spans[place + 1])
+        part = mixed(raw, lanes)
+        if place == 0:
+            maps = part.astype(F32)
+            b_out[...] = maps[:, :NSTATE].astype(BF16)
+            c_out[...] = maps[:, NSTATE:].astype(BF16)
+            b_t = maps.T[:NSTATE].astype(BF16)
+            continue
+        x_out[:, lanes] = part
+        to_end = jnp.dot(scales, matrix[:, lanes], preferred_element_type=F32)
+        scaled = (part.astype(F32) * to_end).astype(BF16)
+        state[0:NSTATE, lanes] = jnp.dot(b_t, scaled, preferred_element_type=F32)
     half = E // 2
     mine = pl.ds(pl.multiple_of(row * half, 128), half)
     theirs = pl.ds(pl.multiple_of((1 - row) * half, 128), half)
@@ -228,61 +235,83 @@
     return values, jnp.broadcast_to(rows[0:1] + rows[1:2], rows.shape)
 
 
-def scale(decay, values):
-    return decay[0:1] * values
+def product(factors):
+    total = factors[0]
+    for factor in factors[1:]:
+        total = total * factor
+    return total
+
+
+def folded(place, pieces):
+    places = [place ^ step for step in range(len(pieces))]
+    steps = range(len(pieces))
+    one = jnp.ones_like(pieces[0][1])
+    all_values, ahead_values = None, None
+    for step in steps:
+        after = [jnp.where(places[k] > places[step], pieces[k][1], one) for k in steps if k != step]
+        between = [
+            jnp.where((places[k] > places[step]) & (places[k] < place), pieces[k][1], one)
+            for k in steps
+            if k not in (0, step)
+        ]
+        term = product(after)[0:1] * pieces[step][0]
+        all_values = term if step == 0 else all_values + term
+        if step:
+            weight = jnp.where(places[step] < place, product([one, *between]), 0.0)
+            term = weight[0:1] * pieces[step][0]
+            ahead_values = term if ahead_values is None else ahead_values + term
+    all_decay = product([decay for _, decay in pieces])
+    ahead_decay = product([jnp.where(places[k] < place, pieces[k][1], one) for k in steps if k])
+    return (all_values, all_decay), (ahead_values, ahead_decay)
+
+
+def read(summary):
+    return summary[0:NSTATE, :], summary[NSTATE : NSTATE + 8, :]
+
+
+def write(summary, piece):
+    summary[0:NSTATE, :] = piece[0]
+    summary[NSTATE : NSTATE + 8, :] = piece[1]
+
+
+def chained(earlier, latter):
+    return latter[1][0:1] * earlier[0] + latter[0], earlier[1] * latter[1]
 
 
 def pair_kernel(keep, received, total_out, message_out):
-    row = lax.axis_index("rows")
-    own, own_decay = keep[0:NSTATE, :], keep[NSTATE : NSTATE + 8, :]
-    other, other_decay = unwire(received)
-    upper = row == 1
-    last_decay = jnp.where(upper, own_decay, other_decay)
-    values = scale(last_decay, jnp.where(upper, other, own)) + jnp.where(upper, own, other)
-    decay = own_decay * other_decay
-    total_out[0:NSTATE, :] = values
-    total_out[NSTATE : NSTATE + 8, :] = decay
-    message_out[...] = wire(values, decay)
-
-
-def join_kernel(bit, first, final, *refs):
+    total, _ = folded(lax.axis_index("rows"), [read(keep), unwire(received)])
+    write(total_out, total)
+    message_out[...] = wire(*total)
+
+
+def join_kernel(low, count, first, *refs):
     refs = list(refs)
-    total = refs.pop(0)
-    before = None if first else refs.pop(0)
-    received = refs.pop(0)
-    col = lax.axis_index("cols")
-    later = (col & bit) != 0
-    values, decay = total[0:NSTATE, :], total[NSTATE : NSTATE + 8, :]
-    came, came_decay = unwire(received)
-    last_decay = jnp.where(later, decay, came_decay)
-    joined = scale(last_decay, jnp.where(later, came, values)) + jnp.where(later, values, came)
+    total = read(refs.pop(0))
+    before = None if first else read(refs.pop(0))
+    pieces = [total] + [unwire(refs.pop(0)) for _ in range(count - 1)]
+    place = (lax.axis_index("cols") // low) & (count - 1)
+    total, ahead = folded(place, pieces)
     before_out, message_out = refs[:2]
-    if not final:
-        refs[2][0:NSTATE, :] = joined
-        refs[2][NSTATE : NSTATE + 8, :] = decay * came_decay
-    message_out[...] = wire(joined, decay * came_decay)
-    if first:
-        before_out[0:NSTATE, :] = jnp.where(later, came, 0.0)
-        before_out[NSTATE : NSTATE + 8, :] = jnp.where(later, came_decay, 1.0)
-    else:
-        ahead, ahead_decay = before[0:NSTATE, :], before[NSTATE : NSTATE + 8, :]
-        before_out[0:NSTATE, :] = jnp.where(later, scale(ahead_decay, came) + ahead, ahead)
-        before_out[NSTATE : NSTATE + 8, :] = jnp.where(later, ahead_decay * came_decay, ahead_decay)
-
-
-def enter_kernel(bit, before, last, keep, received, mine_out, theirs_out):
-    col, row = lax.axis_index("cols"), lax.axis_index("rows")
-    later = (col & bit) != 0
-    ahead, ahead_decay = before[0:NSTATE, :], before[NSTATE : NSTATE + 8, :]
-    came, _ = unwire(last)
-    ahead = jnp.where(later, scale(ahead_decay, came) + ahead, ahead)
-    other, other_decay = unwire(received)
-    upper = row == 1
-    low = jnp.where(upper, other, keep[0:NSTATE, :])
-    low_decay = jnp.where(upper, other_decay, keep[NSTATE : NSTATE + 8, :])
-    second = scale(low_decay, ahead) + low
-    mine_out[...] = jnp.where(upper, second, ahead).astype(BF16)
-    theirs_out[...] = jnp.where(upper, ahead, second).astype(BF16)
+    write(before_out, ahead if first else chained(ahead, before))
+    message_out[...] = wire(*total)
+    write(refs[2], total)
+
+
+def enter_kernel(low, count, first, *refs):
+    refs = list(refs)
+    total = read(refs.pop(0))
+    before = None if first else read(refs.pop(0))
+    pieces = [total] + [unwire(refs.pop(0)) for _ in range(count - 1)]
+    keep, received, mine_out, theirs_out = refs
+    _, ahead = folded((lax.axis_index("cols") // low) & (count - 1), pieces)
+    if not first:
+        ahead = chained(ahead, before)
+    own, other = read(keep), unwire(received)
+    upper = lax.axis_index("rows") == 1
+    low_piece = tuple(jnp.where(upper, b, a) for a, b in zip(own, other))
+    second = chained(ahead, low_piece)[0]
+    mine_out[...] = jnp.where(upper, second, ahead[0]).astype(BF16)
+    theirs_out[...] = jnp.where(upper, ahead[0], second).astype(BF16)
 
 
 def gate_kernel(normed, gate_weight, local_a, local_b, cum, own_out, factor_out):
@@ -484,7 +513,7 @@
             shape((length, HEADS), F32), shape((length, HEADS), F32), shape((packed, half), F32),
             shape((packed, half)),
         ],
-        [pltpu.VMEM((LEAD + length, mixed_width), F32), pltpu.VMEM((packed, E), F32)],
+        [pltpu.VMEM((packed, E), F32)],
         flops=2 * length * D * mixed_width, moved=4 << 20, limit=16,
     )
     came = swap(send, "rows", 1)
@@ -503,27 +532,32 @@
         gate_kernel, (normed, gate_weight, *locals_, cum), [shape((length, E), F32)] * 2,
         flops=2 * length * D * E, moved=4 << 20, limit=8,
     )
-    before, bit = None, 1
-    while 2 * bit < col_count:
-        arrived = swap(out, "cols", bit)
-        first, final = before is None, 4 * bit >= col_count
-        inputs = (total, arrived) if first else (total, before, arrived)
-        before, out, *total = call(
-            partial(join_kernel, bit, first, final), inputs, [summary, message] + [summary] * (not final)
-        )
-        total = total[0] if total else None
-        bit *= 2
-    arrived = swap(out, "cols", bit)
-    entering = shape((NSTATE, half))
-    mine, theirs = call(partial(enter_kernel, bit), (before, arrived, keep, came), [entering, entering])
+    groups, low = [], 1
+    while low < col_count:
+        count = min(4, col_count // low)
+        groups.append((low, count))
+        low *= count
+    before = None
+    for number, (low, count) in enumerate(groups):
+        ending = number + 1 == len(groups)
+        arrived = []
+        for hop in range(1, count):
+            arrived.append(swap(out, "cols", hop * low))
+        first = before is None
+        inputs = ([total] if first else [total, before]) + arrived
+        if ending:
+            entering = shape((NSTATE, half))
+            mine, theirs = call(partial(enter_kernel, low, count, first), (*inputs, keep, came), [entering, entering])
+        else:
+            before, out, total = call(partial(join_kernel, low, count, first), inputs, [summary, message, summary])
     theirs = swap(theirs, "rows", 1)
     common = (own, factor, c_mat, line(out_gain), out_weight)
-    product, squares = call(
+    partial_sum, squares = call(
         first_kernel, (mine, *common), [shape((length, D), F32), shape((length, 128), F32)],
         flops=length * D * E, moved=4 << 20, limit=8,
     )
     return call(
-        finish_kernel, (theirs, *common, product, squares, embedded), shape((length, D)),
+        finish_kernel, (theirs, *common, partial_sum, squares, embedded), shape((length, D)),
         flops=length * D * E, moved=4 << 20, limit=8,
     )
 

time: 57.6 us -> 54.9 us (0.953)
  Pallas kernels: 15.9 us -> 13.2 us
    pallas_call x13 -> x12, Pallas kernels: 15.9 us -> 13.2 us  [call(): pl.pallas_call(kernel, out_shape=outs, in_specs=[pl.BlockSpec(memory_spac...]
    ppermute x13 -> x14, waiting for transfers between devices: 15.9 us -> 16.3 us  [swap(): lax.ppermute(block, axis, [(i, i ^ bit) for i in range(lax.axis_size(axis...]
    ppermute x13 -> x14, starting transfers between devices: 21 us -> 20.7 us  [swap(): lax.ppermute(block, axis, [(i, i ^ bit) for i in range(lax.axis_size(axis...]
  transfers between devices with their start and end apart: 13 -> 14, of which waited for: 6 -> 7; matrix products, arithmetic and copies ran while one was open for 5% -> 5% of each run, Pallas kernels for 10% -> 11%
where the time goes in v2:
time: 54.9 us; the launch traced here: 54.7 us
  starting transfers between devices  20.7 us (38%)
  waiting for transfers between devices  16.3 us (30%)
  Pallas kernels  13.2 us (24%)
  local copies, waits for them, and re-layouts  4.26 us (8%)
    ppermute x14, starting transfers between devices, swap(): lax.ppermute(block, axis, [(i, i ^ bit) for i in range(lax.axis_size(axis...  20.7 us
    ppermute x14, waiting for transfers between devices, swap(): lax.ppermute(block, axis, [(i, i ^ bit) for i in range(lax.axis_size(axis...  16.3 us
    pallas_call x12, Pallas kernels, call(): pl.pallas_call(kernel, out_shape=outs, in_specs=[pl.BlockSpec(memory_spac...  13.2 us
    unnamed x27, local copies, waits for them, and re-layouts  3.71 us
  transfers between devices with their start and end apart: 14, of which 7 were waited for; matrix products, arithmetic and copies ran while one was open for 5% of the time, Pallas kernels for 11%

profile of v2, /device:TPU:0, one launch (start us, length us, event | category | flops | bytes accessed | tf_op | source)
XLA Modules:
  0.0 54.7 jit_solution(5534417109746013746)
XLA Ops:
  0.0 0.5 collective-permute-start
  0.5 1.0 %copy-done.3 = bf16[3,128,512]{2,1,0:T(8,128)(2,1)S(1)} copy-done((bf16[3,128,512]{2,1,0:T(8,128)(2,1)S(1)}, bf16[3,128,512]{2,1,0:T(8,128)(2,1)}, u32[]{:S(2)}) %copy-start.3) | copy-done | bytes 393240
  1.5 0.5 collective-permute-done.partner
  2.1 0.3 shard_map.137
  2.3 2.9 %collective-permute-start.1 = (bf16[80,512]{1,0:T(8,128)(2,1)S(1)}, bf16[80,512]{1,0:T(8,128)(2,1)S(1)}, u32[]{:S(2)}, u32[]{:S(2)}) collective-permute-start(bf16[80,512]{1,0:T(8,128)(2,1)S(1)} %get-tuple-element.33), channel_id=1, source_target_pairs={{0,2},{2,0},{4,6},{6,4},{8,10},{10,8},{12,14},{14,12},{1,3},{3,1},... | collective-permute-start | bytes 245768 | tf_op jit(solution)/shard_map/ppermute | solution.py:392
  5.3 1.6 %collective-permute-start.2 = (bf16[80,512]{1,0:T(8,128)(2,1)S(1)}, bf16[80,512]{1,0:T(8,128)(2,1)S(1)}, u32[]{:S(2)}, u32[]{:S(2)}) collective-permute-start(bf16[80,512]{1,0:T(8,128)(2,1)S(1)} %get-tuple-element.34), channel_id=1, source_target_pairs={{0,4},{2,6},{4,0},{6,2},{8,12},{10,14},{12,8},{14,10},{1,5},{3,7},... | collective-permute-start | bytes 245768 | tf_op jit(solution)/shard_map/ppermute | solution.py:392
  6.8 3.0 %collective-permute-start.4 = (bf16[80,512]{1,0:T(8,128)(2,1)S(1)}, bf16[80,512]{1,0:T(8,128)(2,1)S(1)}, u32[]{:S(2)}, u32[]{:S(2)}) collective-permute-start(bf16[80,512]{1,0:T(8,128)(2,1)S(1)} %get-tuple-element.36), channel_id=1, source_target_pairs={{0,8},{2,10},{4,12},{6,14},{8,0},{10,2},{12,4},{14,6},{1,9},{3,11}... | collective-permute-start | bytes 245768 | tf_op jit(solution)/shard_map/ppermute | solution.py:392
  9.8 1.3 %collective-permute-start.5 = (bf16[80,512]{1,0:T(8,128)(2,1)S(1)}, bf16[80,512]{1,0:T(8,128)(2,1)S(1)}, u32[]{:S(2)}, u32[]{:S(2)}) collective-permute-start(bf16[80,512]{1,0:T(8,128)(2,1)S(1)} %get-tuple-element.37), channel_id=1, source_target_pairs={{0,10},{2,8},{4,14},{6,12},{8,2},{10,0},{12,6},{14,4},{1,11},{3,9}... | collective-permute-start | bytes 245768 | tf_op jit(solution)/shard_map/ppermute | solution.py:392
  11.1 3.6 %collective-permute-start.6 = (bf16[80,512]{1,0:T(8,128)(2,1)S(1)}, bf16[80,512]{1,0:T(8,128)(2,1)S(1)}, u32[]{:S(2)}, u32[]{:S(2)}) collective-permute-start(bf16[80,512]{1,0:T(8,128)(2,1)S(1)} %get-tuple-element.38), channel_id=1, source_target_pairs={{0,12},{2,14},{4,8},{6,10},{8,4},{10,6},{12,0},{14,2},{1,13},{3,15... | collective-permute-start | bytes 245768 | tf_op jit(solution)/shard_map/ppermute | solution.py:392
  14.8 2.3 %copy.15 = bf16[24,24,3,768]{3,0,2,1:T(8,128)(2,1)S(1)} copy(bf16[24,24,3,768]{3,1,2,0:T(8,128)(2,1)} %param.15) | data formatting | bytes 5308416 | tf_op args[1]
  17.1 0.5 pad.4
  17.7 5.2 %collective-permute-done.5.refs_5_ = bf16[80,512]{1,0:T(8,128)(2,1)S(1)} collective-permute-done((bf16[80,512]{1,0:T(8,128)(2,1)S(1)}, bf16[80,512]{1,0:T(8,128)(2,1)S(1)}, u32[]{:S(2)}, u32[]{:S(2)}) %collective-permute-start.5) | collective-permute-done | bytes 81952 | tf_op jit(solution)/shard_map/ppermute | solution.py:392
  23.0 2.4 %shard_map.138.embedded = bf16[264,768]{1,0:T(8,128)(2,1)S(1)} custom-call(bf16[80,512]{1,0:T(8,128)(2,1)S(1)} %get-tuple-element.32.refs_0_, bf16[80,512]{1,0:T(8,128)(2,1)S(1)} %collective-permute-done.1.refs_1_, bf16[80,512]{1,0:T(8,128)(2,1)S(1)} %collective-permute-done.2.refs_2_, bf16[80,512]{1,0:T(8,128)(2,1)S(1)} %collective-permute-done.3.refs_3_, ...), custom_call_target="tpu_custom_call" | custom-call | flops 1207959552 | bytes 6291456 | tf_op jit(solution)/shard_map/pallas_call | solution.py:31
  25.5 2.9 %shard_map.139 = (bf16[256,768]{1,0:T(8,128)(2,1)S(1)}, bf16[256,1536]{1,0:T(8,128)(2,1)S(1)}, bf16[256,64]{1,0:T(8,128)(2,1)S(1)}, bf16[256,64]{1,0:T(8,128)(2,...) custom-call(bf16[264,768]{1,0:T(8,128)(2,1)S(1)} %shard_map.138.embe, ...), custom_call_target="tpu_custom_call" | custom-call | flops 654311424 | bytes 4194304 | tf_op jit(solution)/shard_map/pallas_call | solution.py:31
  28.5 1.3 %collective-permute-done.8.received.refs_4_ = bf16[72,768]{1,0:T(8,128)(2,1)S(1)} collective-permute-done((bf16[72,768]{1,0:T(8,128)(2,1)S(1)}, bf16[72,768]{1,0:T(8,128)(2,1)S(1)}, u32[]{:S(2)}, u32[]{:S(2)}) %collective-permute-start.8) | collective-permute-done | bytes 110624 | tf_op jit(solution)/shard_map/ppermute | solution.py:392
  29.9 3.5 %collective-permute-start.10 = (bf16[72,768]{1,0:T(8,128)(2,1)S(1)}, bf16[72,768]{1,0:T(8,128)(2,1)S(1)}, u32[]{:S(2)}, u32[]{:S(2)}) collective-permute-start(bf16[72,768]{1,0:T(8,128)(2,1)S(1)} %get-tuple-element.43), channel_id=1, source_target_pairs={{0,4},{2,6},{4,0},{6,2},{8,12},{10,14},{12,8},{14,10},{1,5},{3,7},... | collective-permute-start | bytes 331784 | tf_op jit(solution)/shard_map/ppermute | solution.py:392
  33.3 0.5 collective-permute-start.11
  33.8 1.1 %collective-permute-start.9 = (bf16[72,768]{1,0:T(8,128)(2,1)S(1)}, bf16[72,768]{1,0:T(8,128)(2,1)S(1)}, u32[]{:S(2)}, u32[]{:S(2)}) collective-permute-start(bf16[72,768]{1,0:T(8,128)(2,1)S(1)} %get-tuple-element.43), channel_id=1, source_target_pairs={{0,2},{2,0},{4,6},{6,4},{8,10},{10,8},{12,14},{14,12},{1,3},{3,1},... | collective-permute-start | bytes 331784 | tf_op jit(solution)/shard_map/ppermute | solution.py:392
  34.9 2.4 %collective-permute-done.10.refs_2_ = bf16[72,768]{1,0:T(8,128)(2,1)S(1)} collective-permute-done((bf16[72,768]{1,0:T(8,128)(2,1)S(1)}, bf16[72,768]{1,0:T(8,128)(2,1)S(1)}, u32[]{:S(2)}, u32[]{:S(2)}) %collective-permute-start.10) | collective-permute-done | bytes 110624 | tf_op jit(solution)/shard_map/ppermute | solution.py:392
  37.2 2.3 %collective-permute-done.11.refs_3_ = bf16[72,768]{1,0:T(8,128)(2,1)S(1)} collective-permute-done((bf16[72,768]{1,0:T(8,128)(2,1)S(1)}, bf16[72,768]{1,0:T(8,128)(2,1)S(1)}, u32[]{:S(2)}, u32[]{:S(2)}) %collective-permute-start.11) | collective-permute-done | bytes 110624 | tf_op jit(solution)/shard_map/ppermute | solution.py:392
  39.6 1.4 %collective-permute-done.9.refs_1_ = bf16[72,768]{1,0:T(8,128)(2,1)S(1)} collective-permute-done((bf16[72,768]{1,0:T(8,128)(2,1)S(1)}, bf16[72,768]{1,0:T(8,128)(2,1)S(1)}, u32[]{:S(2)}, u32[]{:S(2)}) %collective-permute-start.9) | collective-permute-done | bytes 110624 | tf_op jit(solution)/shard_map/ppermute | solution.py:392
  41.0 0.2 shard_map.141
  41.2 2.6 %collective-permute-start.12 = (bf16[72,768]{1,0:T(8,128)(2,1)S(1)}, bf16[72,768]{1,0:T(8,128)(2,1)S(1)}, u32[]{:S(2)}, u32[]{:S(2)}) collective-permute-start(bf16[72,768]{1,0:T(8,128)(2,1)S(1)} %get-tuple-element.46), channel_id=1, source_target_pairs={{0,8},{2,10},{4,12},{6,14},{8,0},{10,2},{12,4},{14,6},{1,9},{3,11}... | collective-permute-start | bytes 331784 | tf_op jit(solution)/shard_map/ppermute | solution.py:392
  43.8 2.0 %shard_map.144.local_b = f32[256,768]{1,0:T(8,128)S(1)} custom-call(f32[24]{0:T(128)S(1)} %copy-done.6, bf16[256,1536]{1,0:T(8,128)(2,1)S(1)} %get-tuple-element.49.x, bf16[256,64]{1,0:T(8,128)(2,1)S(1)} %get-tuple-element.50.b_mat, bf16[256,64]{1,0:T(8,128)(2,1)S(1)} %get-tuple-element.51.c_mat, f32[256,24]{1,0:T(8,128)S(1)} %get-tuple-element.52.step, ...), custom_call_target="tpu_custom_call" | custom-call | flops 201326592 | bytes 2097152 | tf_op jit(solution)/shard_map/pallas_call | solution.py:31
  45.8 3.1 %collective-permute-done.12.refs_2_ = bf16[72,768]{1,0:T(8,128)(2,1)S(1)} collective-permute-done((bf16[72,768]{1,0:T(8,128)(2,1)S(1)}, bf16[72,768]{1,0:T(8,128)(2,1)S(1)}, u32[]{:S(2)}, u32[]{:S(2)}) %collective-permute-start.12) | collective-permute-done | bytes 110624 | tf_op jit(solution)/shard_map/ppermute | solution.py:392
  48.8 0.1 shard_map.142
  48.9 0.1 collective-permute-start.13
  49.0 2.0 %shard_map.143.local_a = f32[256,768]{1,0:T(8,128)S(1)} custom-call(f32[24]{0:T(128)S(1)} %copy-done.6, bf16[256,1536]{1,0:T(8,128)(2,1)S(1)} %get-tuple-element.49.x, bf16[256,64]{1,0:T(8,128)(2,1)S(1)} %get-tuple-element.50.b_mat, bf16[256,64]{1,0:T(8,128)(2,1)S(1)} %get-tuple-element.51.c_mat, f32[256,24]{1,0:T(8,128)S(1)} %get-tuple-element.52.step, ...), custom_call_target="tpu_custom_call" | custom-call | flops 201326592 | bytes 2097152 | tf_op jit(solution)/shard_map/pallas_call | solution.py:31
  51.0 1.2 %shard_map.145 = (f32[256,1536]{1,0:T(8,128)S(1)}, f32[256,1536]{1,0:T(8,128)S(1)}) custom-call(bf16[256,768]{1,0:T(8,128)(2,1)S(1)} %get-tuple-element.48.normed, bf16[768,1536]{1,0:T(8,128)(2,1)S(1)} %copy-done.2, f32[256,768]{1,0:T(8,128)S(1)} %shard_map.143.local_a, f32[256,768]{1,0:T(8,128)S(1)} %shard_map.144.local_b, f32[256,24]{1,0:T(8,128)S(1)} %get-tuple-element.53.cum), custom_call_target="tpu_custom_call" | custom-call | flops 603979776 | bytes 4194304 | tf_op jit(solution)/shard_map/pallas_call | solution.py:31
  52.3 0.4 copy-done
  52.7 0.6 %shard_map.146 = (f32[256,768]{1,0:T(8,128)S(1)}, f32[256,128]{1,0:T(8,128)S(1)}) custom-call(bf16[64,768]{1,0:T(8,128)(2,1)S(1)} %get-tuple-element.56.mine, f32[256,1536]{1,0:T(8,128)S(1)} %get-tuple-element.54.own, f32[256,1536]{1,0:T(8,128)S(1)} %get-tuple-element.55.factor, bf16[256,64]{1,0:T(8,128)(2,1)S(1)} %get-tuple-element.51.c_mat, ...), custom_call_target="tpu_custom_call" | custom-call | flops 301989888 | bytes 4194304 | tf_op jit(solution)/shard_map/pallas_call | solution.py:31
  53.3 1.4 %shard_map.147 = bf16[256,768]{1,0:T(8,128)(2,1)} custom-call(bf16[64,768]{1,0:T(8,128)(2,1)S(1)} %collective-permute-done.13.theirs, f32[256,1536]{1,0:T(8,128)S(1)} %get-tuple-element.54.own, f32[256,1536]{1,0:T(8,128)S(1)} %get-tuple-element.55.factor, bf16[256,64]{1,0:T(8,128)(2,1)S(1)} %get-tuple-element.51.c_mat, f32[1,1536]{1,0:T(1,128)S(1)} %reshape.31.out_gain, ...), custom_call_target="tpu_custom_call" | custom-call | flops 301989888 | bytes 4194304 | tf_op jit(solution)/shard_map/pallas_call | solution.py:31
  (40 shorter events, 0.3 us)
Async XLA Ops:
  0.0 2.1 %collective-permute-start = (bf16[3,128,512]{2,1,0:T(8,128)(2,1)}, bf16[3,128,512]{2,1,0:T(8,128)(2,1)S(1)}, u32[]{:S(2)}, u32[]{:S(2)}) collective-permute-start(bf16[3,128,512]{2,1,0:T(8,128)(2,1)} %pixels.1), channel_id=1, source_target_pairs={{0,1},{1,0},{2,3},{3,2},{4,5},{5,4},{6,7},{7,6},{8,9},{9,8},{10,11... | collective-permute-start | bytes 1179656 | tf_op jit(solution)/shard_map/ppermute | solution.py:392
  0.5 1.0 %copy-start.3 = (bf16[3,128,512]{2,1,0:T(8,128)(2,1)S(1)}, bf16[3,128,512]{2,1,0:T(8,128)(2,1)}, u32[]{:S(2)}) copy-start(bf16[3,128,512]{2,1,0:T(8,128)(2,1)} %pixels.1) | copy-start | bytes 1179652
  2.3 8.8 %collective-permute-start.1 = (bf16[80,512]{1,0:T(8,128)(2,1)S(1)}, bf16[80,512]{1,0:T(8,128)(2,1)S(1)}, u32[]{:S(2)}, u32[]{:S(2)}) collective-permute-start(bf16[80,512]{1,0:T(8,128)(2,1)S(1)} %get-tuple-element.33), channel_id=1, source_target_pairs={{0,2},{2,0},{4,6},{6,4},{8,10},{10,8},{12,14},{14,12},{1,3},{3,1},... | collective-permute-start | bytes 245768 | tf_op jit(solution)/shard_map/ppermute | solution.py:392
  5.3 9.5 %collective-permute-start.2 = (bf16[80,512]{1,0:T(8,128)(2,1)S(1)}, bf16[80,512]{1,0:T(8,128)(2,1)S(1)}, u32[]{:S(2)}, u32[]{:S(2)}) collective-permute-start(bf16[80,512]{1,0:T(8,128)(2,1)S(1)} %get-tuple-element.34), channel_id=1, source_target_pairs={{0,4},{2,6},{4,0},{6,2},{8,12},{10,14},{12,8},{14,10},{1,5},{3,7},... | collective-permute-start | bytes 245768 | tf_op jit(solution)/shard_map/ppermute | solution.py:392
  6.8 10.8 %collective-permute-start.3 = (bf16[80,512]{1,0:T(8,128)(2,1)S(1)}, bf16[80,512]{1,0:T(8,128)(2,1)S(1)}, u32[]{:S(2)}, u32[]{:S(2)}) collective-permute-start(bf16[80,512]{1,0:T(8,128)(2,1)S(1)} %get-tuple-element.35), channel_id=1, source_target_pairs={{0,6},{2,4},{4,2},{6,0},{8,14},{10,12},{12,10},{14,8},{1,7},{3,5},... | collective-permute-start | bytes 245768 | tf_op jit(solution)/shard_map/ppermute | solution.py:392
  6.8 10.8 %collective-permute-start.4 = (bf16[80,512]{1,0:T(8,128)(2,1)S(1)}, bf16[80,512]{1,0:T(8,128)(2,1)S(1)}, u32[]{:S(2)}, u32[]{:S(2)}) collective-permute-start(bf16[80,512]{1,0:T(8,128)(2,1)S(1)} %get-tuple-element.36), channel_id=1, source_target_pairs={{0,8},{2,10},{4,12},{6,14},{8,0},{10,2},{12,4},{14,6},{1,9},{3,11}... | collective-permute-start | bytes 245768 | tf_op jit(solution)/shard_map/ppermute | solution.py:392
  9.8 13.1 %collective-permute-start.5 = (bf16[80,512]{1,0:T(8,128)(2,1)S(1)}, bf16[80,512]{1,0:T(8,128)(2,1)S(1)}, u32[]{:S(2)}, u32[]{:S(2)}) collective-permute-start(bf16[80,512]{1,0:T(8,128)(2,1)S(1)} %get-tuple-element.37), channel_id=1, source_target_pairs={{0,10},{2,8},{4,14},{6,12},{8,2},{10,0},{12,6},{14,4},{1,11},{3,9}... | collective-permute-start | bytes 245768 | tf_op jit(solution)/shard_map/ppermute | solution.py:392
  11.1 11.8 %collective-permute-start.6 = (bf16[80,512]{1,0:T(8,128)(2,1)S(1)}, bf16[80,512]{1,0:T(8,128)(2,1)S(1)}, u32[]{:S(2)}, u32[]{:S(2)}) collective-permute-start(bf16[80,512]{1,0:T(8,128)(2,1)S(1)} %get-tuple-element.38), channel_id=1, source_target_pairs={{0,12},{2,14},{4,8},{6,10},{8,4},{10,6},{12,0},{14,2},{1,13},{3,15... | collective-permute-start | bytes 245768 | tf_op jit(solution)/shard_map/ppermute | solution.py:392
  14.7 2.4 %copy-start.11 = (f32[768]{0:T(1024)S(1)}, f32[768]{0:T(1024)}, u32[]{:S(2)}) copy-start(f32[768]{0:T(1024)} %param.16) | copy-start | bytes 9220
  14.7 2.4 %copy-start.10 = (f32[1664]{0:T(1024)S(1)}, f32[1664]{0:T(1024)}, u32[]{:S(2)}) copy-start(f32[1664]{0:T(1024)} %param.24) | copy-start | bytes 19972
  14.7 2.4 %copy-start.12 = (f32[768]{0:T(1024)S(1)}, f32[768]{0:T(1024)}, u32[]{:S(2)}) copy-start(f32[768]{0:T(1024)} %param.17) | copy-start | bytes 9220
  14.7 8.2 %collective-permute-start.7 = (bf16[80,512]{1,0:T(8,128)(2,1)S(1)}, bf16[80,512]{1,0:T(8,128)(2,1)S(1)}, u32[]{:S(2)}, u32[]{:S(2)}) collective-permute-start(bf16[80,512]{1,0:T(8,128)(2,1)S(1)} %get-tuple-element.39), channel_id=1, source_target_pairs={{0,14},{2,12},{4,10},{6,8},{8,6},{10,4},{12,2},{14,0},{1,15},{3,13... | collective-permute-start | bytes 245768 | tf_op jit(solution)/shard_map/ppermute | solution.py:392
  22.9 2.5 %copy-start.1 = (bf16[768,1664]{1,0:T(8,128)(2,1)S(1)}, bf16[768,1664]{1,0:T(8,128)(2,1)}, u32[]{:S(2)}) copy-start(bf16[768,1664]{1,0:T(8,128)(2,1)} %mix_weight.1) | copy-start | bytes 7667716
  22.9 2.5 %copy-start.4 = (bf16[768,24]{0,1:T(8,128)(2,1)S(1)}, bf16[768,24]{0,1:T(8,128)(2,1)}, u32[]{:S(2)}) copy-start(bf16[768,24]{0,1:T(8,128)(2,1)} %param.20) | copy-start | bytes 110596
  22.9 2.5 %copy-start.5 = (f32[4,1664]{1,0:T(4,128)S(1)}, f32[4,1664]{1,0:T(4,128)}, u32[]{:S(2)}) copy-start(f32[4,1664]{1,0:T(4,128)} %conv_weight.1) | copy-start | bytes 79876
  23.0 2.5 %copy-start.7 = (f32[24]{0:T(128)S(1)}, f32[24]{0:T(128)}, u32[]{:S(2)}) copy-start(f32[24]{0:T(128)} %param.21) | copy-start | bytes 292
  23.0 2.5 %copy-start.8 = (f32[24]{0:T(128)S(1)}, f32[24]{0:T(128)}, u32[]{:S(2)}) copy-start(f32[24]{0:T(128)} %param.22) | copy-start | bytes 292
  25.4 18.4 %copy-start.9 = (f32[1536]{0:T(1024)S(1)}, f32[1536]{0:T(1024)}, u32[]{:S(2)}) copy-start(f32[1536]{0:T(1024)} %param.26) | copy-start | bytes 18436
  25.4 18.4 %copy-start.6 = (f32[24]{0:T(128)S(1)}, f32[24]{0:T(128)}, u32[]{:S(2)}) copy-start(f32[24]{0:T(128)} %skip.3) | copy-start | bytes 292
  28.4 1.4 %collective-permute-start.8 = (bf16[72,768]{1,0:T(8,128)(2,1)S(1)}, bf16[72,768]{1,0:T(8,128)(2,1)S(1)}, u32[]{:S(2)}, u32[]{:S(2)}) collective-permute-start(bf16[72,768]{1,0:T(8,128)(2,1)S(1)} %get-tuple-element.41), channel_id=1, source_target_pairs={{0,1},{1,0},{2,3},{3,2},{4,5},{5,4},{6,7},{7,6},{8,9},{9,8},{10,11... | collective-permute-start | bytes 331784 | tf_op jit(solution)/shard_map/ppermute | solution.py:392
  29.9 7.4 %collective-permute-start.10 = (bf16[72,768]{1,0:T(8,128)(2,1)S(1)}, bf16[72,768]{1,0:T(8,128)(2,1)S(1)}, u32[]{:S(2)}, u32[]{:S(2)}) collective-permute-start(bf16[72,768]{1,0:T(8,128)(2,1)S(1)} %get-tuple-element.43), channel_id=1, source_target_pairs={{0,4},{2,6},{4,0},{6,2},{8,12},{10,14},{12,8},{14,10},{1,5},{3,7},... | collective-permute-start | bytes 331784 | tf_op jit(solution)/shard_map/ppermute | solution.py:392
  33.3 6.2 %collective-permute-start.11 = (bf16[72,768]{1,0:T(8,128)(2,1)S(1)}, bf16[72,768]{1,0:T(8,128)(2,1)S(1)}, u32[]{:S(2)}, u32[]{:S(2)}) collective-permute-start(bf16[72,768]{1,0:T(8,128)(2,1)S(1)} %get-tuple-element.43), channel_id=1, source_target_pairs={{0,6},{2,4},{4,2},{6,0},{8,14},{10,12},{12,10},{14,8},{1,7},{3,5},... | collective-permute-start | bytes 331784 | tf_op jit(solution)/shard_map/ppermute | solution.py:392
  33.8 7.2 %collective-permute-start.9 = (bf16[72,768]{1,0:T(8,128)(2,1)S(1)}, bf16[72,768]{1,0:T(8,128)(2,1)S(1)}, u32[]{:S(2)}, u32[]{:S(2)}) collective-permute-start(bf16[72,768]{1,0:T(8,128)(2,1)S(1)} %get-tuple-element.43), channel_id=1, source_target_pairs={{0,2},{2,0},{4,6},{6,4},{8,10},{10,8},{12,14},{14,12},{1,3},{3,1},... | collective-permute-start | bytes 331784 | tf_op jit(solution)/shard_map/ppermute | solution.py:392
  41.2 9.8 %copy-start.2 = (bf16[768,1536]{1,0:T(8,128)(2,1)S(1)}, bf16[768,1536]{1,0:T(8,128)(2,1)}, u32[]{:S(2)}) copy-start(bf16[768,1536]{1,0:T(8,128)(2,1)} %gate_weight.1) | copy-start | bytes 7077892
  41.2 7.6 %collective-permute-start.12 = (bf16[72,768]{1,0:T(8,128)(2,1)S(1)}, bf16[72,768]{1,0:T(8,128)(2,1)S(1)}, u32[]{:S(2)}, u32[]{:S(2)}) collective-permute-start(bf16[72,768]{1,0:T(8,128)(2,1)S(1)} %get-tuple-element.46), channel_id=1, source_target_pairs={{0,8},{2,10},{4,12},{6,14},{8,0},{10,2},{12,4},{14,6},{1,9},{3,11}... | collective-permute-start | bytes 331784 | tf_op jit(solution)/shard_map/ppermute | solution.py:392
  48.9 4.3 %collective-permute-start.13 = (bf16[64,768]{1,0:T(8,128)(2,1)S(1)}, bf16[64,768]{1,0:T(8,128)(2,1)S(1)}, u32[]{:S(2)}, u32[]{:S(2)}) collective-permute-start(bf16[64,768]{1,0:T(8,128)(2,1)S(1)} %get-tuple-element.47), channel_id=1, source_target_pairs={{0,1},{1,0},{2,3},{3,2},{4,5},{5,4},{6,7},{7,6},{8,9},{9,8},{10,11... | collective-permute-start | bytes 294920 | tf_op jit(solution)/shard_map/ppermute | solution.py:392
  51.0 1.7 %copy-start = (bf16[1536,768]{1,0:T(8,128)(2,1)S(1)}, bf16[1536,768]{1,0:T(8,128)(2,1)}, u32[]{:S(2)}) copy-start(bf16[1536,768]{1,0:T(8,128)(2,1)} %out_weight.3) | copy-start | bytes 7077892

commit v3 on v2

--- a/solution.py
+++ b/solution.py
@@ -53,18 +53,15 @@
     rows[:, 32 + 2 * local : 64 + 2 * local, :] = edge
     rows[:, pl.ds(pl.multiple_of(32 + local * row, 32), local), :] = own[...]
     rows[:, pl.ds(pl.multiple_of(32 + local * (1 - row), 32), local), :] = partner[...]
+    side = len(outs)
     for step, out in enumerate(outs):
-        token_row = 2 * (col ^ step) + row
-        first = pl.multiple_of(PATCH * token_row, PATCH)
-        pieces, tails = [], []
-        for channel in range(CHAN):
-            block = rows[channel, pl.ds(first, 64), :].astype(F32)
-            pieces.append(block[28:52])
-            before = block[12:28, width - 64 :]
-            tails += [before[:8], before[8:]]
+        chip = side * row + ((col % side) ^ step)
+        first = pl.multiple_of(2 * PATCH * chip, 32)
+        blocks = [rows[channel, pl.ds(first, 80), :].astype(F32) for channel in range(CHAN)]
+        pieces = [block[28 + 8 * group : 36 + 8 * group] for group in range(5) for block in blocks]
+        tails = [block[12 + 8 * group : 20 + 8 * group, width - 64 :] for group in range(2) for block in blocks]
         tails.append(jnp.zeros((8, width - 64 * len(tails)), F32))
-        pieces.append(jnp.concatenate(tails, axis=1))
-        out[...] = jnp.concatenate(pieces, axis=0).astype(BF16)
+        out[...] = jnp.concatenate([*pieces, jnp.concatenate(tails, axis=1)], axis=0).astype(BF16)
 
 
 def stage_kernel(pixels, out):
@@ -83,9 +80,10 @@
 
 def embed_kernel(*refs):
     blocks, (weight, bias, out, picked, tail, wide) = refs[:-6], refs[-6:]
-    col = lax.axis_index("cols")
+    col, row = lax.axis_index("cols"), lax.axis_index("rows")
     width = blocks[0].shape[1]
     count = len(blocks)
+    side = count // 2
     tokens = count * width // PATCH
     local = width // PATCH
     zeros = jnp.zeros((PATCH, LEAD, 128), F32)
@@ -93,25 +91,22 @@
     picked[:, LEAD + tokens :, :] = zeros
     blank = jnp.zeros((128 - WIN, width), BF16)
     pick = pick_matrix()
-    edge = jnp.zeros((WIN + 8, 128), F32)
+    window = pl.ds(pl.multiple_of(2 * KERNEL * row, 16), WIN)
+    edge = jnp.zeros((WIN, 128), F32)
     extra = jnp.zeros((8, 128 * CHAN), F32)
-    for step, block in enumerate(blocks):
-        source = col ^ step
-        values = jnp.concatenate([block[0:WIN, :], blank], axis=0)
+    for place, block in enumerate(blocks):
+        source = side * (row if place < side else 1 - row) + ((col % side) ^ (place % side))
+        values = jnp.concatenate([block[window, :], blank], axis=0)
         for group in range(width // 256):
             found = turned(pick, values[:, 256 * group : 256 * (group + 1)])
             first = pl.multiple_of(LEAD + source * local + 16 * group, 8)
             picked[:, pl.ds(first, 16), :] = found.reshape(PATCH, 16, 128)
         last = source == count - 1
-        edge = jnp.where(last, block[:, width - 128 :].astype(F32), edge)
-        extra = jnp.where(last, block[WIN - 8 : WIN + 8, : 128 * CHAN].astype(F32)[8:], extra)
-    pieces = []
-    for channel in range(CHAN):
-        pieces += [extra[:, 128 * channel : 128 * channel + 64]]
-        pieces += [extra[:, 128 * channel + 64 : 128 * channel + 128]]
-        pieces += [edge[KERNEL * channel : KERNEL * channel + 8, 64:]]
-    pieces.append(jnp.zeros((128 - WIN, 64), F32))
-    last = jnp.concatenate(pieces, axis=0)
+        edge = jnp.where(last, block[0:WIN, width - 128 :].astype(F32), edge)
+        extra = jnp.where(last, block[5 * KERNEL - 8 : 5 * KERNEL + 8, : 128 * CHAN].astype(F32)[8:], extra)
+    before = [extra[:, 64 * piece : 64 * (piece + 1)] for piece in range(2 * CHAN)] + [edge[:KERNEL, 64:]]
+    last = jnp.where(row == 0, jnp.concatenate(before, axis=0), edge[:, 64:])
+    last = jnp.concatenate([last, jnp.zeros((128 - WIN, 64), F32)], axis=0)
     last = jnp.concatenate([jnp.zeros((128, 64), F32), last, jnp.zeros((128, 128), F32)], axis=1)
     tail[:, 0:8, :] = zeros
     tail[:, 8:24, :] = turned(pick, last.astype(BF16)).reshape(PATCH, 16, 128)
@@ -392,22 +387,35 @@
     return lax.ppermute(block, axis, [(i, i ^ bit) for i in range(lax.axis_size(axis))])
 
 
-def sending_order(count):
-    return (1, *range(count // 2, count), *range(2, count // 2))
+def sending_order(side):
+    return tuple(reversed(range(side)))
+
+
+def across(block, step):
+    side = lax.axis_size("cols") // 2
+    pairs = []
+    for col in range(2 * side):
+        for row in range(2):
+            other = side * row + ((col % side) ^ step)
+            pairs.append((2 * col + row, 2 * other + col // side))
+    return lax.ppermute(block, ("cols", "rows"), pairs)
 
 
 def embed_by_rows(pixels, patch_weight, patch_bias):
     col_count = lax.axis_size("cols")
+    side = col_count // 2
     width = pixels.shape[2]
     partner = swap(pixels, "rows", 1)
     pixels = call(stage_kernel, (pixels,), shape(pixels.shape))
-    block = shape((WIN + 8, width))
+    block = shape((5 * KERNEL + 8, width))
     scratch = [pltpu.VMEM((CHAN, 2 * pixels.shape[1] + 64, width), BF16)]
-    blocks = call(pack_kernel, (pixels, partner), [block] * col_count, scratch, limit=8)
-    came = [blocks[0]] + [None] * (col_count - 1)
-    for step in sending_order(col_count):
-        came[step] = swap(blocks[step], "cols", step)
-    weight = patch_weight.transpose(1, 2, 0, 3).reshape(KERNEL, WIN, D)
+    blocks = call(pack_kernel, (pixels, partner), [block] * side, scratch, limit=8)
+    near, far = [None] * side, [None] * side
+    for step in sending_order(side):
+        near[step] = across(blocks[step], step)
+        far[step] = swap(near[step], "rows", 1)
+    came = near + far
+    weight = patch_weight.reshape(3, 8, KERNEL, CHAN, D).transpose(2, 0, 3, 1, 4).reshape(KERNEL, WIN, D)
     weight = jnp.pad(weight, ((0, 0), (0, 128 - WIN), (0, 0))).reshape(KERNEL * 128, D)
     tokens = col_count * width // PATCH
     scratch = [
@@ -493,7 +501,7 @@
 ):
     col_count = lax.axis_size("cols")
     row_local = pixels.shape[1] // PATCH
-    if col_count == row_local:
+    if col_count == row_local and lax.axis_size("rows") == 2:
         embedded = embed_by_rows(pixels, patch_weight, patch_bias)
     else:
         embedded = embed_by_blocks(pixels, patch_weight, patch_bias)

time: 54.9 us -> 54.4 us (level)
  the two profiles are of different devices: /device:TPU:0 before, /device:TPU:1 now
where the time goes in v3:
time: 54.4 us; the launch traced here: 54.2 us
  starting transfers between devices  19.7 us (36%)
  waiting for transfers between devices  16.8 us (31%)
  Pallas kernels  13.1 us (24%)
  local copies, waits for them, and re-layouts  4.28 us (8%)
    pallas_call x12, Pallas kernels, call(): pl.pallas_call(kernel, out_shape=outs, in_specs=[pl.BlockSpec(memory_spac...  13.1 us
    ppermute x4, starting transfers between devices, across(): return lax.ppermute(block, ('cols', 'rows'), pairs)  10.3 us
    ppermute x11, waiting for transfers between devices, swap(): lax.ppermute(block, axis, [(i, i ^ bit) for i in range(lax.axis_size(axis...  10.1 us
    ppermute x11, starting transfers between devices, swap(): lax.ppermute(block, axis, [(i, i ^ bit) for i in range(lax.axis_size(axis...  9.42 us
    ppermute x4, waiting for transfers between devices, across(): return lax.ppermute(block, ('cols', 'rows'), pairs)  6.67 us
    transpose x1, local copies, waits for them, and re-layouts, embed_by_rows(): patch_weight.reshape(3, 8, KERNEL, CHAN, D).transpose(2, 0, 3, 1, 4)  2.29 us
    unnamed x26, local copies, waits for them, and re-layouts  1.45 us
  transfers between devices with their start and end apart: 15, of which 8 were waited for; matrix products, arithmetic and copies ran while one was open for 5% of the time, Pallas kernels for 11%

profile of v3, /device:TPU:1, one launch (start us, length us, event | category | flops | bytes accessed | tf_op | source)
XLA Modules:
  0.0 54.2 jit_solution(7886637003616862899)
XLA Ops:
  0.0 1.0 %copy-done.3 = bf16[3,128,512]{2,1,0:T(8,128)(2,1)S(1)} copy-done((bf16[3,128,512]{2,1,0:T(8,128)(2,1)S(1)}, bf16[3,128,512]{2,1,0:T(8,128)(2,1)}, u32[]{:S(2)}) %copy-start.3) | copy-done | bytes 393240
  1.0 0.9 %collective-permute-done.partner = bf16[3,128,512]{2,1,0:T(8,128)(2,1)S(1)} collective-permute-done((bf16[3,128,512]{2,1,0:T(8,128)(2,1)}, bf16[3,128,512]{2,1,0:T(8,128)(2,1)S(1)}, u32[]{:S(2)}, u32[]{:S(2)}) %collective-permute-start) | collective-permute-done | bytes 393248 | tf_op jit(solution)/shard_map/ppermute | solution.py:387
  1.9 0.2 shard_map.137
  2.2 5.6 %collective-permute-start.1 = (bf16[128,512]{1,0:T(8,128)(2,1)S(1)}, bf16[128,512]{1,0:T(8,128)(2,1)S(1)}, u32[]{:S(2)}, u32[]{:S(2)}) collective-permute-start(bf16[128,512]{1,0:T(8,128)(2,1)S(1)} %get-tuple-element.28), channel_id=1, source_target_pairs={{0,0},{1,8},{2,2},{3,10},{4,4},{5,12},{6,6},{7,14},{8,1},{9,9},{10... | collective-permute-start | bytes 393224 | tf_op jit(solution)/shard_map/ppermute | solution.py:401
  7.8 1.1 %collective-permute-start.2 = (bf16[128,512]{1,0:T(8,128)(2,1)S(1)}, bf16[128,512]{1,0:T(8,128)(2,1)S(1)}, u32[]{:S(2)}, u32[]{:S(2)}) collective-permute-start(bf16[128,512]{1,0:T(8,128)(2,1)S(1)} %get-tuple-element.29), channel_id=1, source_target_pairs={{0,2},{1,10},{2,0},{3,8},{4,6},{5,14},{6,4},{7,12},{8,3},{9,11},{1... | collective-permute-start | bytes 393224 | tf_op jit(solution)/shard_map/ppermute | solution.py:401
  8.9 3.6 %collective-permute-start.3 = (bf16[128,512]{1,0:T(8,128)(2,1)S(1)}, bf16[128,512]{1,0:T(8,128)(2,1)S(1)}, u32[]{:S(2)}, u32[]{:S(2)}) collective-permute-start(bf16[128,512]{1,0:T(8,128)(2,1)S(1)} %get-tuple-element.30), channel_id=1, source_target_pairs={{0,4},{1,12},{2,6},{3,14},{4,0},{5,8},{6,2},{7,10},{8,5},{9,13},{1... | collective-permute-start | bytes 393224 | tf_op jit(solution)/shard_map/ppermute | solution.py:401
  12.5 4.6 %collective-permute-done.2.refs_1_ = bf16[128,512]{1,0:T(8,128)(2,1)S(1)} collective-permute-done((bf16[128,512]{1,0:T(8,128)(2,1)S(1)}, bf16[128,512]{1,0:T(8,128)(2,1)S(1)}, u32[]{:S(2)}, u32[]{:S(2)}) %collective-permute-start.2) | collective-permute-done | bytes 131104 | tf_op jit(solution)/shard_map/ppermute | solution.py:401
  17.0 0.5 collective-permute-start.7
  17.6 2.1 %collective-permute-done.4.refs_3_ = bf16[128,512]{1,0:T(8,128)(2,1)S(1)} collective-permute-done((bf16[128,512]{1,0:T(8,128)(2,1)S(1)}, bf16[128,512]{1,0:T(8,128)(2,1)S(1)}, u32[]{:S(2)}, u32[]{:S(2)}) %collective-permute-start.4) | collective-permute-done | bytes 131104 | tf_op jit(solution)/shard_map/ppermute | solution.py:401
  19.6 2.3 %copy.15 = bf16[24,3,3,8,768]{4,3,2,1,0:T(8,128)(2,1)S(1)} copy(bf16[24,3,3,8,768]{4,0,2,3,1:T(8,128)(2,1)} %bitcast.13) | data formatting | bytes 5308416 | tf_op jit(solution)/shard_map/transpose | solution.py:418
  22.0 0.5 pad.4
  22.6 2.4 %shard_map.138.embedded = bf16[264,768]{1,0:T(8,128)(2,1)S(1)} custom-call(bf16[128,512]{1,0:T(8,128)(2,1)S(1)} %collective-permute-done.1.refs_0_, bf16[128,512]{1,0:T(8,128)(2,1)S(1)} %collective-permute-done.2.refs_1_, bf16[128,512]{1,0:T(8,128)(2,1)S(1)} %collective-permute-done.3.refs_2_, bf16[128,512]{1,0:T(8,128)(2,1)S(1)} %collective-permute-done.4.refs_3_, ...), custom_call_target="tpu_custom_call" | custom-call | flops 1207959552 | bytes 6291456 | tf_op jit(solution)/shard_map/pallas_call | solution.py:31
  25.1 2.9 %shard_map.139 = (bf16[256,768]{1,0:T(8,128)(2,1)S(1)}, bf16[256,1536]{1,0:T(8,128)(2,1)S(1)}, bf16[256,64]{1,0:T(8,128)(2,1)S(1)}, bf16[256,64]{1,0:T(8,128)(2,...) custom-call(bf16[264,768]{1,0:T(8,128)(2,1)S(1)} %shard_map.138.embe, ...), custom_call_target="tpu_custom_call" | custom-call | flops 654311424 | bytes 4194304 | tf_op jit(solution)/shard_map/pallas_call | solution.py:31
  28.1 0.6 %collective-permute-start.9 = (bf16[72,768]{1,0:T(8,128)(2,1)S(1)}, bf16[72,768]{1,0:T(8,128)(2,1)S(1)}, u32[]{:S(2)}, u32[]{:S(2)}) collective-permute-start(bf16[72,768]{1,0:T(8,128)(2,1)S(1)} %get-tuple-element.33), channel_id=1, source_target_pairs={{0,1},{1,0},{2,3},{3,2},{4,5},{5,4},{6,7},{7,6},{8,9},{9,8},{10,11... | collective-permute-start | bytes 331784 | tf_op jit(solution)/shard_map/ppermute | solution.py:387
  28.6 1.0 %collective-permute-done.9.received.refs_4_ = bf16[72,768]{1,0:T(8,128)(2,1)S(1)} collective-permute-done((bf16[72,768]{1,0:T(8,128)(2,1)S(1)}, bf16[72,768]{1,0:T(8,128)(2,1)S(1)}, u32[]{:S(2)}, u32[]{:S(2)}) %collective-permute-start.9) | collective-permute-done | bytes 110624 | tf_op jit(solution)/shard_map/ppermute | solution.py:387
  29.6 0.1 shard_map.140
  29.7 0.2 collective-permute-start.10
  29.9 2.9 %collective-permute-start.11 = (bf16[72,768]{1,0:T(8,128)(2,1)S(1)}, bf16[72,768]{1,0:T(8,128)(2,1)S(1)}, u32[]{:S(2)}, u32[]{:S(2)}) collective-permute-start(bf16[72,768]{1,0:T(8,128)(2,1)S(1)} %get-tuple-element.35), channel_id=1, source_target_pairs={{0,4},{2,6},{4,0},{6,2},{8,12},{10,14},{12,8},{14,10},{1,5},{3,7},... | collective-permute-start | bytes 331784 | tf_op jit(solution)/shard_map/ppermute | solution.py:387
  32.8 1.2 %collective-permute-done.10.refs_1_ = bf16[72,768]{1,0:T(8,128)(2,1)S(1)} collective-permute-done((bf16[72,768]{1,0:T(8,128)(2,1)S(1)}, bf16[72,768]{1,0:T(8,128)(2,1)S(1)}, u32[]{:S(2)}, u32[]{:S(2)}) %collective-permute-start.10) | collective-permute-done | bytes 110624 | tf_op jit(solution)/shard_map/ppermute | solution.py:387
  34.0 1.6 %collective-permute-done.11.refs_2_ = bf16[72,768]{1,0:T(8,128)(2,1)S(1)} collective-permute-done((bf16[72,768]{1,0:T(8,128)(2,1)S(1)}, bf16[72,768]{1,0:T(8,128)(2,1)S(1)}, u32[]{:S(2)}, u32[]{:S(2)}) %collective-permute-start.11) | collective-permute-done | bytes 110624 | tf_op jit(solution)/shard_map/ppermute | solution.py:387
  35.6 1.8 %collective-permute-done.12.refs_3_ = bf16[72,768]{1,0:T(8,128)(2,1)S(1)} collective-permute-done((bf16[72,768]{1,0:T(8,128)(2,1)S(1)}, bf16[72,768]{1,0:T(8,128)(2,1)S(1)}, u32[]{:S(2)}, u32[]{:S(2)}) %collective-permute-start.12) | collective-permute-done | bytes 110624 | tf_op jit(solution)/shard_map/ppermute | solution.py:387
  37.3 0.2 shard_map.141
  37.5 4.4 %collective-permute-start.13 = (bf16[72,768]{1,0:T(8,128)(2,1)S(1)}, bf16[72,768]{1,0:T(8,128)(2,1)S(1)}, u32[]{:S(2)}, u32[]{:S(2)}) collective-permute-start(bf16[72,768]{1,0:T(8,128)(2,1)S(1)} %get-tuple-element.38), channel_id=1, source_target_pairs={{0,8},{2,10},{4,12},{6,14},{8,0},{10,2},{12,4},{14,6},{1,9},{3,11}... | collective-permute-start | bytes 331784 | tf_op jit(solution)/shard_map/ppermute | solution.py:387
  42.0 2.0 %shard_map.144.local_b = f32[256,768]{1,0:T(8,128)S(1)} custom-call(f32[24]{0:T(128)S(1)} %copy-done.6, bf16[256,1536]{1,0:T(8,128)(2,1)S(1)} %get-tuple-element.41.x, bf16[256,64]{1,0:T(8,128)(2,1)S(1)} %get-tuple-element.42.b_mat, bf16[256,64]{1,0:T(8,128)(2,1)S(1)} %get-tuple-element.43.c_mat, f32[256,24]{1,0:T(8,128)S(1)} %get-tuple-element.44.step, ...), custom_call_target="tpu_custom_call" | custom-call | flops 201326592 | bytes 2097152 | tf_op jit(solution)/shard_map/pallas_call | solution.py:31
  43.9 3.7 %collective-permute-done.13.refs_2_ = bf16[72,768]{1,0:T(8,128)(2,1)S(1)} collective-permute-done((bf16[72,768]{1,0:T(8,128)(2,1)S(1)}, bf16[72,768]{1,0:T(8,128)(2,1)S(1)}, u32[]{:S(2)}, u32[]{:S(2)}) %collective-permute-start.13) | collective-permute-done | bytes 110624 | tf_op jit(solution)/shard_map/ppermute | solution.py:387
  47.6 0.1 shard_map.142
  47.7 0.7 %collective-permute-start.14 = (bf16[64,768]{1,0:T(8,128)(2,1)S(1)}, bf16[64,768]{1,0:T(8,128)(2,1)S(1)}, u32[]{:S(2)}, u32[]{:S(2)}) collective-permute-start(bf16[64,768]{1,0:T(8,128)(2,1)S(1)} %get-tuple-element.39), channel_id=1, source_target_pairs={{0,1},{1,0},{2,3},{3,2},{4,5},{5,4},{6,7},{7,6},{8,9},{9,8},{10,11... | collective-permute-start | bytes 294920 | tf_op jit(solution)/shard_map/ppermute | solution.py:387
  48.5 1.9 %shard_map.143.local_a = f32[256,768]{1,0:T(8,128)S(1)} custom-call(f32[24]{0:T(128)S(1)} %copy-done.6, bf16[256,1536]{1,0:T(8,128)(2,1)S(1)} %get-tuple-element.41.x, bf16[256,64]{1,0:T(8,128)(2,1)S(1)} %get-tuple-element.42.b_mat, bf16[256,64]{1,0:T(8,128)(2,1)S(1)} %get-tuple-element.43.c_mat, f32[256,24]{1,0:T(8,128)S(1)} %get-tuple-element.44.step, ...), custom_call_target="tpu_custom_call" | custom-call | flops 201326592 | bytes 2097152 | tf_op jit(solution)/shard_map/pallas_call | solution.py:31
  50.5 1.2 %shard_map.145 = (f32[256,1536]{1,0:T(8,128)S(1)}, f32[256,1536]{1,0:T(8,128)S(1)}) custom-call(bf16[256,768]{1,0:T(8,128)(2,1)S(1)} %get-tuple-element.40.normed, bf16[768,1536]{1,0:T(8,128)(2,1)S(1)} %copy-done.2, f32[256,768]{1,0:T(8,128)S(1)} %shard_map.143.local_a, f32[256,768]{1,0:T(8,128)S(1)} %shard_map.144.local_b, f32[256,24]{1,0:T(8,128)S(1)} %get-tuple-element.45.cum), custom_call_target="tpu_custom_call" | custom-call | flops 603979776 | bytes 4194304 | tf_op jit(solution)/shard_map/pallas_call | solution.py:31
  51.7 0.4 copy-done
  52.1 0.7 %shard_map.146 = (f32[256,768]{1,0:T(8,128)S(1)}, f32[256,128]{1,0:T(8,128)S(1)}) custom-call(bf16[64,768]{1,0:T(8,128)(2,1)S(1)} %get-tuple-element.48.mine, f32[256,1536]{1,0:T(8,128)S(1)} %get-tuple-element.46.own, f32[256,1536]{1,0:T(8,128)S(1)} %get-tuple-element.47.factor, bf16[256,64]{1,0:T(8,128)(2,1)S(1)} %get-tuple-element.43.c_mat, ...), custom_call_target="tpu_custom_call" | custom-call | flops 301989888 | bytes 4194304 | tf_op jit(solution)/shard_map/pallas_call | solution.py:31
  52.8 1.4 %shard_map.147 = bf16[256,768]{1,0:T(8,128)(2,1)} custom-call(bf16[64,768]{1,0:T(8,128)(2,1)S(1)} %collective-permute-done.14.theirs, f32[256,1536]{1,0:T(8,128)S(1)} %get-tuple-element.46.own, f32[256,1536]{1,0:T(8,128)S(1)} %get-tuple-element.47.factor, bf16[256,64]{1,0:T(8,128)(2,1)S(1)} %get-tuple-element.43.c_mat, f32[1,1536]{1,0:T(1,128)S(1)} %reshape.35.out_gain, ...), custom_call_target="tpu_custom_call" | custom-call | flops 301989888 | bytes 4194304 | tf_op jit(solution)/shard_map/pallas_call | solution.py:31
  (42 shorter events, 0.2 us)
Async XLA Ops:
  0.0 1.9 %collective-permute-start = (bf16[3,128,512]{2,1,0:T(8,128)(2,1)}, bf16[3,128,512]{2,1,0:T(8,128)(2,1)S(1)}, u32[]{:S(2)}, u32[]{:S(2)}) collective-permute-start(bf16[3,128,512]{2,1,0:T(8,128)(2,1)} %pixels.1), channel_id=1, source_target_pairs={{0,1},{1,0},{2,3},{3,2},{4,5},{5,4},{6,7},{7,6},{8,9},{9,8},{10,11... | collective-permute-start | bytes 1179656 | tf_op jit(solution)/shard_map/ppermute | solution.py:387
  0.0 1.0 %copy-start.3 = (bf16[3,128,512]{2,1,0:T(8,128)(2,1)S(1)}, bf16[3,128,512]{2,1,0:T(8,128)(2,1)}, u32[]{:S(2)}) copy-start(bf16[3,128,512]{2,1,0:T(8,128)(2,1)} %pixels.1) | copy-start | bytes 1179652
  2.2 10.3 %collective-permute-start.1 = (bf16[128,512]{1,0:T(8,128)(2,1)S(1)}, bf16[128,512]{1,0:T(8,128)(2,1)S(1)}, u32[]{:S(2)}, u32[]{:S(2)}) collective-permute-start(bf16[128,512]{1,0:T(8,128)(2,1)S(1)} %get-tuple-element.28), channel_id=1, source_target_pairs={{0,0},{1,8},{2,2},{3,10},{4,4},{5,12},{6,6},{7,14},{8,1},{9,9},{10... | collective-permute-start | bytes 393224 | tf_op jit(solution)/shard_map/ppermute | solution.py:401
  7.8 9.3 %collective-permute-start.2 = (bf16[128,512]{1,0:T(8,128)(2,1)S(1)}, bf16[128,512]{1,0:T(8,128)(2,1)S(1)}, u32[]{:S(2)}, u32[]{:S(2)}) collective-permute-start(bf16[128,512]{1,0:T(8,128)(2,1)S(1)} %get-tuple-element.29), channel_id=1, source_target_pairs={{0,2},{1,10},{2,0},{3,8},{4,6},{5,14},{6,4},{7,12},{8,3},{9,11},{1... | collective-permute-start | bytes 393224 | tf_op jit(solution)/shard_map/ppermute | solution.py:401
  8.9 8.2 %collective-permute-start.3 = (bf16[128,512]{1,0:T(8,128)(2,1)S(1)}, bf16[128,512]{1,0:T(8,128)(2,1)S(1)}, u32[]{:S(2)}, u32[]{:S(2)}) collective-permute-start(bf16[128,512]{1,0:T(8,128)(2,1)S(1)} %get-tuple-element.30), channel_id=1, source_target_pairs={{0,4},{1,12},{2,6},{3,14},{4,0},{5,8},{6,2},{7,10},{8,5},{9,13},{1... | collective-permute-start | bytes 393224 | tf_op jit(solution)/shard_map/ppermute | solution.py:401
  12.4 7.2 %collective-permute-start.4 = (bf16[128,512]{1,0:T(8,128)(2,1)S(1)}, bf16[128,512]{1,0:T(8,128)(2,1)S(1)}, u32[]{:S(2)}, u32[]{:S(2)}) collective-permute-start(bf16[128,512]{1,0:T(8,128)(2,1)S(1)} %get-tuple-element.31), channel_id=1, source_target_pairs={{0,6},{1,14},{2,4},{3,12},{4,2},{5,10},{6,0},{7,8},{8,7},{9,15},{1... | collective-permute-start | bytes 393224 | tf_op jit(solution)/shard_map/ppermute | solution.py:401
  12.4 10.1 %collective-permute-start.5 = (bf16[128,512]{1,0:T(8,128)(2,1)S(1)}, bf16[128,512]{1,0:T(8,128)(2,1)S(1)}, u32[]{:S(2)}, u32[]{:S(2)}) collective-permute-start(bf16[128,512]{1,0:T(8,128)(2,1)S(1)} %collective-permute-done.1.refs_0_), channel_id=1, source_target_pairs={{0,1},{1,0},{2,3},{3,2},{4,5},{5,4},{6,7},{7,6},{8,9},{9,8},{10,11... | collective-permute-start | bytes 393224 | tf_op jit(solution)/shard_map/ppermute | solution.py:387
  17.0 5.5 %collective-permute-start.6 = (bf16[128,512]{1,0:T(8,128)(2,1)S(1)}, bf16[128,512]{1,0:T(8,128)(2,1)S(1)}, u32[]{:S(2)}, u32[]{:S(2)}) collective-permute-start(bf16[128,512]{1,0:T(8,128)(2,1)S(1)} %collective-permute-done.2.refs_1_), channel_id=1, source_target_pairs={{0,1},{1,0},{2,3},{3,2},{4,5},{5,4},{6,7},{7,6},{8,9},{9,8},{10,11... | collective-permute-start | bytes 393224 | tf_op jit(solution)/shard_map/ppermute | solution.py:387
  17.0 5.5 %collective-permute-start.7 = (bf16[128,512]{1,0:T(8,128)(2,1)S(1)}, bf16[128,512]{1,0:T(8,128)(2,1)S(1)}, u32[]{:S(2)}, u32[]{:S(2)}) collective-permute-start(bf16[128,512]{1,0:T(8,128)(2,1)S(1)} %collective-permute-done.3.refs_2_), channel_id=1, source_target_pairs={{0,1},{1,0},{2,3},{3,2},{4,5},{5,4},{6,7},{7,6},{8,9},{9,8},{10,11... | collective-permute-start | bytes 393224 | tf_op jit(solution)/shard_map/ppermute | solution.py:387
  19.6 2.9 %collective-permute-start.8 = (bf16[128,512]{1,0:T(8,128)(2,1)S(1)}, bf16[128,512]{1,0:T(8,128)(2,1)S(1)}, u32[]{:S(2)}, u32[]{:S(2)}) collective-permute-start(bf16[128,512]{1,0:T(8,128)(2,1)S(1)} %collective-permute-done.4.refs_3_), channel_id=1, source_target_pairs={{0,1},{1,0},{2,3},{3,2},{4,5},{5,4},{6,7},{7,6},{8,9},{9,8},{10,11... | collective-permute-start | bytes 393224 | tf_op jit(solution)/shard_map/ppermute | solution.py:387
  19.6 2.3 %copy-start.11 = (f32[768]{0:T(1024)S(1)}, f32[768]{0:T(1024)}, u32[]{:S(2)}) copy-start(f32[768]{0:T(1024)} %param.16) | copy-start | bytes 9220
  19.6 2.3 %copy-start.10 = (f32[1664]{0:T(1024)S(1)}, f32[1664]{0:T(1024)}, u32[]{:S(2)}) copy-start(f32[1664]{0:T(1024)} %param.24) | copy-start | bytes 19972
  19.6 2.4 %copy-start.12 = (f32[768]{0:T(1024)S(1)}, f32[768]{0:T(1024)}, u32[]{:S(2)}) copy-start(f32[768]{0:T(1024)} %param.17) | copy-start | bytes 9220
  22.6 2.5 %copy-start.1 = (bf16[768,1664]{1,0:T(8,128)(2,1)S(1)}, bf16[768,1664]{1,0:T(8,128)(2,1)}, u32[]{:S(2)}) copy-start(bf16[768,1664]{1,0:T(8,128)(2,1)} %mix_weight.1) | copy-start | bytes 7667716
  22.6 2.5 %copy-start.4 = (bf16[768,24]{0,1:T(8,128)(2,1)S(1)}, bf16[768,24]{0,1:T(8,128)(2,1)}, u32[]{:S(2)}) copy-start(bf16[768,24]{0,1:T(8,128)(2,1)} %param.20) | copy-start | bytes 110596
  22.6 2.5 %copy-start.5 = (f32[4,1664]{1,0:T(4,128)S(1)}, f32[4,1664]{1,0:T(4,128)}, u32[]{:S(2)}) copy-start(f32[4,1664]{1,0:T(4,128)} %conv_weight.1) | copy-start | bytes 79876
  22.6 2.5 %copy-start.7 = (f32[24]{0:T(128)S(1)}, f32[24]{0:T(128)}, u32[]{:S(2)}) copy-start(f32[24]{0:T(128)} %param.21) | copy-start | bytes 292
  22.6 2.5 %copy-start.8 = (f32[24]{0:T(128)S(1)}, f32[24]{0:T(128)}, u32[]{:S(2)}) copy-start(f32[24]{0:T(128)} %param.22) | copy-start | bytes 292
  25.1 16.9 %copy-start.9 = (f32[1536]{0:T(1024)S(1)}, f32[1536]{0:T(1024)}, u32[]{:S(2)}) copy-start(f32[1536]{0:T(1024)} %param.26) | copy-start | bytes 18436
  25.1 16.9 %copy-start.6 = (f32[24]{0:T(128)S(1)}, f32[24]{0:T(128)}, u32[]{:S(2)}) copy-start(f32[24]{0:T(128)} %skip.3) | copy-start | bytes 292
  28.1 1.5 %collective-permute-start.9 = (bf16[72,768]{1,0:T(8,128)(2,1)S(1)}, bf16[72,768]{1,0:T(8,128)(2,1)S(1)}, u32[]{:S(2)}, u32[]{:S(2)}) collective-permute-start(bf16[72,768]{1,0:T(8,128)(2,1)S(1)} %get-tuple-element.33), channel_id=1, source_target_pairs={{0,1},{1,0},{2,3},{3,2},{4,5},{5,4},{6,7},{7,6},{8,9},{9,8},{10,11... | collective-permute-start | bytes 331784 | tf_op jit(solution)/shard_map/ppermute | solution.py:387
  29.7 4.3 %collective-permute-start.10 = (bf16[72,768]{1,0:T(8,128)(2,1)S(1)}, bf16[72,768]{1,0:T(8,128)(2,1)S(1)}, u32[]{:S(2)}, u32[]{:S(2)}) collective-permute-start(bf16[72,768]{1,0:T(8,128)(2,1)S(1)} %get-tuple-element.35), channel_id=1, source_target_pairs={{0,2},{2,0},{4,6},{6,4},{8,10},{10,8},{12,14},{14,12},{1,3},{3,1},... | collective-permute-start | bytes 331784 | tf_op jit(solution)/shard_map/ppermute | solution.py:387
  29.9 5.7 %collective-permute-start.11 = (bf16[72,768]{1,0:T(8,128)(2,1)S(1)}, bf16[72,768]{1,0:T(8,128)(2,1)S(1)}, u32[]{:S(2)}, u32[]{:S(2)}) collective-permute-start(bf16[72,768]{1,0:T(8,128)(2,1)S(1)} %get-tuple-element.35), channel_id=1, source_target_pairs={{0,4},{2,6},{4,0},{6,2},{8,12},{10,14},{12,8},{14,10},{1,5},{3,7},... | collective-permute-start | bytes 331784 | tf_op jit(solution)/shard_map/ppermute | solution.py:387
  32.8 4.6 %collective-permute-start.12 = (bf16[72,768]{1,0:T(8,128)(2,1)S(1)}, bf16[72,768]{1,0:T(8,128)(2,1)S(1)}, u32[]{:S(2)}, u32[]{:S(2)}) collective-permute-start(bf16[72,768]{1,0:T(8,128)(2,1)S(1)} %get-tuple-element.35), channel_id=1, source_target_pairs={{0,6},{2,4},{4,2},{6,0},{8,14},{10,12},{12,10},{14,8},{1,7},{3,5},... | collective-permute-start | bytes 331784 | tf_op jit(solution)/shard_map/ppermute | solution.py:387
  37.5 12.9 %copy-start.2 = (bf16[768,1536]{1,0:T(8,128)(2,1)S(1)}, bf16[768,1536]{1,0:T(8,128)(2,1)}, u32[]{:S(2)}) copy-start(bf16[768,1536]{1,0:T(8,128)(2,1)} %gate_weight.1) | copy-start | bytes 7077892
  37.5 10.1 %collective-permute-start.13 = (bf16[72,768]{1,0:T(8,128)(2,1)S(1)}, bf16[72,768]{1,0:T(8,128)(2,1)S(1)}, u32[]{:S(2)}, u32[]{:S(2)}) collective-permute-start(bf16[72,768]{1,0:T(8,128)(2,1)S(1)} %get-tuple-element.38), channel_id=1, source_target_pairs={{0,8},{2,10},{4,12},{6,14},{8,0},{10,2},{12,4},{14,6},{1,9},{3,11}... | collective-permute-start | bytes 331784 | tf_op jit(solution)/shard_map/ppermute | solution.py:387
  47.7 5.0 %collective-permute-start.14 = (bf16[64,768]{1,0:T(8,128)(2,1)S(1)}, bf16[64,768]{1,0:T(8,128)(2,1)S(1)}, u32[]{:S(2)}, u32[]{:S(2)}) collective-permute-start(bf16[64,768]{1,0:T(8,128)(2,1)S(1)} %get-tuple-element.39), channel_id=1, source_target_pairs={{0,1},{1,0},{2,3},{3,2},{4,5},{5,4},{6,7},{7,6},{8,9},{9,8},{10,11... | collective-permute-start | bytes 294920 | tf_op jit(solution)/shard_map/ppermute | solution.py:387
  50.4 1.7 %copy-start = (bf16[1536,768]{1,0:T(8,128)(2,1)S(1)}, bf16[1536,768]{1,0:T(8,128)(2,1)}, u32[]{:S(2)}) copy-start(bf16[1536,768]{1,0:T(8,128)(2,1)} %out_weight.3) | copy-start | bytes 7077892

commit v4 on v3

--- a/solution.py
+++ b/solution.py
@@ -147,9 +147,44 @@
     return jnp.maximum(values, 0.0) + jnp.log1p(small)
 
 
+def half_mix(which, normed, scales, b_t, mix_weight, conv_weight, conv_bias, x_out):
+    half = E // 2
+    matrix = spread_matrix()
+    states = []
+    chunk = 256
+    spans = [
+        pl.ds(pl.multiple_of(which * half + first, 128), chunk) for first in range(0, half, chunk)
+    ]
+    wanted = jnp.where(which == 0, matrix[:, :half].astype(F32), matrix[:, half:].astype(F32)).astype(BF16)
+    ahead = project(normed, mix_weight, spans[0])
+    for place, lanes in enumerate(spans):
+        raw = ahead
+        if place + 1 < len(spans):
+            ahead = project(normed, mix_weight, spans[place + 1])
+        part = mixed(raw, conv_weight[:, lanes], conv_bias[:, lanes])
+        local = slice(place * chunk, (place + 1) * chunk)
+        x_out[:, local] = part
+        to_end = jnp.dot(scales, wanted[:, local], preferred_element_type=F32)
+        scaled = (part.astype(F32) * to_end).astype(BF16)
+        states.append(jnp.dot(b_t, scaled, preferred_element_type=F32))
+    return jnp.concatenate(states, axis=1)
+
+
+def project(normed, mix_weight, lanes):
+    return jnp.dot(normed, mix_weight[:, lanes], preferred_element_type=F32).astype(BF16)
+
+
+def mixed(raw, weight, bias):
+    raw = raw.astype(F32)
+    total = weight[0:1] * raw
+    for tap in range(1, weight.shape[0]):
+        total = pltpu.roll(total, 1, 0) + weight[tap : tap + 1] * raw
+    return silu(total[LEAD:] + bias).astype(BF16)
+
+
 def mix_kernel(
     embedded, norm_gain, mix_weight, step_weight, step_bias, log_rate, conv_weight, conv_bias,
-    normed_out, x_out, b_out, c_out, step_out, cum_out, keep_out, send_out, state,
+    normed_out, x_out, b_out, c_out, b_t_out, step_out, cum_out, scales_out, decay_out, send_out,
 ):
     col, row = lax.axis_index("cols"), lax.axis_index("rows")
     resid = embedded[...].astype(F32)
@@ -158,8 +193,9 @@
     rows = lax.broadcasted_iota(jnp.int32, normed_f.shape, 0)
     blank = (rows < LEAD) & (col == 0) & (row == 0)
     normed = jnp.where(blank, 0.0, normed_f).astype(BF16)
-    normed_out[...] = normed_f[LEAD:].astype(BF16)
+    normed_out[...] = normed
     length = embedded.shape[0] - LEAD
+    maps_raw = project(normed, mix_weight, slice(E, E + 2 * NSTATE))
     step_raw = lax.dot_general(
         normed, step_weight[...], (((1,), (1,)), ((), ())), preferred_element_type=F32
     )[LEAD:]
@@ -176,45 +212,27 @@
     cum = cum + jnp.dot(lower, low, preferred_element_type=F32)
     step_out[...] = step
     cum_out[...] = cum
-    matrix = spread_matrix()
     last = cum[length - 1 :]
     scales = (jnp.exp(last - cum) * step).astype(BF16)
-    state[NSTATE : NSTATE + 8, :] = spread(jnp.broadcast_to(jnp.exp(last), (8, HEADS)), matrix)
-    taps = conv_weight.shape[0]
-
-    def project(lanes):
-        return jnp.dot(normed, mix_weight[:, lanes], preferred_element_type=F32).astype(BF16)
-
-    def mixed(raw, lanes):
-        raw = raw.astype(F32)
-        total = conv_weight[0:1, lanes] * raw
-        for tap in range(1, taps):
-            total = pltpu.roll(total, 1, 0) + conv_weight[tap : tap + 1, lanes] * raw
-        return silu(total[LEAD:] + conv_bias[:, lanes]).astype(BF16)
-
-    chunk = 512
-    spans = [slice(E, E + 2 * NSTATE)] + [slice(first, first + chunk) for first in range(0, E, chunk)]
-    ahead = project(spans[0])
-    for place, lanes in enumerate(spans):
-        raw = ahead
-        if place + 1 < len(spans):
-            ahead = project(spans[place + 1])
-        part = mixed(raw, lanes)
-        if place == 0:
-            maps = part.astype(F32)
-            b_out[...] = maps[:, :NSTATE].astype(BF16)
-            c_out[...] = maps[:, NSTATE:].astype(BF16)
-            b_t = maps.T[:NSTATE].astype(BF16)
-            continue
-        x_out[:, lanes] = part
-        to_end = jnp.dot(scales, matrix[:, lanes], preferred_element_type=F32)
-        scaled = (part.astype(F32) * to_end).astype(BF16)
-        state[0:NSTATE, lanes] = jnp.dot(b_t, scaled, preferred_element_type=F32)
+    scales_out[...] = scales
+    decay = spread(jnp.broadcast_to(jnp.exp(last), (8, HEADS)), spread_matrix())
+    maps = mixed(maps_raw, conv_weight[:, E:], conv_bias[:, E:]).astype(F32)
+    b_out[...] = maps[:, :NSTATE].astype(BF16)
+    c_out[...] = maps[:, NSTATE:].astype(BF16)
+    b_t = maps.T[:NSTATE].astype(BF16)
+    b_t_out[...] = b_t
+    state = half_mix(1 - row, normed, scales, b_t, mix_weight, conv_weight, conv_bias, x_out)
     half = E // 2
-    mine = pl.ds(pl.multiple_of(row * half, 128), half)
-    theirs = pl.ds(pl.multiple_of((1 - row) * half, 128), half)
-    keep_out[...] = state[:, mine]
-    send_out[...] = wire(state[0:NSTATE, theirs], state[NSTATE : NSTATE + 8, theirs])
+    first = row == 0
+    decay_out[...] = jnp.where(first, decay[:, :half], decay[:, half:])
+    send_out[...] = wire(state, jnp.where(first, decay[:, half:], decay[:, :half]))
+
+
+def rest_kernel(normed, scales, b_t, mix_weight, conv_weight, conv_bias, decay, x_out, keep_out):
+    keep_out[0:NSTATE, :] = half_mix(
+        lax.axis_index("rows"), normed[...], scales[...], b_t[...], mix_weight, conv_weight, conv_bias, x_out
+    )
+    keep_out[NSTATE : NSTATE + 8, :] = decay[...]
 
 
 def wire(values, decay):
@@ -309,16 +327,21 @@
     theirs_out[...] = jnp.where(upper, ahead[0], second).astype(BF16)
 
 
-def gate_kernel(normed, gate_weight, local_a, local_b, cum, own_out, factor_out):
-    gate = jnp.dot(normed[...], gate_weight[...], preferred_element_type=F32).astype(BF16).astype(F32)
+def gate_kernel(normed, gate_weight, local_mine, local_theirs, cum, own_out, factor_out):
+    gate = jnp.dot(normed[...], gate_weight[...], preferred_element_type=F32)[LEAD:].astype(BF16).astype(F32)
     gate = silu(gate)
-    half = local_a.shape[1]
-    own_out[:, :half] = local_a[...] * gate[:, :half]
-    own_out[:, half:] = local_b[...] * gate[:, half:]
+    half = local_mine.shape[1]
+    upper = lax.axis_index("rows") == 1
+    own_out[:, :half] = jnp.where(upper, local_theirs[...], local_mine[...]) * gate[:, :half]
+    own_out[:, half:] = jnp.where(upper, local_mine[...], local_theirs[...]) * gate[:, half:]
     factor_out[...] = spread(jnp.exp(cum[...]), spread_matrix()) * gate
 
 
-def intra_kernel(first, skip, x, b_mat, c_mat, step, cum, out):
+def intra_kernel(flip, skip, x, b_mat, c_mat, step, cum, out):
+    row = lax.axis_index("rows")
+    which = 1 - row if flip else row
+    heads = HEADS // 2
+    upper = which == 1
     length = x.shape[0]
     half = length // 2
     scores = lax.dot_general(c_mat[...], b_mat[...], (((1,), (1,)), ((), ())), preferred_element_type=F32)
@@ -326,12 +349,12 @@
         jnp.int32, (length, length), 1
     )
     scores = jnp.where(causal, scores, 0.0)
-    wide = jnp.zeros((length, 128 - HEADS), F32)
-    cum_v = cum[...]
+    wide = jnp.zeros((length, 128 - heads), F32)
+    cum_v = jnp.where(upper, cum[:, heads:], cum[:, :heads])
     cum_t = jnp.concatenate([cum_v, wide], axis=1).T
-    step_t = jnp.concatenate([step[...], wide], axis=1).T
+    step_t = jnp.concatenate([jnp.where(upper, step[:, heads:], step[:, :heads]), wide], axis=1).T
     for place in range(out.shape[1] // 128):
-        pair = first + place
+        pair = place
         x_pair = x[:, pair * 128 : (pair + 1) * 128]
         tops, bottoms = [], []
         for member in range(2):
@@ -350,7 +373,8 @@
             tops.append(top)
             bottoms.append(bottom)
         lane = lax.broadcasted_iota(jnp.int32, x_pair.shape, 1)
-        direct = jnp.where(lane < HDIM, skip[2 * pair], skip[2 * pair + 1]) * x_pair.astype(F32)
+        base = which * heads + 2 * pair
+        direct = jnp.where(lane < HDIM, skip[base], skip[base + 1]) * x_pair.astype(F32)
         lanes = slice(place * 128, (place + 1) * 128)
         out[0:half, lanes] = jnp.concatenate(tops, axis=1) + direct[:half]
         out[half:length, lanes] = jnp.concatenate(bottoms, axis=1) + direct[half:]
@@ -388,7 +412,7 @@
 
 
 def sending_order(side):
-    return tuple(reversed(range(side)))
+    return (*range(side // 2, side), *reversed(range(side // 2)))
 
 
 def across(block, step):
@@ -510,28 +534,29 @@
     mixed_width = mix_weight.shape[1]
     half = E // 2
     packed = NSTATE + 8
-    normed, x, b_mat, c_mat, step, cum, keep, send = call(
+    conv = (conv_weight, line(conv_bias))
+    normed, x_theirs, b_mat, c_mat, b_t, step, cum, scales, decay, send = call(
         mix_kernel,
-        (
-            embedded, line(norm_gain), mix_weight, step_weight.T, line(step_bias), line(log_rate),
-            conv_weight, line(conv_bias),
-        ),
+        (embedded, line(norm_gain), mix_weight, step_weight.T, line(step_bias), line(log_rate), *conv),
         [
-            shape((length, D)), shape((length, E)), shape((length, NSTATE)), shape((length, NSTATE)),
-            shape((length, HEADS), F32), shape((length, HEADS), F32), shape((packed, half), F32),
-            shape((packed, half)),
+            shape((LEAD + length, D)), shape((length, half)), shape((length, NSTATE)), shape((length, NSTATE)),
+            shape((NSTATE, length)), shape((length, HEADS), F32), shape((length, HEADS), F32),
+            shape((length, HEADS)), shape((8, half), F32), shape((packed, half)),
         ],
-        [pltpu.VMEM((packed, E), F32)],
-        flops=2 * length * D * mixed_width, moved=4 << 20, limit=16,
+        flops=length * D * mixed_width, moved=4 << 20, limit=16,
     )
     came = swap(send, "rows", 1)
     summary, message = shape((packed, half), F32), shape((packed, half))
+    x_mine, keep = call(
+        rest_kernel, (normed, scales, b_t, mix_weight, *conv, decay), [shape((length, half)), summary],
+        flops=length * D * mixed_width, moved=4 << 20, limit=16,
+    )
     total, out = call(pair_kernel, (keep, came), [summary, message])
     locals_ = []
     for part in range(2):
         locals_.append(
             call(
-                partial(intra_kernel, part * HEADS // 4), (skip_gain, x, b_mat, c_mat, step, cum),
+                partial(intra_kernel, bool(part)), (skip_gain, (x_mine, x_theirs)[part], b_mat, c_mat, step, cum),
                 shape((length, half), F32), scalars=1,
                 flops=HEADS * length * length * 128, moved=2 << 20, limit=8,
             )

time: 54.4 us -> 53.7 us (0.987)
  Pallas kernels: 13.1 us -> 15.2 us
  waiting for transfers between devices: 16.8 us -> 14.9 us
  starting transfers between devices: 19.7 us -> 18.9 us
    pallas_call x12 -> x13, Pallas kernels: 13.1 us -> 15.2 us  [call(): pl.pallas_call(kernel, out_shape=outs, in_specs=[pl.BlockSpec(memory_spac...]
    ppermute x11, waiting for transfers between devices: 10.1 us -> 8.23 us  [swap(): lax.ppermute(block, axis, [(i, i ^ bit) for i in range(lax.axis_size(axis...]
    ppermute x11, starting transfers between devices: 9.42 us -> 8.64 us  [swap(): lax.ppermute(block, axis, [(i, i ^ bit) for i in range(lax.axis_size(axis...]
  transfers between devices with their start and end apart: 15 -> 15, of which waited for: 8 -> 7; matrix products, arithmetic and copies ran while one was open for 5% -> 5% of each run, Pallas kernels for 11% -> 16%
where the time goes in v4:
time: 53.7 us; the launch traced here: 53.5 us
  starting transfers between devices  18.9 us (35%)
  Pallas kernels  15.2 us (28%)
  waiting for transfers between devices  14.9 us (28%)
  local copies, waits for them, and re-layouts  4.17 us (8%)
    pallas_call x13, Pallas kernels, call(): pl.pallas_call(kernel, out_shape=outs, in_specs=[pl.BlockSpec(memory_spac...  15.2 us
    ppermute x4, starting transfers between devices, across(): return lax.ppermute(block, ('cols', 'rows'), pairs)  10.3 us
    ppermute x11, starting transfers between devices, swap(): lax.ppermute(block, axis, [(i, i ^ bit) for i in range(lax.axis_size(axis...  8.64 us
    ppermute x11, waiting for transfers between devices, swap(): lax.ppermute(block, axis, [(i, i ^ bit) for i in range(lax.axis_size(axis...  8.23 us
    ppermute x4, waiting for transfers between devices, across(): return lax.ppermute(block, ('cols', 'rows'), pairs)  6.67 us
    transpose x1, local copies, waits for them, and re-layouts, embed_by_rows(): patch_weight.reshape(3, 8, KERNEL, CHAN, D).transpose(2, 0, 3, 1, 4)  2.29 us
    unnamed x26, local copies, waits for them, and re-layouts  1.35 us
  transfers between devices with their start and end apart: 15, of which 7 were waited for; matrix products, arithmetic and copies ran while one was open for 5% of the time, Pallas kernels for 16%

profile of v4, /device:TPU:1, one launch (start us, length us, event | category | flops | bytes accessed | tf_op | source)
XLA Modules:
  0.0 53.5 jit_solution(12096341188677258590)
XLA Ops:
  0.0 1.0 %copy-done.3 = bf16[3,128,512]{2,1,0:T(8,128)(2,1)S(1)} copy-done((bf16[3,128,512]{2,1,0:T(8,128)(2,1)S(1)}, bf16[3,128,512]{2,1,0:T(8,128)(2,1)}, u32[]{:S(2)}) %copy-start.3) | copy-done | bytes 393240
  1.0 0.9 %collective-permute-done.partner = bf16[3,128,512]{2,1,0:T(8,128)(2,1)S(1)} collective-permute-done((bf16[3,128,512]{2,1,0:T(8,128)(2,1)}, bf16[3,128,512]{2,1,0:T(8,128)(2,1)S(1)}, u32[]{:S(2)}, u32[]{:S(2)}) %collective-permute-start) | collective-permute-done | bytes 393248 | tf_op jit(solution)/shard_map/ppermute | solution.py:411
  1.9 0.2 shard_map.137
  2.2 5.6 %collective-permute-start.1 = (bf16[128,512]{1,0:T(8,128)(2,1)S(1)}, bf16[128,512]{1,0:T(8,128)(2,1)S(1)}, u32[]{:S(2)}, u32[]{:S(2)}) collective-permute-start(bf16[128,512]{1,0:T(8,128)(2,1)S(1)} %get-tuple-element.32), channel_id=1, source_target_pairs={{0,0},{1,8},{2,2},{3,10},{4,4},{5,12},{6,6},{7,14},{8,1},{9,9},{10... | collective-permute-start | bytes 393224 | tf_op jit(solution)/shard_map/ppermute | solution.py:425
  7.8 1.1 %collective-permute-start.2 = (bf16[128,512]{1,0:T(8,128)(2,1)S(1)}, bf16[128,512]{1,0:T(8,128)(2,1)S(1)}, u32[]{:S(2)}, u32[]{:S(2)}) collective-permute-start(bf16[128,512]{1,0:T(8,128)(2,1)S(1)} %get-tuple-element.33), channel_id=1, source_target_pairs={{0,2},{1,10},{2,0},{3,8},{4,6},{5,14},{6,4},{7,12},{8,3},{9,11},{1... | collective-permute-start | bytes 393224 | tf_op jit(solution)/shard_map/ppermute | solution.py:425
  8.9 3.6 %collective-permute-start.3 = (bf16[128,512]{1,0:T(8,128)(2,1)S(1)}, bf16[128,512]{1,0:T(8,128)(2,1)S(1)}, u32[]{:S(2)}, u32[]{:S(2)}) collective-permute-start(bf16[128,512]{1,0:T(8,128)(2,1)S(1)} %get-tuple-element.34), channel_id=1, source_target_pairs={{0,4},{1,12},{2,6},{3,14},{4,0},{5,8},{6,2},{7,10},{8,5},{9,13},{1... | collective-permute-start | bytes 393224 | tf_op jit(solution)/shard_map/ppermute | solution.py:425
  12.5 4.6 %collective-permute-done.2.refs_1_ = bf16[128,512]{1,0:T(8,128)(2,1)S(1)} collective-permute-done((bf16[128,512]{1,0:T(8,128)(2,1)S(1)}, bf16[128,512]{1,0:T(8,128)(2,1)S(1)}, u32[]{:S(2)}, u32[]{:S(2)}) %collective-permute-start.2) | collective-permute-done | bytes 131104 | tf_op jit(solution)/shard_map/ppermute | solution.py:425
  17.0 0.5 collective-permute-start.7
  17.6 2.1 %collective-permute-done.4.refs_3_ = bf16[128,512]{1,0:T(8,128)(2,1)S(1)} collective-permute-done((bf16[128,512]{1,0:T(8,128)(2,1)S(1)}, bf16[128,512]{1,0:T(8,128)(2,1)S(1)}, u32[]{:S(2)}, u32[]{:S(2)}) %collective-permute-start.4) | collective-permute-done | bytes 131104 | tf_op jit(solution)/shard_map/ppermute | solution.py:425
  19.6 2.3 %copy.15 = bf16[24,3,3,8,768]{4,3,2,1,0:T(8,128)(2,1)S(1)} copy(bf16[24,3,3,8,768]{4,0,2,3,1:T(8,128)(2,1)} %bitcast.13) | data formatting | bytes 5308416 | tf_op jit(solution)/shard_map/transpose | solution.py:442
  22.0 0.5 pad.4
  22.6 2.4 %shard_map.138.embedded = bf16[264,768]{1,0:T(8,128)(2,1)S(1)} custom-call(bf16[128,512]{1,0:T(8,128)(2,1)S(1)} %collective-permute-done.1.refs_0_, bf16[128,512]{1,0:T(8,128)(2,1)S(1)} %collective-permute-done.2.refs_1_, bf16[128,512]{1,0:T(8,128)(2,1)S(1)} %collective-permute-done.3.refs_2_, bf16[128,512]{1,0:T(8,128)(2,1)S(1)} %collective-permute-done.4.refs_3_, ...), custom_call_target="tpu_custom_call" | custom-call | flops 1207959552 | bytes 6291456 | tf_op jit(solution)/shard_map/pallas_call | solution.py:31
  25.1 2.0 %shard_map.139 = (bf16[264,768]{1,0:T(8,128)(2,1)S(1)}, bf16[256,768]{1,0:T(8,128)(2,1)S(1)}, bf16[256,64]{1,0:T(8,128)(2,1)S(1)}, bf16[256,64]{1,0:T(8,128)(2,1...) custom-call(bf16[264,768]{1,0:T(8,128)(2,1)S(1)} %shard_map.138.embe, ...), custom_call_target="tpu_custom_call" | custom-call | flops 327155712 | bytes 4194304 | tf_op jit(solution)/shard_map/pallas_call | solution.py:31
  27.1 0.6 %collective-permute-start.9 = (bf16[72,768]{1,0:T(8,128)(2,1)S(1)}, bf16[72,768]{1,0:T(8,128)(2,1)S(1)}, u32[]{:S(2)}, u32[]{:S(2)}) collective-permute-start(bf16[72,768]{1,0:T(8,128)(2,1)S(1)} %get-tuple-element.41), channel_id=1, source_target_pairs={{0,1},{1,0},{2,3},{3,2},{4,5},{5,4},{6,7},{7,6},{8,9},{9,8},{10,11... | collective-permute-start | bytes 331784 | tf_op jit(solution)/shard_map/ppermute | solution.py:411
  27.7 1.4 %shard_map.140 = (bf16[256,768]{1,0:T(8,128)(2,1)S(1)}, f32[72,768]{1,0:T(8,128)S(1)}) custom-call(bf16[264,768]{1,0:T(8,128)(2,1)S(1)} %get-tuple-element.36.normed, bf16[256,24]{1,0:T(8,128)(2,1)S(1)} %get-tuple-element.37.scales, bf16[64,256]{1,0:T(8,128)(2,1)S(1)} %get-tuple-element.38.b_t, bf16[768,1664]{1,0:T(8,128)(2,1)S(1)} %copy-done, ...), custom_call_target="tpu_custom_call" | custom-call | flops 327155712 | bytes 4194304 | tf_op jit(solution)/shard_map/pallas_call | solution.py:31
  29.2 0.2 collective-permute-start.10
  29.4 2.9 %collective-permute-start.11 = (bf16[72,768]{1,0:T(8,128)(2,1)S(1)}, bf16[72,768]{1,0:T(8,128)(2,1)S(1)}, u32[]{:S(2)}, u32[]{:S(2)}) collective-permute-start(bf16[72,768]{1,0:T(8,128)(2,1)S(1)} %get-tuple-element.43), channel_id=1, source_target_pairs={{0,4},{2,6},{4,0},{6,2},{8,12},{10,14},{12,8},{14,10},{1,5},{3,7},... | collective-permute-start | bytes 331784 | tf_op jit(solution)/shard_map/ppermute | solution.py:411
  32.3 0.1 collective-permute-start.12
  32.4 1.5 %collective-permute-done.10.refs_1_ = bf16[72,768]{1,0:T(8,128)(2,1)S(1)} collective-permute-done((bf16[72,768]{1,0:T(8,128)(2,1)S(1)}, bf16[72,768]{1,0:T(8,128)(2,1)S(1)}, u32[]{:S(2)}, u32[]{:S(2)}) %collective-permute-start.10) | collective-permute-done | bytes 110624 | tf_op jit(solution)/shard_map/ppermute | solution.py:411
  33.9 1.6 %collective-permute-done.11.refs_2_ = bf16[72,768]{1,0:T(8,128)(2,1)S(1)} collective-permute-done((bf16[72,768]{1,0:T(8,128)(2,1)S(1)}, bf16[72,768]{1,0:T(8,128)(2,1)S(1)}, u32[]{:S(2)}, u32[]{:S(2)}) %collective-permute-start.11) | collective-permute-done | bytes 110624 | tf_op jit(solution)/shard_map/ppermute | solution.py:411
  35.4 1.9 %collective-permute-done.12.refs_3_ = bf16[72,768]{1,0:T(8,128)(2,1)S(1)} collective-permute-done((bf16[72,768]{1,0:T(8,128)(2,1)S(1)}, bf16[72,768]{1,0:T(8,128)(2,1)S(1)}, u32[]{:S(2)}, u32[]{:S(2)}) %collective-permute-start.12) | collective-permute-done | bytes 110624 | tf_op jit(solution)/shard_map/ppermute | solution.py:411
  37.3 0.2 shard_map.142
  37.5 3.0 %collective-permute-start.13 = (bf16[72,768]{1,0:T(8,128)(2,1)S(1)}, bf16[72,768]{1,0:T(8,128)(2,1)S(1)}, u32[]{:S(2)}, u32[]{:S(2)}) collective-permute-start(bf16[72,768]{1,0:T(8,128)(2,1)S(1)} %get-tuple-element.46), channel_id=1, source_target_pairs={{0,8},{2,10},{4,12},{6,14},{8,0},{10,2},{12,4},{14,6},{1,9},{3,11}... | collective-permute-start | bytes 331784 | tf_op jit(solution)/shard_map/ppermute | solution.py:411
  40.5 2.7 %shard_map.145.local_theirs = f32[256,768]{1,0:T(8,128)S(1)} custom-call(f32[24]{0:T(128)S(1)} %copy-done.6, bf16[256,768]{1,0:T(8,128)(2,1)S(1)} %get-tuple-element.53.x, bf16[256,64]{1,0:T(8,128)(2,1)S(1)} %get-tuple-element.49.b_mat, bf16[256,64]{1,0:T(8,128)(2,1)S(1)} %get-tuple-element.50.c_mat, f32[256,24]{1,0:T(8,128)S(1)} %get-tuple-element.51.step, ...), custom_call_target="tpu_custom_call" | custom-call | flops 201326592 | bytes 2097152 | tf_op jit(solution)/shard_map/pallas_call | solution.py:31
  43.2 2.3 %collective-permute-done.13.refs_2_ = bf16[72,768]{1,0:T(8,128)(2,1)S(1)} collective-permute-done((bf16[72,768]{1,0:T(8,128)(2,1)S(1)}, bf16[72,768]{1,0:T(8,128)(2,1)S(1)}, u32[]{:S(2)}, u32[]{:S(2)}) %collective-permute-start.13) | collective-permute-done | bytes 110624 | tf_op jit(solution)/shard_map/ppermute | solution.py:411
  45.5 0.1 shard_map.143
  45.6 1.4 %collective-permute-start.14 = (bf16[64,768]{1,0:T(8,128)(2,1)S(1)}, bf16[64,768]{1,0:T(8,128)(2,1)S(1)}, u32[]{:S(2)}, u32[]{:S(2)}) collective-permute-start(bf16[64,768]{1,0:T(8,128)(2,1)S(1)} %get-tuple-element.47), channel_id=1, source_target_pairs={{0,1},{1,0},{2,3},{3,2},{4,5},{5,4},{6,7},{7,6},{8,9},{9,8},{10,11... | collective-permute-start | bytes 294920 | tf_op jit(solution)/shard_map/ppermute | solution.py:411
  47.0 2.7 %shard_map.144.local_mine = f32[256,768]{1,0:T(8,128)S(1)} custom-call(f32[24]{0:T(128)S(1)} %copy-done.6, bf16[256,768]{1,0:T(8,128)(2,1)S(1)} %get-tuple-element.48.x, bf16[256,64]{1,0:T(8,128)(2,1)S(1)} %get-tuple-element.49.b_mat, bf16[256,64]{1,0:T(8,128)(2,1)S(1)} %get-tuple-element.50.c_mat, f32[256,24]{1,0:T(8,128)S(1)} %get-tuple-element.51.step, ...), custom_call_target="tpu_custom_call" | custom-call | flops 201326592 | bytes 2097152 | tf_op jit(solution)/shard_map/pallas_call | solution.py:31
  49.7 1.4 %shard_map.146 = (f32[256,1536]{1,0:T(8,128)S(1)}, f32[256,1536]{1,0:T(8,128)S(1)}) custom-call(bf16[264,768]{1,0:T(8,128)(2,1)S(1)} %get-tuple-element.36.normed, bf16[768,1536]{1,0:T(8,128)(2,1)S(1)} %copy-done.2, f32[256,768]{1,0:T(8,128)S(1)} %shard_map.144.local_mine, f32[256,768]{1,0:T(8,128)S(1)} %shard_map.145.local_theirs, ...), custom_call_target="tpu_custom_call" | custom-call | flops 603979776 | bytes 4194304 | tf_op jit(solution)/shard_map/pallas_call | solution.py:31
  51.1 0.3 copy-done.1
  51.4 0.7 %shard_map.147 = (f32[256,768]{1,0:T(8,128)S(1)}, f32[256,128]{1,0:T(8,128)S(1)}) custom-call(bf16[64,768]{1,0:T(8,128)(2,1)S(1)} %get-tuple-element.56.mine, f32[256,1536]{1,0:T(8,128)S(1)} %get-tuple-element.54.own, f32[256,1536]{1,0:T(8,128)S(1)} %get-tuple-element.55.factor, bf16[256,64]{1,0:T(8,128)(2,1)S(1)} %get-tuple-element.50.c_mat, ...), custom_call_target="tpu_custom_call" | custom-call | flops 301989888 | bytes 4194304 | tf_op jit(solution)/shard_map/pallas_call | solution.py:31
  52.1 1.4 %shard_map.148 = bf16[256,768]{1,0:T(8,128)(2,1)} custom-call(bf16[64,768]{1,0:T(8,128)(2,1)S(1)} %collective-permute-done.14.theirs, f32[256,1536]{1,0:T(8,128)S(1)} %get-tuple-element.54.own, f32[256,1536]{1,0:T(8,128)S(1)} %get-tuple-element.55.factor, bf16[256,64]{1,0:T(8,128)(2,1)S(1)} %get-tuple-element.50.c_mat, f32[1,1536]{1,0:T(1,128)S(1)} %reshape.35.out_gain, ...), custom_call_target="tpu_custom_call" | custom-call | flops 301989888 | bytes 4194304 | tf_op jit(solution)/shard_map/pallas_call | solution.py:31
  (43 shorter events, 0.2 us)
Async XLA Ops:
  0.0 1.9 %collective-permute-start = (bf16[3,128,512]{2,1,0:T(8,128)(2,1)}, bf16[3,128,512]{2,1,0:T(8,128)(2,1)S(1)}, u32[]{:S(2)}, u32[]{:S(2)}) collective-permute-start(bf16[3,128,512]{2,1,0:T(8,128)(2,1)} %pixels.1), channel_id=1, source_target_pairs={{0,1},{1,0},{2,3},{3,2},{4,5},{5,4},{6,7},{7,6},{8,9},{9,8},{10,11... | collective-permute-start | bytes 1179656 | tf_op jit(solution)/shard_map/ppermute | solution.py:411
  0.0 1.0 %copy-start.3 = (bf16[3,128,512]{2,1,0:T(8,128)(2,1)S(1)}, bf16[3,128,512]{2,1,0:T(8,128)(2,1)}, u32[]{:S(2)}) copy-start(bf16[3,128,512]{2,1,0:T(8,128)(2,1)} %pixels.1) | copy-start | bytes 1179652
  2.2 10.3 %collective-permute-start.1 = (bf16[128,512]{1,0:T(8,128)(2,1)S(1)}, bf16[128,512]{1,0:T(8,128)(2,1)S(1)}, u32[]{:S(2)}, u32[]{:S(2)}) collective-permute-start(bf16[128,512]{1,0:T(8,128)(2,1)S(1)} %get-tuple-element.32), channel_id=1, source_target_pairs={{0,0},{1,8},{2,2},{3,10},{4,4},{5,12},{6,6},{7,14},{8,1},{9,9},{10... | collective-permute-start | bytes 393224 | tf_op jit(solution)/shard_map/ppermute | solution.py:425
  7.8 9.3 %collective-permute-start.2 = (bf16[128,512]{1,0:T(8,128)(2,1)S(1)}, bf16[128,512]{1,0:T(8,128)(2,1)S(1)}, u32[]{:S(2)}, u32[]{:S(2)}) collective-permute-start(bf16[128,512]{1,0:T(8,128)(2,1)S(1)} %get-tuple-element.33), channel_id=1, source_target_pairs={{0,2},{1,10},{2,0},{3,8},{4,6},{5,14},{6,4},{7,12},{8,3},{9,11},{1... | collective-permute-start | bytes 393224 | tf_op jit(solution)/shard_map/ppermute | solution.py:425
  8.9 8.2 %collective-permute-start.3 = (bf16[128,512]{1,0:T(8,128)(2,1)S(1)}, bf16[128,512]{1,0:T(8,128)(2,1)S(1)}, u32[]{:S(2)}, u32[]{:S(2)}) collective-permute-start(bf16[128,512]{1,0:T(8,128)(2,1)S(1)} %get-tuple-element.34), channel_id=1, source_target_pairs={{0,4},{1,12},{2,6},{3,14},{4,0},{5,8},{6,2},{7,10},{8,5},{9,13},{1... | collective-permute-start | bytes 393224 | tf_op jit(solution)/shard_map/ppermute | solution.py:425
  12.4 7.2 %collective-permute-start.4 = (bf16[128,512]{1,0:T(8,128)(2,1)S(1)}, bf16[128,512]{1,0:T(8,128)(2,1)S(1)}, u32[]{:S(2)}, u32[]{:S(2)}) collective-permute-start(bf16[128,512]{1,0:T(8,128)(2,1)S(1)} %get-tuple-element.35), channel_id=1, source_target_pairs={{0,6},{1,14},{2,4},{3,12},{4,2},{5,10},{6,0},{7,8},{8,7},{9,15},{1... | collective-permute-start | bytes 393224 | tf_op jit(solution)/shard_map/ppermute | solution.py:425
  12.4 10.1 %collective-permute-start.5 = (bf16[128,512]{1,0:T(8,128)(2,1)S(1)}, bf16[128,512]{1,0:T(8,128)(2,1)S(1)}, u32[]{:S(2)}, u32[]{:S(2)}) collective-permute-start(bf16[128,512]{1,0:T(8,128)(2,1)S(1)} %collective-permute-done.1.refs_0_), channel_id=1, source_target_pairs={{0,1},{1,0},{2,3},{3,2},{4,5},{5,4},{6,7},{7,6},{8,9},{9,8},{10,11... | collective-permute-start | bytes 393224 | tf_op jit(solution)/shard_map/ppermute | solution.py:411
  17.0 5.5 %collective-permute-start.6 = (bf16[128,512]{1,0:T(8,128)(2,1)S(1)}, bf16[128,512]{1,0:T(8,128)(2,1)S(1)}, u32[]{:S(2)}, u32[]{:S(2)}) collective-permute-start(bf16[128,512]{1,0:T(8,128)(2,1)S(1)} %collective-permute-done.2.refs_1_), channel_id=1, source_target_pairs={{0,1},{1,0},{2,3},{3,2},{4,5},{5,4},{6,7},{7,6},{8,9},{9,8},{10,11... | collective-permute-start | bytes 393224 | tf_op jit(solution)/shard_map/ppermute | solution.py:411
  17.0 5.5 %collective-permute-start.7 = (bf16[128,512]{1,0:T(8,128)(2,1)S(1)}, bf16[128,512]{1,0:T(8,128)(2,1)S(1)}, u32[]{:S(2)}, u32[]{:S(2)}) collective-permute-start(bf16[128,512]{1,0:T(8,128)(2,1)S(1)} %collective-permute-done.3.refs_2_), channel_id=1, source_target_pairs={{0,1},{1,0},{2,3},{3,2},{4,5},{5,4},{6,7},{7,6},{8,9},{9,8},{10,11... | collective-permute-start | bytes 393224 | tf_op jit(solution)/shard_map/ppermute | solution.py:411
  19.6 2.9 %collective-permute-start.8 = (bf16[128,512]{1,0:T(8,128)(2,1)S(1)}, bf16[128,512]{1,0:T(8,128)(2,1)S(1)}, u32[]{:S(2)}, u32[]{:S(2)}) collective-permute-start(bf16[128,512]{1,0:T(8,128)(2,1)S(1)} %collective-permute-done.4.refs_3_), channel_id=1, source_target_pairs={{0,1},{1,0},{2,3},{3,2},{4,5},{5,4},{6,7},{7,6},{8,9},{9,8},{10,11... | collective-permute-start | bytes 393224 | tf_op jit(solution)/shard_map/ppermute | solution.py:411
  19.6 2.3 %copy-start.11 = (f32[768]{0:T(1024)S(1)}, f32[768]{0:T(1024)}, u32[]{:S(2)}) copy-start(f32[768]{0:T(1024)} %param.16) | copy-start | bytes 9220
  19.6 2.3 %copy-start.10 = (f32[1664]{0:T(1024)S(1)}, f32[1664]{0:T(1024)}, u32[]{:S(2)}) copy-start(f32[1664]{0:T(1024)} %param.24) | copy-start | bytes 19972
  19.6 2.4 %copy-start.12 = (f32[768]{0:T(1024)S(1)}, f32[768]{0:T(1024)}, u32[]{:S(2)}) copy-start(f32[768]{0:T(1024)} %param.17) | copy-start | bytes 9220
  22.6 2.5 %copy-start = (bf16[768,1664]{1,0:T(8,128)(2,1)S(1)}, bf16[768,1664]{1,0:T(8,128)(2,1)}, u32[]{:S(2)}) copy-start(bf16[768,1664]{1,0:T(8,128)(2,1)} %mix_weight.3) | copy-start | bytes 7667716
  22.6 2.5 %copy-start.4 = (f32[4,1664]{1,0:T(4,128)S(1)}, f32[4,1664]{1,0:T(4,128)}, u32[]{:S(2)}) copy-start(f32[4,1664]{1,0:T(4,128)} %conv_weight.3) | copy-start | bytes 79876
  22.6 2.5 %copy-start.5 = (bf16[768,24]{0,1:T(8,128)(2,1)S(1)}, bf16[768,24]{0,1:T(8,128)(2,1)}, u32[]{:S(2)}) copy-start(bf16[768,24]{0,1:T(8,128)(2,1)} %param.20) | copy-start | bytes 110596
  22.6 2.5 %copy-start.7 = (f32[24]{0:T(128)S(1)}, f32[24]{0:T(128)}, u32[]{:S(2)}) copy-start(f32[24]{0:T(128)} %param.21) | copy-start | bytes 292
  22.6 2.5 %copy-start.8 = (f32[24]{0:T(128)S(1)}, f32[24]{0:T(128)}, u32[]{:S(2)}) copy-start(f32[24]{0:T(128)} %param.22) | copy-start | bytes 292
  27.1 13.4 %copy-start.9 = (f32[1536]{0:T(1024)S(1)}, f32[1536]{0:T(1024)}, u32[]{:S(2)}) copy-start(f32[1536]{0:T(1024)} %param.26) | copy-start | bytes 18436
  27.1 13.4 %copy-start.6 = (f32[24]{0:T(128)S(1)}, f32[24]{0:T(128)}, u32[]{:S(2)}) copy-start(f32[24]{0:T(128)} %skip.3) | copy-start | bytes 292
  27.1 2.0 %collective-permute-start.9 = (bf16[72,768]{1,0:T(8,128)(2,1)S(1)}, bf16[72,768]{1,0:T(8,128)(2,1)S(1)}, u32[]{:S(2)}, u32[]{:S(2)}) collective-permute-start(bf16[72,768]{1,0:T(8,128)(2,1)S(1)} %get-tuple-element.41), channel_id=1, source_target_pairs={{0,1},{1,0},{2,3},{3,2},{4,5},{5,4},{6,7},{7,6},{8,9},{9,8},{10,11... | collective-permute-start | bytes 331784 | tf_op jit(solution)/shard_map/ppermute | solution.py:411
  29.1 20.6 %copy-start.2 = (bf16[768,1536]{1,0:T(8,128)(2,1)S(1)}, bf16[768,1536]{1,0:T(8,128)(2,1)}, u32[]{:S(2)}) copy-start(bf16[768,1536]{1,0:T(8,128)(2,1)} %gate_weight.1) | copy-start | bytes 7077892
  29.2 4.7 %collective-permute-start.10 = (bf16[72,768]{1,0:T(8,128)(2,1)S(1)}, bf16[72,768]{1,0:T(8,128)(2,1)S(1)}, u32[]{:S(2)}, u32[]{:S(2)}) collective-permute-start(bf16[72,768]{1,0:T(8,128)(2,1)S(1)} %get-tuple-element.43), channel_id=1, source_target_pairs={{0,2},{2,0},{4,6},{6,4},{8,10},{10,8},{12,14},{14,12},{1,3},{3,1},... | collective-permute-start | bytes 331784 | tf_op jit(solution)/shard_map/ppermute | solution.py:411
  29.4 6.0 %collective-permute-start.11 = (bf16[72,768]{1,0:T(8,128)(2,1)S(1)}, bf16[72,768]{1,0:T(8,128)(2,1)S(1)}, u32[]{:S(2)}, u32[]{:S(2)}) collective-permute-start(bf16[72,768]{1,0:T(8,128)(2,1)S(1)} %get-tuple-element.43), channel_id=1, source_target_pairs={{0,4},{2,6},{4,0},{6,2},{8,12},{10,14},{12,8},{14,10},{1,5},{3,7},... | collective-permute-start | bytes 331784 | tf_op jit(solution)/shard_map/ppermute | solution.py:411
  32.3 5.0 %collective-permute-start.12 = (bf16[72,768]{1,0:T(8,128)(2,1)S(1)}, bf16[72,768]{1,0:T(8,128)(2,1)S(1)}, u32[]{:S(2)}, u32[]{:S(2)}) collective-permute-start(bf16[72,768]{1,0:T(8,128)(2,1)S(1)} %get-tuple-element.43), channel_id=1, source_target_pairs={{0,6},{2,4},{4,2},{6,0},{8,14},{10,12},{12,10},{14,8},{1,7},{3,5},... | collective-permute-start | bytes 331784 | tf_op jit(solution)/shard_map/ppermute | solution.py:411
  37.5 8.0 %collective-permute-start.13 = (bf16[72,768]{1,0:T(8,128)(2,1)S(1)}, bf16[72,768]{1,0:T(8,128)(2,1)S(1)}, u32[]{:S(2)}, u32[]{:S(2)}) collective-permute-start(bf16[72,768]{1,0:T(8,128)(2,1)S(1)} %get-tuple-element.46), channel_id=1, source_target_pairs={{0,8},{2,10},{4,12},{6,14},{8,0},{10,2},{12,4},{14,6},{1,9},{3,11}... | collective-permute-start | bytes 331784 | tf_op jit(solution)/shard_map/ppermute | solution.py:411
  45.6 6.5 %collective-permute-start.14 = (bf16[64,768]{1,0:T(8,128)(2,1)S(1)}, bf16[64,768]{1,0:T(8,128)(2,1)S(1)}, u32[]{:S(2)}, u32[]{:S(2)}) collective-permute-start(bf16[64,768]{1,0:T(8,128)(2,1)S(1)} %get-tuple-element.47), channel_id=1, source_target_pairs={{0,1},{1,0},{2,3},{3,2},{4,5},{5,4},{6,7},{7,6},{8,9},{9,8},{10,11... | collective-permute-start | bytes 294920 | tf_op jit(solution)/shard_map/ppermute | solution.py:411
  49.7 1.7 %copy-start.1 = (bf16[1536,768]{1,0:T(8,128)(2,1)S(1)}, bf16[1536,768]{1,0:T(8,128)(2,1)}, u32[]{:S(2)}) copy-start(bf16[1536,768]{1,0:T(8,128)(2,1)} %out_weight.3) | copy-start | bytes 7077892

commit v5 on v4

--- a/solution.py
+++ b/solution.py
@@ -78,47 +78,114 @@
     return lax.dot_general(pick, values, (((1,), (1,)), ((), ())), preferred_element_type=F32)
 
 
-def embed_kernel(*refs):
-    blocks, (weight, bias, out, picked, tail, wide) = refs[:-6], refs[-6:]
+def window_pixel(offset):
+    place = offset - MARGIN + PATCH
+    return place % PATCH, place // PATCH - 1
+
+
+def neighbours():
+    return [offset for offset in range(KERNEL) if window_pixel(offset)[1]]
+
+
+def place_tokens(pick, values, first, wide, beside):
+    found = turned(pick, values).reshape(PATCH, 16, 128)
+    rounded = found.astype(BF16)
+    for offset in range(KERNEL):
+        pixel, shift = window_pixel(offset)
+        if shift == 0:
+            wide[pl.ds(first, 16), offset * 128 : (offset + 1) * 128] = rounded[pixel]
+    for slot, offset in enumerate(neighbours()):
+        beside[slot, pl.ds(pl.multiple_of(LEAD + first, 8), 16), :] = found[window_pixel(offset)[0]]
+
+
+def place_beside(count, first, wide, beside):
+    for slot, offset in enumerate(neighbours()):
+        start = LEAD + window_pixel(offset)[1]
+        part = beside[slot, start : start + count, :]
+        wide[first : first + count, offset * 128 : (offset + 1) * 128] = part.astype(BF16)
+
+
+def clear_ends(count, beside):
+    zeros = jnp.zeros((beside.shape[0], LEAD, 128), F32)
+    beside[:, 0:LEAD, :] = zeros
+    beside[:, LEAD + count : LEAD + count + LEAD, :] = zeros
+
+
+def windows_of(block, row, lanes):
+    window = pl.ds(pl.multiple_of(2 * KERNEL * row, 16), WIN)
+    values = block[window, lanes]
+    return jnp.concatenate([values, jnp.zeros((128 - WIN, values.shape[1]), BF16)], axis=0)
+
+
+def own_kernel(*refs):
+    blocks, (weight, bias, out, wide, beside) = refs[:-5], refs[-5:]
     col, row = lax.axis_index("cols"), lax.axis_index("rows")
+    side = len(blocks)
     width = blocks[0].shape[1]
+    tokens = side * width // PATCH
+    pick = pick_matrix()
+    clear_ends(tokens, beside)
+    for step, block in enumerate(blocks):
+        for group in range(width // 256):
+            first = pl.multiple_of(((col % side) ^ step) * (width // PATCH) + 16 * group, 16)
+            values = windows_of(block, row, slice(256 * group, 256 * (group + 1)))
+            place_tokens(pick, values, first, wide, beside)
+    place_beside(tokens, 0, wide, beside)
+    grid = jnp.dot(wide[...], weight[...], preferred_element_type=F32)
+    out[...] = (grid + bias[...]).astype(BF16)
+
+
+def rest_of_row_kernel(*refs):
+    blocks, (weight, bias, own, out, wide, beside, tail) = refs[:-7], refs[-7:]
+    col, row = lax.axis_index("cols"), lax.axis_index("rows")
     count = len(blocks)
     side = count // 2
-    tokens = count * width // PATCH
-    local = width // PATCH
-    zeros = jnp.zeros((PATCH, LEAD, 128), F32)
-    picked[:, 0:LEAD, :] = zeros
-    picked[:, LEAD + tokens :, :] = zeros
-    blank = jnp.zeros((128 - WIN, width), BF16)
+    width = blocks[0].shape[1]
+    tokens = side * width // PATCH
+    reach = tokens + 16
     pick = pick_matrix()
-    window = pl.ds(pl.multiple_of(2 * KERNEL * row, 16), WIN)
+    clear_ends(reach, beside)
+    lower = row == 0
+    for step, block in enumerate(blocks[side:]):
+        for group in range(width // 256):
+            place = ((col % side) ^ step) * (width // PATCH) + 16 * group + 16 * (1 - row)
+            values = windows_of(block, row, slice(256 * group, 256 * (group + 1)))
+            place_tokens(pick, values, pl.multiple_of(place, 16), wide, beside)
+    middle = jnp.zeros((128, 256), F32)
+    for step, block in enumerate(blocks[:side]):
+        here = ((col % side) ^ step) == jnp.where(lower, side - 1, 0)
+        values = jnp.where(
+            lower, windows_of(block, row, slice(width - 256, width)).astype(F32),
+            windows_of(block, row, slice(0, 256)).astype(F32),
+        )
+        middle = jnp.where(here, values, middle)
+    place_tokens(pick, middle.astype(BF16), pl.multiple_of(tokens * row, 16), wide, beside)
+    place_beside(reach, 0, wide, beside)
     edge = jnp.zeros((WIN, 128), F32)
     extra = jnp.zeros((8, 128 * CHAN), F32)
     for place, block in enumerate(blocks):
         source = side * (row if place < side else 1 - row) + ((col % side) ^ (place % side))
-        values = jnp.concatenate([block[window, :], blank], axis=0)
-        for group in range(width // 256):
-            found = turned(pick, values[:, 256 * group : 256 * (group + 1)])
-            first = pl.multiple_of(LEAD + source * local + 16 * group, 8)
-            picked[:, pl.ds(first, 16), :] = found.reshape(PATCH, 16, 128)
         last = source == count - 1
         edge = jnp.where(last, block[0:WIN, width - 128 :].astype(F32), edge)
         extra = jnp.where(last, block[5 * KERNEL - 8 : 5 * KERNEL + 8, : 128 * CHAN].astype(F32)[8:], extra)
     before = [extra[:, 64 * piece : 64 * (piece + 1)] for piece in range(2 * CHAN)] + [edge[:KERNEL, 64:]]
-    last = jnp.where(row == 0, jnp.concatenate(before, axis=0), edge[:, 64:])
+    last = jnp.where(lower, jnp.concatenate(before, axis=0), edge[:, 64:])
     last = jnp.concatenate([last, jnp.zeros((128 - WIN, 64), F32)], axis=0)
     last = jnp.concatenate([jnp.zeros((128, 64), F32), last, jnp.zeros((128, 128), F32)], axis=1)
-    tail[:, 0:8, :] = zeros
+    tail[:, 0:8, :] = jnp.zeros((PATCH, 8, 128), F32)
     tail[:, 8:24, :] = turned(pick, last.astype(BF16)).reshape(PATCH, 16, 128)
-
     for offset in range(KERNEL):
-        place = offset - MARGIN + PATCH
-        shift, pixel = place // PATCH - 1, place % PATCH
-        ahead = tail[pixel, 8 + shift : 16 + shift, :]
-        part = jnp.concatenate([ahead, picked[pixel, LEAD + shift : LEAD + shift + tokens, :]], axis=0)
-        wide[:, offset * 128 : (offset + 1) * 128] = part.astype(BF16)
-    grid = jnp.dot(wide[...], weight[...], preferred_element_type=F32)
-    out[...] = (grid + bias[...]).astype(BF16)
+        pixel, shift = window_pixel(offset)
+        part = tail[pixel, 8 + shift : 16 + shift, :]
+        wide[reach:, offset * 128 : (offset + 1) * 128] = part.astype(BF16)
+    grid = jnp.dot(wide[...], weight[...], preferred_element_type=F32) + bias[...]
+    near, far = pl.ds(pl.multiple_of(tokens * row, 16), tokens), pl.ds(pl.multiple_of(tokens * (1 - row), 16), tokens)
+    spot = lax.broadcasted_iota(jnp.int32, own.shape, 0)
+    midway = jnp.where(lower, grid[15:16], grid[tokens : tokens + 1])
+    here = spot == jnp.where(lower, tokens - 1, 0)
+    out[near, :] = jnp.where(here, midway, own[...].astype(F32)).astype(BF16)
+    out[far, :] = jnp.where(lower, grid[16:reach], grid[:tokens]).astype(BF16)
+    out[2 * tokens :, :] = grid[reach:].astype(BF16)
 
 
 def spread_matrix():
@@ -179,7 +246,7 @@
     total = weight[0:1] * raw
     for tap in range(1, weight.shape[0]):
         total = pltpu.roll(total, 1, 0) + weight[tap : tap + 1] * raw
-    return silu(total[LEAD:] + bias).astype(BF16)
+    return silu(total[:-LEAD] + bias).astype(BF16)
 
 
 def mix_kernel(
@@ -191,14 +258,14 @@
     mean_sq = jnp.mean(resid * resid, axis=-1, keepdims=True)
     normed_f = resid * lax.rsqrt(mean_sq + 1e-05) * norm_gain[...]
     rows = lax.broadcasted_iota(jnp.int32, normed_f.shape, 0)
-    blank = (rows < LEAD) & (col == 0) & (row == 0)
+    blank = (rows >= embedded.shape[0] - LEAD) & (col == 0) & (row == 0)
     normed = jnp.where(blank, 0.0, normed_f).astype(BF16)
     normed_out[...] = normed
     length = embedded.shape[0] - LEAD
     maps_raw = project(normed, mix_weight, slice(E, E + 2 * NSTATE))
     step_raw = lax.dot_general(
         normed, step_weight[...], (((1,), (1,)), ((), ())), preferred_element_type=F32
-    )[LEAD:]
+    )[:-LEAD]
     step = softplus(step_raw + step_bias[...])
     log_decay = -step * jnp.exp(log_rate[...])
     lower = (
@@ -328,7 +395,7 @@
 
 
 def gate_kernel(normed, gate_weight, local_mine, local_theirs, cum, own_out, factor_out):
-    gate = jnp.dot(normed[...], gate_weight[...], preferred_element_type=F32)[LEAD:].astype(BF16).astype(F32)
+    gate = jnp.dot(normed[...], gate_weight[...], preferred_element_type=F32)[:-LEAD].astype(BF16).astype(F32)
     gate = silu(gate)
     half = local_mine.shape[1]
     upper = lax.axis_index("rows") == 1
@@ -404,7 +471,7 @@
     )
     mean_sq = (squares[:, 0:1] + more) / own.shape[1]
     result = (product[...] + rest) * lax.rsqrt(mean_sq + 1e-05)
-    out[...] = (result + embedded[...].astype(F32)[LEAD:]).astype(BF16)
+    out[...] = (result + embedded[...].astype(F32)[:-LEAD]).astype(BF16)
 
 
 def swap(block, axis, bit):
@@ -438,19 +505,24 @@
     for step in sending_order(side):
         near[step] = across(blocks[step], step)
         far[step] = swap(near[step], "rows", 1)
-    came = near + far
     weight = patch_weight.reshape(3, 8, KERNEL, CHAN, D).transpose(2, 0, 3, 1, 4).reshape(KERNEL, WIN, D)
     weight = jnp.pad(weight, ((0, 0), (0, 128 - WIN), (0, 0))).reshape(KERNEL * 128, D)
     tokens = col_count * width // PATCH
-    scratch = [
-        pltpu.VMEM((PATCH, 2 * LEAD + tokens, 128), F32),
-        pltpu.VMEM((PATCH, 24, 128), F32),
-        pltpu.VMEM((LEAD + tokens, KERNEL * 128), BF16),
-    ]
-    flops = 2 * tokens * KERNEL * 128 * D
+    half = tokens // 2
+    line = patch_bias.reshape(1, -1)
+    slots = len(neighbours())
+
+    def scratch(rows, reach):
+        return [pltpu.VMEM((rows, KERNEL * 128), BF16), pltpu.VMEM((slots, reach + 2 * LEAD, 128), F32)]
+
+    own = call(
+        own_kernel, (*near, weight, line), shape((half, D)), scratch(half, half),
+        flops=tokens * KERNEL * 128 * D, moved=6 << 20, limit=16,
+    )
     return call(
-        embed_kernel, (*came, weight, patch_bias.reshape(1, -1)), shape((LEAD + tokens, D)), scratch,
-        flops=flops, moved=6 << 20, limit=16,
+        rest_of_row_kernel, (*near, *far, weight, line, own), shape((tokens + LEAD, D)),
+        [*scratch(half + 16 + LEAD, half + 16), pltpu.VMEM((PATCH, 24, 128), F32)],
+        flops=tokens * KERNEL * 128 * D, moved=6 << 20, limit=16,
     )
 
 
@@ -504,7 +576,7 @@
     )
     tokens = landed.transpose(1, 0, 2).reshape(row_local * col_local, feature_width)
     tail = shifted(tokens[tokens.shape[0] - LEAD :], ("cols", "rows"), 1)
-    return jnp.concatenate([tail, tokens], axis=0)
+    return jnp.concatenate([tokens, tail], axis=0)
 
 
 def body(

time: 53.7 us -> 54.9 us (1.022)
  Pallas kernels: 15.2 us -> 16.3 us
    pallas_call x13 -> x14, Pallas kernels: 15.2 us -> 16.3 us  [call(): pl.pallas_call(kernel, out_shape=outs, in_specs=[pl.BlockSpec(memory_spac...]
  transfers between devices with their start and end apart: 15 -> 15, of which waited for: 7 -> 7; matrix products, arithmetic and copies ran while one was open for 5% -> 5% of each run, Pallas kernels for 16% -> 19%
where the time goes in v5:
time: 54.9 us; the launch traced here: 54.6 us
  starting transfers between devices  18.9 us (34%)
  Pallas kernels  16.3 us (30%)
  waiting for transfers between devices  14.9 us (27%)
  local copies, waits for them, and re-layouts  4.15 us (8%)
    pallas_call x14, Pallas kernels, call(): pl.pallas_call(kernel, out_shape=outs, in_specs=[pl.BlockSpec(memory_spac...  16.3 us
    ppermute x4, starting transfers between devices, across(): return lax.ppermute(block, ('cols', 'rows'), pairs)  10.3 us
    ppermute x11, starting transfers between devices, swap(): lax.ppermute(block, axis, [(i, i ^ bit) for i in range(lax.axis_size(axis...  8.64 us
    ppermute x11, waiting for transfers between devices, swap(): lax.ppermute(block, axis, [(i, i ^ bit) for i in range(lax.axis_size(axis...  8.24 us
    ppermute x4, waiting for transfers between devices, across(): return lax.ppermute(block, ('cols', 'rows'), pairs)  6.67 us
    transpose x1, local copies, waits for them, and re-layouts, embed_by_rows(): patch_weight.reshape(3, 8, KERNEL, CHAN, D).transpose(2, 0, 3, 1, 4)  2.29 us
    unnamed x26, local copies, waits for them, and re-layouts  1.32 us
  transfers between devices with their start and end apart: 15, of which 7 were waited for; matrix products, arithmetic and copies ran while one was open for 5% of the time, Pallas kernels for 19%

profile of v5, /device:TPU:1, one launch (start us, length us, event | category | flops | bytes accessed | tf_op | source)
XLA Modules:
  0.0 54.6 jit_solution(16903869339447937499)
XLA Ops:
  0.0 1.0 %copy-done.3 = bf16[3,128,512]{2,1,0:T(8,128)(2,1)S(1)} copy-done((bf16[3,128,512]{2,1,0:T(8,128)(2,1)S(1)}, bf16[3,128,512]{2,1,0:T(8,128)(2,1)}, u32[]{:S(2)}) %copy-start.3) | copy-done | bytes 393240
  1.0 0.9 %collective-permute-done.partner = bf16[3,128,512]{2,1,0:T(8,128)(2,1)S(1)} collective-permute-done((bf16[3,128,512]{2,1,0:T(8,128)(2,1)}, bf16[3,128,512]{2,1,0:T(8,128)(2,1)S(1)}, u32[]{:S(2)}, u32[]{:S(2)}) %collective-permute-start) | collective-permute-done | bytes 393248 | tf_op jit(solution)/shard_map/ppermute | solution.py:478
  1.9 0.2 shard_map.137
  2.2 5.6 %collective-permute-start.1 = (bf16[128,512]{1,0:T(8,128)(2,1)S(1)}, bf16[128,512]{1,0:T(8,128)(2,1)S(1)}, u32[]{:S(2)}, u32[]{:S(2)}) collective-permute-start(bf16[128,512]{1,0:T(8,128)(2,1)S(1)} %get-tuple-element.32), channel_id=1, source_target_pairs={{0,0},{1,8},{2,2},{3,10},{4,4},{5,12},{6,6},{7,14},{8,1},{9,9},{10... | collective-permute-start | bytes 393224 | tf_op jit(solution)/shard_map/ppermute | solution.py:492
  7.8 1.1 %collective-permute-start.2 = (bf16[128,512]{1,0:T(8,128)(2,1)S(1)}, bf16[128,512]{1,0:T(8,128)(2,1)S(1)}, u32[]{:S(2)}, u32[]{:S(2)}) collective-permute-start(bf16[128,512]{1,0:T(8,128)(2,1)S(1)} %get-tuple-element.33), channel_id=1, source_target_pairs={{0,2},{1,10},{2,0},{3,8},{4,6},{5,14},{6,4},{7,12},{8,3},{9,11},{1... | collective-permute-start | bytes 393224 | tf_op jit(solution)/shard_map/ppermute | solution.py:492
  8.9 3.6 %collective-permute-start.3 = (bf16[128,512]{1,0:T(8,128)(2,1)S(1)}, bf16[128,512]{1,0:T(8,128)(2,1)S(1)}, u32[]{:S(2)}, u32[]{:S(2)}) collective-permute-start(bf16[128,512]{1,0:T(8,128)(2,1)S(1)} %get-tuple-element.34), channel_id=1, source_target_pairs={{0,4},{1,12},{2,6},{3,14},{4,0},{5,8},{6,2},{7,10},{8,5},{9,13},{1... | collective-permute-start | bytes 393224 | tf_op jit(solution)/shard_map/ppermute | solution.py:492
  12.5 4.6 %collective-permute-done.2.refs_1_ = bf16[128,512]{1,0:T(8,128)(2,1)S(1)} collective-permute-done((bf16[128,512]{1,0:T(8,128)(2,1)S(1)}, bf16[128,512]{1,0:T(8,128)(2,1)S(1)}, u32[]{:S(2)}, u32[]{:S(2)}) %collective-permute-start.2) | collective-permute-done | bytes 131104 | tf_op jit(solution)/shard_map/ppermute | solution.py:492
  17.0 0.5 collective-permute-start.7
  17.6 2.1 %collective-permute-done.4.refs_3_ = bf16[128,512]{1,0:T(8,128)(2,1)S(1)} collective-permute-done((bf16[128,512]{1,0:T(8,128)(2,1)S(1)}, bf16[128,512]{1,0:T(8,128)(2,1)S(1)}, u32[]{:S(2)}, u32[]{:S(2)}) %collective-permute-start.4) | collective-permute-done | bytes 131104 | tf_op jit(solution)/shard_map/ppermute | solution.py:492
  19.6 2.3 %copy.15 = bf16[24,3,3,8,768]{4,3,2,1,0:T(8,128)(2,1)S(1)} copy(bf16[24,3,3,8,768]{4,0,2,3,1:T(8,128)(2,1)} %bitcast.14) | data formatting | bytes 5308416 | tf_op jit(solution)/shard_map/transpose | solution.py:508
  22.0 0.5 pad.4
  22.5 1.6 %shard_map.138.refs_10_ = bf16[128,768]{1,0:T(8,128)(2,1)S(1)} custom-call(bf16[128,512]{1,0:T(8,128)(2,1)S(1)} %collective-permute-done.1.refs_0_, bf16[128,512]{1,0:T(8,128)(2,1)S(1)} %collective-permute-done.2.refs_1_, bf16[128,512]{1,0:T(8,128)(2,1)S(1)} %collective-permute-done.3.refs_2_, bf16[128,512]{1,0:T(8,128)(2,1)S(1)} %collective-permute-done.4.refs_3_, ...), custom_call_target="tpu_custom_call" | custom-call | flops 603979776 | bytes 6291456 | tf_op jit(solution)/shard_map/pallas_call | solution.py:31
  24.3 1.9 %shard_map.139.embedded = bf16[264,768]{1,0:T(8,128)(2,1)S(1)} custom-call(bf16[128,512]{1,0:T(8,128)(2,1)S(1)} %collective-permute-done.1.refs_0_, bf16[128,512]{1,0:T(8,128)(2,1)S(1)} %collective-permute-done.2.refs_1_, bf16[128,512]{1,0:T(8,128)(2,1)S(1)} %collective-permute-done.3.refs_2_, bf16[128,512]{1,0:T(8,128)(2,1)S(1)} %collective-permute-done.4.refs_3_, ...), custom_call_target="tpu_custom_call" | custom-call | flops 603979776 | bytes 6291456 | tf_op jit(solution)/shard_map/pallas_call | solution.py:31
  26.2 2.0 %shard_map.140 = (bf16[264,768]{1,0:T(8,128)(2,1)S(1)}, bf16[256,768]{1,0:T(8,128)(2,1)S(1)}, bf16[256,64]{1,0:T(8,128)(2,1)S(1)}, bf16[256,64]{1,0:T(8,128)(2,1...) custom-call(bf16[264,768]{1,0:T(8,128)(2,1)S(1)} %shard_map.139.embe, ...), custom_call_target="tpu_custom_call" | custom-call | flops 327155712 | bytes 4194304 | tf_op jit(solution)/shard_map/pallas_call | solution.py:31
  28.2 0.6 %collective-permute-start.9 = (bf16[72,768]{1,0:T(8,128)(2,1)S(1)}, bf16[72,768]{1,0:T(8,128)(2,1)S(1)}, u32[]{:S(2)}, u32[]{:S(2)}) collective-permute-start(bf16[72,768]{1,0:T(8,128)(2,1)S(1)} %get-tuple-element.41), channel_id=1, source_target_pairs={{0,1},{1,0},{2,3},{3,2},{4,5},{5,4},{6,7},{7,6},{8,9},{9,8},{10,11... | collective-permute-start | bytes 331784 | tf_op jit(solution)/shard_map/ppermute | solution.py:478
  28.8 1.4 %shard_map.141 = (bf16[256,768]{1,0:T(8,128)(2,1)S(1)}, f32[72,768]{1,0:T(8,128)S(1)}) custom-call(bf16[264,768]{1,0:T(8,128)(2,1)S(1)} %get-tuple-element.36.normed, bf16[256,24]{1,0:T(8,128)(2,1)S(1)} %get-tuple-element.37.scales, bf16[64,256]{1,0:T(8,128)(2,1)S(1)} %get-tuple-element.38.b_t, bf16[768,1664]{1,0:T(8,128)(2,1)S(1)} %copy-done, ...), custom_call_target="tpu_custom_call" | custom-call | flops 327155712 | bytes 4194304 | tf_op jit(solution)/shard_map/pallas_call | solution.py:31
  30.3 0.2 collective-permute-start.10
  30.5 2.9 %collective-permute-start.11 = (bf16[72,768]{1,0:T(8,128)(2,1)S(1)}, bf16[72,768]{1,0:T(8,128)(2,1)S(1)}, u32[]{:S(2)}, u32[]{:S(2)}) collective-permute-start(bf16[72,768]{1,0:T(8,128)(2,1)S(1)} %get-tuple-element.43), channel_id=1, source_target_pairs={{0,4},{2,6},{4,0},{6,2},{8,12},{10,14},{12,8},{14,10},{1,5},{3,7},... | collective-permute-start | bytes 331784 | tf_op jit(solution)/shard_map/ppermute | solution.py:478
  33.5 1.5 %collective-permute-done.10.refs_1_ = bf16[72,768]{1,0:T(8,128)(2,1)S(1)} collective-permute-done((bf16[72,768]{1,0:T(8,128)(2,1)S(1)}, bf16[72,768]{1,0:T(8,128)(2,1)S(1)}, u32[]{:S(2)}, u32[]{:S(2)}) %collective-permute-start.10) | collective-permute-done | bytes 110624 | tf_op jit(solution)/shard_map/ppermute | solution.py:478
  35.0 1.6 %collective-permute-done.11.refs_2_ = bf16[72,768]{1,0:T(8,128)(2,1)S(1)} collective-permute-done((bf16[72,768]{1,0:T(8,128)(2,1)S(1)}, bf16[72,768]{1,0:T(8,128)(2,1)S(1)}, u32[]{:S(2)}, u32[]{:S(2)}) %collective-permute-start.11) | collective-permute-done | bytes 110624 | tf_op jit(solution)/shard_map/ppermute | solution.py:478
  36.6 1.9 %collective-permute-done.12.refs_3_ = bf16[72,768]{1,0:T(8,128)(2,1)S(1)} collective-permute-done((bf16[72,768]{1,0:T(8,128)(2,1)S(1)}, bf16[72,768]{1,0:T(8,128)(2,1)S(1)}, u32[]{:S(2)}, u32[]{:S(2)}) %collective-permute-start.12) | collective-permute-done | bytes 110624 | tf_op jit(solution)/shard_map/ppermute | solution.py:478
  38.5 0.2 shard_map.143
  38.6 3.0 %collective-permute-start.13 = (bf16[72,768]{1,0:T(8,128)(2,1)S(1)}, bf16[72,768]{1,0:T(8,128)(2,1)S(1)}, u32[]{:S(2)}, u32[]{:S(2)}) collective-permute-start(bf16[72,768]{1,0:T(8,128)(2,1)S(1)} %get-tuple-element.46), channel_id=1, source_target_pairs={{0,8},{2,10},{4,12},{6,14},{8,0},{10,2},{12,4},{14,6},{1,9},{3,11}... | collective-permute-start | bytes 331784 | tf_op jit(solution)/shard_map/ppermute | solution.py:478
  41.6 2.6 %shard_map.146.local_theirs = f32[256,768]{1,0:T(8,128)S(1)} custom-call(f32[24]{0:T(128)S(1)} %copy-done.6, bf16[256,768]{1,0:T(8,128)(2,1)S(1)} %get-tuple-element.53.x, bf16[256,64]{1,0:T(8,128)(2,1)S(1)} %get-tuple-element.49.b_mat, bf16[256,64]{1,0:T(8,128)(2,1)S(1)} %get-tuple-element.50.c_mat, f32[256,24]{1,0:T(8,128)S(1)} %get-tuple-element.51.step, ...), custom_call_target="tpu_custom_call" | custom-call | flops 201326592 | bytes 2097152 | tf_op jit(solution)/shard_map/pallas_call | solution.py:31
  44.3 2.4 %collective-permute-done.13.refs_2_ = bf16[72,768]{1,0:T(8,128)(2,1)S(1)} collective-permute-done((bf16[72,768]{1,0:T(8,128)(2,1)S(1)}, bf16[72,768]{1,0:T(8,128)(2,1)S(1)}, u32[]{:S(2)}, u32[]{:S(2)}) %collective-permute-start.13) | collective-permute-done | bytes 110624 | tf_op jit(solution)/shard_map/ppermute | solution.py:478
  46.7 0.1 shard_map.144
  46.7 1.4 %collective-permute-start.14 = (bf16[64,768]{1,0:T(8,128)(2,1)S(1)}, bf16[64,768]{1,0:T(8,128)(2,1)S(1)}, u32[]{:S(2)}, u32[]{:S(2)}) collective-permute-start(bf16[64,768]{1,0:T(8,128)(2,1)S(1)} %get-tuple-element.47), channel_id=1, source_target_pairs={{0,1},{1,0},{2,3},{3,2},{4,5},{5,4},{6,7},{7,6},{8,9},{9,8},{10,11... | collective-permute-start | bytes 294920 | tf_op jit(solution)/shard_map/ppermute | solution.py:478
  48.2 2.7 %shard_map.145.local_mine = f32[256,768]{1,0:T(8,128)S(1)} custom-call(f32[24]{0:T(128)S(1)} %copy-done.6, bf16[256,768]{1,0:T(8,128)(2,1)S(1)} %get-tuple-element.48.x, bf16[256,64]{1,0:T(8,128)(2,1)S(1)} %get-tuple-element.49.b_mat, bf16[256,64]{1,0:T(8,128)(2,1)S(1)} %get-tuple-element.50.c_mat, f32[256,24]{1,0:T(8,128)S(1)} %get-tuple-element.51.step, ...), custom_call_target="tpu_custom_call" | custom-call | flops 201326592 | bytes 2097152 | tf_op jit(solution)/shard_map/pallas_call | solution.py:31
  50.9 1.4 %shard_map.147 = (f32[256,1536]{1,0:T(8,128)S(1)}, f32[256,1536]{1,0:T(8,128)S(1)}) custom-call(bf16[264,768]{1,0:T(8,128)(2,1)S(1)} %get-tuple-element.36.normed, bf16[768,1536]{1,0:T(8,128)(2,1)S(1)} %copy-done.2, f32[256,768]{1,0:T(8,128)S(1)} %shard_map.145.local_mine, f32[256,768]{1,0:T(8,128)S(1)} %shard_map.146.local_theirs, ...), custom_call_target="tpu_custom_call" | custom-call | flops 603979776 | bytes 4194304 | tf_op jit(solution)/shard_map/pallas_call | solution.py:31
  52.2 0.3 copy-done.1
  52.5 0.7 %shard_map.148 = (f32[256,768]{1,0:T(8,128)S(1)}, f32[256,128]{1,0:T(8,128)S(1)}) custom-call(bf16[64,768]{1,0:T(8,128)(2,1)S(1)} %get-tuple-element.56.mine, f32[256,1536]{1,0:T(8,128)S(1)} %get-tuple-element.54.own, f32[256,1536]{1,0:T(8,128)S(1)} %get-tuple-element.55.factor, bf16[256,64]{1,0:T(8,128)(2,1)S(1)} %get-tuple-element.50.c_mat, ...), custom_call_target="tpu_custom_call" | custom-call | flops 301989888 | bytes 4194304 | tf_op jit(solution)/shard_map/pallas_call | solution.py:31
  53.2 1.4 %shard_map.149 = bf16[256,768]{1,0:T(8,128)(2,1)} custom-call(bf16[64,768]{1,0:T(8,128)(2,1)S(1)} %collective-permute-done.14.theirs, f32[256,1536]{1,0:T(8,128)S(1)} %get-tuple-element.54.own, f32[256,1536]{1,0:T(8,128)S(1)} %get-tuple-element.55.factor, bf16[256,64]{1,0:T(8,128)(2,1)S(1)} %get-tuple-element.50.c_mat, f32[1,1536]{1,0:T(1,128)S(1)} %reshape.35.out_gain, ...), custom_call_target="tpu_custom_call" | custom-call | flops 301989888 | bytes 4194304 | tf_op jit(solution)/shard_map/pallas_call | solution.py:31
  (44 shorter events, 0.2 us)
Async XLA Ops:
  0.0 1.9 %collective-permute-start = (bf16[3,128,512]{2,1,0:T(8,128)(2,1)}, bf16[3,128,512]{2,1,0:T(8,128)(2,1)S(1)}, u32[]{:S(2)}, u32[]{:S(2)}) collective-permute-start(bf16[3,128,512]{2,1,0:T(8,128)(2,1)} %pixels.1), channel_id=1, source_target_pairs={{0,1},{1,0},{2,3},{3,2},{4,5},{5,4},{6,7},{7,6},{8,9},{9,8},{10,11... | collective-permute-start | bytes 1179656 | tf_op jit(solution)/shard_map/ppermute | solution.py:478
  0.0 1.0 %copy-start.3 = (bf16[3,128,512]{2,1,0:T(8,128)(2,1)S(1)}, bf16[3,128,512]{2,1,0:T(8,128)(2,1)}, u32[]{:S(2)}) copy-start(bf16[3,128,512]{2,1,0:T(8,128)(2,1)} %pixels.1) | copy-start | bytes 1179652
  2.2 10.3 %collective-permute-start.1 = (bf16[128,512]{1,0:T(8,128)(2,1)S(1)}, bf16[128,512]{1,0:T(8,128)(2,1)S(1)}, u32[]{:S(2)}, u32[]{:S(2)}) collective-permute-start(bf16[128,512]{1,0:T(8,128)(2,1)S(1)} %get-tuple-element.32), channel_id=1, source_target_pairs={{0,0},{1,8},{2,2},{3,10},{4,4},{5,12},{6,6},{7,14},{8,1},{9,9},{10... | collective-permute-start | bytes 393224 | tf_op jit(solution)/shard_map/ppermute | solution.py:492
  7.8 9.3 %collective-permute-start.2 = (bf16[128,512]{1,0:T(8,128)(2,1)S(1)}, bf16[128,512]{1,0:T(8,128)(2,1)S(1)}, u32[]{:S(2)}, u32[]{:S(2)}) collective-permute-start(bf16[128,512]{1,0:T(8,128)(2,1)S(1)} %get-tuple-element.33), channel_id=1, source_target_pairs={{0,2},{1,10},{2,0},{3,8},{4,6},{5,14},{6,4},{7,12},{8,3},{9,11},{1... | collective-permute-start | bytes 393224 | tf_op jit(solution)/shard_map/ppermute | solution.py:492
  8.9 8.2 %collective-permute-start.3 = (bf16[128,512]{1,0:T(8,128)(2,1)S(1)}, bf16[128,512]{1,0:T(8,128)(2,1)S(1)}, u32[]{:S(2)}, u32[]{:S(2)}) collective-permute-start(bf16[128,512]{1,0:T(8,128)(2,1)S(1)} %get-tuple-element.34), channel_id=1, source_target_pairs={{0,4},{1,12},{2,6},{3,14},{4,0},{5,8},{6,2},{7,10},{8,5},{9,13},{1... | collective-permute-start | bytes 393224 | tf_op jit(solution)/shard_map/ppermute | solution.py:492
  12.4 7.2 %collective-permute-start.4 = (bf16[128,512]{1,0:T(8,128)(2,1)S(1)}, bf16[128,512]{1,0:T(8,128)(2,1)S(1)}, u32[]{:S(2)}, u32[]{:S(2)}) collective-permute-start(bf16[128,512]{1,0:T(8,128)(2,1)S(1)} %get-tuple-element.35), channel_id=1, source_target_pairs={{0,6},{1,14},{2,4},{3,12},{4,2},{5,10},{6,0},{7,8},{8,7},{9,15},{1... | collective-permute-start | bytes 393224 | tf_op jit(solution)/shard_map/ppermute | solution.py:492
  12.4 11.8 %collective-permute-start.5 = (bf16[128,512]{1,0:T(8,128)(2,1)S(1)}, bf16[128,512]{1,0:T(8,128)(2,1)S(1)}, u32[]{:S(2)}, u32[]{:S(2)}) collective-permute-start(bf16[128,512]{1,0:T(8,128)(2,1)S(1)} %collective-permute-done.1.refs_0_), channel_id=1, source_target_pairs={{0,1},{1,0},{2,3},{3,2},{4,5},{5,4},{6,7},{7,6},{8,9},{9,8},{10,11... | collective-permute-start | bytes 393224 | tf_op jit(solution)/shard_map/ppermute | solution.py:478
  17.0 7.2 %collective-permute-start.6 = (bf16[128,512]{1,0:T(8,128)(2,1)S(1)}, bf16[128,512]{1,0:T(8,128)(2,1)S(1)}, u32[]{:S(2)}, u32[]{:S(2)}) collective-permute-start(bf16[128,512]{1,0:T(8,128)(2,1)S(1)} %collective-permute-done.2.refs_1_), channel_id=1, source_target_pairs={{0,1},{1,0},{2,3},{3,2},{4,5},{5,4},{6,7},{7,6},{8,9},{9,8},{10,11... | collective-permute-start | bytes 393224 | tf_op jit(solution)/shard_map/ppermute | solution.py:478
  17.0 7.2 %collective-permute-start.7 = (bf16[128,512]{1,0:T(8,128)(2,1)S(1)}, bf16[128,512]{1,0:T(8,128)(2,1)S(1)}, u32[]{:S(2)}, u32[]{:S(2)}) collective-permute-start(bf16[128,512]{1,0:T(8,128)(2,1)S(1)} %collective-permute-done.3.refs_2_), channel_id=1, source_target_pairs={{0,1},{1,0},{2,3},{3,2},{4,5},{5,4},{6,7},{7,6},{8,9},{9,8},{10,11... | collective-permute-start | bytes 393224 | tf_op jit(solution)/shard_map/ppermute | solution.py:478
  19.6 4.6 %collective-permute-start.8 = (bf16[128,512]{1,0:T(8,128)(2,1)S(1)}, bf16[128,512]{1,0:T(8,128)(2,1)S(1)}, u32[]{:S(2)}, u32[]{:S(2)}) collective-permute-start(bf16[128,512]{1,0:T(8,128)(2,1)S(1)} %collective-permute-done.4.refs_3_), channel_id=1, source_target_pairs={{0,1},{1,0},{2,3},{3,2},{4,5},{5,4},{6,7},{7,6},{8,9},{9,8},{10,11... | collective-permute-start | bytes 393224 | tf_op jit(solution)/shard_map/ppermute | solution.py:478
  19.6 2.3 %copy-start.11 = (f32[768]{0:T(1024)S(1)}, f32[768]{0:T(1024)}, u32[]{:S(2)}) copy-start(f32[768]{0:T(1024)} %param.16) | copy-start | bytes 9220
  19.6 2.3 %copy-start.10 = (f32[1664]{0:T(1024)S(1)}, f32[1664]{0:T(1024)}, u32[]{:S(2)}) copy-start(f32[1664]{0:T(1024)} %param.24) | copy-start | bytes 19972
  19.6 2.4 %copy-start.12 = (f32[768]{0:T(1024)S(1)}, f32[768]{0:T(1024)}, u32[]{:S(2)}) copy-start(f32[768]{0:T(1024)} %param.17) | copy-start | bytes 9220
  24.2 2.0 %copy-start = (bf16[768,1664]{1,0:T(8,128)(2,1)S(1)}, bf16[768,1664]{1,0:T(8,128)(2,1)}, u32[]{:S(2)}) copy-start(bf16[768,1664]{1,0:T(8,128)(2,1)} %mix_weight.3) | copy-start | bytes 7667716
  24.2 2.0 %copy-start.4 = (f32[4,1664]{1,0:T(4,128)S(1)}, f32[4,1664]{1,0:T(4,128)}, u32[]{:S(2)}) copy-start(f32[4,1664]{1,0:T(4,128)} %conv_weight.3) | copy-start | bytes 79876
  24.2 2.0 %copy-start.5 = (bf16[768,24]{0,1:T(8,128)(2,1)S(1)}, bf16[768,24]{0,1:T(8,128)(2,1)}, u32[]{:S(2)}) copy-start(bf16[768,24]{0,1:T(8,128)(2,1)} %param.20) | copy-start | bytes 110596
  24.2 2.0 %copy-start.7 = (f32[24]{0:T(128)S(1)}, f32[24]{0:T(128)}, u32[]{:S(2)}) copy-start(f32[24]{0:T(128)} %param.21) | copy-start | bytes 292
  24.2 2.0 %copy-start.8 = (f32[24]{0:T(128)S(1)}, f32[24]{0:T(128)}, u32[]{:S(2)}) copy-start(f32[24]{0:T(128)} %param.22) | copy-start | bytes 292
  28.2 13.4 %copy-start.9 = (f32[1536]{0:T(1024)S(1)}, f32[1536]{0:T(1024)}, u32[]{:S(2)}) copy-start(f32[1536]{0:T(1024)} %param.26) | copy-start | bytes 18436
  28.2 13.4 %copy-start.6 = (f32[24]{0:T(128)S(1)}, f32[24]{0:T(128)}, u32[]{:S(2)}) copy-start(f32[24]{0:T(128)} %skip.3) | copy-start | bytes 292
  28.2 2.0 %collective-permute-start.9 = (bf16[72,768]{1,0:T(8,128)(2,1)S(1)}, bf16[72,768]{1,0:T(8,128)(2,1)S(1)}, u32[]{:S(2)}, u32[]{:S(2)}) collective-permute-start(bf16[72,768]{1,0:T(8,128)(2,1)S(1)} %get-tuple-element.41), channel_id=1, source_target_pairs={{0,1},{1,0},{2,3},{3,2},{4,5},{5,4},{6,7},{7,6},{8,9},{9,8},{10,11... | collective-permute-start | bytes 331784 | tf_op jit(solution)/shard_map/ppermute | solution.py:478
  30.2 20.6 %copy-start.2 = (bf16[768,1536]{1,0:T(8,128)(2,1)S(1)}, bf16[768,1536]{1,0:T(8,128)(2,1)}, u32[]{:S(2)}) copy-start(bf16[768,1536]{1,0:T(8,128)(2,1)} %gate_weight.1) | copy-start | bytes 7077892
  30.3 4.7 %collective-permute-start.10 = (bf16[72,768]{1,0:T(8,128)(2,1)S(1)}, bf16[72,768]{1,0:T(8,128)(2,1)S(1)}, u32[]{:S(2)}, u32[]{:S(2)}) collective-permute-start(bf16[72,768]{1,0:T(8,128)(2,1)S(1)} %get-tuple-element.43), channel_id=1, source_target_pairs={{0,2},{2,0},{4,6},{6,4},{8,10},{10,8},{12,14},{14,12},{1,3},{3,1},... | collective-permute-start | bytes 331784 | tf_op jit(solution)/shard_map/ppermute | solution.py:478
  30.5 6.1 %collective-permute-start.11 = (bf16[72,768]{1,0:T(8,128)(2,1)S(1)}, bf16[72,768]{1,0:T(8,128)(2,1)S(1)}, u32[]{:S(2)}, u32[]{:S(2)}) collective-permute-start(bf16[72,768]{1,0:T(8,128)(2,1)S(1)} %get-tuple-element.43), channel_id=1, source_target_pairs={{0,4},{2,6},{4,0},{6,2},{8,12},{10,14},{12,8},{14,10},{1,5},{3,7},... | collective-permute-start | bytes 331784 | tf_op jit(solution)/shard_map/ppermute | solution.py:478
  33.4 5.0 %collective-permute-start.12 = (bf16[72,768]{1,0:T(8,128)(2,1)S(1)}, bf16[72,768]{1,0:T(8,128)(2,1)S(1)}, u32[]{:S(2)}, u32[]{:S(2)}) collective-permute-start(bf16[72,768]{1,0:T(8,128)(2,1)S(1)} %get-tuple-element.43), channel_id=1, source_target_pairs={{0,6},{2,4},{4,2},{6,0},{8,14},{10,12},{12,10},{14,8},{1,7},{3,5},... | collective-permute-start | bytes 331784 | tf_op jit(solution)/shard_map/ppermute | solution.py:478
  38.6 8.0 %collective-permute-start.13 = (bf16[72,768]{1,0:T(8,128)(2,1)S(1)}, bf16[72,768]{1,0:T(8,128)(2,1)S(1)}, u32[]{:S(2)}, u32[]{:S(2)}) collective-permute-start(bf16[72,768]{1,0:T(8,128)(2,1)S(1)} %get-tuple-element.46), channel_id=1, source_target_pairs={{0,8},{2,10},{4,12},{6,14},{8,0},{10,2},{12,4},{14,6},{1,9},{3,11}... | collective-permute-start | bytes 331784 | tf_op jit(solution)/shard_map/ppermute | solution.py:478
  46.7 6.5 %collective-permute-start.14 = (bf16[64,768]{1,0:T(8,128)(2,1)S(1)}, bf16[64,768]{1,0:T(8,128)(2,1)S(1)}, u32[]{:S(2)}, u32[]{:S(2)}) collective-permute-start(bf16[64,768]{1,0:T(8,128)(2,1)S(1)} %get-tuple-element.47), channel_id=1, source_target_pairs={{0,1},{1,0},{2,3},{3,2},{4,5},{5,4},{6,7},{7,6},{8,9},{9,8},{10,11... | collective-permute-start | bytes 294920 | tf_op jit(solution)/shard_map/ppermute | solution.py:478
  50.8 1.7 %copy-start.1 = (bf16[1536,768]{1,0:T(8,128)(2,1)S(1)}, bf16[1536,768]{1,0:T(8,128)(2,1)}, u32[]{:S(2)}) copy-start(bf16[1536,768]{1,0:T(8,128)(2,1)} %out_weight.3) | copy-start | bytes 7077892

commit v6 on v4

--- a/solution.py
+++ b/solution.py
@@ -27,12 +27,12 @@
     return pl.BlockSpec(memory_space=pltpu.VMEM)
 
 
-def call(kernel, inputs, outs, scratch=(), limit=4, flops=0, moved=0, scalars=0):
+def call(kernel, inputs, outs, scratch=(), limit=4, flops=0, moved=0, scalars=0, outside=False):
     return pl.pallas_call(
         kernel,
         out_shape=outs,
         in_specs=[pl.BlockSpec(memory_space=pltpu.SMEM)] * scalars + [vmem()] * (len(inputs) - scalars),
-        out_specs=jax.tree.map(lambda _: vmem(), outs),
+        out_specs=jax.tree.map(lambda _: pl.BlockSpec(memory_space=pl.ANY) if outside else vmem(), outs),
         scratch_shapes=scratch,
         compiler_params=pltpu.CompilerParams(vmem_limit_bytes=limit << 20),
         cost_estimate=pl.CostEstimate(flops=flops, bytes_accessed=moved, transcendentals=0),
@@ -78,29 +78,61 @@
     return lax.dot_general(pick, values, (((1,), (1,)), ((), ())), preferred_element_type=F32)
 
 
+def window_pixel(offset):
+    place = offset - MARGIN + PATCH
+    return place % PATCH, place // PATCH - 1
+
+
+def neighbours():
+    return [offset for offset in range(KERNEL) if window_pixel(offset)[1]]
+
+
+def place_tokens(pick, values, first, wide, beside):
+    found = turned(pick, values).reshape(PATCH, 16, 128)
+    rounded = found.astype(BF16)
+    for offset in range(KERNEL):
+        pixel, shift = window_pixel(offset)
+        if shift == 0:
+            wide[pl.ds(first, 16), offset * 128 : (offset + 1) * 128] = rounded[pixel]
+    for slot, offset in enumerate(neighbours()):
+        beside[slot, pl.ds(pl.multiple_of(LEAD + first, 8), 16), :] = found[window_pixel(offset)[0]]
+
+
+def place_beside(count, first, wide, beside):
+    for slot, offset in enumerate(neighbours()):
+        start = LEAD + window_pixel(offset)[1]
+        part = beside[slot, start : start + count, :]
+        wide[first : first + count, offset * 128 : (offset + 1) * 128] = part.astype(BF16)
+
+
+def clear_ends(count, beside):
+    zeros = jnp.zeros((beside.shape[0], LEAD, 128), F32)
+    beside[:, 0:LEAD, :] = zeros
+    beside[:, LEAD + count : LEAD + count + LEAD, :] = zeros
+
+
+def windows_of(block, row, lanes):
+    window = pl.ds(pl.multiple_of(2 * KERNEL * row, 16), WIN)
+    values = block[window, lanes]
+    return jnp.concatenate([values, jnp.zeros((128 - WIN, values.shape[1]), BF16)], axis=0)
+
+
 def embed_kernel(*refs):
-    blocks, (weight, bias, out, picked, tail, wide) = refs[:-6], refs[-6:]
+    blocks, (weight, bias, out, wide, beside, tail) = refs[:-6], refs[-6:]
     col, row = lax.axis_index("cols"), lax.axis_index("rows")
-    width = blocks[0].shape[1]
     count = len(blocks)
     side = count // 2
+    width = blocks[0].shape[1]
     tokens = count * width // PATCH
-    local = width // PATCH
-    zeros = jnp.zeros((PATCH, LEAD, 128), F32)
-    picked[:, 0:LEAD, :] = zeros
-    picked[:, LEAD + tokens :, :] = zeros
-    blank = jnp.zeros((128 - WIN, width), BF16)
     pick = pick_matrix()
-    window = pl.ds(pl.multiple_of(2 * KERNEL * row, 16), WIN)
+    clear_ends(tokens, beside)
     edge = jnp.zeros((WIN, 128), F32)
     extra = jnp.zeros((8, 128 * CHAN), F32)
     for place, block in enumerate(blocks):
         source = side * (row if place < side else 1 - row) + ((col % side) ^ (place % side))
-        values = jnp.concatenate([block[window, :], blank], axis=0)
         for group in range(width // 256):
-            found = turned(pick, values[:, 256 * group : 256 * (group + 1)])
-            first = pl.multiple_of(LEAD + source * local + 16 * group, 8)
-            picked[:, pl.ds(first, 16), :] = found.reshape(PATCH, 16, 128)
+            first = pl.multiple_of(source * (width // PATCH) + 16 * group, 16)
+            place_tokens(pick, windows_of(block, row, slice(256 * group, 256 * (group + 1))), first, wide, beside)
         last = source == count - 1
         edge = jnp.where(last, block[0:WIN, width - 128 :].astype(F32), edge)
         extra = jnp.where(last, block[5 * KERNEL - 8 : 5 * KERNEL + 8, : 128 * CHAN].astype(F32)[8:], extra)
@@ -108,15 +140,13 @@
     last = jnp.where(row == 0, jnp.concatenate(before, axis=0), edge[:, 64:])
     last = jnp.concatenate([last, jnp.zeros((128 - WIN, 64), F32)], axis=0)
     last = jnp.concatenate([jnp.zeros((128, 64), F32), last, jnp.zeros((128, 128), F32)], axis=1)
-    tail[:, 0:8, :] = zeros
+    tail[:, 0:8, :] = jnp.zeros((PATCH, 8, 128), F32)
     tail[:, 8:24, :] = turned(pick, last.astype(BF16)).reshape(PATCH, 16, 128)
-
     for offset in range(KERNEL):
-        place = offset - MARGIN + PATCH
-        shift, pixel = place // PATCH - 1, place % PATCH
-        ahead = tail[pixel, 8 + shift : 16 + shift, :]
-        part = jnp.concatenate([ahead, picked[pixel, LEAD + shift : LEAD + shift + tokens, :]], axis=0)
-        wide[:, offset * 128 : (offset + 1) * 128] = part.astype(BF16)
+        pixel, shift = window_pixel(offset)
+        part = tail[pixel, 8 + shift : 16 + shift, :]
+        wide[tokens:, offset * 128 : (offset + 1) * 128] = part.astype(BF16)
+    place_beside(tokens, 0, wide, beside)
     grid = jnp.dot(wide[...], weight[...], preferred_element_type=F32)
     out[...] = (grid + bias[...]).astype(BF16)
 
@@ -179,7 +209,7 @@
     total = weight[0:1] * raw
     for tap in range(1, weight.shape[0]):
         total = pltpu.roll(total, 1, 0) + weight[tap : tap + 1] * raw
-    return silu(total[LEAD:] + bias).astype(BF16)
+    return silu(total[:-LEAD] + bias).astype(BF16)
 
 
 def mix_kernel(
@@ -191,14 +221,14 @@
     mean_sq = jnp.mean(resid * resid, axis=-1, keepdims=True)
     normed_f = resid * lax.rsqrt(mean_sq + 1e-05) * norm_gain[...]
     rows = lax.broadcasted_iota(jnp.int32, normed_f.shape, 0)
-    blank = (rows < LEAD) & (col == 0) & (row == 0)
+    blank = (rows >= embedded.shape[0] - LEAD) & (col == 0) & (row == 0)
     normed = jnp.where(blank, 0.0, normed_f).astype(BF16)
     normed_out[...] = normed
     length = embedded.shape[0] - LEAD
     maps_raw = project(normed, mix_weight, slice(E, E + 2 * NSTATE))
     step_raw = lax.dot_general(
         normed, step_weight[...], (((1,), (1,)), ((), ())), preferred_element_type=F32
-    )[LEAD:]
+    )[:-LEAD]
     step = softplus(step_raw + step_bias[...])
     log_decay = -step * jnp.exp(log_rate[...])
     lower = (
@@ -235,17 +265,28 @@
     keep_out[NSTATE : NSTATE + 8, :] = decay[...]
 
 
+TILES = E // 2 // 128
+MESSAGE = (TILES * NSTATE + 16, 128)
+
+
 def wire(values, decay):
     high = decay.astype(BF16).astype(F32)
-    rest = decay - high
-    place = lax.broadcasted_iota(jnp.int32, decay.shape, 0)
-    return jnp.concatenate([values, jnp.where(place == 0, high, rest)], axis=0).astype(BF16)
+    place = lax.broadcasted_iota(jnp.int32, (8, 128), 0)
+    rows = [jnp.zeros((8, 128), F32)] * 2
+    for tile in range(TILES):
+        lanes = slice(128 * tile, 128 * (tile + 1))
+        for part, piece in enumerate((high, decay - high)):
+            rows[part] = jnp.where(place == tile, piece[:, lanes], rows[part])
+    columns = [values[:, 128 * tile : 128 * (tile + 1)] for tile in range(TILES)]
+    return jnp.concatenate([*columns, *rows], axis=0).astype(BF16)
 
 
 def unwire(message):
-    values = message[0:NSTATE, :].astype(F32)
-    rows = message[NSTATE : NSTATE + 8, :].astype(F32)
-    return values, jnp.broadcast_to(rows[0:1] + rows[1:2], rows.shape)
+    columns = [message[NSTATE * tile : NSTATE * (tile + 1), :].astype(F32) for tile in range(TILES)]
+    rows = message[TILES * NSTATE :, :].astype(F32)
+    decay = rows[:8] + rows[8:]
+    decays = [jnp.broadcast_to(decay[tile : tile + 1], (8, 128)) for tile in range(TILES)]
+    return jnp.concatenate(columns, axis=1), jnp.concatenate(decays, axis=1)
 
 
 def product(factors):
@@ -328,7 +369,7 @@
 
 
 def gate_kernel(normed, gate_weight, local_mine, local_theirs, cum, own_out, factor_out):
-    gate = jnp.dot(normed[...], gate_weight[...], preferred_element_type=F32)[LEAD:].astype(BF16).astype(F32)
+    gate = jnp.dot(normed[...], gate_weight[...], preferred_element_type=F32)[:-LEAD].astype(BF16).astype(F32)
     gate = silu(gate)
     half = local_mine.shape[1]
     upper = lax.axis_index("rows") == 1
@@ -355,8 +396,10 @@
     step_t = jnp.concatenate([jnp.where(upper, step[:, heads:], step[:, :heads]), wide], axis=1).T
     for place in range(out.shape[1] // 128):
         pair = place
-        x_pair = x[:, pair * 128 : (pair + 1) * 128]
-        tops, bottoms = [], []
+        lanes = slice(place * 128, (place + 1) * 128)
+        x_pair = x[:, lanes].astype(F32)
+        lane = lax.broadcasted_iota(jnp.int32, x_pair.shape, 1)
+        top = bottom = None
         for member in range(2):
             head = 2 * pair + member
             column = cum_v[:, head : head + 1]
@@ -367,44 +410,56 @@
                 gap = jnp.minimum(column[rows] - cum_row[:, span], 0.0)
                 return (scores[rows, span] * jnp.exp(gap) * step_row[:, span]).astype(BF16)
 
-            inputs = x_pair[:, member * HDIM : (member + 1) * HDIM]
-            top = jnp.dot(weights(slice(0, half), slice(0, half)), inputs[:half], preferred_element_type=F32)
-            bottom = jnp.dot(weights(slice(half, length), slice(0, length)), inputs, preferred_element_type=F32)
-            tops.append(top)
-            bottoms.append(bottom)
-        lane = lax.broadcasted_iota(jnp.int32, x_pair.shape, 1)
+            inputs = jnp.where((lane < HDIM) == (member == 0), x_pair, 0.0).astype(BF16)
+            upper_part = jnp.dot(
+                weights(slice(0, half), slice(0, half)), inputs[:half], preferred_element_type=F32
+            )
+            lower_part = jnp.dot(
+                weights(slice(half, length), slice(0, length)), inputs, preferred_element_type=F32
+            )
+            top = upper_part if top is None else top + upper_part
+            bottom = lower_part if bottom is None else bottom + lower_part
         base = which * heads + 2 * pair
-        direct = jnp.where(lane < HDIM, skip[base], skip[base + 1]) * x_pair.astype(F32)
-        lanes = slice(place * 128, (place + 1) * 128)
-        out[0:half, lanes] = jnp.concatenate(tops, axis=1) + direct[:half]
-        out[half:length, lanes] = jnp.concatenate(bottoms, axis=1) + direct[half:]
-
-
-def half_product(which, state, own, factor, c_mat, out_gain, out_weight):
-    half = own.shape[1] // 2
-    lanes = pl.ds(pl.multiple_of(which * half, 128), half)
+        direct = jnp.where(lane < HDIM, skip[base], skip[base + 1]) * x_pair
+        out[0:half, lanes] = top + direct[:half]
+        out[half:length, lanes] = bottom + direct[half:]
+
+
+def half_hidden(lanes, state, own, factor, c_mat, out_gain):
     carried = jnp.dot(c_mat[...], state[...], preferred_element_type=F32)
     gated = own[:, lanes] + carried * factor[:, lanes]
     squares = jnp.sum(gated * gated, axis=-1, keepdims=True)
-    hidden = (gated * out_gain[:, lanes]).astype(BF16)
-    return jnp.dot(hidden, out_weight[lanes, :], preferred_element_type=F32), squares
+    return (gated * out_gain[:, lanes]).astype(BF16), squares
 
 
 def first_kernel(mine, own, factor, c_mat, out_gain, out_weight, product_out, squares_out):
-    product, squares = half_product(
-        lax.axis_index("rows"), mine, own, factor, c_mat, out_gain, out_weight
-    )
+    half = own.shape[1] // 2
+    lanes = pl.ds(pl.multiple_of(lax.axis_index("rows") * half, 128), half)
+    hidden, squares = half_hidden(lanes, mine, own, factor, c_mat, out_gain)
+    product = jnp.dot(hidden, out_weight[lanes, :], preferred_element_type=F32)
     product_out[...] = product
     squares_out[...] = jnp.broadcast_to(squares, squares_out.shape)
 
 
-def finish_kernel(theirs, own, factor, c_mat, out_gain, out_weight, product, squares, embedded, out):
-    rest, more = half_product(
-        1 - lax.axis_index("rows"), theirs, own, factor, c_mat, out_gain, out_weight
-    )
-    mean_sq = (squares[:, 0:1] + more) / own.shape[1]
-    result = (product[...] + rest) * lax.rsqrt(mean_sq + 1e-05)
-    out[...] = (result + embedded[...].astype(F32)[LEAD:]).astype(BF16)
+def finish_kernel(
+    theirs, own, factor, c_mat, out_gain, out_weight, product, squares, embedded, out, result, sems
+):
+    which = 1 - lax.axis_index("rows")
+    half = own.shape[1] // 2
+    lanes = pl.ds(pl.multiple_of(which * half, 128), half)
+    hidden, more = half_hidden(lanes, theirs, own, factor, c_mat, out_gain)
+    scale = lax.rsqrt((squares[:, 0:1] + more) / own.shape[1] + 1e-05)
+    chunk = result.shape[2]
+    copies = []
+    for place in range(result.shape[0]):
+        span = slice(place * chunk, (place + 1) * chunk)
+        rest = jnp.dot(hidden, out_weight[lanes, span], preferred_element_type=F32)
+        resid = embedded[:, span].astype(F32)[:-LEAD]
+        result[place] = ((product[:, span] + rest) * scale + resid).astype(BF16)
+        copies.append(pltpu.make_async_copy(result.at[place], out.at[:, span], sems.at[place]))
+        copies[-1].start()
+    for copy in copies:
+        copy.wait()
 
 
 def swap(block, axis, bit):
@@ -443,14 +498,13 @@
     weight = jnp.pad(weight, ((0, 0), (0, 128 - WIN), (0, 0))).reshape(KERNEL * 128, D)
     tokens = col_count * width // PATCH
     scratch = [
-        pltpu.VMEM((PATCH, 2 * LEAD + tokens, 128), F32),
+        pltpu.VMEM((tokens + LEAD, KERNEL * 128), BF16),
+        pltpu.VMEM((len(neighbours()), tokens + 2 * LEAD, 128), F32),
         pltpu.VMEM((PATCH, 24, 128), F32),
-        pltpu.VMEM((LEAD + tokens, KERNEL * 128), BF16),
     ]
-    flops = 2 * tokens * KERNEL * 128 * D
     return call(
-        embed_kernel, (*came, weight, patch_bias.reshape(1, -1)), shape((LEAD + tokens, D)), scratch,
-        flops=flops, moved=6 << 20, limit=16,
+        embed_kernel, (*came, weight, patch_bias.reshape(1, -1)), shape((tokens + LEAD, D)), scratch,
+        flops=2 * tokens * KERNEL * 128 * D, moved=6 << 20, limit=16,
     )
 
 
@@ -504,7 +558,7 @@
     )
     tokens = landed.transpose(1, 0, 2).reshape(row_local * col_local, feature_width)
     tail = shifted(tokens[tokens.shape[0] - LEAD :], ("cols", "rows"), 1)
-    return jnp.concatenate([tail, tokens], axis=0)
+    return jnp.concatenate([tokens, tail], axis=0)
 
 
 def body(
@@ -541,12 +595,12 @@
         [
             shape((LEAD + length, D)), shape((length, half)), shape((length, NSTATE)), shape((length, NSTATE)),
             shape((NSTATE, length)), shape((length, HEADS), F32), shape((length, HEADS), F32),
-            shape((length, HEADS)), shape((8, half), F32), shape((packed, half)),
+            shape((length, HEADS)), shape((8, half), F32), shape(MESSAGE),
         ],
         flops=length * D * mixed_width, moved=4 << 20, limit=16,
     )
     came = swap(send, "rows", 1)
-    summary, message = shape((packed, half), F32), shape((packed, half))
+    summary, message = shape((packed, half), F32), shape(MESSAGE)
     x_mine, keep = call(
         rest_kernel, (normed, scales, b_t, mix_weight, *conv, decay), [shape((length, half)), summary],
         flops=length * D * mixed_width, moved=4 << 20, limit=16,
@@ -591,7 +645,8 @@
     )
     return call(
         finish_kernel, (theirs, *common, partial_sum, squares, embedded), shape((length, D)),
-        flops=length * D * E, moved=4 << 20, limit=8,
+        [pltpu.VMEM((3, length, D // 3), BF16), pltpu.SemaphoreType.DMA((3,))],
+        flops=length * D * E, moved=4 << 20, limit=8, outside=True,
     )
 
 

time: 53.7 us -> 52 us (0.968)
  Pallas kernels: 15.2 us -> 13.2 us
  starting transfers between devices: 18.9 us -> 20 us
  waiting for transfers between devices: 14.9 us -> 14.1 us
    pallas_call x13, Pallas kernels: 15.2 us -> 13.2 us  [call(): pl.pallas_call(kernel, out_shape=outs, in_specs=[pl.BlockSpec(memory_spac...]
    ppermute x11, starting transfers between devices: 8.64 us -> 9.73 us  [swap(): lax.ppermute(block, axis, [(i, i ^ bit) for i in range(lax.axis_size(axis...]
    ppermute x11, waiting for transfers between devices: 8.23 us -> 7.4 us  [swap(): lax.ppermute(block, axis, [(i, i ^ bit) for i in range(lax.axis_size(axis...]
  transfers between devices with their start and end apart: 15 -> 15, of which waited for: 7 -> 7; matrix products, arithmetic and copies ran while one was open for 5% -> 5% of each run, Pallas kernels for 16% -> 13%
where the time goes in v6:
time: 52 us; the launch traced here: 51.8 us
  starting transfers between devices  20 us (38%)
  waiting for transfers between devices  14.1 us (27%)
  Pallas kernels  13.2 us (25%)
  local copies, waits for them, and re-layouts  4.15 us (8%)
    pallas_call x13, Pallas kernels, call(): pl.pallas_call(kernel, out_shape=outs, in_specs=[pl.BlockSpec(memory_spac...  13.2 us
    ppermute x4, starting transfers between devices, across(): return lax.ppermute(block, ('cols', 'rows'), pairs)  10.3 us
    ppermute x11, starting transfers between devices, swap(): lax.ppermute(block, axis, [(i, i ^ bit) for i in range(lax.axis_size(axis...  9.73 us
    ppermute x11, waiting for transfers between devices, swap(): lax.ppermute(block, axis, [(i, i ^ bit) for i in range(lax.axis_size(axis...  7.4 us
    ppermute x4, waiting for transfers between devices, across(): return lax.ppermute(block, ('cols', 'rows'), pairs)  6.67 us
    transpose x1, local copies, waits for them, and re-layouts, embed_by_rows(): patch_weight.reshape(3, 8, KERNEL, CHAN, D).transpose(2, 0, 3, 1, 4)  2.29 us
    unnamed x26, local copies, waits for them, and re-layouts  1.33 us
  transfers between devices with their start and end apart: 15, of which 7 were waited for; matrix products, arithmetic and copies ran while one was open for 5% of the time, Pallas kernels for 13%

profile of v6, /device:TPU:1, one launch (start us, length us, event | category | flops | bytes accessed | tf_op | source)
XLA Modules:
  0.0 51.8 jit_solution(12375773638183920144)
XLA Ops:
  0.0 1.0 %copy-done.3 = bf16[3,128,512]{2,1,0:T(8,128)(2,1)S(1)} copy-done((bf16[3,128,512]{2,1,0:T(8,128)(2,1)S(1)}, bf16[3,128,512]{2,1,0:T(8,128)(2,1)}, u32[]{:S(2)}) %copy-start.3) | copy-done | bytes 393240
  1.0 0.9 %collective-permute-done.partner = bf16[3,128,512]{2,1,0:T(8,128)(2,1)S(1)} collective-permute-done((bf16[3,128,512]{2,1,0:T(8,128)(2,1)}, bf16[3,128,512]{2,1,0:T(8,128)(2,1)S(1)}, u32[]{:S(2)}, u32[]{:S(2)}) %collective-permute-start) | collective-permute-done | bytes 393248 | tf_op jit(solution)/shard_map/ppermute | solution.py:466
  1.9 0.2 shard_map.137
  2.2 5.6 %collective-permute-start.1 = (bf16[128,512]{1,0:T(8,128)(2,1)S(1)}, bf16[128,512]{1,0:T(8,128)(2,1)S(1)}, u32[]{:S(2)}, u32[]{:S(2)}) collective-permute-start(bf16[128,512]{1,0:T(8,128)(2,1)S(1)} %get-tuple-element.32), channel_id=1, source_target_pairs={{0,0},{1,8},{2,2},{3,10},{4,4},{5,12},{6,6},{7,14},{8,1},{9,9},{10... | collective-permute-start | bytes 393224 | tf_op jit(solution)/shard_map/ppermute | solution.py:480
  7.8 1.1 %collective-permute-start.2 = (bf16[128,512]{1,0:T(8,128)(2,1)S(1)}, bf16[128,512]{1,0:T(8,128)(2,1)S(1)}, u32[]{:S(2)}, u32[]{:S(2)}) collective-permute-start(bf16[128,512]{1,0:T(8,128)(2,1)S(1)} %get-tuple-element.33), channel_id=1, source_target_pairs={{0,2},{1,10},{2,0},{3,8},{4,6},{5,14},{6,4},{7,12},{8,3},{9,11},{1... | collective-permute-start | bytes 393224 | tf_op jit(solution)/shard_map/ppermute | solution.py:480
  8.9 3.6 %collective-permute-start.3 = (bf16[128,512]{1,0:T(8,128)(2,1)S(1)}, bf16[128,512]{1,0:T(8,128)(2,1)S(1)}, u32[]{:S(2)}, u32[]{:S(2)}) collective-permute-start(bf16[128,512]{1,0:T(8,128)(2,1)S(1)} %get-tuple-element.34), channel_id=1, source_target_pairs={{0,4},{1,12},{2,6},{3,14},{4,0},{5,8},{6,2},{7,10},{8,5},{9,13},{1... | collective-permute-start | bytes 393224 | tf_op jit(solution)/shard_map/ppermute | solution.py:480
  12.5 4.6 %collective-permute-done.2.refs_1_ = bf16[128,512]{1,0:T(8,128)(2,1)S(1)} collective-permute-done((bf16[128,512]{1,0:T(8,128)(2,1)S(1)}, bf16[128,512]{1,0:T(8,128)(2,1)S(1)}, u32[]{:S(2)}, u32[]{:S(2)}) %collective-permute-start.2) | collective-permute-done | bytes 131104 | tf_op jit(solution)/shard_map/ppermute | solution.py:480
  17.0 0.5 collective-permute-start.7
  17.6 2.1 %collective-permute-done.4.refs_3_ = bf16[128,512]{1,0:T(8,128)(2,1)S(1)} collective-permute-done((bf16[128,512]{1,0:T(8,128)(2,1)S(1)}, bf16[128,512]{1,0:T(8,128)(2,1)S(1)}, u32[]{:S(2)}, u32[]{:S(2)}) %collective-permute-start.4) | collective-permute-done | bytes 131104 | tf_op jit(solution)/shard_map/ppermute | solution.py:480
  19.6 2.3 %copy.15 = bf16[24,3,3,8,768]{4,3,2,1,0:T(8,128)(2,1)S(1)} copy(bf16[24,3,3,8,768]{4,0,2,3,1:T(8,128)(2,1)} %bitcast.13) | data formatting | bytes 5308416 | tf_op jit(solution)/shard_map/transpose | solution.py:497
  22.0 0.5 pad.4
  22.6 2.3 %shard_map.138.embedded = bf16[264,768]{1,0:T(8,128)(2,1)S(1)} custom-call(bf16[128,512]{1,0:T(8,128)(2,1)S(1)} %collective-permute-done.1.refs_0_, bf16[128,512]{1,0:T(8,128)(2,1)S(1)} %collective-permute-done.2.refs_1_, bf16[128,512]{1,0:T(8,128)(2,1)S(1)} %collective-permute-done.3.refs_2_, bf16[128,512]{1,0:T(8,128)(2,1)S(1)} %collective-permute-done.4.refs_3_, ...), custom_call_target="tpu_custom_call" | custom-call | flops 1207959552 | bytes 6291456 | tf_op jit(solution)/shard_map/pallas_call | solution.py:31
  25.0 2.0 %shard_map.139 = (bf16[264,768]{1,0:T(8,128)(2,1)S(1)}, bf16[256,768]{1,0:T(8,128)(2,1)S(1)}, bf16[256,64]{1,0:T(8,128)(2,1)S(1)}, bf16[256,64]{1,0:T(8,128)(2,1...) custom-call(bf16[264,768]{1,0:T(8,128)(2,1)S(1)} %shard_map.138.embe, ...), custom_call_target="tpu_custom_call" | custom-call | flops 327155712 | bytes 4194304 | tf_op jit(solution)/shard_map/pallas_call | solution.py:31
  27.1 0.6 %collective-permute-start.9 = (bf16[400,128]{1,0:T(8,128)(2,1)S(1)}, bf16[400,128]{1,0:T(8,128)(2,1)S(1)}, u32[]{:S(2)}, u32[]{:S(2)}) collective-permute-start(bf16[400,128]{1,0:T(8,128)(2,1)S(1)} %get-tuple-element.41), channel_id=1, source_target_pairs={{0,1},{1,0},{2,3},{3,2},{4,5},{5,4},{6,7},{7,6},{8,9},{9,8},{10,11... | collective-permute-start | bytes 307208 | tf_op jit(solution)/shard_map/ppermute | solution.py:466
  27.6 1.4 %shard_map.140 = (bf16[256,768]{1,0:T(8,128)(2,1)S(1)}, f32[72,768]{1,0:T(8,128)S(1)}) custom-call(bf16[264,768]{1,0:T(8,128)(2,1)S(1)} %get-tuple-element.36.normed, bf16[256,24]{1,0:T(8,128)(2,1)S(1)} %get-tuple-element.37.scales, bf16[64,256]{1,0:T(8,128)(2,1)S(1)} %get-tuple-element.38.b_t, bf16[768,1664]{1,0:T(8,128)(2,1)S(1)} %copy-done, ...), custom_call_target="tpu_custom_call" | custom-call | flops 327155712 | bytes 4194304 | tf_op jit(solution)/shard_map/pallas_call | solution.py:31
  29.1 0.2 collective-permute-start.10
  29.3 2.9 %collective-permute-start.11 = (bf16[400,128]{1,0:T(8,128)(2,1)S(1)}, bf16[400,128]{1,0:T(8,128)(2,1)S(1)}, u32[]{:S(2)}, u32[]{:S(2)}) collective-permute-start(bf16[400,128]{1,0:T(8,128)(2,1)S(1)} %get-tuple-element.43), channel_id=1, source_target_pairs={{0,4},{2,6},{4,0},{6,2},{8,12},{10,14},{12,8},{14,10},{1,5},{3,7},... | collective-permute-start | bytes 307208 | tf_op jit(solution)/shard_map/ppermute | solution.py:466
  32.2 0.1 collective-permute-start.12
  32.3 1.3 %collective-permute-done.10.refs_1_ = bf16[400,128]{1,0:T(8,128)(2,1)S(1)} collective-permute-done((bf16[400,128]{1,0:T(8,128)(2,1)S(1)}, bf16[400,128]{1,0:T(8,128)(2,1)S(1)}, u32[]{:S(2)}, u32[]{:S(2)}) %collective-permute-start.10) | collective-permute-done | bytes 102432 | tf_op jit(solution)/shard_map/ppermute | solution.py:466
  33.6 1.6 %collective-permute-done.11.refs_2_ = bf16[400,128]{1,0:T(8,128)(2,1)S(1)} collective-permute-done((bf16[400,128]{1,0:T(8,128)(2,1)S(1)}, bf16[400,128]{1,0:T(8,128)(2,1)S(1)}, u32[]{:S(2)}, u32[]{:S(2)}) %collective-permute-start.11) | collective-permute-done | bytes 102432 | tf_op jit(solution)/shard_map/ppermute | solution.py:466
  35.2 1.8 %collective-permute-done.12.refs_3_ = bf16[400,128]{1,0:T(8,128)(2,1)S(1)} collective-permute-done((bf16[400,128]{1,0:T(8,128)(2,1)S(1)}, bf16[400,128]{1,0:T(8,128)(2,1)S(1)}, u32[]{:S(2)}, u32[]{:S(2)}) %collective-permute-start.12) | collective-permute-done | bytes 102432 | tf_op jit(solution)/shard_map/ppermute | solution.py:466
  37.0 0.2 shard_map.142
  37.2 2.9 %collective-permute-start.13 = (bf16[400,128]{1,0:T(8,128)(2,1)S(1)}, bf16[400,128]{1,0:T(8,128)(2,1)S(1)}, u32[]{:S(2)}, u32[]{:S(2)}) collective-permute-start(bf16[400,128]{1,0:T(8,128)(2,1)S(1)} %get-tuple-element.46), channel_id=1, source_target_pairs={{0,8},{2,10},{4,12},{6,14},{8,0},{10,2},{12,4},{14,6},{1,9},{3,11}... | collective-permute-start | bytes 307208 | tf_op jit(solution)/shard_map/ppermute | solution.py:466
  40.1 1.7 %shard_map.145.local_theirs = f32[256,768]{1,0:T(8,128)S(1)} custom-call(f32[24]{0:T(128)S(1)} %copy-done.6, bf16[256,768]{1,0:T(8,128)(2,1)S(1)} %get-tuple-element.53.x, bf16[256,64]{1,0:T(8,128)(2,1)S(1)} %get-tuple-element.49.b_mat, bf16[256,64]{1,0:T(8,128)(2,1)S(1)} %get-tuple-element.50.c_mat, f32[256,24]{1,0:T(8,128)S(1)} %get-tuple-element.51.step, ...), custom_call_target="tpu_custom_call" | custom-call | flops 201326592 | bytes 2097152 | tf_op jit(solution)/shard_map/pallas_call | solution.py:31
  41.8 1.8 %collective-permute-done.13.refs_2_ = bf16[400,128]{1,0:T(8,128)(2,1)S(1)} collective-permute-done((bf16[400,128]{1,0:T(8,128)(2,1)S(1)}, bf16[400,128]{1,0:T(8,128)(2,1)S(1)}, u32[]{:S(2)}, u32[]{:S(2)}) %collective-permute-start.13) | collective-permute-done | bytes 102432 | tf_op jit(solution)/shard_map/ppermute | solution.py:466
  43.6 0.1 shard_map.143
  43.7 2.6 %collective-permute-start.14 = (bf16[64,768]{1,0:T(8,128)(2,1)S(1)}, bf16[64,768]{1,0:T(8,128)(2,1)S(1)}, u32[]{:S(2)}, u32[]{:S(2)}) collective-permute-start(bf16[64,768]{1,0:T(8,128)(2,1)S(1)} %get-tuple-element.47), channel_id=1, source_target_pairs={{0,1},{1,0},{2,3},{3,2},{4,5},{5,4},{6,7},{7,6},{8,9},{9,8},{10,11... | collective-permute-start | bytes 294920 | tf_op jit(solution)/shard_map/ppermute | solution.py:466
  46.3 1.8 %shard_map.144.local_mine = f32[256,768]{1,0:T(8,128)S(1)} custom-call(f32[24]{0:T(128)S(1)} %copy-done.6, bf16[256,768]{1,0:T(8,128)(2,1)S(1)} %get-tuple-element.48.x, bf16[256,64]{1,0:T(8,128)(2,1)S(1)} %get-tuple-element.49.b_mat, bf16[256,64]{1,0:T(8,128)(2,1)S(1)} %get-tuple-element.50.c_mat, f32[256,24]{1,0:T(8,128)S(1)} %get-tuple-element.51.step, ...), custom_call_target="tpu_custom_call" | custom-call | flops 201326592 | bytes 2097152 | tf_op jit(solution)/shard_map/pallas_call | solution.py:31
  48.1 1.4 %shard_map.146 = (f32[256,1536]{1,0:T(8,128)S(1)}, f32[256,1536]{1,0:T(8,128)S(1)}) custom-call(bf16[264,768]{1,0:T(8,128)(2,1)S(1)} %get-tuple-element.36.normed, bf16[768,1536]{1,0:T(8,128)(2,1)S(1)} %copy-done.2, f32[256,768]{1,0:T(8,128)S(1)} %shard_map.144.local_mine, f32[256,768]{1,0:T(8,128)S(1)} %shard_map.145.local_theirs, ...), custom_call_target="tpu_custom_call" | custom-call | flops 603979776 | bytes 4194304 | tf_op jit(solution)/shard_map/pallas_call | solution.py:31
  49.5 0.3 copy-done.1
  49.7 0.7 %shard_map.147 = (f32[256,768]{1,0:T(8,128)S(1)}, f32[256,128]{1,0:T(8,128)S(1)}) custom-call(bf16[64,768]{1,0:T(8,128)(2,1)S(1)} %get-tuple-element.56.mine, f32[256,1536]{1,0:T(8,128)S(1)} %get-tuple-element.54.own, f32[256,1536]{1,0:T(8,128)S(1)} %get-tuple-element.55.factor, bf16[256,64]{1,0:T(8,128)(2,1)S(1)} %get-tuple-element.50.c_mat, ...), custom_call_target="tpu_custom_call" | custom-call | flops 301989888 | bytes 4194304 | tf_op jit(solution)/shard_map/pallas_call | solution.py:31
  50.4 1.4 %shard_map.148 = bf16[256,768]{1,0:T(8,128)(2,1)} custom-call(bf16[64,768]{1,0:T(8,128)(2,1)S(1)} %collective-permute-done.14.theirs, f32[256,1536]{1,0:T(8,128)S(1)} %get-tuple-element.54.own, f32[256,1536]{1,0:T(8,128)S(1)} %get-tuple-element.55.factor, bf16[256,64]{1,0:T(8,128)(2,1)S(1)} %get-tuple-element.50.c_mat, f32[1,1536]{1,0:T(1,128)S(1)} %reshape.35.out_gain, ...), custom_call_target="tpu_custom_call" | custom-call | flops 301989888 | bytes 4194304 | tf_op jit(solution)/shard_map/pallas_call | solution.py:31
  (43 shorter events, 0.2 us)
Async XLA Ops:
  0.0 1.9 %collective-permute-start = (bf16[3,128,512]{2,1,0:T(8,128)(2,1)}, bf16[3,128,512]{2,1,0:T(8,128)(2,1)S(1)}, u32[]{:S(2)}, u32[]{:S(2)}) collective-permute-start(bf16[3,128,512]{2,1,0:T(8,128)(2,1)} %pixels.1), channel_id=1, source_target_pairs={{0,1},{1,0},{2,3},{3,2},{4,5},{5,4},{6,7},{7,6},{8,9},{9,8},{10,11... | collective-permute-start | bytes 1179656 | tf_op jit(solution)/shard_map/ppermute | solution.py:466
  0.0 1.0 %copy-start.3 = (bf16[3,128,512]{2,1,0:T(8,128)(2,1)S(1)}, bf16[3,128,512]{2,1,0:T(8,128)(2,1)}, u32[]{:S(2)}) copy-start(bf16[3,128,512]{2,1,0:T(8,128)(2,1)} %pixels.1) | copy-start | bytes 1179652
  2.2 10.3 %collective-permute-start.1 = (bf16[128,512]{1,0:T(8,128)(2,1)S(1)}, bf16[128,512]{1,0:T(8,128)(2,1)S(1)}, u32[]{:S(2)}, u32[]{:S(2)}) collective-permute-start(bf16[128,512]{1,0:T(8,128)(2,1)S(1)} %get-tuple-element.32), channel_id=1, source_target_pairs={{0,0},{1,8},{2,2},{3,10},{4,4},{5,12},{6,6},{7,14},{8,1},{9,9},{10... | collective-permute-start | bytes 393224 | tf_op jit(solution)/shard_map/ppermute | solution.py:480
  7.8 9.3 %collective-permute-start.2 = (bf16[128,512]{1,0:T(8,128)(2,1)S(1)}, bf16[128,512]{1,0:T(8,128)(2,1)S(1)}, u32[]{:S(2)}, u32[]{:S(2)}) collective-permute-start(bf16[128,512]{1,0:T(8,128)(2,1)S(1)} %get-tuple-element.33), channel_id=1, source_target_pairs={{0,2},{1,10},{2,0},{3,8},{4,6},{5,14},{6,4},{7,12},{8,3},{9,11},{1... | collective-permute-start | bytes 393224 | tf_op jit(solution)/shard_map/ppermute | solution.py:480
  8.9 8.2 %collective-permute-start.3 = (bf16[128,512]{1,0:T(8,128)(2,1)S(1)}, bf16[128,512]{1,0:T(8,128)(2,1)S(1)}, u32[]{:S(2)}, u32[]{:S(2)}) collective-permute-start(bf16[128,512]{1,0:T(8,128)(2,1)S(1)} %get-tuple-element.34), channel_id=1, source_target_pairs={{0,4},{1,12},{2,6},{3,14},{4,0},{5,8},{6,2},{7,10},{8,5},{9,13},{1... | collective-permute-start | bytes 393224 | tf_op jit(solution)/shard_map/ppermute | solution.py:480
  12.4 7.2 %collective-permute-start.4 = (bf16[128,512]{1,0:T(8,128)(2,1)S(1)}, bf16[128,512]{1,0:T(8,128)(2,1)S(1)}, u32[]{:S(2)}, u32[]{:S(2)}) collective-permute-start(bf16[128,512]{1,0:T(8,128)(2,1)S(1)} %get-tuple-element.35), channel_id=1, source_target_pairs={{0,6},{1,14},{2,4},{3,12},{4,2},{5,10},{6,0},{7,8},{8,7},{9,15},{1... | collective-permute-start | bytes 393224 | tf_op jit(solution)/shard_map/ppermute | solution.py:480
  12.4 10.1 %collective-permute-start.5 = (bf16[128,512]{1,0:T(8,128)(2,1)S(1)}, bf16[128,512]{1,0:T(8,128)(2,1)S(1)}, u32[]{:S(2)}, u32[]{:S(2)}) collective-permute-start(bf16[128,512]{1,0:T(8,128)(2,1)S(1)} %collective-permute-done.1.refs_0_), channel_id=1, source_target_pairs={{0,1},{1,0},{2,3},{3,2},{4,5},{5,4},{6,7},{7,6},{8,9},{9,8},{10,11... | collective-permute-start | bytes 393224 | tf_op jit(solution)/shard_map/ppermute | solution.py:466
  17.0 5.5 %collective-permute-start.6 = (bf16[128,512]{1,0:T(8,128)(2,1)S(1)}, bf16[128,512]{1,0:T(8,128)(2,1)S(1)}, u32[]{:S(2)}, u32[]{:S(2)}) collective-permute-start(bf16[128,512]{1,0:T(8,128)(2,1)S(1)} %collective-permute-done.2.refs_1_), channel_id=1, source_target_pairs={{0,1},{1,0},{2,3},{3,2},{4,5},{5,4},{6,7},{7,6},{8,9},{9,8},{10,11... | collective-permute-start | bytes 393224 | tf_op jit(solution)/shard_map/ppermute | solution.py:466
  17.0 5.5 %collective-permute-start.7 = (bf16[128,512]{1,0:T(8,128)(2,1)S(1)}, bf16[128,512]{1,0:T(8,128)(2,1)S(1)}, u32[]{:S(2)}, u32[]{:S(2)}) collective-permute-start(bf16[128,512]{1,0:T(8,128)(2,1)S(1)} %collective-permute-done.3.refs_2_), channel_id=1, source_target_pairs={{0,1},{1,0},{2,3},{3,2},{4,5},{5,4},{6,7},{7,6},{8,9},{9,8},{10,11... | collective-permute-start | bytes 393224 | tf_op jit(solution)/shard_map/ppermute | solution.py:466
  19.6 2.9 %collective-permute-start.8 = (bf16[128,512]{1,0:T(8,128)(2,1)S(1)}, bf16[128,512]{1,0:T(8,128)(2,1)S(1)}, u32[]{:S(2)}, u32[]{:S(2)}) collective-permute-start(bf16[128,512]{1,0:T(8,128)(2,1)S(1)} %collective-permute-done.4.refs_3_), channel_id=1, source_target_pairs={{0,1},{1,0},{2,3},{3,2},{4,5},{5,4},{6,7},{7,6},{8,9},{9,8},{10,11... | collective-permute-start | bytes 393224 | tf_op jit(solution)/shard_map/ppermute | solution.py:466
  19.6 2.3 %copy-start.11 = (f32[768]{0:T(1024)S(1)}, f32[768]{0:T(1024)}, u32[]{:S(2)}) copy-start(f32[768]{0:T(1024)} %param.16) | copy-start | bytes 9220
  19.6 2.3 %copy-start.10 = (f32[1664]{0:T(1024)S(1)}, f32[1664]{0:T(1024)}, u32[]{:S(2)}) copy-start(f32[1664]{0:T(1024)} %param.24) | copy-start | bytes 19972
  19.6 2.4 %copy-start.12 = (f32[768]{0:T(1024)S(1)}, f32[768]{0:T(1024)}, u32[]{:S(2)}) copy-start(f32[768]{0:T(1024)} %param.17) | copy-start | bytes 9220
  22.6 2.4 %copy-start = (bf16[768,1664]{1,0:T(8,128)(2,1)S(1)}, bf16[768,1664]{1,0:T(8,128)(2,1)}, u32[]{:S(2)}) copy-start(bf16[768,1664]{1,0:T(8,128)(2,1)} %mix_weight.3) | copy-start | bytes 7667716
  22.6 2.4 %copy-start.4 = (f32[4,1664]{1,0:T(4,128)S(1)}, f32[4,1664]{1,0:T(4,128)}, u32[]{:S(2)}) copy-start(f32[4,1664]{1,0:T(4,128)} %conv_weight.3) | copy-start | bytes 79876
  22.6 2.4 %copy-start.5 = (bf16[768,24]{0,1:T(8,128)(2,1)S(1)}, bf16[768,24]{0,1:T(8,128)(2,1)}, u32[]{:S(2)}) copy-start(bf16[768,24]{0,1:T(8,128)(2,1)} %param.20) | copy-start | bytes 110596
  22.6 2.4 %copy-start.7 = (f32[24]{0:T(128)S(1)}, f32[24]{0:T(128)}, u32[]{:S(2)}) copy-start(f32[24]{0:T(128)} %param.21) | copy-start | bytes 292
  22.6 2.4 %copy-start.8 = (f32[24]{0:T(128)S(1)}, f32[24]{0:T(128)}, u32[]{:S(2)}) copy-start(f32[24]{0:T(128)} %param.22) | copy-start | bytes 292
  27.0 13.1 %copy-start.9 = (f32[1536]{0:T(1024)S(1)}, f32[1536]{0:T(1024)}, u32[]{:S(2)}) copy-start(f32[1536]{0:T(1024)} %param.26) | copy-start | bytes 18436
  27.0 13.1 %copy-start.6 = (f32[24]{0:T(128)S(1)}, f32[24]{0:T(128)}, u32[]{:S(2)}) copy-start(f32[24]{0:T(128)} %skip.3) | copy-start | bytes 292
  27.1 2.0 %collective-permute-start.9 = (bf16[400,128]{1,0:T(8,128)(2,1)S(1)}, bf16[400,128]{1,0:T(8,128)(2,1)S(1)}, u32[]{:S(2)}, u32[]{:S(2)}) collective-permute-start(bf16[400,128]{1,0:T(8,128)(2,1)S(1)} %get-tuple-element.41), channel_id=1, source_target_pairs={{0,1},{1,0},{2,3},{3,2},{4,5},{5,4},{6,7},{7,6},{8,9},{9,8},{10,11... | collective-permute-start | bytes 307208 | tf_op jit(solution)/shard_map/ppermute | solution.py:466
  29.1 19.0 %copy-start.2 = (bf16[768,1536]{1,0:T(8,128)(2,1)S(1)}, bf16[768,1536]{1,0:T(8,128)(2,1)}, u32[]{:S(2)}) copy-start(bf16[768,1536]{1,0:T(8,128)(2,1)} %gate_weight.1) | copy-start | bytes 7077892
  29.1 4.5 %collective-permute-start.10 = (bf16[400,128]{1,0:T(8,128)(2,1)S(1)}, bf16[400,128]{1,0:T(8,128)(2,1)S(1)}, u32[]{:S(2)}, u32[]{:S(2)}) collective-permute-start(bf16[400,128]{1,0:T(8,128)(2,1)S(1)} %get-tuple-element.43), channel_id=1, source_target_pairs={{0,2},{2,0},{4,6},{6,4},{8,10},{10,8},{12,14},{14,12},{1,3},{3,1},... | collective-permute-start | bytes 307208 | tf_op jit(solution)/shard_map/ppermute | solution.py:466
  29.3 5.9 %collective-permute-start.11 = (bf16[400,128]{1,0:T(8,128)(2,1)S(1)}, bf16[400,128]{1,0:T(8,128)(2,1)S(1)}, u32[]{:S(2)}, u32[]{:S(2)}) collective-permute-start(bf16[400,128]{1,0:T(8,128)(2,1)S(1)} %get-tuple-element.43), channel_id=1, source_target_pairs={{0,4},{2,6},{4,0},{6,2},{8,12},{10,14},{12,8},{14,10},{1,5},{3,7},... | collective-permute-start | bytes 307208 | tf_op jit(solution)/shard_map/ppermute | solution.py:466
  32.2 4.8 %collective-permute-start.12 = (bf16[400,128]{1,0:T(8,128)(2,1)S(1)}, bf16[400,128]{1,0:T(8,128)(2,1)S(1)}, u32[]{:S(2)}, u32[]{:S(2)}) collective-permute-start(bf16[400,128]{1,0:T(8,128)(2,1)S(1)} %get-tuple-element.43), channel_id=1, source_target_pairs={{0,6},{2,4},{4,2},{6,0},{8,14},{10,12},{12,10},{14,8},{1,7},{3,5},... | collective-permute-start | bytes 307208 | tf_op jit(solution)/shard_map/ppermute | solution.py:466
  37.2 6.5 %collective-permute-start.13 = (bf16[400,128]{1,0:T(8,128)(2,1)S(1)}, bf16[400,128]{1,0:T(8,128)(2,1)S(1)}, u32[]{:S(2)}, u32[]{:S(2)}) collective-permute-start(bf16[400,128]{1,0:T(8,128)(2,1)S(1)} %get-tuple-element.46), channel_id=1, source_target_pairs={{0,8},{2,10},{4,12},{6,14},{8,0},{10,2},{12,4},{14,6},{1,9},{3,11}... | collective-permute-start | bytes 307208 | tf_op jit(solution)/shard_map/ppermute | solution.py:466
  43.7 6.7 %collective-permute-start.14 = (bf16[64,768]{1,0:T(8,128)(2,1)S(1)}, bf16[64,768]{1,0:T(8,128)(2,1)S(1)}, u32[]{:S(2)}, u32[]{:S(2)}) collective-permute-start(bf16[64,768]{1,0:T(8,128)(2,1)S(1)} %get-tuple-element.47), channel_id=1, source_target_pairs={{0,1},{1,0},{2,3},{3,2},{4,5},{5,4},{6,7},{7,6},{8,9},{9,8},{10,11... | collective-permute-start | bytes 294920 | tf_op jit(solution)/shard_map/ppermute | solution.py:466
  48.1 1.7 %copy-start.1 = (bf16[1536,768]{1,0:T(8,128)(2,1)S(1)}, bf16[1536,768]{1,0:T(8,128)(2,1)}, u32[]{:S(2)}) copy-start(bf16[1536,768]{1,0:T(8,128)(2,1)} %out_weight.3) | copy-start | bytes 7077892

commit v7 on v6

--- a/solution.py
+++ b/solution.py
@@ -88,14 +88,19 @@
 
 
 def place_tokens(pick, values, first, wide, beside):
-    found = turned(pick, values).reshape(PATCH, 16, 128)
-    rounded = found.astype(BF16)
-    for offset in range(KERNEL):
-        pixel, shift = window_pixel(offset)
-        if shift == 0:
-            wide[pl.ds(first, 16), offset * 128 : (offset + 1) * 128] = rounded[pixel]
-    for slot, offset in enumerate(neighbours()):
-        beside[slot, pl.ds(pl.multiple_of(LEAD + first, 8), 16), :] = found[window_pixel(offset)[0]]
+    both = jnp.concatenate([values[:, :256], values[:, 256:]], axis=0)
+    found = turned(pick, both).reshape(PATCH, 16, 256)
+    for group in range(2):
+        piece = found[:, :, 128 * group : 128 * (group + 1)]
+        rounded = piece.astype(BF16)
+        rows = pl.ds(pl.multiple_of(first + 16 * group, 16), 16)
+        for offset in range(KERNEL):
+            pixel, shift = window_pixel(offset)
+            if shift == 0:
+                wide[rows, offset * 128 : (offset + 1) * 128] = rounded[pixel]
+        rows = pl.ds(pl.multiple_of(LEAD + first + 16 * group, 8), 16)
+        for slot, offset in enumerate(neighbours()):
+            beside[slot, rows, :] = piece[window_pixel(offset)[0]]
 
 
 def place_beside(count, first, wide, beside):
@@ -130,9 +135,9 @@
     extra = jnp.zeros((8, 128 * CHAN), F32)
     for place, block in enumerate(blocks):
         source = side * (row if place < side else 1 - row) + ((col % side) ^ (place % side))
-        for group in range(width // 256):
-            first = pl.multiple_of(source * (width // PATCH) + 16 * group, 16)
-            place_tokens(pick, windows_of(block, row, slice(256 * group, 256 * (group + 1))), first, wide, beside)
+        for group in range(width // 512):
+            first = source * (width // PATCH) + 32 * group
+            place_tokens(pick, windows_of(block, row, slice(512 * group, 512 * (group + 1))), first, wide, beside)
         last = source == count - 1
         edge = jnp.where(last, block[0:WIN, width - 128 :].astype(F32), edge)
         extra = jnp.where(last, block[5 * KERNEL - 8 : 5 * KERNEL + 8, : 128 * CHAN].astype(F32)[8:], extra)
@@ -177,24 +182,32 @@
     return jnp.maximum(values, 0.0) + jnp.log1p(small)
 
 
-def half_mix(which, normed, scales, b_t, mix_weight, conv_weight, conv_bias, x_out):
+def half_inputs(which, normed, mix_weight, conv_weight, conv_bias, x_out):
     half = E // 2
-    matrix = spread_matrix()
-    states = []
     chunk = 256
+    parts = []
     spans = [
         pl.ds(pl.multiple_of(which * half + first, 128), chunk) for first in range(0, half, chunk)
     ]
-    wanted = jnp.where(which == 0, matrix[:, :half].astype(F32), matrix[:, half:].astype(F32)).astype(BF16)
     ahead = project(normed, mix_weight, spans[0])
     for place, lanes in enumerate(spans):
         raw = ahead
         if place + 1 < len(spans):
             ahead = project(normed, mix_weight, spans[place + 1])
         part = mixed(raw, conv_weight[:, lanes], conv_bias[:, lanes])
-        local = slice(place * chunk, (place + 1) * chunk)
-        x_out[:, local] = part
-        to_end = jnp.dot(scales, wanted[:, local], preferred_element_type=F32)
+        x_out[:, place * chunk : (place + 1) * chunk] = part
+        parts.append(part)
+    return parts
+
+
+def half_state(which, parts, scales, b_t):
+    half = E // 2
+    matrix = spread_matrix().astype(F32)
+    wanted = jnp.where(which == 0, matrix[:, :half], matrix[:, half:]).astype(BF16)
+    states = []
+    for place, part in enumerate(parts):
+        chunk = part.shape[1]
+        to_end = jnp.dot(scales, wanted[:, place * chunk : (place + 1) * chunk], preferred_element_type=F32)
         scaled = (part.astype(F32) * to_end).astype(BF16)
         states.append(jnp.dot(b_t, scaled, preferred_element_type=F32))
     return jnp.concatenate(states, axis=1)
@@ -242,6 +255,7 @@
     cum = cum + jnp.dot(lower, low, preferred_element_type=F32)
     step_out[...] = step
     cum_out[...] = cum
+    parts = half_inputs(1 - row, normed, mix_weight, conv_weight, conv_bias, x_out)
     last = cum[length - 1 :]
     scales = (jnp.exp(last - cum) * step).astype(BF16)
     scales_out[...] = scales
@@ -251,7 +265,7 @@
     c_out[...] = maps[:, NSTATE:].astype(BF16)
     b_t = maps.T[:NSTATE].astype(BF16)
     b_t_out[...] = b_t
-    state = half_mix(1 - row, normed, scales, b_t, mix_weight, conv_weight, conv_bias, x_out)
+    state = half_state(1 - row, parts, scales, b_t)
     half = E // 2
     first = row == 0
     decay_out[...] = jnp.where(first, decay[:, :half], decay[:, half:])
@@ -259,9 +273,9 @@
 
 
 def rest_kernel(normed, scales, b_t, mix_weight, conv_weight, conv_bias, decay, x_out, keep_out):
-    keep_out[0:NSTATE, :] = half_mix(
-        lax.axis_index("rows"), normed[...], scales[...], b_t[...], mix_weight, conv_weight, conv_bias, x_out
-    )
+    row = lax.axis_index("rows")
+    parts = half_inputs(row, normed[...], mix_weight, conv_weight, conv_bias, x_out)
+    keep_out[0:NSTATE, :] = half_state(row, parts, scales[...], b_t[...])
     keep_out[NSTATE : NSTATE + 8, :] = decay[...]
 
 

time: 52 us -> 51.7 us (level)
  no operation moved by 1% of the time
where the time goes in v7:
time: 51.7 us; the launch traced here: 51.4 us
  starting transfers between devices  20 us (39%)
  waiting for transfers between devices  14.1 us (27%)
  Pallas kernels  12.9 us (25%)
  local copies, waits for them, and re-layouts  4.16 us (8%)
    pallas_call x13, Pallas kernels, call(): pl.pallas_call(kernel, out_shape=outs, in_specs=[pl.BlockSpec(memory_spac...  12.9 us
    ppermute x4, starting transfers between devices, across(): return lax.ppermute(block, ('cols', 'rows'), pairs)  10.3 us
    ppermute x11, starting transfers between devices, swap(): lax.ppermute(block, axis, [(i, i ^ bit) for i in range(lax.axis_size(axis...  9.72 us
    ppermute x11, waiting for transfers between devices, swap(): lax.ppermute(block, axis, [(i, i ^ bit) for i in range(lax.axis_size(axis...  7.39 us
    ppermute x4, waiting for transfers between devices, across(): return lax.ppermute(block, ('cols', 'rows'), pairs)  6.67 us
    transpose x1, local copies, waits for them, and re-layouts, embed_by_rows(): patch_weight.reshape(3, 8, KERNEL, CHAN, D).transpose(2, 0, 3, 1, 4)  2.29 us
    unnamed x26, local copies, waits for them, and re-layouts  1.33 us
  transfers between devices with their start and end apart: 15, of which 7 were waited for; matrix products, arithmetic and copies ran while one was open for 5% of the time, Pallas kernels for 13%

profile of v7, /device:TPU:1, one launch (start us, length us, event | category | flops | bytes accessed | tf_op | source)
XLA Modules:
  0.0 51.4 jit_solution(16620236643886847341)
XLA Ops:
  0.0 1.0 %copy-done.3 = bf16[3,128,512]{2,1,0:T(8,128)(2,1)S(1)} copy-done((bf16[3,128,512]{2,1,0:T(8,128)(2,1)S(1)}, bf16[3,128,512]{2,1,0:T(8,128)(2,1)}, u32[]{:S(2)}) %copy-start.3) | copy-done | bytes 393240
  1.0 0.9 %collective-permute-done.partner = bf16[3,128,512]{2,1,0:T(8,128)(2,1)S(1)} collective-permute-done((bf16[3,128,512]{2,1,0:T(8,128)(2,1)}, bf16[3,128,512]{2,1,0:T(8,128)(2,1)S(1)}, u32[]{:S(2)}, u32[]{:S(2)}) %collective-permute-start) | collective-permute-done | bytes 393248 | tf_op jit(solution)/shard_map/ppermute | solution.py:480
  1.9 0.2 shard_map.137
  2.2 5.6 %collective-permute-start.1 = (bf16[128,512]{1,0:T(8,128)(2,1)S(1)}, bf16[128,512]{1,0:T(8,128)(2,1)S(1)}, u32[]{:S(2)}, u32[]{:S(2)}) collective-permute-start(bf16[128,512]{1,0:T(8,128)(2,1)S(1)} %get-tuple-element.32), channel_id=1, source_target_pairs={{0,0},{1,8},{2,2},{3,10},{4,4},{5,12},{6,6},{7,14},{8,1},{9,9},{10... | collective-permute-start | bytes 393224 | tf_op jit(solution)/shard_map/ppermute | solution.py:494
  7.8 1.1 %collective-permute-start.2 = (bf16[128,512]{1,0:T(8,128)(2,1)S(1)}, bf16[128,512]{1,0:T(8,128)(2,1)S(1)}, u32[]{:S(2)}, u32[]{:S(2)}) collective-permute-start(bf16[128,512]{1,0:T(8,128)(2,1)S(1)} %get-tuple-element.33), channel_id=1, source_target_pairs={{0,2},{1,10},{2,0},{3,8},{4,6},{5,14},{6,4},{7,12},{8,3},{9,11},{1... | collective-permute-start | bytes 393224 | tf_op jit(solution)/shard_map/ppermute | solution.py:494
  8.9 3.6 %collective-permute-start.3 = (bf16[128,512]{1,0:T(8,128)(2,1)S(1)}, bf16[128,512]{1,0:T(8,128)(2,1)S(1)}, u32[]{:S(2)}, u32[]{:S(2)}) collective-permute-start(bf16[128,512]{1,0:T(8,128)(2,1)S(1)} %get-tuple-element.34), channel_id=1, source_target_pairs={{0,4},{1,12},{2,6},{3,14},{4,0},{5,8},{6,2},{7,10},{8,5},{9,13},{1... | collective-permute-start | bytes 393224 | tf_op jit(solution)/shard_map/ppermute | solution.py:494
  12.5 4.6 %collective-permute-done.2.refs_1_ = bf16[128,512]{1,0:T(8,128)(2,1)S(1)} collective-permute-done((bf16[128,512]{1,0:T(8,128)(2,1)S(1)}, bf16[128,512]{1,0:T(8,128)(2,1)S(1)}, u32[]{:S(2)}, u32[]{:S(2)}) %collective-permute-start.2) | collective-permute-done | bytes 131104 | tf_op jit(solution)/shard_map/ppermute | solution.py:494
  17.0 0.5 collective-permute-start.7
  17.6 2.1 %collective-permute-done.4.refs_3_ = bf16[128,512]{1,0:T(8,128)(2,1)S(1)} collective-permute-done((bf16[128,512]{1,0:T(8,128)(2,1)S(1)}, bf16[128,512]{1,0:T(8,128)(2,1)S(1)}, u32[]{:S(2)}, u32[]{:S(2)}) %collective-permute-start.4) | collective-permute-done | bytes 131104 | tf_op jit(solution)/shard_map/ppermute | solution.py:494
  19.6 2.3 %copy.15 = bf16[24,3,3,8,768]{4,3,2,1,0:T(8,128)(2,1)S(1)} copy(bf16[24,3,3,8,768]{4,0,2,3,1:T(8,128)(2,1)} %bitcast.13) | data formatting | bytes 5308416 | tf_op jit(solution)/shard_map/transpose | solution.py:511
  22.0 0.5 pad.4
  22.6 2.1 %shard_map.138.embedded = bf16[264,768]{1,0:T(8,128)(2,1)S(1)} custom-call(bf16[128,512]{1,0:T(8,128)(2,1)S(1)} %collective-permute-done.1.refs_0_, bf16[128,512]{1,0:T(8,128)(2,1)S(1)} %collective-permute-done.2.refs_1_, bf16[128,512]{1,0:T(8,128)(2,1)S(1)} %collective-permute-done.3.refs_2_, bf16[128,512]{1,0:T(8,128)(2,1)S(1)} %collective-permute-done.4.refs_3_, ...), custom_call_target="tpu_custom_call" | custom-call | flops 1207959552 | bytes 6291456 | tf_op jit(solution)/shard_map/pallas_call | solution.py:31
  24.8 2.0 %shard_map.139 = (bf16[264,768]{1,0:T(8,128)(2,1)S(1)}, bf16[256,768]{1,0:T(8,128)(2,1)S(1)}, bf16[256,64]{1,0:T(8,128)(2,1)S(1)}, bf16[256,64]{1,0:T(8,128)(2,1...) custom-call(bf16[264,768]{1,0:T(8,128)(2,1)S(1)} %shard_map.138.embe, ...), custom_call_target="tpu_custom_call" | custom-call | flops 327155712 | bytes 4194304 | tf_op jit(solution)/shard_map/pallas_call | solution.py:31
  26.8 0.6 %collective-permute-start.9 = (bf16[400,128]{1,0:T(8,128)(2,1)S(1)}, bf16[400,128]{1,0:T(8,128)(2,1)S(1)}, u32[]{:S(2)}, u32[]{:S(2)}) collective-permute-start(bf16[400,128]{1,0:T(8,128)(2,1)S(1)} %get-tuple-element.41), channel_id=1, source_target_pairs={{0,1},{1,0},{2,3},{3,2},{4,5},{5,4},{6,7},{7,6},{8,9},{9,8},{10,11... | collective-permute-start | bytes 307208 | tf_op jit(solution)/shard_map/ppermute | solution.py:480
  27.4 1.3 %shard_map.140 = (bf16[256,768]{1,0:T(8,128)(2,1)S(1)}, f32[72,768]{1,0:T(8,128)S(1)}) custom-call(bf16[264,768]{1,0:T(8,128)(2,1)S(1)} %get-tuple-element.36.normed, bf16[256,24]{1,0:T(8,128)(2,1)S(1)} %get-tuple-element.37.scales, bf16[64,256]{1,0:T(8,128)(2,1)S(1)} %get-tuple-element.38.b_t, bf16[768,1664]{1,0:T(8,128)(2,1)S(1)} %copy-done, ...), custom_call_target="tpu_custom_call" | custom-call | flops 327155712 | bytes 4194304 | tf_op jit(solution)/shard_map/pallas_call | solution.py:31
  28.7 0.1 shard_map.141
  28.8 0.2 collective-permute-start.10
  29.0 2.9 %collective-permute-start.11 = (bf16[400,128]{1,0:T(8,128)(2,1)S(1)}, bf16[400,128]{1,0:T(8,128)(2,1)S(1)}, u32[]{:S(2)}, u32[]{:S(2)}) collective-permute-start(bf16[400,128]{1,0:T(8,128)(2,1)S(1)} %get-tuple-element.43), channel_id=1, source_target_pairs={{0,4},{2,6},{4,0},{6,2},{8,12},{10,14},{12,8},{14,10},{1,5},{3,7},... | collective-permute-start | bytes 307208 | tf_op jit(solution)/shard_map/ppermute | solution.py:480
  31.9 1.3 %collective-permute-done.10.refs_1_ = bf16[400,128]{1,0:T(8,128)(2,1)S(1)} collective-permute-done((bf16[400,128]{1,0:T(8,128)(2,1)S(1)}, bf16[400,128]{1,0:T(8,128)(2,1)S(1)}, u32[]{:S(2)}, u32[]{:S(2)}) %collective-permute-start.10) | collective-permute-done | bytes 102432 | tf_op jit(solution)/shard_map/ppermute | solution.py:480
  33.3 1.6 %collective-permute-done.11.refs_2_ = bf16[400,128]{1,0:T(8,128)(2,1)S(1)} collective-permute-done((bf16[400,128]{1,0:T(8,128)(2,1)S(1)}, bf16[400,128]{1,0:T(8,128)(2,1)S(1)}, u32[]{:S(2)}, u32[]{:S(2)}) %collective-permute-start.11) | collective-permute-done | bytes 102432 | tf_op jit(solution)/shard_map/ppermute | solution.py:480
  34.8 1.8 %collective-permute-done.12.refs_3_ = bf16[400,128]{1,0:T(8,128)(2,1)S(1)} collective-permute-done((bf16[400,128]{1,0:T(8,128)(2,1)S(1)}, bf16[400,128]{1,0:T(8,128)(2,1)S(1)}, u32[]{:S(2)}, u32[]{:S(2)}) %collective-permute-start.12) | collective-permute-done | bytes 102432 | tf_op jit(solution)/shard_map/ppermute | solution.py:480
  36.6 0.2 shard_map.142
  36.8 2.9 %collective-permute-start.13 = (bf16[400,128]{1,0:T(8,128)(2,1)S(1)}, bf16[400,128]{1,0:T(8,128)(2,1)S(1)}, u32[]{:S(2)}, u32[]{:S(2)}) collective-permute-start(bf16[400,128]{1,0:T(8,128)(2,1)S(1)} %get-tuple-element.46), channel_id=1, source_target_pairs={{0,8},{2,10},{4,12},{6,14},{8,0},{10,2},{12,4},{14,6},{1,9},{3,11}... | collective-permute-start | bytes 307208 | tf_op jit(solution)/shard_map/ppermute | solution.py:480
  39.7 1.7 %shard_map.145.local_theirs = f32[256,768]{1,0:T(8,128)S(1)} custom-call(f32[24]{0:T(128)S(1)} %copy-done.6, bf16[256,768]{1,0:T(8,128)(2,1)S(1)} %get-tuple-element.53.x, bf16[256,64]{1,0:T(8,128)(2,1)S(1)} %get-tuple-element.49.b_mat, bf16[256,64]{1,0:T(8,128)(2,1)S(1)} %get-tuple-element.50.c_mat, f32[256,24]{1,0:T(8,128)S(1)} %get-tuple-element.51.step, ...), custom_call_target="tpu_custom_call" | custom-call | flops 201326592 | bytes 2097152 | tf_op jit(solution)/shard_map/pallas_call | solution.py:31
  41.5 1.8 %collective-permute-done.13.refs_2_ = bf16[400,128]{1,0:T(8,128)(2,1)S(1)} collective-permute-done((bf16[400,128]{1,0:T(8,128)(2,1)S(1)}, bf16[400,128]{1,0:T(8,128)(2,1)S(1)}, u32[]{:S(2)}, u32[]{:S(2)}) %collective-permute-start.13) | collective-permute-done | bytes 102432 | tf_op jit(solution)/shard_map/ppermute | solution.py:480
  43.3 0.1 shard_map.143
  43.4 2.6 %collective-permute-start.14 = (bf16[64,768]{1,0:T(8,128)(2,1)S(1)}, bf16[64,768]{1,0:T(8,128)(2,1)S(1)}, u32[]{:S(2)}, u32[]{:S(2)}) collective-permute-start(bf16[64,768]{1,0:T(8,128)(2,1)S(1)} %get-tuple-element.47), channel_id=1, source_target_pairs={{0,1},{1,0},{2,3},{3,2},{4,5},{5,4},{6,7},{7,6},{8,9},{9,8},{10,11... | collective-permute-start | bytes 294920 | tf_op jit(solution)/shard_map/ppermute | solution.py:480
  45.9 1.8 %shard_map.144.local_mine = f32[256,768]{1,0:T(8,128)S(1)} custom-call(f32[24]{0:T(128)S(1)} %copy-done.6, bf16[256,768]{1,0:T(8,128)(2,1)S(1)} %get-tuple-element.48.x, bf16[256,64]{1,0:T(8,128)(2,1)S(1)} %get-tuple-element.49.b_mat, bf16[256,64]{1,0:T(8,128)(2,1)S(1)} %get-tuple-element.50.c_mat, f32[256,24]{1,0:T(8,128)S(1)} %get-tuple-element.51.step, ...), custom_call_target="tpu_custom_call" | custom-call | flops 201326592 | bytes 2097152 | tf_op jit(solution)/shard_map/pallas_call | solution.py:31
  47.7 1.4 %shard_map.146 = (f32[256,1536]{1,0:T(8,128)S(1)}, f32[256,1536]{1,0:T(8,128)S(1)}) custom-call(bf16[264,768]{1,0:T(8,128)(2,1)S(1)} %get-tuple-element.36.normed, bf16[768,1536]{1,0:T(8,128)(2,1)S(1)} %copy-done.2, f32[256,768]{1,0:T(8,128)S(1)} %shard_map.144.local_mine, f32[256,768]{1,0:T(8,128)S(1)} %shard_map.145.local_theirs, ...), custom_call_target="tpu_custom_call" | custom-call | flops 603979776 | bytes 4194304 | tf_op jit(solution)/shard_map/pallas_call | solution.py:31
  49.1 0.3 copy-done.1
  49.4 0.7 %shard_map.147 = (f32[256,768]{1,0:T(8,128)S(1)}, f32[256,128]{1,0:T(8,128)S(1)}) custom-call(bf16[64,768]{1,0:T(8,128)(2,1)S(1)} %get-tuple-element.56.mine, f32[256,1536]{1,0:T(8,128)S(1)} %get-tuple-element.54.own, f32[256,1536]{1,0:T(8,128)S(1)} %get-tuple-element.55.factor, bf16[256,64]{1,0:T(8,128)(2,1)S(1)} %get-tuple-element.50.c_mat, ...), custom_call_target="tpu_custom_call" | custom-call | flops 301989888 | bytes 4194304 | tf_op jit(solution)/shard_map/pallas_call | solution.py:31
  50.1 1.4 %shard_map.148 = bf16[256,768]{1,0:T(8,128)(2,1)} custom-call(bf16[64,768]{1,0:T(8,128)(2,1)S(1)} %collective-permute-done.14.theirs, f32[256,1536]{1,0:T(8,128)S(1)} %get-tuple-element.54.own, f32[256,1536]{1,0:T(8,128)S(1)} %get-tuple-element.55.factor, bf16[256,64]{1,0:T(8,128)(2,1)S(1)} %get-tuple-element.50.c_mat, f32[1,1536]{1,0:T(1,128)S(1)} %reshape.35.out_gain, ...), custom_call_target="tpu_custom_call" | custom-call | flops 301989888 | bytes 4194304 | tf_op jit(solution)/shard_map/pallas_call | solution.py:31
  (43 shorter events, 0.2 us)
Async XLA Ops:
  0.0 1.9 %collective-permute-start = (bf16[3,128,512]{2,1,0:T(8,128)(2,1)}, bf16[3,128,512]{2,1,0:T(8,128)(2,1)S(1)}, u32[]{:S(2)}, u32[]{:S(2)}) collective-permute-start(bf16[3,128,512]{2,1,0:T(8,128)(2,1)} %pixels.1), channel_id=1, source_target_pairs={{0,1},{1,0},{2,3},{3,2},{4,5},{5,4},{6,7},{7,6},{8,9},{9,8},{10,11... | collective-permute-start | bytes 1179656 | tf_op jit(solution)/shard_map/ppermute | solution.py:480
  0.0 1.0 %copy-start.3 = (bf16[3,128,512]{2,1,0:T(8,128)(2,1)S(1)}, bf16[3,128,512]{2,1,0:T(8,128)(2,1)}, u32[]{:S(2)}) copy-start(bf16[3,128,512]{2,1,0:T(8,128)(2,1)} %pixels.1) | copy-start | bytes 1179652
  2.2 10.3 %collective-permute-start.1 = (bf16[128,512]{1,0:T(8,128)(2,1)S(1)}, bf16[128,512]{1,0:T(8,128)(2,1)S(1)}, u32[]{:S(2)}, u32[]{:S(2)}) collective-permute-start(bf16[128,512]{1,0:T(8,128)(2,1)S(1)} %get-tuple-element.32), channel_id=1, source_target_pairs={{0,0},{1,8},{2,2},{3,10},{4,4},{5,12},{6,6},{7,14},{8,1},{9,9},{10... | collective-permute-start | bytes 393224 | tf_op jit(solution)/shard_map/ppermute | solution.py:494
  7.8 9.3 %collective-permute-start.2 = (bf16[128,512]{1,0:T(8,128)(2,1)S(1)}, bf16[128,512]{1,0:T(8,128)(2,1)S(1)}, u32[]{:S(2)}, u32[]{:S(2)}) collective-permute-start(bf16[128,512]{1,0:T(8,128)(2,1)S(1)} %get-tuple-element.33), channel_id=1, source_target_pairs={{0,2},{1,10},{2,0},{3,8},{4,6},{5,14},{6,4},{7,12},{8,3},{9,11},{1... | collective-permute-start | bytes 393224 | tf_op jit(solution)/shard_map/ppermute | solution.py:494
  8.9 8.2 %collective-permute-start.3 = (bf16[128,512]{1,0:T(8,128)(2,1)S(1)}, bf16[128,512]{1,0:T(8,128)(2,1)S(1)}, u32[]{:S(2)}, u32[]{:S(2)}) collective-permute-start(bf16[128,512]{1,0:T(8,128)(2,1)S(1)} %get-tuple-element.34), channel_id=1, source_target_pairs={{0,4},{1,12},{2,6},{3,14},{4,0},{5,8},{6,2},{7,10},{8,5},{9,13},{1... | collective-permute-start | bytes 393224 | tf_op jit(solution)/shard_map/ppermute | solution.py:494
  12.4 7.2 %collective-permute-start.4 = (bf16[128,512]{1,0:T(8,128)(2,1)S(1)}, bf16[128,512]{1,0:T(8,128)(2,1)S(1)}, u32[]{:S(2)}, u32[]{:S(2)}) collective-permute-start(bf16[128,512]{1,0:T(8,128)(2,1)S(1)} %get-tuple-element.35), channel_id=1, source_target_pairs={{0,6},{1,14},{2,4},{3,12},{4,2},{5,10},{6,0},{7,8},{8,7},{9,15},{1... | collective-permute-start | bytes 393224 | tf_op jit(solution)/shard_map/ppermute | solution.py:494
  12.4 10.1 %collective-permute-start.5 = (bf16[128,512]{1,0:T(8,128)(2,1)S(1)}, bf16[128,512]{1,0:T(8,128)(2,1)S(1)}, u32[]{:S(2)}, u32[]{:S(2)}) collective-permute-start(bf16[128,512]{1,0:T(8,128)(2,1)S(1)} %collective-permute-done.1.refs_0_), channel_id=1, source_target_pairs={{0,1},{1,0},{2,3},{3,2},{4,5},{5,4},{6,7},{7,6},{8,9},{9,8},{10,11... | collective-permute-start | bytes 393224 | tf_op jit(solution)/shard_map/ppermute | solution.py:480
  17.0 5.5 %collective-permute-start.6 = (bf16[128,512]{1,0:T(8,128)(2,1)S(1)}, bf16[128,512]{1,0:T(8,128)(2,1)S(1)}, u32[]{:S(2)}, u32[]{:S(2)}) collective-permute-start(bf16[128,512]{1,0:T(8,128)(2,1)S(1)} %collective-permute-done.2.refs_1_), channel_id=1, source_target_pairs={{0,1},{1,0},{2,3},{3,2},{4,5},{5,4},{6,7},{7,6},{8,9},{9,8},{10,11... | collective-permute-start | bytes 393224 | tf_op jit(solution)/shard_map/ppermute | solution.py:480
  17.0 5.5 %collective-permute-start.7 = (bf16[128,512]{1,0:T(8,128)(2,1)S(1)}, bf16[128,512]{1,0:T(8,128)(2,1)S(1)}, u32[]{:S(2)}, u32[]{:S(2)}) collective-permute-start(bf16[128,512]{1,0:T(8,128)(2,1)S(1)} %collective-permute-done.3.refs_2_), channel_id=1, source_target_pairs={{0,1},{1,0},{2,3},{3,2},{4,5},{5,4},{6,7},{7,6},{8,9},{9,8},{10,11... | collective-permute-start | bytes 393224 | tf_op jit(solution)/shard_map/ppermute | solution.py:480
  19.6 2.9 %collective-permute-start.8 = (bf16[128,512]{1,0:T(8,128)(2,1)S(1)}, bf16[128,512]{1,0:T(8,128)(2,1)S(1)}, u32[]{:S(2)}, u32[]{:S(2)}) collective-permute-start(bf16[128,512]{1,0:T(8,128)(2,1)S(1)} %collective-permute-done.4.refs_3_), channel_id=1, source_target_pairs={{0,1},{1,0},{2,3},{3,2},{4,5},{5,4},{6,7},{7,6},{8,9},{9,8},{10,11... | collective-permute-start | bytes 393224 | tf_op jit(solution)/shard_map/ppermute | solution.py:480
  19.6 2.3 %copy-start.11 = (f32[768]{0:T(1024)S(1)}, f32[768]{0:T(1024)}, u32[]{:S(2)}) copy-start(f32[768]{0:T(1024)} %param.16) | copy-start | bytes 9220
  19.6 2.3 %copy-start.10 = (f32[1664]{0:T(1024)S(1)}, f32[1664]{0:T(1024)}, u32[]{:S(2)}) copy-start(f32[1664]{0:T(1024)} %param.24) | copy-start | bytes 19972
  19.6 2.4 %copy-start.12 = (f32[768]{0:T(1024)S(1)}, f32[768]{0:T(1024)}, u32[]{:S(2)}) copy-start(f32[768]{0:T(1024)} %param.17) | copy-start | bytes 9220
  22.6 2.2 %copy-start = (bf16[768,1664]{1,0:T(8,128)(2,1)S(1)}, bf16[768,1664]{1,0:T(8,128)(2,1)}, u32[]{:S(2)}) copy-start(bf16[768,1664]{1,0:T(8,128)(2,1)} %mix_weight.3) | copy-start | bytes 7667716
  22.6 2.2 %copy-start.4 = (f32[4,1664]{1,0:T(4,128)S(1)}, f32[4,1664]{1,0:T(4,128)}, u32[]{:S(2)}) copy-start(f32[4,1664]{1,0:T(4,128)} %conv_weight.3) | copy-start | bytes 79876
  22.6 2.2 %copy-start.5 = (bf16[768,24]{0,1:T(8,128)(2,1)S(1)}, bf16[768,24]{0,1:T(8,128)(2,1)}, u32[]{:S(2)}) copy-start(bf16[768,24]{0,1:T(8,128)(2,1)} %param.20) | copy-start | bytes 110596
  22.6 2.2 %copy-start.7 = (f32[24]{0:T(128)S(1)}, f32[24]{0:T(128)}, u32[]{:S(2)}) copy-start(f32[24]{0:T(128)} %param.21) | copy-start | bytes 292
  22.6 2.2 %copy-start.8 = (f32[24]{0:T(128)S(1)}, f32[24]{0:T(128)}, u32[]{:S(2)}) copy-start(f32[24]{0:T(128)} %param.22) | copy-start | bytes 292
  26.8 12.9 %copy-start.9 = (f32[1536]{0:T(1024)S(1)}, f32[1536]{0:T(1024)}, u32[]{:S(2)}) copy-start(f32[1536]{0:T(1024)} %param.26) | copy-start | bytes 18436
  26.8 12.9 %copy-start.6 = (f32[24]{0:T(128)S(1)}, f32[24]{0:T(128)}, u32[]{:S(2)}) copy-start(f32[24]{0:T(128)} %skip.3) | copy-start | bytes 292
  26.8 1.9 %collective-permute-start.9 = (bf16[400,128]{1,0:T(8,128)(2,1)S(1)}, bf16[400,128]{1,0:T(8,128)(2,1)S(1)}, u32[]{:S(2)}, u32[]{:S(2)}) collective-permute-start(bf16[400,128]{1,0:T(8,128)(2,1)S(1)} %get-tuple-element.41), channel_id=1, source_target_pairs={{0,1},{1,0},{2,3},{3,2},{4,5},{5,4},{6,7},{7,6},{8,9},{9,8},{10,11... | collective-permute-start | bytes 307208 | tf_op jit(solution)/shard_map/ppermute | solution.py:480
  28.7 19.0 %copy-start.2 = (bf16[768,1536]{1,0:T(8,128)(2,1)S(1)}, bf16[768,1536]{1,0:T(8,128)(2,1)}, u32[]{:S(2)}) copy-start(bf16[768,1536]{1,0:T(8,128)(2,1)} %gate_weight.1) | copy-start | bytes 7077892
  28.8 4.5 %collective-permute-start.10 = (bf16[400,128]{1,0:T(8,128)(2,1)S(1)}, bf16[400,128]{1,0:T(8,128)(2,1)S(1)}, u32[]{:S(2)}, u32[]{:S(2)}) collective-permute-start(bf16[400,128]{1,0:T(8,128)(2,1)S(1)} %get-tuple-element.43), channel_id=1, source_target_pairs={{0,2},{2,0},{4,6},{6,4},{8,10},{10,8},{12,14},{14,12},{1,3},{3,1},... | collective-permute-start | bytes 307208 | tf_op jit(solution)/shard_map/ppermute | solution.py:480
  29.0 5.9 %collective-permute-start.11 = (bf16[400,128]{1,0:T(8,128)(2,1)S(1)}, bf16[400,128]{1,0:T(8,128)(2,1)S(1)}, u32[]{:S(2)}, u32[]{:S(2)}) collective-permute-start(bf16[400,128]{1,0:T(8,128)(2,1)S(1)} %get-tuple-element.43), channel_id=1, source_target_pairs={{0,4},{2,6},{4,0},{6,2},{8,12},{10,14},{12,8},{14,10},{1,5},{3,7},... | collective-permute-start | bytes 307208 | tf_op jit(solution)/shard_map/ppermute | solution.py:480
  31.9 4.8 %collective-permute-start.12 = (bf16[400,128]{1,0:T(8,128)(2,1)S(1)}, bf16[400,128]{1,0:T(8,128)(2,1)S(1)}, u32[]{:S(2)}, u32[]{:S(2)}) collective-permute-start(bf16[400,128]{1,0:T(8,128)(2,1)S(1)} %get-tuple-element.43), channel_id=1, source_target_pairs={{0,6},{2,4},{4,2},{6,0},{8,14},{10,12},{12,10},{14,8},{1,7},{3,5},... | collective-permute-start | bytes 307208 | tf_op jit(solution)/shard_map/ppermute | solution.py:480
  36.8 6.4 %collective-permute-start.13 = (bf16[400,128]{1,0:T(8,128)(2,1)S(1)}, bf16[400,128]{1,0:T(8,128)(2,1)S(1)}, u32[]{:S(2)}, u32[]{:S(2)}) collective-permute-start(bf16[400,128]{1,0:T(8,128)(2,1)S(1)} %get-tuple-element.46), channel_id=1, source_target_pairs={{0,8},{2,10},{4,12},{6,14},{8,0},{10,2},{12,4},{14,6},{1,9},{3,11}... | collective-permute-start | bytes 307208 | tf_op jit(solution)/shard_map/ppermute | solution.py:480
  43.4 6.7 %collective-permute-start.14 = (bf16[64,768]{1,0:T(8,128)(2,1)S(1)}, bf16[64,768]{1,0:T(8,128)(2,1)S(1)}, u32[]{:S(2)}, u32[]{:S(2)}) collective-permute-start(bf16[64,768]{1,0:T(8,128)(2,1)S(1)} %get-tuple-element.47), channel_id=1, source_target_pairs={{0,1},{1,0},{2,3},{3,2},{4,5},{5,4},{6,7},{7,6},{8,9},{9,8},{10,11... | collective-permute-start | bytes 294920 | tf_op jit(solution)/shard_map/ppermute | solution.py:480
  47.7 1.7 %copy-start.1 = (bf16[1536,768]{1,0:T(8,128)(2,1)S(1)}, bf16[1536,768]{1,0:T(8,128)(2,1)}, u32[]{:S(2)}) copy-start(bf16[1536,768]{1,0:T(8,128)(2,1)} %out_weight.3) | copy-start | bytes 7077892

commit v8 on v7

--- a/solution.py
+++ b/solution.py
@@ -152,8 +152,10 @@
         part = tail[pixel, 8 + shift : 16 + shift, :]
         wide[tokens:, offset * 128 : (offset + 1) * 128] = part.astype(BF16)
     place_beside(tokens, 0, wide, beside)
-    grid = jnp.dot(wide[...], weight[...], preferred_element_type=F32)
-    out[...] = (grid + bias[...]).astype(BF16)
+    for first in range(0, D, 256):
+        lanes = slice(first, first + 256)
+        grid = jnp.dot(wide[...], weight[:, lanes], preferred_element_type=F32)
+        out[:, lanes] = (grid + bias[:, lanes]).astype(BF16)
 
 
 def spread_matrix():
@@ -184,7 +186,7 @@
 
 def half_inputs(which, normed, mix_weight, conv_weight, conv_bias, x_out):
     half = E // 2
-    chunk = 256
+    chunk = 384
     parts = []
     spans = [
         pl.ds(pl.multiple_of(which * half + first, 128), chunk) for first in range(0, half, chunk)

time: 51.7 us -> 51.5 us (level)
  transfers between devices with their start and end apart: 15 -> 15, of which waited for: 7 -> 7; matrix products, arithmetic and copies ran while one was open for 5% -> 6% of each run, Pallas kernels for 13% -> 13%
where the time goes in v8:
time: 51.5 us; the launch traced here: 51.3 us
  starting transfers between devices  20 us (39%)
  waiting for transfers between devices  14.1 us (27%)
  Pallas kernels  12.7 us (25%)
  local copies, waits for them, and re-layouts  4.15 us (8%)
    pallas_call x13, Pallas kernels, call(): pl.pallas_call(kernel, out_shape=outs, in_specs=[pl.BlockSpec(memory_spac...  12.7 us
    ppermute x4, starting transfers between devices, across(): return lax.ppermute(block, ('cols', 'rows'), pairs)  10.3 us
    ppermute x11, starting transfers between devices, swap(): lax.ppermute(block, axis, [(i, i ^ bit) for i in range(lax.axis_size(axis...  9.72 us
    ppermute x11, waiting for transfers between devices, swap(): lax.ppermute(block, axis, [(i, i ^ bit) for i in range(lax.axis_size(axis...  7.39 us
    ppermute x4, waiting for transfers between devices, across(): return lax.ppermute(block, ('cols', 'rows'), pairs)  6.67 us
    transpose x1, local copies, waits for them, and re-layouts, embed_by_rows(): patch_weight.reshape(3, 8, KERNEL, CHAN, D).transpose(2, 0, 3, 1, 4)  2.29 us
    unnamed x26, local copies, waits for them, and re-layouts  1.33 us
  transfers between devices with their start and end apart: 15, of which 7 were waited for; matrix products, arithmetic and copies ran while one was open for 6% of the time, Pallas kernels for 13%

profile of v8, /device:TPU:1, one launch (start us, length us, event | category | flops | bytes accessed | tf_op | source)
XLA Modules:
  0.0 51.3 jit_solution(17885534008965194323)
XLA Ops:
  0.0 1.0 %copy-done.3 = bf16[3,128,512]{2,1,0:T(8,128)(2,1)S(1)} copy-done((bf16[3,128,512]{2,1,0:T(8,128)(2,1)S(1)}, bf16[3,128,512]{2,1,0:T(8,128)(2,1)}, u32[]{:S(2)}) %copy-start.3) | copy-done | bytes 393240
  1.0 0.9 %collective-permute-done.partner = bf16[3,128,512]{2,1,0:T(8,128)(2,1)S(1)} collective-permute-done((bf16[3,128,512]{2,1,0:T(8,128)(2,1)}, bf16[3,128,512]{2,1,0:T(8,128)(2,1)S(1)}, u32[]{:S(2)}, u32[]{:S(2)}) %collective-permute-start) | collective-permute-done | bytes 393248 | tf_op jit(solution)/shard_map/ppermute | solution.py:482
  1.9 0.2 shard_map.137
  2.2 5.6 %collective-permute-start.1 = (bf16[128,512]{1,0:T(8,128)(2,1)S(1)}, bf16[128,512]{1,0:T(8,128)(2,1)S(1)}, u32[]{:S(2)}, u32[]{:S(2)}) collective-permute-start(bf16[128,512]{1,0:T(8,128)(2,1)S(1)} %get-tuple-element.32), channel_id=1, source_target_pairs={{0,0},{1,8},{2,2},{3,10},{4,4},{5,12},{6,6},{7,14},{8,1},{9,9},{10... | collective-permute-start | bytes 393224 | tf_op jit(solution)/shard_map/ppermute | solution.py:496
  7.8 1.1 %collective-permute-start.2 = (bf16[128,512]{1,0:T(8,128)(2,1)S(1)}, bf16[128,512]{1,0:T(8,128)(2,1)S(1)}, u32[]{:S(2)}, u32[]{:S(2)}) collective-permute-start(bf16[128,512]{1,0:T(8,128)(2,1)S(1)} %get-tuple-element.33), channel_id=1, source_target_pairs={{0,2},{1,10},{2,0},{3,8},{4,6},{5,14},{6,4},{7,12},{8,3},{9,11},{1... | collective-permute-start | bytes 393224 | tf_op jit(solution)/shard_map/ppermute | solution.py:496
  8.9 3.6 %collective-permute-start.3 = (bf16[128,512]{1,0:T(8,128)(2,1)S(1)}, bf16[128,512]{1,0:T(8,128)(2,1)S(1)}, u32[]{:S(2)}, u32[]{:S(2)}) collective-permute-start(bf16[128,512]{1,0:T(8,128)(2,1)S(1)} %get-tuple-element.34), channel_id=1, source_target_pairs={{0,4},{1,12},{2,6},{3,14},{4,0},{5,8},{6,2},{7,10},{8,5},{9,13},{1... | collective-permute-start | bytes 393224 | tf_op jit(solution)/shard_map/ppermute | solution.py:496
  12.5 4.6 %collective-permute-done.2.refs_1_ = bf16[128,512]{1,0:T(8,128)(2,1)S(1)} collective-permute-done((bf16[128,512]{1,0:T(8,128)(2,1)S(1)}, bf16[128,512]{1,0:T(8,128)(2,1)S(1)}, u32[]{:S(2)}, u32[]{:S(2)}) %collective-permute-start.2) | collective-permute-done | bytes 131104 | tf_op jit(solution)/shard_map/ppermute | solution.py:496
  17.0 0.5 collective-permute-start.7
  17.6 2.1 %collective-permute-done.4.refs_3_ = bf16[128,512]{1,0:T(8,128)(2,1)S(1)} collective-permute-done((bf16[128,512]{1,0:T(8,128)(2,1)S(1)}, bf16[128,512]{1,0:T(8,128)(2,1)S(1)}, u32[]{:S(2)}, u32[]{:S(2)}) %collective-permute-start.4) | collective-permute-done | bytes 131104 | tf_op jit(solution)/shard_map/ppermute | solution.py:496
  19.6 2.3 %copy.15 = bf16[24,3,3,8,768]{4,3,2,1,0:T(8,128)(2,1)S(1)} copy(bf16[24,3,3,8,768]{4,0,2,3,1:T(8,128)(2,1)} %bitcast.13) | data formatting | bytes 5308416 | tf_op jit(solution)/shard_map/transpose | solution.py:513
  22.0 0.5 %pad.4 = bf16[24,128,768]{2,1,0:T(8,128)(2,1)S(1)} pad(bf16[24,72,768]{2,1,0:T(8,128)(2,1)S(1)} %bitcast.12, bf16[]{:T(256)} %constant.2.clone.1), padding=0_0x0_56x0_0 | pad | bytes 7372802 | tf_op jit(solution)/shard_map/jit(_pad)/pad | solution.py:514
  22.6 2.1 %shard_map.138.embedded = bf16[264,768]{1,0:T(8,128)(2,1)S(1)} custom-call(bf16[128,512]{1,0:T(8,128)(2,1)S(1)} %collective-permute-done.1.refs_0_, bf16[128,512]{1,0:T(8,128)(2,1)S(1)} %collective-permute-done.2.refs_1_, bf16[128,512]{1,0:T(8,128)(2,1)S(1)} %collective-permute-done.3.refs_2_, bf16[128,512]{1,0:T(8,128)(2,1)S(1)} %collective-permute-done.4.refs_3_, ...), custom_call_target="tpu_custom_call" | custom-call | flops 1207959552 | bytes 6291456 | tf_op jit(solution)/shard_map/pallas_call | solution.py:31
  24.8 1.9 %shard_map.139 = (bf16[264,768]{1,0:T(8,128)(2,1)S(1)}, bf16[256,768]{1,0:T(8,128)(2,1)S(1)}, bf16[256,64]{1,0:T(8,128)(2,1)S(1)}, bf16[256,64]{1,0:T(8,128)(2,1...) custom-call(bf16[264,768]{1,0:T(8,128)(2,1)S(1)} %shard_map.138.embe, ...), custom_call_target="tpu_custom_call" | custom-call | flops 327155712 | bytes 4194304 | tf_op jit(solution)/shard_map/pallas_call | solution.py:31
  26.7 0.6 %collective-permute-start.9 = (bf16[400,128]{1,0:T(8,128)(2,1)S(1)}, bf16[400,128]{1,0:T(8,128)(2,1)S(1)}, u32[]{:S(2)}, u32[]{:S(2)}) collective-permute-start(bf16[400,128]{1,0:T(8,128)(2,1)S(1)} %get-tuple-element.41), channel_id=1, source_target_pairs={{0,1},{1,0},{2,3},{3,2},{4,5},{5,4},{6,7},{7,6},{8,9},{9,8},{10,11... | collective-permute-start | bytes 307208 | tf_op jit(solution)/shard_map/ppermute | solution.py:482
  27.3 1.2 %shard_map.140 = (bf16[256,768]{1,0:T(8,128)(2,1)S(1)}, f32[72,768]{1,0:T(8,128)S(1)}) custom-call(bf16[264,768]{1,0:T(8,128)(2,1)S(1)} %get-tuple-element.36.normed, bf16[256,24]{1,0:T(8,128)(2,1)S(1)} %get-tuple-element.37.scales, bf16[64,256]{1,0:T(8,128)(2,1)S(1)} %get-tuple-element.38.b_t, bf16[768,1664]{1,0:T(8,128)(2,1)S(1)} %copy-done, ...), custom_call_target="tpu_custom_call" | custom-call | flops 327155712 | bytes 4194304 | tf_op jit(solution)/shard_map/pallas_call | solution.py:31
  28.6 0.1 shard_map.141
  28.6 0.2 collective-permute-start.10
  28.8 2.9 %collective-permute-start.11 = (bf16[400,128]{1,0:T(8,128)(2,1)S(1)}, bf16[400,128]{1,0:T(8,128)(2,1)S(1)}, u32[]{:S(2)}, u32[]{:S(2)}) collective-permute-start(bf16[400,128]{1,0:T(8,128)(2,1)S(1)} %get-tuple-element.43), channel_id=1, source_target_pairs={{0,4},{2,6},{4,0},{6,2},{8,12},{10,14},{12,8},{14,10},{1,5},{3,7},... | collective-permute-start | bytes 307208 | tf_op jit(solution)/shard_map/ppermute | solution.py:482
  31.8 1.3 %collective-permute-done.10.refs_1_ = bf16[400,128]{1,0:T(8,128)(2,1)S(1)} collective-permute-done((bf16[400,128]{1,0:T(8,128)(2,1)S(1)}, bf16[400,128]{1,0:T(8,128)(2,1)S(1)}, u32[]{:S(2)}, u32[]{:S(2)}) %collective-permute-start.10) | collective-permute-done | bytes 102432 | tf_op jit(solution)/shard_map/ppermute | solution.py:482
  33.1 1.6 %collective-permute-done.11.refs_2_ = bf16[400,128]{1,0:T(8,128)(2,1)S(1)} collective-permute-done((bf16[400,128]{1,0:T(8,128)(2,1)S(1)}, bf16[400,128]{1,0:T(8,128)(2,1)S(1)}, u32[]{:S(2)}, u32[]{:S(2)}) %collective-permute-start.11) | collective-permute-done | bytes 102432 | tf_op jit(solution)/shard_map/ppermute | solution.py:482
  34.7 1.8 %collective-permute-done.12.refs_3_ = bf16[400,128]{1,0:T(8,128)(2,1)S(1)} collective-permute-done((bf16[400,128]{1,0:T(8,128)(2,1)S(1)}, bf16[400,128]{1,0:T(8,128)(2,1)S(1)}, u32[]{:S(2)}, u32[]{:S(2)}) %collective-permute-start.12) | collective-permute-done | bytes 102432 | tf_op jit(solution)/shard_map/ppermute | solution.py:482
  36.5 0.2 shard_map.142
  36.7 2.9 %collective-permute-start.13 = (bf16[400,128]{1,0:T(8,128)(2,1)S(1)}, bf16[400,128]{1,0:T(8,128)(2,1)S(1)}, u32[]{:S(2)}, u32[]{:S(2)}) collective-permute-start(bf16[400,128]{1,0:T(8,128)(2,1)S(1)} %get-tuple-element.46), channel_id=1, source_target_pairs={{0,8},{2,10},{4,12},{6,14},{8,0},{10,2},{12,4},{14,6},{1,9},{3,11}... | collective-permute-start | bytes 307208 | tf_op jit(solution)/shard_map/ppermute | solution.py:482
  39.6 1.7 %shard_map.145.local_theirs = f32[256,768]{1,0:T(8,128)S(1)} custom-call(f32[24]{0:T(128)S(1)} %copy-done.6, bf16[256,768]{1,0:T(8,128)(2,1)S(1)} %get-tuple-element.53.x, bf16[256,64]{1,0:T(8,128)(2,1)S(1)} %get-tuple-element.49.b_mat, bf16[256,64]{1,0:T(8,128)(2,1)S(1)} %get-tuple-element.50.c_mat, f32[256,24]{1,0:T(8,128)S(1)} %get-tuple-element.51.step, ...), custom_call_target="tpu_custom_call" | custom-call | flops 201326592 | bytes 2097152 | tf_op jit(solution)/shard_map/pallas_call | solution.py:31
  41.3 1.8 %collective-permute-done.13.refs_2_ = bf16[400,128]{1,0:T(8,128)(2,1)S(1)} collective-permute-done((bf16[400,128]{1,0:T(8,128)(2,1)S(1)}, bf16[400,128]{1,0:T(8,128)(2,1)S(1)}, u32[]{:S(2)}, u32[]{:S(2)}) %collective-permute-start.13) | collective-permute-done | bytes 102432 | tf_op jit(solution)/shard_map/ppermute | solution.py:482
  43.1 0.1 shard_map.143
  43.2 2.6 %collective-permute-start.14 = (bf16[64,768]{1,0:T(8,128)(2,1)S(1)}, bf16[64,768]{1,0:T(8,128)(2,1)S(1)}, u32[]{:S(2)}, u32[]{:S(2)}) collective-permute-start(bf16[64,768]{1,0:T(8,128)(2,1)S(1)} %get-tuple-element.47), channel_id=1, source_target_pairs={{0,1},{1,0},{2,3},{3,2},{4,5},{5,4},{6,7},{7,6},{8,9},{9,8},{10,11... | collective-permute-start | bytes 294920 | tf_op jit(solution)/shard_map/ppermute | solution.py:482
  45.8 1.8 %shard_map.144.local_mine = f32[256,768]{1,0:T(8,128)S(1)} custom-call(f32[24]{0:T(128)S(1)} %copy-done.6, bf16[256,768]{1,0:T(8,128)(2,1)S(1)} %get-tuple-element.48.x, bf16[256,64]{1,0:T(8,128)(2,1)S(1)} %get-tuple-element.49.b_mat, bf16[256,64]{1,0:T(8,128)(2,1)S(1)} %get-tuple-element.50.c_mat, f32[256,24]{1,0:T(8,128)S(1)} %get-tuple-element.51.step, ...), custom_call_target="tpu_custom_call" | custom-call | flops 201326592 | bytes 2097152 | tf_op jit(solution)/shard_map/pallas_call | solution.py:31
  47.6 1.4 %shard_map.146 = (f32[256,1536]{1,0:T(8,128)S(1)}, f32[256,1536]{1,0:T(8,128)S(1)}) custom-call(bf16[264,768]{1,0:T(8,128)(2,1)S(1)} %get-tuple-element.36.normed, bf16[768,1536]{1,0:T(8,128)(2,1)S(1)} %copy-done.2, f32[256,768]{1,0:T(8,128)S(1)} %shard_map.144.local_mine, f32[256,768]{1,0:T(8,128)S(1)} %shard_map.145.local_theirs, ...), custom_call_target="tpu_custom_call" | custom-call | flops 603979776 | bytes 4194304 | tf_op jit(solution)/shard_map/pallas_call | solution.py:31
  48.9 0.3 copy-done.1
  49.2 0.7 %shard_map.147 = (f32[256,768]{1,0:T(8,128)S(1)}, f32[256,128]{1,0:T(8,128)S(1)}) custom-call(bf16[64,768]{1,0:T(8,128)(2,1)S(1)} %get-tuple-element.56.mine, f32[256,1536]{1,0:T(8,128)S(1)} %get-tuple-element.54.own, f32[256,1536]{1,0:T(8,128)S(1)} %get-tuple-element.55.factor, bf16[256,64]{1,0:T(8,128)(2,1)S(1)} %get-tuple-element.50.c_mat, ...), custom_call_target="tpu_custom_call" | custom-call | flops 301989888 | bytes 4194304 | tf_op jit(solution)/shard_map/pallas_call | solution.py:31
  49.9 1.4 %shard_map.148 = bf16[256,768]{1,0:T(8,128)(2,1)} custom-call(bf16[64,768]{1,0:T(8,128)(2,1)S(1)} %collective-permute-done.14.theirs, f32[256,1536]{1,0:T(8,128)S(1)} %get-tuple-element.54.own, f32[256,1536]{1,0:T(8,128)S(1)} %get-tuple-element.55.factor, bf16[256,64]{1,0:T(8,128)(2,1)S(1)} %get-tuple-element.50.c_mat, f32[1,1536]{1,0:T(1,128)S(1)} %reshape.35.out_gain, ...), custom_call_target="tpu_custom_call" | custom-call | flops 301989888 | bytes 4194304 | tf_op jit(solution)/shard_map/pallas_call | solution.py:31
  (43 shorter events, 0.2 us)
Async XLA Ops:
  0.0 1.9 %collective-permute-start = (bf16[3,128,512]{2,1,0:T(8,128)(2,1)}, bf16[3,128,512]{2,1,0:T(8,128)(2,1)S(1)}, u32[]{:S(2)}, u32[]{:S(2)}) collective-permute-start(bf16[3,128,512]{2,1,0:T(8,128)(2,1)} %pixels.1), channel_id=1, source_target_pairs={{0,1},{1,0},{2,3},{3,2},{4,5},{5,4},{6,7},{7,6},{8,9},{9,8},{10,11... | collective-permute-start | bytes 1179656 | tf_op jit(solution)/shard_map/ppermute | solution.py:482
  0.0 1.0 %copy-start.3 = (bf16[3,128,512]{2,1,0:T(8,128)(2,1)S(1)}, bf16[3,128,512]{2,1,0:T(8,128)(2,1)}, u32[]{:S(2)}) copy-start(bf16[3,128,512]{2,1,0:T(8,128)(2,1)} %pixels.1) | copy-start | bytes 1179652
  2.2 10.3 %collective-permute-start.1 = (bf16[128,512]{1,0:T(8,128)(2,1)S(1)}, bf16[128,512]{1,0:T(8,128)(2,1)S(1)}, u32[]{:S(2)}, u32[]{:S(2)}) collective-permute-start(bf16[128,512]{1,0:T(8,128)(2,1)S(1)} %get-tuple-element.32), channel_id=1, source_target_pairs={{0,0},{1,8},{2,2},{3,10},{4,4},{5,12},{6,6},{7,14},{8,1},{9,9},{10... | collective-permute-start | bytes 393224 | tf_op jit(solution)/shard_map/ppermute | solution.py:496
  7.8 9.3 %collective-permute-start.2 = (bf16[128,512]{1,0:T(8,128)(2,1)S(1)}, bf16[128,512]{1,0:T(8,128)(2,1)S(1)}, u32[]{:S(2)}, u32[]{:S(2)}) collective-permute-start(bf16[128,512]{1,0:T(8,128)(2,1)S(1)} %get-tuple-element.33), channel_id=1, source_target_pairs={{0,2},{1,10},{2,0},{3,8},{4,6},{5,14},{6,4},{7,12},{8,3},{9,11},{1... | collective-permute-start | bytes 393224 | tf_op jit(solution)/shard_map/ppermute | solution.py:496
  8.9 8.2 %collective-permute-start.3 = (bf16[128,512]{1,0:T(8,128)(2,1)S(1)}, bf16[128,512]{1,0:T(8,128)(2,1)S(1)}, u32[]{:S(2)}, u32[]{:S(2)}) collective-permute-start(bf16[128,512]{1,0:T(8,128)(2,1)S(1)} %get-tuple-element.34), channel_id=1, source_target_pairs={{0,4},{1,12},{2,6},{3,14},{4,0},{5,8},{6,2},{7,10},{8,5},{9,13},{1... | collective-permute-start | bytes 393224 | tf_op jit(solution)/shard_map/ppermute | solution.py:496
  12.4 7.2 %collective-permute-start.4 = (bf16[128,512]{1,0:T(8,128)(2,1)S(1)}, bf16[128,512]{1,0:T(8,128)(2,1)S(1)}, u32[]{:S(2)}, u32[]{:S(2)}) collective-permute-start(bf16[128,512]{1,0:T(8,128)(2,1)S(1)} %get-tuple-element.35), channel_id=1, source_target_pairs={{0,6},{1,14},{2,4},{3,12},{4,2},{5,10},{6,0},{7,8},{8,7},{9,15},{1... | collective-permute-start | bytes 393224 | tf_op jit(solution)/shard_map/ppermute | solution.py:496
  12.4 10.1 %collective-permute-start.5 = (bf16[128,512]{1,0:T(8,128)(2,1)S(1)}, bf16[128,512]{1,0:T(8,128)(2,1)S(1)}, u32[]{:S(2)}, u32[]{:S(2)}) collective-permute-start(bf16[128,512]{1,0:T(8,128)(2,1)S(1)} %collective-permute-done.1.refs_0_), channel_id=1, source_target_pairs={{0,1},{1,0},{2,3},{3,2},{4,5},{5,4},{6,7},{7,6},{8,9},{9,8},{10,11... | collective-permute-start | bytes 393224 | tf_op jit(solution)/shard_map/ppermute | solution.py:482
  17.0 5.5 %collective-permute-start.6 = (bf16[128,512]{1,0:T(8,128)(2,1)S(1)}, bf16[128,512]{1,0:T(8,128)(2,1)S(1)}, u32[]{:S(2)}, u32[]{:S(2)}) collective-permute-start(bf16[128,512]{1,0:T(8,128)(2,1)S(1)} %collective-permute-done.2.refs_1_), channel_id=1, source_target_pairs={{0,1},{1,0},{2,3},{3,2},{4,5},{5,4},{6,7},{7,6},{8,9},{9,8},{10,11... | collective-permute-start | bytes 393224 | tf_op jit(solution)/shard_map/ppermute | solution.py:482
  17.0 5.5 %collective-permute-start.7 = (bf16[128,512]{1,0:T(8,128)(2,1)S(1)}, bf16[128,512]{1,0:T(8,128)(2,1)S(1)}, u32[]{:S(2)}, u32[]{:S(2)}) collective-permute-start(bf16[128,512]{1,0:T(8,128)(2,1)S(1)} %collective-permute-done.3.refs_2_), channel_id=1, source_target_pairs={{0,1},{1,0},{2,3},{3,2},{4,5},{5,4},{6,7},{7,6},{8,9},{9,8},{10,11... | collective-permute-start | bytes 393224 | tf_op jit(solution)/shard_map/ppermute | solution.py:482
  19.6 2.9 %collective-permute-start.8 = (bf16[128,512]{1,0:T(8,128)(2,1)S(1)}, bf16[128,512]{1,0:T(8,128)(2,1)S(1)}, u32[]{:S(2)}, u32[]{:S(2)}) collective-permute-start(bf16[128,512]{1,0:T(8,128)(2,1)S(1)} %collective-permute-done.4.refs_3_), channel_id=1, source_target_pairs={{0,1},{1,0},{2,3},{3,2},{4,5},{5,4},{6,7},{7,6},{8,9},{9,8},{10,11... | collective-permute-start | bytes 393224 | tf_op jit(solution)/shard_map/ppermute | solution.py:482
  19.6 2.3 %copy-start.11 = (f32[768]{0:T(1024)S(1)}, f32[768]{0:T(1024)}, u32[]{:S(2)}) copy-start(f32[768]{0:T(1024)} %param.16) | copy-start | bytes 9220
  19.6 2.3 %copy-start.10 = (f32[1664]{0:T(1024)S(1)}, f32[1664]{0:T(1024)}, u32[]{:S(2)}) copy-start(f32[1664]{0:T(1024)} %param.24) | copy-start | bytes 19972
  19.6 2.4 %copy-start.12 = (f32[768]{0:T(1024)S(1)}, f32[768]{0:T(1024)}, u32[]{:S(2)}) copy-start(f32[768]{0:T(1024)} %param.17) | copy-start | bytes 9220
  22.6 2.2 %copy-start = (bf16[768,1664]{1,0:T(8,128)(2,1)S(1)}, bf16[768,1664]{1,0:T(8,128)(2,1)}, u32[]{:S(2)}) copy-start(bf16[768,1664]{1,0:T(8,128)(2,1)} %mix_weight.3) | copy-start | bytes 7667716
  22.6 2.2 %copy-start.4 = (f32[4,1664]{1,0:T(4,128)S(1)}, f32[4,1664]{1,0:T(4,128)}, u32[]{:S(2)}) copy-start(f32[4,1664]{1,0:T(4,128)} %conv_weight.3) | copy-start | bytes 79876
  22.6 2.2 %copy-start.5 = (bf16[768,24]{0,1:T(8,128)(2,1)S(1)}, bf16[768,24]{0,1:T(8,128)(2,1)}, u32[]{:S(2)}) copy-start(bf16[768,24]{0,1:T(8,128)(2,1)} %param.20) | copy-start | bytes 110596
  22.6 2.2 %copy-start.7 = (f32[24]{0:T(128)S(1)}, f32[24]{0:T(128)}, u32[]{:S(2)}) copy-start(f32[24]{0:T(128)} %param.21) | copy-start | bytes 292
  22.6 2.1 %copy-start.8 = (f32[24]{0:T(128)S(1)}, f32[24]{0:T(128)}, u32[]{:S(2)}) copy-start(f32[24]{0:T(128)} %param.22) | copy-start | bytes 292
  26.7 12.9 %copy-start.9 = (f32[1536]{0:T(1024)S(1)}, f32[1536]{0:T(1024)}, u32[]{:S(2)}) copy-start(f32[1536]{0:T(1024)} %param.26) | copy-start | bytes 18436
  26.7 12.9 %copy-start.6 = (f32[24]{0:T(128)S(1)}, f32[24]{0:T(128)}, u32[]{:S(2)}) copy-start(f32[24]{0:T(128)} %skip.3) | copy-start | bytes 292
  26.7 1.9 %collective-permute-start.9 = (bf16[400,128]{1,0:T(8,128)(2,1)S(1)}, bf16[400,128]{1,0:T(8,128)(2,1)S(1)}, u32[]{:S(2)}, u32[]{:S(2)}) collective-permute-start(bf16[400,128]{1,0:T(8,128)(2,1)S(1)} %get-tuple-element.41), channel_id=1, source_target_pairs={{0,1},{1,0},{2,3},{3,2},{4,5},{5,4},{6,7},{7,6},{8,9},{9,8},{10,11... | collective-permute-start | bytes 307208 | tf_op jit(solution)/shard_map/ppermute | solution.py:482
  28.5 19.0 %copy-start.2 = (bf16[768,1536]{1,0:T(8,128)(2,1)S(1)}, bf16[768,1536]{1,0:T(8,128)(2,1)}, u32[]{:S(2)}) copy-start(bf16[768,1536]{1,0:T(8,128)(2,1)} %gate_weight.1) | copy-start | bytes 7077892
  28.6 4.5 %collective-permute-start.10 = (bf16[400,128]{1,0:T(8,128)(2,1)S(1)}, bf16[400,128]{1,0:T(8,128)(2,1)S(1)}, u32[]{:S(2)}, u32[]{:S(2)}) collective-permute-start(bf16[400,128]{1,0:T(8,128)(2,1)S(1)} %get-tuple-element.43), channel_id=1, source_target_pairs={{0,2},{2,0},{4,6},{6,4},{8,10},{10,8},{12,14},{14,12},{1,3},{3,1},... | collective-permute-start | bytes 307208 | tf_op jit(solution)/shard_map/ppermute | solution.py:482
  28.8 5.9 %collective-permute-start.11 = (bf16[400,128]{1,0:T(8,128)(2,1)S(1)}, bf16[400,128]{1,0:T(8,128)(2,1)S(1)}, u32[]{:S(2)}, u32[]{:S(2)}) collective-permute-start(bf16[400,128]{1,0:T(8,128)(2,1)S(1)} %get-tuple-element.43), channel_id=1, source_target_pairs={{0,4},{2,6},{4,0},{6,2},{8,12},{10,14},{12,8},{14,10},{1,5},{3,7},... | collective-permute-start | bytes 307208 | tf_op jit(solution)/shard_map/ppermute | solution.py:482
  31.7 4.8 %collective-permute-start.12 = (bf16[400,128]{1,0:T(8,128)(2,1)S(1)}, bf16[400,128]{1,0:T(8,128)(2,1)S(1)}, u32[]{:S(2)}, u32[]{:S(2)}) collective-permute-start(bf16[400,128]{1,0:T(8,128)(2,1)S(1)} %get-tuple-element.43), channel_id=1, source_target_pairs={{0,6},{2,4},{4,2},{6,0},{8,14},{10,12},{12,10},{14,8},{1,7},{3,5},... | collective-permute-start | bytes 307208 | tf_op jit(solution)/shard_map/ppermute | solution.py:482
  36.7 6.4 %collective-permute-start.13 = (bf16[400,128]{1,0:T(8,128)(2,1)S(1)}, bf16[400,128]{1,0:T(8,128)(2,1)S(1)}, u32[]{:S(2)}, u32[]{:S(2)}) collective-permute-start(bf16[400,128]{1,0:T(8,128)(2,1)S(1)} %get-tuple-element.46), channel_id=1, source_target_pairs={{0,8},{2,10},{4,12},{6,14},{8,0},{10,2},{12,4},{14,6},{1,9},{3,11}... | collective-permute-start | bytes 307208 | tf_op jit(solution)/shard_map/ppermute | solution.py:482
  43.2 6.7 %collective-permute-start.14 = (bf16[64,768]{1,0:T(8,128)(2,1)S(1)}, bf16[64,768]{1,0:T(8,128)(2,1)S(1)}, u32[]{:S(2)}, u32[]{:S(2)}) collective-permute-start(bf16[64,768]{1,0:T(8,128)(2,1)S(1)} %get-tuple-element.47), channel_id=1, source_target_pairs={{0,1},{1,0},{2,3},{3,2},{4,5},{5,4},{6,7},{7,6},{8,9},{9,8},{10,11... | collective-permute-start | bytes 294920 | tf_op jit(solution)/shard_map/ppermute | solution.py:482
  47.5 1.7 %copy-start.1 = (bf16[1536,768]{1,0:T(8,128)(2,1)S(1)}, bf16[1536,768]{1,0:T(8,128)(2,1)}, u32[]{:S(2)}) copy-start(bf16[1536,768]{1,0:T(8,128)(2,1)} %out_weight.3) | copy-start | bytes 7077892

commit v9 on v8

--- a/solution.py
+++ b/solution.py
@@ -465,14 +465,14 @@
     lanes = pl.ds(pl.multiple_of(which * half, 128), half)
     hidden, more = half_hidden(lanes, theirs, own, factor, c_mat, out_gain)
     scale = lax.rsqrt((squares[:, 0:1] + more) / own.shape[1] + 1e-05)
-    chunk = result.shape[2]
+    chunk = result.shape[1]
     copies = []
+    rest = jnp.dot(hidden, out_weight[lanes, :], preferred_element_type=F32)
     for place in range(result.shape[0]):
-        span = slice(place * chunk, (place + 1) * chunk)
-        rest = jnp.dot(hidden, out_weight[lanes, span], preferred_element_type=F32)
-        resid = embedded[:, span].astype(F32)[:-LEAD]
-        result[place] = ((product[:, span] + rest) * scale + resid).astype(BF16)
-        copies.append(pltpu.make_async_copy(result.at[place], out.at[:, span], sems.at[place]))
+        rows = slice(place * chunk, (place + 1) * chunk)
+        resid = embedded[rows, :].astype(F32)
+        result[place] = ((product[rows, :] + rest[rows]) * scale[rows] + resid).astype(BF16)
+        copies.append(pltpu.make_async_copy(result.at[place], out.at[rows, :], sems.at[place]))
         copies[-1].start()
     for copy in copies:
         copy.wait()
@@ -661,7 +661,7 @@
     )
     return call(
         finish_kernel, (theirs, *common, partial_sum, squares, embedded), shape((length, D)),
-        [pltpu.VMEM((3, length, D // 3), BF16), pltpu.SemaphoreType.DMA((3,))],
+        [pltpu.VMEM((8, length // 8, D), BF16), pltpu.SemaphoreType.DMA((8,))],
         flops=length * D * E, moved=4 << 20, limit=8, outside=True,
     )
 

time: 51.5 us -> 51.6 us (level)
  no operation moved by 1% of the time
where the time goes in v9:
time: 51.6 us; the launch traced here: 51.3 us
  starting transfers between devices  20 us (39%)
  waiting for transfers between devices  14.1 us (27%)
  Pallas kernels  12.8 us (25%)
  local copies, waits for them, and re-layouts  4.15 us (8%)
    pallas_call x13, Pallas kernels, call(): pl.pallas_call(kernel, out_shape=outs, in_specs=[pl.BlockSpec(memory_spac...  12.8 us
    ppermute x4, starting transfers between devices, across(): return lax.ppermute(block, ('cols', 'rows'), pairs)  10.3 us
    ppermute x11, starting transfers between devices, swap(): lax.ppermute(block, axis, [(i, i ^ bit) for i in range(lax.axis_size(axis...  9.72 us
    ppermute x11, waiting for transfers between devices, swap(): lax.ppermute(block, axis, [(i, i ^ bit) for i in range(lax.axis_size(axis...  7.39 us
    ppermute x4, waiting for transfers between devices, across(): return lax.ppermute(block, ('cols', 'rows'), pairs)  6.67 us
    transpose x1, local copies, waits for them, and re-layouts, embed_by_rows(): patch_weight.reshape(3, 8, KERNEL, CHAN, D).transpose(2, 0, 3, 1, 4)  2.29 us
    unnamed x26, local copies, waits for them, and re-layouts  1.33 us
  transfers between devices with their start and end apart: 15, of which 7 were waited for; matrix products, arithmetic and copies ran while one was open for 6% of the time, Pallas kernels for 13%

profile of v9, /device:TPU:1, one launch (start us, length us, event | category | flops | bytes accessed | tf_op | source)
XLA Modules:
  0.0 51.3 jit_solution(3294789423091063840)
XLA Ops:
  0.0 1.0 %copy-done.3 = bf16[3,128,512]{2,1,0:T(8,128)(2,1)S(1)} copy-done((bf16[3,128,512]{2,1,0:T(8,128)(2,1)S(1)}, bf16[3,128,512]{2,1,0:T(8,128)(2,1)}, u32[]{:S(2)}) %copy-start.3) | copy-done | bytes 393240
  1.0 0.9 %collective-permute-done.partner = bf16[3,128,512]{2,1,0:T(8,128)(2,1)S(1)} collective-permute-done((bf16[3,128,512]{2,1,0:T(8,128)(2,1)}, bf16[3,128,512]{2,1,0:T(8,128)(2,1)S(1)}, u32[]{:S(2)}, u32[]{:S(2)}) %collective-permute-start) | collective-permute-done | bytes 393248 | tf_op jit(solution)/shard_map/ppermute | solution.py:482
  1.9 0.2 shard_map.137
  2.2 5.6 %collective-permute-start.1 = (bf16[128,512]{1,0:T(8,128)(2,1)S(1)}, bf16[128,512]{1,0:T(8,128)(2,1)S(1)}, u32[]{:S(2)}, u32[]{:S(2)}) collective-permute-start(bf16[128,512]{1,0:T(8,128)(2,1)S(1)} %get-tuple-element.32), channel_id=1, source_target_pairs={{0,0},{1,8},{2,2},{3,10},{4,4},{5,12},{6,6},{7,14},{8,1},{9,9},{10... | collective-permute-start | bytes 393224 | tf_op jit(solution)/shard_map/ppermute | solution.py:496
  7.8 1.1 %collective-permute-start.2 = (bf16[128,512]{1,0:T(8,128)(2,1)S(1)}, bf16[128,512]{1,0:T(8,128)(2,1)S(1)}, u32[]{:S(2)}, u32[]{:S(2)}) collective-permute-start(bf16[128,512]{1,0:T(8,128)(2,1)S(1)} %get-tuple-element.33), channel_id=1, source_target_pairs={{0,2},{1,10},{2,0},{3,8},{4,6},{5,14},{6,4},{7,12},{8,3},{9,11},{1... | collective-permute-start | bytes 393224 | tf_op jit(solution)/shard_map/ppermute | solution.py:496
  8.9 3.6 %collective-permute-start.3 = (bf16[128,512]{1,0:T(8,128)(2,1)S(1)}, bf16[128,512]{1,0:T(8,128)(2,1)S(1)}, u32[]{:S(2)}, u32[]{:S(2)}) collective-permute-start(bf16[128,512]{1,0:T(8,128)(2,1)S(1)} %get-tuple-element.34), channel_id=1, source_target_pairs={{0,4},{1,12},{2,6},{3,14},{4,0},{5,8},{6,2},{7,10},{8,5},{9,13},{1... | collective-permute-start | bytes 393224 | tf_op jit(solution)/shard_map/ppermute | solution.py:496
  12.5 4.6 %collective-permute-done.2.refs_1_ = bf16[128,512]{1,0:T(8,128)(2,1)S(1)} collective-permute-done((bf16[128,512]{1,0:T(8,128)(2,1)S(1)}, bf16[128,512]{1,0:T(8,128)(2,1)S(1)}, u32[]{:S(2)}, u32[]{:S(2)}) %collective-permute-start.2) | collective-permute-done | bytes 131104 | tf_op jit(solution)/shard_map/ppermute | solution.py:496
  17.0 0.5 collective-permute-start.7
  17.6 2.1 %collective-permute-done.4.refs_3_ = bf16[128,512]{1,0:T(8,128)(2,1)S(1)} collective-permute-done((bf16[128,512]{1,0:T(8,128)(2,1)S(1)}, bf16[128,512]{1,0:T(8,128)(2,1)S(1)}, u32[]{:S(2)}, u32[]{:S(2)}) %collective-permute-start.4) | collective-permute-done | bytes 131104 | tf_op jit(solution)/shard_map/ppermute | solution.py:496
  19.6 2.3 %copy.15 = bf16[24,3,3,8,768]{4,3,2,1,0:T(8,128)(2,1)S(1)} copy(bf16[24,3,3,8,768]{4,0,2,3,1:T(8,128)(2,1)} %bitcast.13) | data formatting | bytes 5308416 | tf_op jit(solution)/shard_map/transpose | solution.py:513
  22.0 0.5 pad.4
  22.6 2.1 %shard_map.138.embedded = bf16[264,768]{1,0:T(8,128)(2,1)S(1)} custom-call(bf16[128,512]{1,0:T(8,128)(2,1)S(1)} %collective-permute-done.1.refs_0_, bf16[128,512]{1,0:T(8,128)(2,1)S(1)} %collective-permute-done.2.refs_1_, bf16[128,512]{1,0:T(8,128)(2,1)S(1)} %collective-permute-done.3.refs_2_, bf16[128,512]{1,0:T(8,128)(2,1)S(1)} %collective-permute-done.4.refs_3_, ...), custom_call_target="tpu_custom_call" | custom-call | flops 1207959552 | bytes 6291456 | tf_op jit(solution)/shard_map/pallas_call | solution.py:31
  24.8 1.9 %shard_map.139 = (bf16[264,768]{1,0:T(8,128)(2,1)S(1)}, bf16[256,768]{1,0:T(8,128)(2,1)S(1)}, bf16[256,64]{1,0:T(8,128)(2,1)S(1)}, bf16[256,64]{1,0:T(8,128)(2,1...) custom-call(bf16[264,768]{1,0:T(8,128)(2,1)S(1)} %shard_map.138.embe, ...), custom_call_target="tpu_custom_call" | custom-call | flops 327155712 | bytes 4194304 | tf_op jit(solution)/shard_map/pallas_call | solution.py:31
  26.7 0.6 %collective-permute-start.9 = (bf16[400,128]{1,0:T(8,128)(2,1)S(1)}, bf16[400,128]{1,0:T(8,128)(2,1)S(1)}, u32[]{:S(2)}, u32[]{:S(2)}) collective-permute-start(bf16[400,128]{1,0:T(8,128)(2,1)S(1)} %get-tuple-element.41), channel_id=1, source_target_pairs={{0,1},{1,0},{2,3},{3,2},{4,5},{5,4},{6,7},{7,6},{8,9},{9,8},{10,11... | collective-permute-start | bytes 307208 | tf_op jit(solution)/shard_map/ppermute | solution.py:482
  27.3 1.2 %shard_map.140 = (bf16[256,768]{1,0:T(8,128)(2,1)S(1)}, f32[72,768]{1,0:T(8,128)S(1)}) custom-call(bf16[264,768]{1,0:T(8,128)(2,1)S(1)} %get-tuple-element.36.normed, bf16[256,24]{1,0:T(8,128)(2,1)S(1)} %get-tuple-element.37.scales, bf16[64,256]{1,0:T(8,128)(2,1)S(1)} %get-tuple-element.38.b_t, bf16[768,1664]{1,0:T(8,128)(2,1)S(1)} %copy-done, ...), custom_call_target="tpu_custom_call" | custom-call | flops 327155712 | bytes 4194304 | tf_op jit(solution)/shard_map/pallas_call | solution.py:31
  28.6 0.1 shard_map.141
  28.6 0.2 collective-permute-start.10
  28.8 2.9 %collective-permute-start.11 = (bf16[400,128]{1,0:T(8,128)(2,1)S(1)}, bf16[400,128]{1,0:T(8,128)(2,1)S(1)}, u32[]{:S(2)}, u32[]{:S(2)}) collective-permute-start(bf16[400,128]{1,0:T(8,128)(2,1)S(1)} %get-tuple-element.43), channel_id=1, source_target_pairs={{0,4},{2,6},{4,0},{6,2},{8,12},{10,14},{12,8},{14,10},{1,5},{3,7},... | collective-permute-start | bytes 307208 | tf_op jit(solution)/shard_map/ppermute | solution.py:482
  31.8 1.3 %collective-permute-done.10.refs_1_ = bf16[400,128]{1,0:T(8,128)(2,1)S(1)} collective-permute-done((bf16[400,128]{1,0:T(8,128)(2,1)S(1)}, bf16[400,128]{1,0:T(8,128)(2,1)S(1)}, u32[]{:S(2)}, u32[]{:S(2)}) %collective-permute-start.10) | collective-permute-done | bytes 102432 | tf_op jit(solution)/shard_map/ppermute | solution.py:482
  33.1 1.6 %collective-permute-done.11.refs_2_ = bf16[400,128]{1,0:T(8,128)(2,1)S(1)} collective-permute-done((bf16[400,128]{1,0:T(8,128)(2,1)S(1)}, bf16[400,128]{1,0:T(8,128)(2,1)S(1)}, u32[]{:S(2)}, u32[]{:S(2)}) %collective-permute-start.11) | collective-permute-done | bytes 102432 | tf_op jit(solution)/shard_map/ppermute | solution.py:482
  34.7 1.8 %collective-permute-done.12.refs_3_ = bf16[400,128]{1,0:T(8,128)(2,1)S(1)} collective-permute-done((bf16[400,128]{1,0:T(8,128)(2,1)S(1)}, bf16[400,128]{1,0:T(8,128)(2,1)S(1)}, u32[]{:S(2)}, u32[]{:S(2)}) %collective-permute-start.12) | collective-permute-done | bytes 102432 | tf_op jit(solution)/shard_map/ppermute | solution.py:482
  36.5 0.2 shard_map.142
  36.7 2.9 %collective-permute-start.13 = (bf16[400,128]{1,0:T(8,128)(2,1)S(1)}, bf16[400,128]{1,0:T(8,128)(2,1)S(1)}, u32[]{:S(2)}, u32[]{:S(2)}) collective-permute-start(bf16[400,128]{1,0:T(8,128)(2,1)S(1)} %get-tuple-element.46), channel_id=1, source_target_pairs={{0,8},{2,10},{4,12},{6,14},{8,0},{10,2},{12,4},{14,6},{1,9},{3,11}... | collective-permute-start | bytes 307208 | tf_op jit(solution)/shard_map/ppermute | solution.py:482
  39.6 1.7 %shard_map.145.local_theirs = f32[256,768]{1,0:T(8,128)S(1)} custom-call(f32[24]{0:T(128)S(1)} %copy-done.6, bf16[256,768]{1,0:T(8,128)(2,1)S(1)} %get-tuple-element.53.x, bf16[256,64]{1,0:T(8,128)(2,1)S(1)} %get-tuple-element.49.b_mat, bf16[256,64]{1,0:T(8,128)(2,1)S(1)} %get-tuple-element.50.c_mat, f32[256,24]{1,0:T(8,128)S(1)} %get-tuple-element.51.step, ...), custom_call_target="tpu_custom_call" | custom-call | flops 201326592 | bytes 2097152 | tf_op jit(solution)/shard_map/pallas_call | solution.py:31
  41.3 1.8 %collective-permute-done.13.refs_2_ = bf16[400,128]{1,0:T(8,128)(2,1)S(1)} collective-permute-done((bf16[400,128]{1,0:T(8,128)(2,1)S(1)}, bf16[400,128]{1,0:T(8,128)(2,1)S(1)}, u32[]{:S(2)}, u32[]{:S(2)}) %collective-permute-start.13) | collective-permute-done | bytes 102432 | tf_op jit(solution)/shard_map/ppermute | solution.py:482
  43.1 0.1 shard_map.143
  43.2 2.6 %collective-permute-start.14 = (bf16[64,768]{1,0:T(8,128)(2,1)S(1)}, bf16[64,768]{1,0:T(8,128)(2,1)S(1)}, u32[]{:S(2)}, u32[]{:S(2)}) collective-permute-start(bf16[64,768]{1,0:T(8,128)(2,1)S(1)} %get-tuple-element.47), channel_id=1, source_target_pairs={{0,1},{1,0},{2,3},{3,2},{4,5},{5,4},{6,7},{7,6},{8,9},{9,8},{10,11... | collective-permute-start | bytes 294920 | tf_op jit(solution)/shard_map/ppermute | solution.py:482
  45.8 1.8 %shard_map.144.local_mine = f32[256,768]{1,0:T(8,128)S(1)} custom-call(f32[24]{0:T(128)S(1)} %copy-done.6, bf16[256,768]{1,0:T(8,128)(2,1)S(1)} %get-tuple-element.48.x, bf16[256,64]{1,0:T(8,128)(2,1)S(1)} %get-tuple-element.49.b_mat, bf16[256,64]{1,0:T(8,128)(2,1)S(1)} %get-tuple-element.50.c_mat, f32[256,24]{1,0:T(8,128)S(1)} %get-tuple-element.51.step, ...), custom_call_target="tpu_custom_call" | custom-call | flops 201326592 | bytes 2097152 | tf_op jit(solution)/shard_map/pallas_call | solution.py:31
  47.6 1.4 %shard_map.146 = (f32[256,1536]{1,0:T(8,128)S(1)}, f32[256,1536]{1,0:T(8,128)S(1)}) custom-call(bf16[264,768]{1,0:T(8,128)(2,1)S(1)} %get-tuple-element.36.normed, bf16[768,1536]{1,0:T(8,128)(2,1)S(1)} %copy-done.2, f32[256,768]{1,0:T(8,128)S(1)} %shard_map.144.local_mine, f32[256,768]{1,0:T(8,128)S(1)} %shard_map.145.local_theirs, ...), custom_call_target="tpu_custom_call" | custom-call | flops 603979776 | bytes 4194304 | tf_op jit(solution)/shard_map/pallas_call | solution.py:31
  48.9 0.3 copy-done.1
  49.2 0.7 %shard_map.147 = (f32[256,768]{1,0:T(8,128)S(1)}, f32[256,128]{1,0:T(8,128)S(1)}) custom-call(bf16[64,768]{1,0:T(8,128)(2,1)S(1)} %get-tuple-element.56.mine, f32[256,1536]{1,0:T(8,128)S(1)} %get-tuple-element.54.own, f32[256,1536]{1,0:T(8,128)S(1)} %get-tuple-element.55.factor, bf16[256,64]{1,0:T(8,128)(2,1)S(1)} %get-tuple-element.50.c_mat, ...), custom_call_target="tpu_custom_call" | custom-call | flops 301989888 | bytes 4194304 | tf_op jit(solution)/shard_map/pallas_call | solution.py:31
  49.9 1.4 %shard_map.148 = bf16[256,768]{1,0:T(8,128)(2,1)} custom-call(bf16[64,768]{1,0:T(8,128)(2,1)S(1)} %collective-permute-done.14.theirs, f32[256,1536]{1,0:T(8,128)S(1)} %get-tuple-element.54.own, f32[256,1536]{1,0:T(8,128)S(1)} %get-tuple-element.55.factor, bf16[256,64]{1,0:T(8,128)(2,1)S(1)} %get-tuple-element.50.c_mat, f32[1,1536]{1,0:T(1,128)S(1)} %reshape.35.out_gain, ...), custom_call_target="tpu_custom_call" | custom-call | flops 301989888 | bytes 4194304 | tf_op jit(solution)/shard_map/pallas_call | solution.py:31
  (43 shorter events, 0.2 us)
Async XLA Ops:
  0.0 1.9 %collective-permute-start = (bf16[3,128,512]{2,1,0:T(8,128)(2,1)}, bf16[3,128,512]{2,1,0:T(8,128)(2,1)S(1)}, u32[]{:S(2)}, u32[]{:S(2)}) collective-permute-start(bf16[3,128,512]{2,1,0:T(8,128)(2,1)} %pixels.1), channel_id=1, source_target_pairs={{0,1},{1,0},{2,3},{3,2},{4,5},{5,4},{6,7},{7,6},{8,9},{9,8},{10,11... | collective-permute-start | bytes 1179656 | tf_op jit(solution)/shard_map/ppermute | solution.py:482
  0.0 1.0 %copy-start.3 = (bf16[3,128,512]{2,1,0:T(8,128)(2,1)S(1)}, bf16[3,128,512]{2,1,0:T(8,128)(2,1)}, u32[]{:S(2)}) copy-start(bf16[3,128,512]{2,1,0:T(8,128)(2,1)} %pixels.1) | copy-start | bytes 1179652
  2.2 10.3 %collective-permute-start.1 = (bf16[128,512]{1,0:T(8,128)(2,1)S(1)}, bf16[128,512]{1,0:T(8,128)(2,1)S(1)}, u32[]{:S(2)}, u32[]{:S(2)}) collective-permute-start(bf16[128,512]{1,0:T(8,128)(2,1)S(1)} %get-tuple-element.32), channel_id=1, source_target_pairs={{0,0},{1,8},{2,2},{3,10},{4,4},{5,12},{6,6},{7,14},{8,1},{9,9},{10... | collective-permute-start | bytes 393224 | tf_op jit(solution)/shard_map/ppermute | solution.py:496
  7.8 9.3 %collective-permute-start.2 = (bf16[128,512]{1,0:T(8,128)(2,1)S(1)}, bf16[128,512]{1,0:T(8,128)(2,1)S(1)}, u32[]{:S(2)}, u32[]{:S(2)}) collective-permute-start(bf16[128,512]{1,0:T(8,128)(2,1)S(1)} %get-tuple-element.33), channel_id=1, source_target_pairs={{0,2},{1,10},{2,0},{3,8},{4,6},{5,14},{6,4},{7,12},{8,3},{9,11},{1... | collective-permute-start | bytes 393224 | tf_op jit(solution)/shard_map/ppermute | solution.py:496
  8.9 8.2 %collective-permute-start.3 = (bf16[128,512]{1,0:T(8,128)(2,1)S(1)}, bf16[128,512]{1,0:T(8,128)(2,1)S(1)}, u32[]{:S(2)}, u32[]{:S(2)}) collective-permute-start(bf16[128,512]{1,0:T(8,128)(2,1)S(1)} %get-tuple-element.34), channel_id=1, source_target_pairs={{0,4},{1,12},{2,6},{3,14},{4,0},{5,8},{6,2},{7,10},{8,5},{9,13},{1... | collective-permute-start | bytes 393224 | tf_op jit(solution)/shard_map/ppermute | solution.py:496
  12.4 7.2 %collective-permute-start.4 = (bf16[128,512]{1,0:T(8,128)(2,1)S(1)}, bf16[128,512]{1,0:T(8,128)(2,1)S(1)}, u32[]{:S(2)}, u32[]{:S(2)}) collective-permute-start(bf16[128,512]{1,0:T(8,128)(2,1)S(1)} %get-tuple-element.35), channel_id=1, source_target_pairs={{0,6},{1,14},{2,4},{3,12},{4,2},{5,10},{6,0},{7,8},{8,7},{9,15},{1... | collective-permute-start | bytes 393224 | tf_op jit(solution)/shard_map/ppermute | solution.py:496
  12.4 10.1 %collective-permute-start.5 = (bf16[128,512]{1,0:T(8,128)(2,1)S(1)}, bf16[128,512]{1,0:T(8,128)(2,1)S(1)}, u32[]{:S(2)}, u32[]{:S(2)}) collective-permute-start(bf16[128,512]{1,0:T(8,128)(2,1)S(1)} %collective-permute-done.1.refs_0_), channel_id=1, source_target_pairs={{0,1},{1,0},{2,3},{3,2},{4,5},{5,4},{6,7},{7,6},{8,9},{9,8},{10,11... | collective-permute-start | bytes 393224 | tf_op jit(solution)/shard_map/ppermute | solution.py:482
  17.0 5.5 %collective-permute-start.6 = (bf16[128,512]{1,0:T(8,128)(2,1)S(1)}, bf16[128,512]{1,0:T(8,128)(2,1)S(1)}, u32[]{:S(2)}, u32[]{:S(2)}) collective-permute-start(bf16[128,512]{1,0:T(8,128)(2,1)S(1)} %collective-permute-done.2.refs_1_), channel_id=1, source_target_pairs={{0,1},{1,0},{2,3},{3,2},{4,5},{5,4},{6,7},{7,6},{8,9},{9,8},{10,11... | collective-permute-start | bytes 393224 | tf_op jit(solution)/shard_map/ppermute | solution.py:482
  17.0 5.5 %collective-permute-start.7 = (bf16[128,512]{1,0:T(8,128)(2,1)S(1)}, bf16[128,512]{1,0:T(8,128)(2,1)S(1)}, u32[]{:S(2)}, u32[]{:S(2)}) collective-permute-start(bf16[128,512]{1,0:T(8,128)(2,1)S(1)} %collective-permute-done.3.refs_2_), channel_id=1, source_target_pairs={{0,1},{1,0},{2,3},{3,2},{4,5},{5,4},{6,7},{7,6},{8,9},{9,8},{10,11... | collective-permute-start | bytes 393224 | tf_op jit(solution)/shard_map/ppermute | solution.py:482
  19.6 2.9 %collective-permute-start.8 = (bf16[128,512]{1,0:T(8,128)(2,1)S(1)}, bf16[128,512]{1,0:T(8,128)(2,1)S(1)}, u32[]{:S(2)}, u32[]{:S(2)}) collective-permute-start(bf16[128,512]{1,0:T(8,128)(2,1)S(1)} %collective-permute-done.4.refs_3_), channel_id=1, source_target_pairs={{0,1},{1,0},{2,3},{3,2},{4,5},{5,4},{6,7},{7,6},{8,9},{9,8},{10,11... | collective-permute-start | bytes 393224 | tf_op jit(solution)/shard_map/ppermute | solution.py:482
  19.6 2.3 %copy-start.11 = (f32[768]{0:T(1024)S(1)}, f32[768]{0:T(1024)}, u32[]{:S(2)}) copy-start(f32[768]{0:T(1024)} %param.16) | copy-start | bytes 9220
  19.6 2.3 %copy-start.10 = (f32[1664]{0:T(1024)S(1)}, f32[1664]{0:T(1024)}, u32[]{:S(2)}) copy-start(f32[1664]{0:T(1024)} %param.24) | copy-start | bytes 19972
  19.6 2.4 %copy-start.12 = (f32[768]{0:T(1024)S(1)}, f32[768]{0:T(1024)}, u32[]{:S(2)}) copy-start(f32[768]{0:T(1024)} %param.17) | copy-start | bytes 9220
  22.6 2.2 %copy-start = (bf16[768,1664]{1,0:T(8,128)(2,1)S(1)}, bf16[768,1664]{1,0:T(8,128)(2,1)}, u32[]{:S(2)}) copy-start(bf16[768,1664]{1,0:T(8,128)(2,1)} %mix_weight.3) | copy-start | bytes 7667716
  22.6 2.2 %copy-start.4 = (f32[4,1664]{1,0:T(4,128)S(1)}, f32[4,1664]{1,0:T(4,128)}, u32[]{:S(2)}) copy-start(f32[4,1664]{1,0:T(4,128)} %conv_weight.3) | copy-start | bytes 79876
  22.6 2.2 %copy-start.5 = (bf16[768,24]{0,1:T(8,128)(2,1)S(1)}, bf16[768,24]{0,1:T(8,128)(2,1)}, u32[]{:S(2)}) copy-start(bf16[768,24]{0,1:T(8,128)(2,1)} %param.20) | copy-start | bytes 110596
  22.6 2.2 %copy-start.7 = (f32[24]{0:T(128)S(1)}, f32[24]{0:T(128)}, u32[]{:S(2)}) copy-start(f32[24]{0:T(128)} %param.21) | copy-start | bytes 292
  22.6 2.1 %copy-start.8 = (f32[24]{0:T(128)S(1)}, f32[24]{0:T(128)}, u32[]{:S(2)}) copy-start(f32[24]{0:T(128)} %param.22) | copy-start | bytes 292
  26.7 12.9 %copy-start.9 = (f32[1536]{0:T(1024)S(1)}, f32[1536]{0:T(1024)}, u32[]{:S(2)}) copy-start(f32[1536]{0:T(1024)} %param.26) | copy-start | bytes 18436
  26.7 12.9 %copy-start.6 = (f32[24]{0:T(128)S(1)}, f32[24]{0:T(128)}, u32[]{:S(2)}) copy-start(f32[24]{0:T(128)} %skip.3) | copy-start | bytes 292
  26.7 1.9 %collective-permute-start.9 = (bf16[400,128]{1,0:T(8,128)(2,1)S(1)}, bf16[400,128]{1,0:T(8,128)(2,1)S(1)}, u32[]{:S(2)}, u32[]{:S(2)}) collective-permute-start(bf16[400,128]{1,0:T(8,128)(2,1)S(1)} %get-tuple-element.41), channel_id=1, source_target_pairs={{0,1},{1,0},{2,3},{3,2},{4,5},{5,4},{6,7},{7,6},{8,9},{9,8},{10,11... | collective-permute-start | bytes 307208 | tf_op jit(solution)/shard_map/ppermute | solution.py:482
  28.5 19.0 %copy-start.2 = (bf16[768,1536]{1,0:T(8,128)(2,1)S(1)}, bf16[768,1536]{1,0:T(8,128)(2,1)}, u32[]{:S(2)}) copy-start(bf16[768,1536]{1,0:T(8,128)(2,1)} %gate_weight.1) | copy-start | bytes 7077892
  28.6 4.5 %collective-permute-start.10 = (bf16[400,128]{1,0:T(8,128)(2,1)S(1)}, bf16[400,128]{1,0:T(8,128)(2,1)S(1)}, u32[]{:S(2)}, u32[]{:S(2)}) collective-permute-start(bf16[400,128]{1,0:T(8,128)(2,1)S(1)} %get-tuple-element.43), channel_id=1, source_target_pairs={{0,2},{2,0},{4,6},{6,4},{8,10},{10,8},{12,14},{14,12},{1,3},{3,1},... | collective-permute-start | bytes 307208 | tf_op jit(solution)/shard_map/ppermute | solution.py:482
  28.8 5.9 %collective-permute-start.11 = (bf16[400,128]{1,0:T(8,128)(2,1)S(1)}, bf16[400,128]{1,0:T(8,128)(2,1)S(1)}, u32[]{:S(2)}, u32[]{:S(2)}) collective-permute-start(bf16[400,128]{1,0:T(8,128)(2,1)S(1)} %get-tuple-element.43), channel_id=1, source_target_pairs={{0,4},{2,6},{4,0},{6,2},{8,12},{10,14},{12,8},{14,10},{1,5},{3,7},... | collective-permute-start | bytes 307208 | tf_op jit(solution)/shard_map/ppermute | solution.py:482
  31.7 4.8 %collective-permute-start.12 = (bf16[400,128]{1,0:T(8,128)(2,1)S(1)}, bf16[400,128]{1,0:T(8,128)(2,1)S(1)}, u32[]{:S(2)}, u32[]{:S(2)}) collective-permute-start(bf16[400,128]{1,0:T(8,128)(2,1)S(1)} %get-tuple-element.43), channel_id=1, source_target_pairs={{0,6},{2,4},{4,2},{6,0},{8,14},{10,12},{12,10},{14,8},{1,7},{3,5},... | collective-permute-start | bytes 307208 | tf_op jit(solution)/shard_map/ppermute | solution.py:482
  36.7 6.4 %collective-permute-start.13 = (bf16[400,128]{1,0:T(8,128)(2,1)S(1)}, bf16[400,128]{1,0:T(8,128)(2,1)S(1)}, u32[]{:S(2)}, u32[]{:S(2)}) collective-permute-start(bf16[400,128]{1,0:T(8,128)(2,1)S(1)} %get-tuple-element.46), channel_id=1, source_target_pairs={{0,8},{2,10},{4,12},{6,14},{8,0},{10,2},{12,4},{14,6},{1,9},{3,11}... | collective-permute-start | bytes 307208 | tf_op jit(solution)/shard_map/ppermute | solution.py:482
  43.2 6.7 %collective-permute-start.14 = (bf16[64,768]{1,0:T(8,128)(2,1)S(1)}, bf16[64,768]{1,0:T(8,128)(2,1)S(1)}, u32[]{:S(2)}, u32[]{:S(2)}) collective-permute-start(bf16[64,768]{1,0:T(8,128)(2,1)S(1)} %get-tuple-element.47), channel_id=1, source_target_pairs={{0,1},{1,0},{2,3},{3,2},{4,5},{5,4},{6,7},{7,6},{8,9},{9,8},{10,11... | collective-permute-start | bytes 294920 | tf_op jit(solution)/shard_map/ppermute | solution.py:482
  47.5 1.7 %copy-start.1 = (bf16[1536,768]{1,0:T(8,128)(2,1)S(1)}, bf16[1536,768]{1,0:T(8,128)(2,1)}, u32[]{:S(2)}) copy-start(bf16[1536,768]{1,0:T(8,128)(2,1)} %out_weight.3) | copy-start | bytes 7077892
